TPU v7x, 32 devices: a whole 2x2x4 slice. The times are simulated.
32 devices in a mesh: dp: 8 (over y, x, core), shard: 4 (over z).
Axes of the slice: x: 2, y: 2, z: 4, core: 2. Of those that a mesh axis runs over, the one named last changes fastest.
Arguments:
- token_ids: int32 [64, 128], P(('dp', 'shard')), may hold values from 0 to 49151
- lengths: int32 [64], P(('dp', 'shard')), may hold values from 1 to 128, 6144 in all
- deal_order: int32 [64], replicated, may hold values from 0 to 63, each once
- embed_table: float32 [576, 49152], P('dp', 'shard'), may hold values from -0.4 to 0.4
- table_mom: float32 [576, 49152], P('dp', 'shard'), may hold values from -1 to 1
- table_avg: float32 [576, 49152], P('dp', 'shard'), may hold values from -0.4 to 0.4
- model_flat: float32 [7413120], P(('dp', 'shard')), may hold values from -1 to 2
- model_mom: float32 [7413120], P(('dp', 'shard')), may hold values from -1 to 1
- model_avg: float32 [7413120], P(('dp', 'shard')), may hold values from -1 to 2
Outputs:
- loss_total: float32 [], replicated
- seq_loss: float32 [64], P(('dp', 'shard'))
- slot_loss: float32 [64], P(('dp', 'shard'))
- grad_norm: float32 [], replicated
- table_grad: float32 [576, 49152], P('dp', 'shard')
- table_new: float32 [576, 49152], P('dp', 'shard')
- table_mom_new: float32 [576, 49152], P('dp', 'shard')
- table_avg_new: float32 [576, 49152], P('dp', 'shard')
- table_bf16: bfloat16 [576, 49152], P('dp', 'shard')
- model_grad: float32 [7413120], P(('dp', 'shard'))
- model_new: float32 [7413120], P(('dp', 'shard'))
- model_mom_new: float32 [7413120], P(('dp', 'shard'))
- model_avg_new: float32 [7413120], P(('dp', 'shard'))
- model_bf16: bfloat16 [7413120], P(('dp', 'shard'))
Inputs may be any that keep to these rules, and one draw needn't show every extreme that they name: The lengths add up to 6144 and one of them is 128. `deal_order`: every sequence number appears once.
All inputs are finite; a program needn't handle non-finite values. No bound on the sum of `lengths` on one device may be relied on, other than what follows from the above.
Results may differ from a plain program's by a relative error of at most 0.009.
Values may be sent and summed in bfloat16 or wider, within the bound.
No kernel may reach another device: no remote copies, remote signals or barrier semaphores. Data moves between devices by JAX's collectives and lax.ppermute only.
A program may use at most 448 MiB of HBM per device.

v0:
```python
import jax
import jax.numpy as jnp
from jax import lax
from jax.sharding import PartitionSpec as P

MODEL_WIDTH = 576
QUERY_HEADS = 9
KEY_VALUE_HEADS = 3
HEAD_SIZE = 64
FEED_UNITS = 1536
LAYERS = 2
MICRO = 2
LEN = 128
PL = 3540096
NP = 7413120


EPSILON = 1e-05
ROPE_BASE = 100000.0
CLIP_NORM = 0.01
LEARN_RATE = 6000.0
MOMENTUM = 0.9
AVERAGE_KEEP = 0.9
SECOND_WEIGHT = 0.3
MASKED_SCORE = -1e30


def combined_all(shard, axis, combine):
    everything = jax.tree.map(lambda part: lax.all_gather(part, axis), shard)
    first = jax.tree.map(lambda part: part[0], everything)

    def step(k, so_far):
        return combine(so_far, jax.tree.map(lambda part: part[k], everything))

    return lax.fori_loop(1, lax.axis_size(axis), step, first)


def rms_norm(values, gain_vec):
    return (
        values * lax.rsqrt(jnp.mean(values * values, axis=-1, keepdims=True) + EPSILON) * gain_vec
    )


def rope_tables(length):
    halves = HEAD_SIZE // 2
    inverse = ROPE_BASE ** (-jnp.arange(halves, dtype=jnp.float32) * 2.0 / HEAD_SIZE)
    angles = jnp.arange(length, dtype=jnp.float32)[:, None] * inverse[None, :]
    return (jnp.cos(angles), jnp.sin(angles))


def rotate(values, cosine, sine_table):
    halves = values.shape[-1] // 2
    first_half = values[..., :halves]
    second_half = values[..., halves:]
    cos_part = cosine[:, None, :]
    sin_part = sine_table[:, None, :]
    return jnp.concatenate(
        [
            first_half * cos_part - second_half * sin_part,
            second_half * cos_part + first_half * sin_part,
        ],
        axis=-1,
    )


def split_rope(packed_heads, cosine, sine_table):
    sequence_length = packed_heads.shape[0]
    query_rows = packed_heads[:, : QUERY_HEADS * HEAD_SIZE].reshape(
        sequence_length, QUERY_HEADS, HEAD_SIZE
    )
    key_matrix = packed_heads[
        :, QUERY_HEADS * HEAD_SIZE : (QUERY_HEADS + KEY_VALUE_HEADS) * HEAD_SIZE
    ].reshape(sequence_length, KEY_VALUE_HEADS, HEAD_SIZE)
    return (rotate(query_rows, cosine, sine_table), rotate(key_matrix, cosine, sine_table))


def swiglu(gate_up):
    return jax.nn.silu(gate_up[:, :FEED_UNITS]) * gate_up[:, FEED_UNITS:]


def unpack_layer(vector):
    head_arrangement = [
        (MODEL_WIDTH, (QUERY_HEADS + 2 * KEY_VALUE_HEADS) * HEAD_SIZE),
        (QUERY_HEADS * HEAD_SIZE, MODEL_WIDTH),
        (MODEL_WIDTH, 2 * FEED_UNITS),
        (FEED_UNITS, MODEL_WIDTH),
        (1, MODEL_WIDTH),
        (1, MODEL_WIDTH),
    ]
    pieces = []
    offset = 0
    for height, breadth in head_arrangement:
        pieces.append(vector[offset : offset + height * breadth].reshape(height, breadth))
        offset += height * breadth
    return (pieces[0], pieces[1], pieces[2], pieces[3], pieces[4][0], pieces[5][0])


def add_packed(flat, start, pieces):
    offset = start
    for piece in pieces:
        count_here = piece.size
        flat = flat.at[offset : offset + count_here].add(piece.reshape(-1))
        offset += count_here
    return flat


def attention_forward(query_reduced, key_reduced, value_reduced, length):
    sequence_length = query_reduced.shape[0]
    grouped_queries = query_reduced.reshape(
        sequence_length, KEY_VALUE_HEADS, QUERY_HEADS // KEY_VALUE_HEADS, HEAD_SIZE
    )
    scores = jnp.einsum(
        "mnya,lna->nyml", grouped_queries, key_reduced, preferred_element_type=jnp.float32
    ) * HEAD_SIZE ** (-0.5)
    places = jnp.arange(sequence_length)
    allowed = (places[None, :] <= places[:, None]) & (places[None, :] < length)
    attention_weights = jax.nn.softmax(jnp.where(allowed, scores, MASKED_SCORE), axis=-1)
    attended_rows = jnp.einsum(
        "ycvo,oyh->vych",
        attention_weights.astype(jnp.bfloat16),
        value_reduced,
        preferred_element_type=jnp.float32,
    )
    return (attention_weights, attended_rows.reshape(sequence_length, QUERY_HEADS * HEAD_SIZE))


def attention_backward(
    query_reduced, key_reduced, value_reduced, attention_weights, attended_gradient
):
    sequence_length = query_reduced.shape[0]
    heads_per_group = QUERY_HEADS // KEY_VALUE_HEADS
    grouped_gradient = attended_gradient.reshape(
        sequence_length, KEY_VALUE_HEADS, heads_per_group, HEAD_SIZE
    )
    grad_probs = jnp.einsum(
        "mnya,lna->nyml", grouped_gradient, value_reduced, preferred_element_type=jnp.float32
    )
    value_gradient = jnp.einsum(
        "vhuj,uvhc->jvc",
        attention_weights.astype(jnp.bfloat16),
        grouped_gradient,
        preferred_element_type=jnp.float32,
    )
    score_gradient = (
        attention_weights
        * (grad_probs - jnp.sum(grad_probs * attention_weights, axis=-1, keepdims=True))
    ).astype(jnp.bfloat16)
    grouped_queries = query_reduced.reshape(
        sequence_length, KEY_VALUE_HEADS, heads_per_group, HEAD_SIZE
    )
    grad_query = jnp.einsum(
        "ycvo,oyh->vych", score_gradient, key_reduced, preferred_element_type=jnp.float32
    ) * HEAD_SIZE ** (-0.5)
    grad_key = jnp.einsum(
        "vhuj,uvhc->jvc", score_gradient, grouped_queries, preferred_element_type=jnp.float32
    ) * HEAD_SIZE ** (-0.5)
    return (
        grad_query.reshape(sequence_length, QUERY_HEADS, HEAD_SIZE).astype(jnp.bfloat16),
        grad_key.astype(jnp.bfloat16),
        value_gradient.astype(jnp.bfloat16),
    )


def layer_forward(hidden, vector, length, cosine, sine_table):
    w_qkv, w_out, w_gateup, w_down, gain_one, gain_two = unpack_layer(vector)
    sequence_length = hidden.shape[0]
    normed, norm_one_pull = jax.vjp(rms_norm, hidden, gain_one.astype(jnp.float32))
    normed_low = normed.astype(jnp.bfloat16)
    query_key_value = jnp.dot(normed_low, w_qkv, preferred_element_type=jnp.float32)
    (query_rows, key_matrix), rope_pull = jax.vjp(
        lambda packed_heads: split_rope(packed_heads, cosine, sine_table), query_key_value
    )
    query_reduced = query_rows.astype(jnp.bfloat16)
    key_reduced = key_matrix.astype(jnp.bfloat16)
    value_reduced = (
        query_key_value[:, (QUERY_HEADS + KEY_VALUE_HEADS) * HEAD_SIZE :]
        .reshape(sequence_length, KEY_VALUE_HEADS, HEAD_SIZE)
        .astype(jnp.bfloat16)
    )
    attention_weights, attended_rows = attention_forward(
        query_reduced, key_reduced, value_reduced, length
    )
    attended_low = attended_rows.astype(jnp.bfloat16)
    mid_hidden = hidden + jnp.dot(attended_low, w_out, preferred_element_type=jnp.float32)
    normed_two, norm_two_pull = jax.vjp(rms_norm, mid_hidden, gain_two.astype(jnp.float32))
    normed_two_low = normed_two.astype(jnp.bfloat16)
    gate_up = jnp.dot(normed_two_low, w_gateup, preferred_element_type=jnp.float32)
    activated, swiglu_pull = jax.vjp(swiglu, gate_up)
    activated_low = activated.astype(jnp.bfloat16)
    output = mid_hidden + jnp.dot(activated_low, w_down, preferred_element_type=jnp.float32)
    kept_state = (
        normed_low,
        norm_one_pull,
        rope_pull,
        query_reduced,
        key_reduced,
        value_reduced,
        attention_weights,
        attended_low,
        norm_two_pull,
        normed_two_low,
        swiglu_pull,
        activated_low,
    )
    return (output, kept_state)


def layer_backward(hidden, vector, length, cosine, sine_table, grad_output):
    w_qkv, w_out, w_gateup, w_down, gain_one, gain_two = unpack_layer(vector)
    sequence_length = hidden.shape[0]
    (
        normed_low,
        norm_one_pull,
        rope_pull,
        query_reduced,
        key_reduced,
        value_reduced,
        attention_weights,
        attended_low,
        norm_two_pull,
        normed_two_low,
        swiglu_pull,
        activated_low,
    ) = layer_forward(hidden, vector, length, cosine, sine_table)[1]
    grad_low = grad_output.astype(jnp.bfloat16)
    grad_down = jnp.einsum("tf,td->fd", activated_low, grad_low, preferred_element_type=jnp.float32)
    grad_act = (
        jnp.dot(grad_low, w_down.T, preferred_element_type=jnp.float32)
        .astype(jnp.bfloat16)
        .astype(jnp.float32)
    )
    (grad_gate_up,) = swiglu_pull(grad_act)
    grad_gu_low = grad_gate_up.astype(jnp.bfloat16)
    grad_gateup = jnp.einsum(
        "td,tf->df", normed_two_low, grad_gu_low, preferred_element_type=jnp.float32
    )
    grad_normed_two = jnp.dot(grad_gu_low, w_gateup.T, preferred_element_type=jnp.float32)
    grad_mid, grad_gain_two = norm_two_pull(grad_normed_two)
    grad_mid = grad_mid + grad_output
    grad_mid_low = grad_mid.astype(jnp.bfloat16)
    grad_out_w = jnp.einsum(
        "tk,td->kd", attended_low, grad_mid_low, preferred_element_type=jnp.float32
    )
    attended_gradient = jnp.dot(grad_mid_low, w_out.T, preferred_element_type=jnp.float32).astype(
        jnp.bfloat16
    )
    grad_query, grad_key, value_gradient = attention_backward(
        query_reduced, key_reduced, value_reduced, attention_weights, attended_gradient
    )
    (packed_gradient,) = rope_pull((grad_query.astype(jnp.float32), grad_key.astype(jnp.float32)))
    grad_qkv_low = jnp.concatenate(
        [
            packed_gradient[:, : (QUERY_HEADS + KEY_VALUE_HEADS) * HEAD_SIZE],
            value_gradient.reshape(sequence_length, KEY_VALUE_HEADS * HEAD_SIZE).astype(
                jnp.float32
            ),
        ],
        axis=1,
    ).astype(jnp.bfloat16)
    grad_qkv_w = jnp.einsum(
        "td,tk->dk", normed_low, grad_qkv_low, preferred_element_type=jnp.float32
    )
    grad_normed = jnp.dot(grad_qkv_low, w_qkv.T, preferred_element_type=jnp.float32)
    grad_input, grad_gain_one = norm_one_pull(grad_normed)
    grad_input = grad_input + grad_mid
    return (
        grad_input,
        (grad_qkv_w, grad_out_w, grad_gateup, grad_down, grad_gain_one, grad_gain_two),
    )


def merge_stats(first_stats, second_stats):
    peak_a, spread_a, picked_a = first_stats
    peak_b, spread_b, picked_b = second_stats
    peak_max = jnp.maximum(peak_a, peak_b)
    return (
        peak_max,
        spread_a * jnp.exp(peak_a - peak_max) + spread_b * jnp.exp(peak_b - peak_max),
        picked_a + picked_b,
    )


def fetch_weights(embed_table, model_flat):
    table_low = lax.all_gather(embed_table.astype(jnp.bfloat16), "dp", axis=0, tiled=True)
    model_low = lax.all_gather(model_flat.astype(jnp.bfloat16), ("dp", "shard"), axis=0, tiled=True)
    return (table_low, model_low)


def fetch_again(embed_table, model_flat):
    table_low = lax.all_gather(embed_table.astype(jnp.bfloat16), "dp", axis=0, tiled=True)
    model_low = lax.all_gather(model_flat.astype(jnp.bfloat16), ("dp", "shard"), axis=0, tiled=True)
    return (table_low, model_low)


def reduce_grads(table_part, model_part):
    table_share = lax.psum_scatter(
        table_part.astype(jnp.bfloat16), "dp", scatter_dimension=0, tiled=True
    ).astype(jnp.float32)
    model_share = lax.psum_scatter(model_part, ("dp", "shard"), scatter_dimension=0, tiled=True)
    return (table_share, model_share)


def shards(
    token_ids,
    lengths,
    deal_order,
    embed_table,
    table_mom,
    table_avg,
    model_flat,
    model_mom,
    model_avg,
):
    shard_count = lax.axis_size("shard")
    shard_idx = lax.axis_index("shard")
    data_idx = lax.axis_index("dp")
    device_idx = lax.axis_index(("dp", "shard"))
    all_ids, all_lengths = (
        lax.all_gather(token_ids, ("dp", "shard"), axis=0, tiled=True),
        lax.all_gather(lengths, ("dp", "shard"), axis=0, tiled=True),
    )
    target_count = jnp.sum(all_lengths - 1).astype(jnp.float32)
    vocab_rows = embed_table.shape[1]
    vocab_start = shard_idx * vocab_rows
    cosine, sine_table = rope_tables(LEN)
    group_rows = LEN * shard_count
    block_rows = min(512, group_rows)
    places = jnp.arange(LEN)
    table_sum = jnp.zeros(embed_table.shape, jnp.float32)
    model_sum = jnp.zeros(model_flat.shape, jnp.float32)
    slot_values = []
    for micro_idx in range(MICRO):
        table_low, model_low = fetch_weights(embed_table, model_flat)
        slot_base = (
            data_idx * shard_count + jnp.arange(shard_count, dtype=jnp.int32)
        ) * MICRO + micro_idx
        group_seqs = deal_order[slot_base]
        group_ids = all_ids[group_seqs]
        group_lens = all_lengths[group_seqs]
        own_len = group_lens[shard_idx]
        local_ids = group_ids.reshape(-1) - vocab_start
        inside = (local_ids >= 0) & (local_ids < vocab_rows)
        safe_ids = jnp.clip(local_ids, 0, vocab_rows - 1)
        picked_cols = jnp.take(table_low, safe_ids, axis=1).T.astype(jnp.float32)
        picked_rows = jnp.where(inside[:, None], picked_cols, 0.0)
        hidden = lax.psum_scatter(
            picked_rows.astype(jnp.bfloat16), "shard", scatter_dimension=0, tiled=True
        ).astype(jnp.float32)
        layer_inputs = []
        for layer_idx in range(LAYERS):
            layer_inputs.append(hidden)
            hidden = layer_forward(
                hidden,
                model_low[layer_idx * PL : (layer_idx + 1) * PL],
                own_len,
                cosine,
                sine_table,
            )[0]
        head_params = model_low[LAYERS * PL :]
        w_second = head_params[: MODEL_WIDTH * MODEL_WIDTH].reshape(MODEL_WIDTH, MODEL_WIDTH)
        gain_final = head_params[
            MODEL_WIDTH * MODEL_WIDTH : MODEL_WIDTH * MODEL_WIDTH + MODEL_WIDTH
        ].astype(jnp.float32)
        gain_second = head_params[MODEL_WIDTH * MODEL_WIDTH + MODEL_WIDTH :].astype(jnp.float32)
        final_norm, final_pull = jax.vjp(rms_norm, hidden, gain_final)
        head_one = final_norm.astype(jnp.bfloat16)
        projected = jnp.dot(head_one, w_second, preferred_element_type=jnp.float32)
        second_norm, second_pull = jax.vjp(rms_norm, projected, gain_second)
        head_two = second_norm.astype(jnp.bfloat16)
        group_one, group_two = (
            lax.all_gather(head_one, "shard", axis=0, tiled=True),
            lax.all_gather(head_two, "shard", axis=0, tiled=True),
        )
        target_one = jnp.roll(group_ids, -1, axis=1).reshape(-1)
        target_two = jnp.roll(group_ids, -2, axis=1).reshape(-1)
        weight_one = (places[None, :] + 1 < group_lens[:, None]).astype(jnp.float32).reshape(-1)
        weight_two = SECOND_WEIGHT * (places[None, :] + 2 < group_lens[:, None]).astype(
            jnp.float32
        ).reshape(-1)
        weights_both = jnp.stack([weight_one, weight_two])
        stacked_rows = jnp.stack([group_one, group_two]).reshape(-1, block_rows, MODEL_WIDTH)
        stacked_tgt = (jnp.stack([target_one, target_two]) - vocab_start).reshape(-1, block_rows)

        def block_stats(block_items):
            rows_in, targets = block_items
            logits = jnp.dot(rows_in, table_low, preferred_element_type=jnp.float32)
            peak_max = jnp.max(logits, axis=1)
            spread = jnp.sum(jnp.exp(logits - peak_max[:, None]), axis=1)
            inside_tgt = (targets >= 0) & (targets < vocab_rows)
            chosen = jnp.take_along_axis(
                logits, jnp.clip(targets, 0, vocab_rows - 1)[:, None], axis=1
            )[:, 0]
            return (peak_max, spread, jnp.where(inside_tgt, chosen, 0.0))

        peak_blocks, spread_blocks, picked_blocks = lax.map(
            block_stats, (stacked_rows, stacked_tgt)
        )
        peak_all, spread_all, picked_all = combined_all(
            (peak_blocks, spread_blocks, picked_blocks), "shard", merge_stats
        )
        log_total = (peak_all + jnp.log(spread_all)).reshape(2, group_rows)
        row_terms = jnp.sum(
            weights_both * (log_total - picked_all.reshape(2, group_rows)), axis=0
        ).reshape(shard_count, LEN)
        slot_values.append(jnp.sum(row_terms[shard_idx]) / target_count)
        table_low, model_low = fetch_again(embed_table, model_flat)
        coef_blocks = (weights_both / target_count).reshape(-1, block_rows)
        lse_blocks = log_total.reshape(-1, block_rows)

        def block_grads(table_acc, block_items):
            rows_in, targets, lse_rows, coef_rows = block_items
            logits = jnp.dot(rows_in, table_low, preferred_element_type=jnp.float32)
            onehot = (jnp.arange(vocab_rows)[None, :] == targets[:, None]).astype(jnp.float32)
            grad_logits = (
                (jnp.exp(logits - lse_rows[:, None]) - onehot) * coef_rows[:, None]
            ).astype(jnp.bfloat16)
            grad_rows = jnp.einsum(
                "bv,dv->bd", grad_logits, table_low, preferred_element_type=jnp.float32
            )
            table_acc = table_acc + jnp.einsum(
                "bd,bv->dv", rows_in, grad_logits, preferred_element_type=jnp.float32
            )
            return (table_acc, grad_rows)

        table_grad, grad_rows = lax.scan(
            block_grads,
            jnp.zeros((MODEL_WIDTH, vocab_rows), jnp.float32),
            (stacked_rows, stacked_tgt, lse_blocks, coef_blocks),
        )
        grad_rows = grad_rows.reshape(2, group_rows, MODEL_WIDTH)
        grad_one, grad_two = (
            lax.psum_scatter(
                grad_rows[0].astype(jnp.bfloat16), "shard", scatter_dimension=0, tiled=True
            ).astype(jnp.float32),
            lax.psum_scatter(
                grad_rows[1].astype(jnp.bfloat16), "shard", scatter_dimension=0, tiled=True
            ).astype(jnp.float32),
        )
        grad_proj, grad_gain_second = second_pull(grad_two)
        grad_proj_low = grad_proj.astype(jnp.bfloat16)
        grad_w_second = jnp.einsum(
            "td,te->de", head_one, grad_proj_low, preferred_element_type=jnp.float32
        )
        grad_final = grad_one + jnp.dot(
            grad_proj_low, w_second.T, preferred_element_type=jnp.float32
        )
        grad_hidden, grad_gain_final = final_pull(grad_final)
        model_acc = jnp.zeros((NP,), jnp.float32)
        model_acc = add_packed(
            model_acc, LAYERS * PL, (grad_w_second, grad_gain_final, grad_gain_second)
        )
        for layer_idx in reversed(range(LAYERS)):
            grad_hidden, layer_pieces = layer_backward(
                layer_inputs[layer_idx],
                model_low[layer_idx * PL : (layer_idx + 1) * PL],
                own_len,
                cosine,
                sine_table,
                grad_hidden,
            )
            model_acc = add_packed(model_acc, layer_idx * PL, layer_pieces)
        grad_embed = lax.all_gather(grad_hidden.astype(jnp.bfloat16), "shard", axis=0, tiled=True)
        embed_terms = jnp.where(inside[None, :], grad_embed.astype(jnp.float32).T, 0.0)
        table_grad = table_grad.at[:, safe_ids].add(embed_terms)
        table_share, model_share = reduce_grads(table_grad, model_acc)
        table_sum = table_sum + table_share
        model_sum = model_sum + model_share
    square_sum = lax.psum(
        jnp.sum(table_sum * table_sum) + jnp.sum(model_sum * model_sum), ("dp", "shard")
    )
    grad_norm = jnp.sqrt(square_sum)
    factor = jnp.minimum(1.0, CLIP_NORM / (grad_norm + 1e-06))
    slot_local = jnp.stack(slot_values)
    slot_all = lax.all_gather(slot_local, ("dp", "shard"), axis=0, tiled=True)
    loss_total = jnp.sum(slot_all)
    seq_total = slot_all.shape[0]
    inverse_order = (
        jnp.zeros((seq_total,), jnp.int32)
        .at[deal_order]
        .set(jnp.arange(seq_total, dtype=jnp.int32))
    )
    own_slots = device_idx * MICRO + jnp.arange(MICRO, dtype=jnp.int32)
    seq_loss = slot_all[inverse_order[own_slots]]
    results = []
    for weights, gradient, moment, average in (
        (embed_table, table_sum, table_mom, table_avg),
        (model_flat, model_sum, model_mom, model_avg),
    ):
        clipped = gradient * factor
        new_moment = MOMENTUM * moment + clipped
        new_weight = weights - LEARN_RATE * (clipped + MOMENTUM * new_moment)
        new_average = AVERAGE_KEEP * average + (1.0 - AVERAGE_KEEP) * new_weight
        results.append(
            (clipped, new_weight, new_moment, new_average, new_weight.astype(jnp.bfloat16))
        )
    return (
        loss_total,
        seq_loss,
        slot_local,
        grad_norm,
        results[0][0],
        results[0][1],
        results[0][2],
        results[0][3],
        results[0][4],
        results[1][0],
        results[1][1],
        results[1][2],
        results[1][3],
        results[1][4],
    )


def solution(mesh):
    return jax.shard_map(
        shards,
        mesh=mesh,
        in_specs=(
            P(("dp", "shard"), None),
            P(("dp", "shard")),
            P(),
            P("dp", "shard"),
            P("dp", "shard"),
            P("dp", "shard"),
            P(("dp", "shard")),
            P(("dp", "shard")),
            P(("dp", "shard")),
        ),
        out_specs=(
            P(),
            P(("dp", "shard")),
            P(("dp", "shard")),
            P(),
            P("dp", "shard"),
            P("dp", "shard"),
            P("dp", "shard"),
            P("dp", "shard"),
            P("dp", "shard"),
            P(("dp", "shard")),
            P(("dp", "shard")),
            P(("dp", "shard")),
            P(("dp", "shard")),
            P(("dp", "shard")),
        ),
        check_vma=False,
    )
```

profile of v0, /device:TPU:0, one launch (start us, length us, event | category | flops | bytes accessed | tf_op | source)
XLA Modules:
  0.0 2227.9 jit_solution(7573199143012226565)
XLA Ops:
  26.3 70.5 %all-gather.6 = s32[32,2,128]{2,1,0:T(2,128)S(1)} all-gather(s32[1,2,128]{2,1,0:T(2,128)S(1)} %bitcast.840), channel_id=1, replica_groups=mesh['dp'=8,'shard'=4] {'dp','shard'}, dimensions={0}, use_global_device_ids=true | all-gather | bytes 33792 | tf_op jit(solution)/shard_map/all_gather | solution.py:319
  99.3 38.7 %all-reduce.34 = s32[64]{0:T(128)S(1)} all-reduce(s32[64]{0:T(128)S(1)} %dynamic-update-slice.60), channel_id=1, replica_groups=mesh['dp'=8,'shard'=4] {'dp','shard'}, use_global_device_ids=true, to_apply=%add.34 | all-reduce | flops 64 | bytes 512
  147.3 175.2 %all-reduce.42.cloned.1.call-done = bf16[7413120]{0:T(1024)(128)(2,1)} async-done(((bf16[7413120]{0:T(1024)(128)(2,1)}), bf16[7413120]{0:T(1024)(128)(2,1)}) %all-reduce.42.cloned.1.call-update) | async-done | bytes 14826256
  334.9 20.2 copy.145
  402.1 10.4 gather_fusion.11
  448.7 16.0 all_gather.79
  465.4 14.7 all_gather.80
  481.1 75.2 %while.122 = (s32[]{:T(128)}, f32[2,512]{1,0:T(2,128)S(1)}, f32[2,512]{1,0:T(2,128)S(1)}, f32[2,512]{1,0:T(2,128)S(1)}, bf16[2,512,576]{2,1,0:T(8,128)(2,1)S(1)}...) while((s32[]{:T(128)}, f32[2,512]{1,0:T(2,128)S(1)}, ...), condition=%wide.region_14.17_spmd, body=%wide.region_11.16_spmd.sunk | while | flops 7266642432 | bytes 65196156 | solution.py:395
  481.1 19.1 fusion.424
  500.3 10.5 exponential_reduce_fusion.4
  518.7 19.1 fusion.424
  537.9 10.5 exponential_reduce_fusion.4
  556.3 13.2 all-gather.7
  569.5 13.1 all-gather.8
  582.6 13.3 all-gather.9
  596.7 113.0 %while.126 = (s32[]{:T(128)}, f32[576,12288]{1,0:T(8,128)}, bf16[2,512,576]{1,2,0:T(8,128)(2,1)S(1)}, bf16[2,512,576]{2,1,0:T(8,128)(2,1)S(1)}, bf16[576,12288]{...) while((s32[]{:T(128)}, f32[576,12288]{1,0:T(8,128)}, ...), condition=%wide.region_42.45_spmd.clone, body=%wide.region_41.44_spmd.clone.sunk | while | flops 21795176448 | bytes 125192328 | solution.py:425
  596.7 20.7 multiply_convert_fusion.34
  617.4 16.7 select_add_fusion.4
  634.1 14.3 fusion.439
  648.5 20.7 multiply_convert_fusion.34
  669.1 26.2 %select_add_fusion.4 = f32[576,12288]{1,0:T(8,128)} fusion(f32[576,12288]{1,0:T(8,128)} %get-tuple-element.1775, bf16[512,12288]{1,0:T(8,128)(2,1)} %multiply_convert_fusion.34, pred[]{:T(512)S(6)} %compare.190, bf16[2,512,576]{2,1,0:T(8,128)(2,1)S(1)} %get-tuple-element.1787, s32[]{:T(128)S(6)} %copy.279), kind=kOutput, calls=%fused_computation.27.clone.1 | convolution fusion | flops 7261913088 | bytes 69861384 | tf_op jit(solution)/shard_map/while/body/eval_jaxpr/bd,bv->dv/dot_general | solution.py:420
  695.3 14.3 fusion.439
  723.2 12.0 reduce-scatter.31.cloned.1.call-done
  739.2 20.0 reduce-scatter.29.cloned.1.call-done
  806.5 15.0 all_gather.87
  835.4 14.8 all_gather.88
  851.2 75.1 %while.124 = (s32[]{:T(128)}, f32[2,512]{1,0:T(2,128)S(1)}, f32[2,512]{1,0:T(2,128)S(1)}, f32[2,512]{1,0:T(2,128)S(1)}, bf16[2,512,576]{2,1,0:T(8,128)(2,1)S(1)}...) while((s32[]{:T(128)}, f32[2,512]{1,0:T(2,128)S(1)}, ...), condition=%wide.region_34.37_spmd, body=%wide.region_31.36_spmd.sunk | while | flops 7266642432 | bytes 65196156 | solution.py:395
  851.2 19.1 fusion.429
  870.4 10.5 exponential_reduce_fusion.5
  888.8 19.1 fusion.429
  908.0 10.5 exponential_reduce_fusion.5
  926.3 13.1 all-gather.10
  939.5 13.1 all-gather.11
  952.6 13.5 all-gather.12
  967.0 112.9 %while.127 = (s32[]{:T(128)}, f32[576,12288]{1,0:T(8,128)}, bf16[2,512,576]{1,2,0:T(8,128)(2,1)S(1)}, bf16[2,512,576]{2,1,0:T(8,128)(2,1)S(1)}, bf16[576,12288]{...) while((s32[]{:T(128)}, f32[576,12288]{1,0:T(8,128)}, ...), condition=%wide.region_56.59_spmd.clone, body=%wide.region_55.58_spmd.clone.sunk | while | flops 21795176448 | bytes 125192328 | solution.py:425
  967.0 20.7 multiply_convert_fusion.35
  987.7 16.5 select_add_fusion.5
  1004.2 14.3 fusion.446
  1018.6 20.7 multiply_convert_fusion.35
  1039.3 26.0 %select_add_fusion.5 = f32[576,12288]{1,0:T(8,128)} fusion(f32[576,12288]{1,0:T(8,128)} %get-tuple-element.1862, bf16[512,12288]{1,0:T(8,128)(2,1)} %multiply_convert_fusion.35, pred[]{:T(512)S(6)} %compare.191, bf16[2,512,576]{2,1,0:T(8,128)(2,1)S(1)} %get-tuple-element.1874, s32[]{:T(128)S(6)} %copy.313), kind=kOutput, calls=%fused_computation.41.clone.1 | convolution fusion | flops 7261913088 | bytes 69861384 | tf_op jit(solution)/shard_map/while/body/eval_jaxpr/bd,bv->dv/dot_general | solution.py:420
  1065.3 14.3 fusion.446
  1141.0 9.9 copy-done.2
  1152.5 19.6 scatter-add.121
  1175.0 12.5 scatter-add.124
  1196.0 60.9 %scatter-add.125 = f32[7413120]{0:T(1024)} dynamic-update-slice(f32[7413120]{0:T(1024)} %scatter-add.124, f32[1769472]{0:T(1024)} %slice_add_fusion.3, s32[]{:T(128)} %constant.873.clone.1) | dynamic-update-slice | bytes 14155780 | tf_op jit(solution)/shard_map/scatter-add | solution.py:102
  1261.0 31.3 %scatter-add.126 = f32[7413120]{0:T(1024)} dynamic-update-slice(f32[7413120]{0:T(1024)} %scatter-add.125, f32[884736]{0:T(1024)} %slice_add_fusion.7, s32[]{:T(128)} %constant.874.clone.1) | dynamic-update-slice | bytes 7077892 | tf_op jit(solution)/shard_map/scatter-add | solution.py:102
  1385.1 18.7 scatter-add.146
  1407.1 11.9 scatter-add.149
  1428.9 60.8 %scatter-add.150 = f32[7413120]{0:T(1024)} dynamic-update-slice(f32[7413120]{0:T(1024)} %scatter-add.149, f32[1769472]{0:T(1024)} %slice_add_fusion.1, s32[]{:T(128)} %constant.873.clone.1) | dynamic-update-slice | bytes 14155780 | tf_op jit(solution)/shard_map/scatter-add | solution.py:102
  1498.4 29.6 %scatter-add.151 = f32[7413120]{0:T(1024)} dynamic-update-slice(f32[7413120]{0:T(1024)} %scatter-add.150, f32[884736]{0:T(1024)S(1)} %slice_add_fusion.5, s32[]{:T(128)} %constant.874.clone.1) | dynamic-update-slice | bytes 7077892 | tf_op jit(solution)/shard_map/scatter-add | solution.py:102
  1571.4 29.7 %add.984 = f32[7413120]{0:T(1024)} add(f32[7413120]{0:T(1024)} %fusion.212, f32[7413120]{0:T(1024)} %fusion.207) | non-fusion elementwise | flops 7413120 | bytes 88957440 | tf_op jit(solution)/shard_map/add | solution.py:467
  1601.8 30.5 %copy.171 = f32[576,12288]{0,1:T(8,128)} copy(f32[576,12288]{1,0:T(8,128)} %get-tuple-element.910) | data formatting | bytes 56623104 | tf_op jit(solution)/shard_map/while | solution.py:425
  1632.7 22.7 %all_gather.97 = bf16[512,576]{0,1:T(8,128)(2,1)S(1)} all-gather(bf16[128,576]{0,1:T(8,128)(2,1)S(1)} %get-tuple-element.1351), channel_id=1, replica_groups=mesh['dp'=8,'shard'=4] {'shard'}, dimensions={0}, use_global_device_ids=true | all-gather | bytes 737280 | tf_op jit(solution)/shard_map/all_gather | solution.py:462
  1655.9 26.4 %scatter_fusion.1 = f32[576,12288]{0,1:T(8,128)} fusion(f32[576,12288]{0,1:T(8,128)} %copy.171, s32[512]{0:T(512)S(1)} %bitcast.828, f32[512,576]{1,0:T(8,128)S(1)} %copy.172), kind=kCustom, calls=%fused_computation.14 | custom fusion | flops 294912 | bytes 3540992 | tf_op jit(solution)/shard_map/scatter-add | solution.py:464
  1682.4 16.7 convert_element_type.718
  1699.1 19.8 copy.235
  1719.6 32.2 %copy.162 = f32[576,12288]{0,1:T(8,128)} copy(f32[576,12288]{1,0:T(8,128)} %get-tuple-element.908) | data formatting | bytes 56623104 | tf_op jit(solution)/shard_map/while | solution.py:425
  1751.7 18.0 all_gather.96
  1770.4 27.4 %scatter_fusion = f32[576,12288]{0,1:T(8,128)} fusion(f32[576,12288]{0,1:T(8,128)} %copy.162, s32[512]{0:T(512)S(1)} %bitcast.829, f32[512,576]{1,0:T(8,128)S(1)} %copy.163), kind=kCustom, calls=%fused_computation.13 | custom fusion | flops 294912 | bytes 3540992 | tf_op jit(solution)/shard_map/scatter-add | solution.py:464
  1797.8 16.7 convert_element_type.675
  1814.5 19.6 copy.229
  1858.6 246.5 %all-reduce.44.cloned.1.call-done = f32[7413120]{0:T(1024)} async-done(((f32[7413120]{0:T(1024)}), f32[7413120]{0:T(1024)}) %all-reduce.44.cloned.1.call-update) | async-done | bytes 29652496
  2120.1 39.9 %all-reduce.38 = (f32[64]{0:T(128)S(1)}, f32[]{:T(128)}) all-reduce(f32[64]{0:T(128)S(1)} %get-tuple-element.1267, f32[]{:T(128)S(6)} %add.972), channel_id=1, replica_groups=mesh['dp'=8,'shard'=4] {'dp','shard'}, use_global_device_ids=true, to_apply=%add.36 | all-reduce | flops 65 | bytes 520
  2160.7 10.1 fusion.290
  (1044 shorter events, 559.8 us)
Async XLA Ops:
  8.0 314.6 %all-reduce.42.cloned.1.call-start = ((), (), s32[]{:S(2)}) async-start(), calls=%async_computation.9 | async-start | bytes 29655040
  22.8 74.0 %copy-start = (s32[64]{0:T(128)S(1)}, s32[64]{0:T(128)}, u32[]{:S(2)}) copy-start(s32[64]{0:T(128)} %param.87) | copy-start | bytes 772
  22.9 76.2 %copy-start.298 = (s32[2]{0:T(128)S(1)}, s32[2]{0:T(128)}, u32[]{:S(2)}) copy-start(s32[2]{0:T(128)} %param.86) | copy-start | bytes 28
  22.9 312.0 %all-gather.15.cloned.1.call-start = ((), (), s32[]{:S(2)}) async-start(), calls=%async_computation.8 | async-start | bytes 15925248 | tf_op jit(solution)/shard_map/all_gather | solution.py:284
  26.2 389.0 %reduce-scatter.25.cloned.1.call-start = ((), (), s32[]{:S(2)}) async-start(), calls=%async_computation.10 | async-start | bytes 819200
  98.6 224.0 %copy-start.213 = (s32[4,128]{1,0:T(4,128)}, s32[4,128]{1,0:T(4,128)S(1)}, u32[]{:S(2)}) copy-start(s32[4,128]{1,0:T(4,128)S(1)} %get-tuple-element.1276) | copy-start | bytes 6148
  138.6 184.0 %copy-start.260 = (s32[4]{0:T(128)}, s32[4]{0:T(128)S(1)}, u32[]{:S(2)}) copy-start(s32[4]{0:T(128)S(1)} %gather_fusion.6) | copy-start | bytes 52
  140.5 182.1 %copy-start.211 = (s32[4,128]{1,0:T(4,128)}, s32[4,128]{1,0:T(4,128)S(1)}, u32[]{:S(2)}) copy-start(s32[4,128]{1,0:T(4,128)S(1)} %get-tuple-element.1272) | copy-start | bytes 6148
  140.5 224.2 %copy-start.262 = (pred[512]{0:T(512)(128)(4,1)}, pred[512]{0:T(512)(128)(4,1)S(1)}, u32[]{:S(2)}) copy-start(pred[512]{0:T(512)(128)(4,1)S(1)} %and_bitcast_fusion.1) | copy-start | bytes 1540
  144.6 293.3 %copy-start.83 = (f32[128,32]{0,1:T(8,128)}, f32[128,32]{0,1:T(8,128)S(1)}, u32[]{:S(2)}) copy-start(f32[128,32]{0,1:T(8,128)S(1)} %get-tuple-element.1360) | copy-start | bytes 49156
  365.9 351.4 %reduce-scatter.27.cloned.1.call-start = ((), (), s32[]{:S(2)}) async-start(), calls=%async_computation.11 | async-start | bytes 819200
  377.2 53.9 %copy-start.4 = (bf16[576,3072]{1,0:T(8,128)(2,1)}, bf16[576,3072]{1,0:T(8,128)(2,1)S(1)}, u32[]{:S(2)}) copy-start(bf16[576,3072]{1,0:T(8,128)(2,1)S(1)} %reshape.1584) | copy-start | bytes 10616836
  414.8 320.4 %reduce-scatter.31.cloned.1.call-start = ((), (), s32[]{:S(2)}) async-start(), calls=%async_computation.13 | async-start | bytes 819200
  447.0 18.3 copy-start.180
  447.2 32.9 %copy-start.99 = (bf16[128,1536]{1,0:T(8,128)(2,1)}, bf16[128,1536]{1,0:T(8,128)(2,1)S(1)}, u32[]{:S(2)}) copy-start(bf16[128,1536]{1,0:T(8,128)(2,1)S(1)} %multiply_convert_fusion.4) | copy-start | bytes 1179652
  448.0 32.1 %copy-start.70 = (f32[128,576]{0,1:T(8,128)}, f32[128,576]{0,1:T(8,128)S(1)}, u32[]{:S(2)}) copy-start(f32[128,576]{0,1:T(8,128)S(1)} %get-tuple-element.1373) | copy-start | bytes 884740
  448.1 32.1 %copy-start.294 = (f32[128]{0:T(128)}, f32[128]{0:T(128)S(1)}, u32[]{:S(2)}) copy-start(f32[128]{0:T(128)S(1)} %get-tuple-element.1372) | copy-start | bytes 1540
  448.7 31.4 %copy-start.125 = (bf16[128,576]{0,1:T(8,128)(2,1)}, bf16[128,576]{0,1:T(8,128)(2,1)S(1)}, u32[]{:S(2)}) copy-start(bf16[128,576]{0,1:T(8,128)(2,1)S(1)} %multiply_convert_fusion.16) | copy-start | bytes 442372
  481.1 114.9 %copy-start.237 = (f32[4,128]{1,0:T(4,128)S(1)}, f32[4,128]{1,0:T(4,128)}, u32[]{:S(2)}) copy-start(f32[4,128]{1,0:T(4,128)} %get-tuple-element.1358) | copy-start | bytes 6148
  481.1 114.9 %copy-start.238 = (f32[4,128]{1,0:T(4,128)S(1)}, f32[4,128]{1,0:T(4,128)}, u32[]{:S(2)}) copy-start(f32[4,128]{1,0:T(4,128)} %get-tuple-element.1356) | copy-start | bytes 6148
  710.6 25.7 %copy-start.181 = (f32[576]{0:T(1024)S(1)}, f32[576]{0:T(1024)}, u32[]{:S(2)}) copy-start(f32[576]{0:T(1024)} %get-tuple-element.1287) | copy-start | bytes 6916
  710.6 25.7 %copy-start.259 = (f32[128]{0:T(128)S(1)}, f32[128]{0:T(128)}, u32[]{:S(2)}) copy-start(f32[128]{0:T(128)} %copy-done.258) | copy-start | bytes 1540
  712.7 25.4 %copy-start.297 = (f32[128]{0:T(128)S(1)}, f32[128]{0:T(128)}, u32[]{:S(2)}) copy-start(f32[128]{0:T(128)} %copy-done.296) | copy-start | bytes 1540
  712.8 47.5 %copy-start.18 = (bf16[576,576]{1,0:T(8,128)(2,1)S(1)}, bf16[576,576]{1,0:T(8,128)(2,1)}, u32[]{:S(2)}) copy-start(bf16[576,576]{1,0:T(8,128)(2,1)} %reshape.1592) | copy-start | bytes 1990660
  712.8 47.5 %copy-start.177 = (f32[576]{0:T(1024)S(1)}, f32[576]{0:T(1024)}, u32[]{:S(2)}) copy-start(f32[576]{0:T(1024)} %get-tuple-element.1288) | copy-start | bytes 6916
  712.8 47.5 %copy-start.257 = (f32[128]{0:T(128)S(1)}, f32[128]{0:T(128)}, u32[]{:S(2)}) copy-start(f32[128]{0:T(128)} %copy-done.256) | copy-start | bytes 1540
  712.8 46.4 %reduce-scatter.29.cloned.1.call-start = ((), (), s32[]{:S(2)}) async-start(), calls=%async_computation.12 | async-start | bytes 819200
  716.7 45.6 %copy-start.295 = (f32[128]{0:T(128)S(1)}, f32[128]{0:T(128)}, u32[]{:S(2)}) copy-start(f32[128]{0:T(128)} %copy-done.294) | copy-start | bytes 1540
  716.8 595.3 %reduce-scatter.37.cloned.1.call-start = ((), (), s32[]{:S(2)}) async-start(), calls=%async_computation.16 | async-start | bytes 819200
  719.0 44.5 %copy-start.60 = (f32[128,3072]{1,0:T(8,128)S(1)}, f32[128,3072]{1,0:T(8,128)}, u32[]{:S(2)}) copy-start(f32[128,3072]{1,0:T(8,128)} %copy-done.59) | copy-start | bytes 4718596
  739.2 26.8 %copy-start.128 = (bf16[128,576]{0,1:T(8,128)(2,1)}, bf16[128,576]{0,1:T(8,128)(2,1)S(1)}, u32[]{:S(2)}) copy-start(bf16[128,576]{0,1:T(8,128)(2,1)S(1)} %fusion.129) | copy-start | bytes 442372
  804.5 19.0 copy-start.126
  804.5 19.0 copy-start.129
  805.4 19.6 copy-start.53
  805.4 19.6 copy-start.147
  805.4 19.6 copy-start.173
  805.4 19.6 copy-start.208
  805.4 19.6 copy-start.251
  806.5 28.7 %copy-start.290 = (f32[128]{0:T(128)}, f32[128]{0:T(128)S(1)}, u32[]{:S(2)}) copy-start(f32[128]{0:T(128)S(1)} %get-tuple-element.1396) | copy-start | bytes 1540
  806.5 28.7 %copy-start.71 = (f32[128,576]{0,1:T(8,128)}, f32[128,576]{0,1:T(8,128)S(1)}, u32[]{:S(2)}) copy-start(f32[128,576]{0,1:T(8,128)S(1)} %get-tuple-element.1397) | copy-start | bytes 884740
  851.2 115.1 %copy-start.235 = (f32[4,128]{1,0:T(4,128)S(1)}, f32[4,128]{1,0:T(4,128)}, u32[]{:S(2)}) copy-start(f32[4,128]{1,0:T(4,128)} %get-tuple-element.1359) | copy-start | bytes 6148
  851.2 115.1 %copy-start.236 = (f32[4,128]{1,0:T(4,128)S(1)}, f32[4,128]{1,0:T(4,128)}, u32[]{:S(2)}) copy-start(f32[4,128]{1,0:T(4,128)} %get-tuple-element.1357) | copy-start | bytes 6148
  1083.0 232.3 %reduce-scatter.35.cloned.1.call-start = ((), (), s32[]{:S(2)}) async-start(), calls=%async_computation.15 | async-start | bytes 819200
  1132.5 972.6 %all-reduce.44.cloned.1.call-start = ((), (), s32[]{:S(2)}) async-start(), calls=%async_computation.18 | async-start | bytes 59310080
  1132.6 18.4 copy-start.47
  1261.0 31.3 %copy-start.271 = (f32[576]{0:T(1024)S(1)}, f32[576]{0:T(1024)}, u32[]{:S(2)}) copy-start(f32[576]{0:T(1024)} %get-tuple-element.1154) | copy-start | bytes 6916
  1261.0 32.7 %copy-start.217 = (f32[576]{0:T(1024)S(1)}, f32[576]{0:T(1024)}, u32[]{:S(2)}) copy-start(f32[576]{0:T(1024)} %get-tuple-element.1152) | copy-start | bytes 6916
  1261.0 40.9 %slice-start = ((s8[7077888]{0:T(1024)(128)(4,1)}), s8[2883584]{0:T(1024)(128)(4,1)S(1)}, s32[]{:S(2)}) async-start(s8[7077888]{0:T(1024)(128)(4,1)} %bitcast.707), calls=%async_computation.19 | async-start | bytes 5767168
  1333.1 18.4 copy-start.76
  1601.1 506.2 %reduce-scatter.39.cloned.1.call-start = ((), (), s32[]{:S(2)}) async-start(), calls=%async_computation.17 | async-start | bytes 15925248
  1601.7 30.6 %copy-start.279 = (f32[128]{0:T(128)S(1)}, f32[128]{0:T(128)}, u32[]{:S(2)}) copy-start(f32[128]{0:T(128)} %copy-done.278) | copy-start | bytes 1540
  1601.7 30.6 %copy-start.299 = (f32[128]{0:T(128)S(1)}, f32[128]{0:T(128)}, u32[]{:S(2)}) copy-start(f32[128]{0:T(128)} %get-tuple-element.1163) | copy-start | bytes 1540
  1601.7 30.6 %copy-start.281 = (f32[128]{0:T(128)S(1)}, f32[128]{0:T(128)}, u32[]{:S(2)}) copy-start(f32[128]{0:T(128)} %copy-done.280) | copy-start | bytes 1540
  1601.7 30.6 %copy-start.63 = (bf16[128,576]{0,1:T(8,128)(2,1)S(1)}, bf16[128,576]{0,1:T(8,128)(2,1)}, u32[]{:S(2)}) copy-start(bf16[128,576]{0,1:T(8,128)(2,1)} %copy.222) | copy-start | bytes 442372
  1601.8 30.6 %copy-start.65 = (bf16[128,576]{0,1:T(8,128)(2,1)S(1)}, bf16[128,576]{0,1:T(8,128)(2,1)}, u32[]{:S(2)}) copy-start(bf16[128,576]{0,1:T(8,128)(2,1)} %copy.224) | copy-start | bytes 442372
  1601.8 30.6 %copy-start.75 = (f32[128,576]{0,1:T(8,128)S(1)}, f32[128,576]{0,1:T(8,128)}, u32[]{:S(2)}) copy-start(f32[128,576]{0,1:T(8,128)} %copy-done.74) | copy-start | bytes 884740
  1601.8 30.6 %copy-start.77 = (f32[128,576]{0,1:T(8,128)S(1)}, f32[128,576]{0,1:T(8,128)}, u32[]{:S(2)}) copy-start(f32[128,576]{0,1:T(8,128)} %copy-done.76) | copy-start | bytes 884740
  1601.8 30.6 %copy-start.134 = (f32[128,576]{0,1:T(8,128)S(1)}, f32[128,576]{0,1:T(8,128)}, u32[]{:S(2)}) copy-start(f32[128,576]{0,1:T(8,128)} %copy-done.133) | copy-start | bytes 884740
  1601.8 30.6 %copy-start.161 = (f32[128,576]{0,1:T(8,128)S(1)}, f32[128,576]{0,1:T(8,128)}, u32[]{:S(2)}) copy-start(f32[128,576]{0,1:T(8,128)} %get-tuple-element.1406) | copy-start | bytes 884740
  1601.8 30.6 %copy-start.188 = (f32[576]{0:T(1024)S(1)}, f32[576]{0:T(1024)}, u32[]{:S(2)}) copy-start(f32[576]{0:T(1024)} %get-tuple-element.1292) | copy-start | bytes 6916
  1601.8 30.6 %copy-start.270 = (f32[128]{0:T(128)S(1)}, f32[128]{0:T(128)}, u32[]{:S(2)}) copy-start(f32[128]{0:T(128)} %copy-done.268) | copy-start | bytes 1540
  1601.8 53.5 %copy-start.264 = (pred[512]{0:T(512)(128)(4,1)S(1)}, pred[512]{0:T(512)(128)(4,1)}, u32[]{:S(2)}) copy-start(pred[512]{0:T(512)(128)(4,1)} %and_bitcast_fusion) | copy-start | bytes 1540
  1718.9 391.6 %reduce-scatter.33.cloned.1.call-start = ((), (), s32[]{:S(2)}) async-start(), calls=%async_computation.14 | async-start | bytes 15925248
  1719.6 50.2 %copy-start.263 = (pred[512]{0:T(512)(128)(4,1)S(1)}, pred[512]{0:T(512)(128)(4,1)}, u32[]{:S(2)}) copy-start(pred[512]{0:T(512)(128)(4,1)} %copy-done.262) | copy-start | bytes 1540
  (253 other events, 1096.1 us)
Sparse Core Ops, SparseCore 0:
  22.9 299.5 all-reduce.41
  1601.2 503.8 all-reduce.43
Sparse Core Ops, SparseCore 1:
  26.3 85.0 all-gather.14
  366.0 22.0 reduce-scatter.24
  414.9 22.1 reduce-scatter.26
  712.8 22.3 reduce-scatter.30
  738.1 21.0 reduce-scatter.28
  1083.1 22.4 reduce-scatter.36
  1132.6 22.5 reduce-scatter.34
  1719.0 100.0 reduce-scatter.38
  1834.3 111.3 reduce-scatter.32
where the time goes:
time: 2260 us; the launch traced here: 2230 us
  local copies, waits for them, and re-layouts  686 us (30%)
  waiting for transfers between devices  454 us (20%)
  matrix products  421 us (19%)
  blocking collectives  330 us (15%)
  other arithmetic  310 us (14%)
  between operations  25.4 us (1%)
    unnamed x21, waiting for transfers between devices  454 us
    scatter-add x12, local copies, waits for them, and re-layouts, add_packed(): flat = flat.at[offset:offset + count_here].add(piece.reshape(-1))  262 us
    unnamed x639, local copies, waits for them, and re-layouts  181 us
    dot_general x4, matrix products, block_grads(): jnp.einsum('bd,bv->dv', rows_in, grad_logits, preferred_element_type=jnp....  85.4 us
    dot_general x4, matrix products, block_grads(): logits = jnp.dot(rows_in, table_low, preferred_element_type=jnp.float32)  82.8 us
    all_gather x6, blocking collectives, combined_all(): everything = jax.tree.map(lambda part: lax.all_gather(part, axis), shard)  79.3 us
    unnamed x2, blocking collectives  78.5 us
    dot_general x4, matrix products, block_stats(): logits = jnp.dot(rows_in, table_low, preferred_element_type=jnp.float32)  76.6 us
  transfers between devices with their start and end apart: 11, of which 4 were waited for; matrix products, arithmetic and copies ran while one was open for 34% of the time, Pallas kernels for 0%

commit v1 on v0

v1 whole, which is shorter than its diff:
```python
import jax
import jax.numpy as jnp
from jax import lax
from jax.experimental import pallas as pl
from jax.experimental.pallas import tpu as pltpu
from jax.sharding import PartitionSpec as P

MODEL_WIDTH = 576
QUERY_HEADS = 9
KEY_VALUE_HEADS = 3
HEAD_SIZE = 64
FEED_UNITS = 1536
LAYERS = 2
LEN = 128
PL = 3540096
NP = 7413120
QKV = (QUERY_HEADS + 2 * KEY_VALUE_HEADS) * HEAD_SIZE
ROPED = (QUERY_HEADS + KEY_VALUE_HEADS) * HEAD_SIZE
MEAN_LENGTH = 96

EPSILON = 1e-05
ROPE_BASE = 100000.0
CLIP_NORM = 0.01
LEARN_RATE = 6000.0
MOMENTUM = 0.9
AVERAGE_KEEP = 0.9
SECOND_WEIGHT = 0.3
MASKED_SCORE = -1e30

GRAIN = 2048
GRANULE = 16
BLOCK = 512
CHUNK = 1024
LANES = 128
COLUMNS = 256
VMEM_LIMIT = 62 * 1024 * 1024
F32 = jnp.float32
BF16 = jnp.bfloat16


def flip_dp(values, bit):
    return lax.ppermute(values, "dp", [(i, i ^ bit) for i in range(lax.axis_size("dp"))])


def flip_shard(values, bit):
    return lax.ppermute(values, "shard", [(i, i ^ bit) for i in range(lax.axis_size("shard"))])


def next_shard(values):
    size = lax.axis_size("shard")
    return lax.ppermute(values, "shard", [(i, (i + 1) % size) for i in range(size)])


def bits_below(size):
    return [1 << k for k in range(size.bit_length() - 1)]


def dp_bit(bit):
    return (lax.axis_index("dp") // bit) % 2


def join(own, other, bit, axis):
    return jnp.where(
        dp_bit(bit) == 0,
        jnp.concatenate([own, other], axis),
        jnp.concatenate([other, own], axis),
    )


def pick(values, idx, axis):
    return lax.dynamic_index_in_dim(values, idx, axis, keepdims=False)


def high_bits():
    return bits_below(lax.axis_size("dp"))[1:]


def gather_cube(values, order):
    bits = sorted(order, reverse=True)
    out = values.reshape((1,) * len(bits) + values.shape)
    for bit in order:
        out = join(out, flip_dp(out, bit), bit, bits.index(bit))
    return out.reshape((-1,) + values.shape)


def reduce_cube(values, order):
    bits = sorted(order, reverse=True)
    left = list(bits)
    out = values.reshape((2,) * len(bits) + values.shape[1:])
    for bit in order:
        axis = left.index(bit)
        mine = dp_bit(bit)
        got = flip_dp(pick(out, 1 - mine, axis).astype(BF16), bit)
        out = pick(out, mine, axis).astype(F32) + got.astype(F32)
        left.remove(bit)
    return out


def ring_gather(values):
    size = lax.axis_size("shard")
    me = lax.axis_index("shard")
    parts = [values]
    for _ in range(size - 1):
        parts.append(next_shard(parts[-1]))
    stacked = jnp.stack(parts[::-1])
    return jnp.roll(stacked, me + 1, axis=0)


def ring_reduce(values):
    size = lax.axis_size("shard")
    me = lax.axis_index("shard")
    total = None
    for step in range(size - 1):
        term = pick(values, (me - 1 - step) % size, 0).astype(F32)
        if total is not None:
            term = term + total
        total = next_shard(term.astype(BF16)).astype(F32)
    return total + pick(values, me, 0).astype(F32)


def group_gather(rows):
    parts = ring_gather(rows)
    other = flip_dp(parts, 1)
    return join(parts[None], other[None], 1, 0)


def group_reduce(parts):
    mine = dp_bit(1)
    got = flip_dp(pick(parts, 1 - mine, 0).astype(BF16), 1)
    return ring_reduce(pick(parts, mine, 0).astype(F32) + got.astype(F32))


def sum_all(value):
    total = value
    for bit in bits_below(lax.axis_size("dp")):
        total = total + flip_dp(total, bit)
    for bit in bits_below(lax.axis_size("shard")):
        total = total + flip_shard(total, bit)
    return total


def top_bit():
    return high_bits()[-1]


def block_starts(length, total):
    return [length * i // GRAIN for i in range(total)] + [-(-length * total // GRAIN)]


def own_blocks(model_flat):
    length = model_flat.shape[0]
    total = lax.axis_size("dp") * lax.axis_size("shard")
    device = lax.axis_index(("dp", "shard"))
    low = model_flat.astype(BF16)
    before = lax.ppermute(
        low[length - GRAIN :], ("dp", "shard"), [(i, i + 1) for i in range(total - 1)]
    )
    starts = block_starts(length, total)
    blocks = max(starts[i + 1] - starts[i] for i in range(total))
    extended = jnp.concatenate([before, low, jnp.zeros((3 * GRAIN,), BF16)])
    shift = (length * device) % GRAIN
    whole = lax.dynamic_slice_in_dim(extended, GRAIN - shift, blocks * GRAIN, 0)
    return whole.reshape(-1, 128)


LAYER_SHAPES = (
    (MODEL_WIDTH, QKV),
    (MODEL_WIDTH, MODEL_WIDTH),
    (MODEL_WIDTH, 2 * FEED_UNITS),
    (FEED_UNITS, MODEL_WIDTH),
)
SQUARE = ((MODEL_WIDTH, MODEL_WIDTH),)
TALL = 64


def line_up(flat_at, out, height, breadth):
    tiles, odd = breadth // 128, breadth % 128
    if not odd:
        for j in range(tiles):
            out(0, j, flat_at(j, height, tiles))
        return
    period = 2 * tiles + 1
    loads = [flat_at(j, height // 2, period) for j in range(period)]
    for j in range(tiles + 1):
        out(0, j, loads[j])
        after = loads[min(tiles + j + 1, period - 1)]
        out(1, j, jnp.concatenate([loads[tiles + j][:, 64:], after[:, :64]], 1))


def unpack_matrix(flat_ref, at, out_ref, wide_ref, tall_ref):
    height, breadth = out_ref.shape
    rows = TALL * breadth // 128
    shift = at % 16
    load = rows + (16 if shift else 0)

    @pl.loop(0, height // TALL)
    def _(k):
        first = pl.multiple_of(k * rows + (at - shift), 16)
        wide_ref[:load, :] = flat_ref[pl.ds(first, load), :].astype(F32)
        out_at = pl.multiple_of(k * TALL, TALL)

        def flat_at(j, count, stride):
            return wide_ref[pl.ds(shift + j, count, stride=stride), :]

        if breadth % 128:
            def put(parity, j, values):
                tall_ref[j, pl.ds(parity, TALL // 2, stride=2), :] = values

            line_up(flat_at, put, TALL, breadth)
            for j in range(breadth // 128 + 1):
                stop = min((j + 1) * 128, breadth)
                out_ref[pl.ds(out_at, TALL), j * 128 : stop] = tall_ref[
                    j, :, : stop - j * 128
                ].astype(BF16)
        else:
            def put(_, j, values):
                out_ref[pl.ds(out_at, TALL), j * 128 : (j + 1) * 128] = values.astype(BF16)

            line_up(flat_at, put, TALL, breadth)


def unpack_rows(everything, length, first_row, last_row, shapes, gaps, lead, tails):
    total = lax.axis_size("dp") * lax.axis_size("shard")
    starts = block_starts(length, total)
    per = GRAIN // 128
    moves = []
    for owner in range(total):
        low = max(starts[owner] * per, first_row)
        high = min(starts[owner + 1] * per, last_row)
        if low < high:
            moves.append((owner, low - starts[owner] * per, low - first_row, high - low))
    outs = [jax.ShapeDtypeStruct(shape, BF16) for shape in shapes]
    outs += [jax.ShapeDtypeStruct((rows, 128), BF16) for _, rows in tails]
    wide_rows = TALL * max(shape[1] for shape in shapes) // 128 + 16
    height = last_row - first_row

    def kernel(all_ref, *refs):
        outs, (flat_ref, wide_ref, tall_ref, sems) = refs[:-4], refs[-4:]
        copies = [
            pltpu.make_async_copy(
                all_ref.at[owner, pl.ds(source, rows)], flat_ref.at[pl.ds(at, rows)], sems.at[k]
            )
            for k, (owner, source, at, rows) in enumerate(moves)
        ]
        for copy in copies:
            copy.start()
        arrived = 0
        at = lead
        for k, (tall, wide) in enumerate(shapes):
            end = at + tall * wide // 128
            while arrived < len(moves) and moves[arrived][2] < end:
                copies[arrived].wait()
                arrived += 1
            unpack_matrix(flat_ref, at, outs[k], wide_ref, tall_ref)
            at = end + gaps.get(k, 0)
        for copy in copies[arrived:]:
            copy.wait()
        for k, (start, rows) in enumerate(tails):
            outs[len(shapes) + k][...] = flat_ref[pl.ds(start, rows), :]

    return pl.pallas_call(
        kernel,
        in_specs=[pl.BlockSpec(memory_space=pl.ANY)],
        out_specs=[pl.BlockSpec(memory_space=pltpu.VMEM)] * len(outs),
        out_shape=outs,
        scratch_shapes=[
            pltpu.VMEM((height, 128), BF16),
            pltpu.VMEM((wide_rows, 128), F32),
            pltpu.VMEM((8, TALL, 128), F32),
            pltpu.SemaphoreType.DMA((len(moves),)),
        ],
        compiler_params=pltpu.CompilerParams(vmem_limit_bytes=VMEM_LIMIT),
        cost_estimate=pl.CostEstimate(flops=0, bytes_accessed=512 * height, transcendentals=0),
        name="unpack_rows",
    )(everything)


def pack_matrix(left_ref, right_ref, flat_ref, at, tall_ref):
    height, breadth = left_ref.shape[1], right_ref.shape[1]
    part = 512 if height % 512 == 0 else height
    tiles, odd = breadth // 128, breadth % 128
    for k in range(height // part):
        first = at + k * part * breadth // 128
        product = against(left_ref[:, k * part : (k + 1) * part], right_ref[...])
        for j in range(tiles + (1 if odd else 0)):
            stop = min((j + 1) * 128, breadth)
            tall_ref[j, :part, : stop - j * 128] = product[:, j * 128 : stop]
        if not odd:
            for j in range(tiles):
                flat_ref[pl.ds(first + j, part, stride=tiles), :] = tall_ref[j, :part, :]
            continue
        period = 2 * tiles + 1
        count = part // 2

        def half(parity, j):
            return tall_ref[j, pl.ds(parity, count, stride=2), :]

        for j in range(tiles):
            flat_ref[pl.ds(first + j, count, stride=period), :] = half(0, j)
        flat_ref[pl.ds(first + tiles, count, stride=period), :] = jnp.concatenate(
            [half(0, tiles)[:, :64], half(1, 0)[:, :64]], 1
        )
        for j in range(tiles):
            flat_ref[pl.ds(first + tiles + 1 + j, count, stride=period), :] = jnp.concatenate(
                [half(1, j)[:, 64:], half(1, j + 1)[:, :64]], 1
            )


def pack_kernel(info_ref, *refs, pairs, loose, early, lead, gaps, count, sub_rows, keep, first_loose):
    lefts, rights, refs = refs[:pairs], refs[pairs : 2 * pairs], refs[2 * pairs :]
    loose_refs, refs = refs[:loose], refs[loose:]
    if early:
        early_ref, refs = refs[0], refs[1:]
    own_ref, send_ref, refs = refs[0], refs[1], refs[2:]
    if keep:
        keep_ref, refs = refs[0], refs[1:]
    flat_ref, low_ref, tall_ref, sems = refs
    height = flat_ref.shape[0]
    at = lead
    for k in range(pairs):
        pack_matrix(lefts[k], rights[k], flat_ref, at, tall_ref)
        at += lefts[k].shape[1] * rights[k].shape[1] // 128
        if k in gaps:
            flat_ref[at : at + gaps[k], :] = loose_refs[list(gaps).index(k)][...]
            at += gaps[k]
    if early:
        flat_ref[at : at + early, :] = early_ref[...].astype(F32)[first_loose : first_loose + early]
        at += early
    if at < height:
        flat_ref[at:height, :] = jnp.zeros((height - at, 128), F32)
    step = 16 * 32
    for row in range(0, height, step):
        rows = min(step, height - row)
        low_ref[row : row + rows, :] = flat_ref[row : row + rows, :].astype(BF16)
    copies = []
    for idx in range(count):
        for k, ref in enumerate((own_ref, send_ref)):
            row = pl.multiple_of(info_ref[k * count + idx], 16)
            copies.append(
                pltpu.make_async_copy(
                    low_ref.at[pl.ds(row, sub_rows)], ref.at[idx], sems.at[k * count + idx]
                )
            )
    for copy in copies:
        copy.start()
    if keep:
        keep_ref[...] = low_ref[:keep, :]
    for copy in copies:
        copy.wait()


def pack_half(info, pairs, loose, early, lead, gaps, height, sub_rows, keep, skip):
    count = info.shape[0] // 2
    lefts = [left for left, _ in pairs]
    rights = [right for _, right in pairs]
    in_place = pl.BlockSpec(memory_space=pltpu.VMEM)
    anywhere = pl.BlockSpec(memory_space=pl.ANY)
    operands = lefts + rights + loose + ([early[0]] if early is not None else [])
    outs = [jax.ShapeDtypeStruct((count, sub_rows, 128), BF16)] * 2
    specs = [anywhere] * 2
    if keep:
        outs.append(jax.ShapeDtypeStruct((keep, 128), BF16))
        specs.append(in_place)

    def kernel(info_ref, *refs):
        pack_kernel(
            info_ref, *refs, pairs=len(pairs), loose=len(loose),
            early=0 if early is None else early[1], lead=lead, gaps=gaps,
            count=count, sub_rows=sub_rows, keep=keep, first_loose=skip,
        )

    flops = sum(2 * left.size * right.shape[1] for left, right in pairs)
    return pl.pallas_call(
        kernel,
        in_specs=[pl.BlockSpec(memory_space=pltpu.SMEM)] + [in_place] * len(operands),
        out_specs=specs,
        out_shape=outs,
        scratch_shapes=[
            pltpu.VMEM((height, 128), F32),
            pltpu.VMEM((height, 128), BF16),
            pltpu.VMEM((max(right.shape[1] for right in rights) // 128, MODEL_WIDTH, 128), F32),
            pltpu.SemaphoreType.DMA((2 * count,)),
        ],
        compiler_params=pltpu.CompilerParams(vmem_limit_bytes=VMEM_LIMIT),
        cost_estimate=pl.CostEstimate(
            flops=flops, bytes_accessed=512 * height, transcendentals=0
        ),
        name="pack_half",
    )(info, *operands)


def owner_rows(length, which, first_row):
    dp_size, shard_size = lax.axis_size("dp"), lax.axis_size("shard")
    sub_rows = owner_sub_rows(length)
    per = GRAIN // 128
    j = jnp.arange(2)[:, None, None]
    x = jnp.arange(dp_size // 4)[None, :, None]
    z = jnp.arange(shard_size)[None, None, :]
    rows = []
    for core in (dp_bit(1), 1 - dp_bit(1)):
        owner = ((which * (dp_size // 4) + x) * 2 + core) * shard_size + z
        rows.append((length * owner // GRAIN * per + sub_rows * j - first_row).reshape(-1))
    return jnp.concatenate(rows).astype(jnp.int32)


def owner_sub_rows(length):
    blocks = -(-(GRAIN - 1 + length) // GRAIN)
    return (blocks + blocks % 2) * (GRAIN // 128) // 2


def reduce_half(own, send, which):
    dp_size, shard_size = lax.axis_size("dp"), lax.axis_size("shard")
    paired = (own.astype(F32) + flip_dp(send, 1).astype(F32)).astype(BF16)
    paired = paired.reshape((-1, shard_size) + own.shape[1:])
    half = shard_size // 2
    order = high_bits()
    first = reduce_cube(paired[:, :half], order)
    second = reduce_cube(paired[:, half:], order[::-1])
    done = ring_reduce(jnp.concatenate([first, second], 0).astype(BF16))
    top = top_bit()
    away = [(i, i ^ top) for i in range(dp_size) if (i // top) % 2 != which]
    got = lax.ppermute(done.astype(BF16), "dp", away).astype(F32)
    return done, got


def own_part(halves, length):
    (done_zero, got_zero), (done_one, got_one) = halves
    top = dp_bit(top_bit())
    lower = jnp.where(top == 0, done_zero, got_one)
    upper = jnp.where(top == 0, got_zero, done_one)
    shift = (length * lax.axis_index(("dp", "shard"))) % GRAIN
    flat = jnp.concatenate([lower, upper], 0).reshape(-1)
    return lax.dynamic_slice_in_dim(flat, shift, length, 0)


def gather_table(embed_table):
    low = embed_table.astype(BF16)
    half = low.shape[1] // 2
    core = dp_bit(1)
    own = lax.dynamic_slice_in_dim(low, core * half, half, 1)
    send = lax.dynamic_slice_in_dim(low, (1 - core) * half, half, 1)
    pair = join(own, flip_dp(send, 1), 1, 0)
    bits = sorted(high_bits(), reverse=True)
    shape = (1,) * len(bits) + (pair.shape[0], half // 2)
    sides = [pair[:, : half // 2].reshape(shape), pair[:, half // 2 :].reshape(shape)]
    orders = [high_bits(), high_bits()[::-1]]
    for k in range(len(bits)):
        got = [flip_dp(side, order[k]) for side, order in zip(sides, orders)]
        sides = [
            join(side, other, order[k], bits.index(order[k]))
            for side, other, order in zip(sides, got, orders)
        ]
    return jnp.concatenate([side.reshape(MODEL_WIDTH, -1) for side in sides], 1)


def reduce_table(table_grad, features):
    half = table_grad.shape[1]
    parts = table_grad.reshape(-1, 2 * features, half)
    order = high_bits()
    first = reduce_cube(parts[:, :, : half // 2], order)
    second = reduce_cube(parts[:, :, half // 2 :], order[::-1])
    return jnp.concatenate([first, second], 1)


def to_owner(joined, features):
    core = dp_bit(1)
    own = lax.dynamic_slice_in_dim(joined, core * features, features, 0)
    send = lax.dynamic_slice_in_dim(joined, (1 - core) * features, features, 0)
    return join(own, flip_dp(send, 1), 1, 1)


def rms_scale(values):
    return lax.rsqrt(jnp.mean(values * values, axis=-1, keepdims=True) + EPSILON)


def rms_back(values, scale, gain, grad):
    weighted = grad * gain
    inner = jnp.sum(weighted * values, axis=-1, keepdims=True)
    grad_values = scale * weighted - values * (scale * scale * scale * inner / MODEL_WIDTH)
    grad_gain = jnp.sum(grad * values * scale, axis=0)
    return grad_values, grad_gain


def rope_rows(rows):
    halves = HEAD_SIZE // 2
    inverse = ROPE_BASE ** (-jnp.arange(halves, dtype=F32) * 2.0 / HEAD_SIZE)
    angles = jnp.arange(LEN, dtype=F32)[:, None] * inverse[None, :]
    cosine, sine = jnp.cos(angles), jnp.sin(angles)
    heads = ROPED // HEAD_SIZE
    cos_full = jnp.tile(jnp.concatenate([cosine, cosine], 1), (rows // LEN, heads))
    sin_full = jnp.tile(jnp.concatenate([-sine, sine], 1), (rows // LEN, heads))
    return cos_full, sin_full


def swap_halves(values):
    halves = HEAD_SIZE // 2
    lanes = lax.broadcasted_iota(jnp.int32, values.shape, 1) % HEAD_SIZE
    return jnp.where(lanes < halves, jnp.roll(values, -halves, 1), jnp.roll(values, halves, 1))


def split_heads(rows, heads):
    return rows.reshape(-1, LEN, heads, HEAD_SIZE)


def layer_forward(hidden, pieces, allowed, rope):
    w_qkv, w_out, w_gateup, w_down, gains = pieces
    cos_full, sin_full = rope
    gains = gains.astype(F32)
    group = QUERY_HEADS // KEY_VALUE_HEADS
    scale_one = rms_scale(hidden)
    normed = (hidden * scale_one * gains[0]).astype(BF16)
    qkv = jnp.dot(normed, w_qkv, preferred_element_type=F32)
    straight = qkv[:, :ROPED]
    turned = (straight * cos_full + swap_halves(straight) * sin_full).astype(BF16)
    query = turned[:, : QUERY_HEADS * HEAD_SIZE].reshape(
        -1, LEN, KEY_VALUE_HEADS, group, HEAD_SIZE
    )
    key = split_heads(turned[:, QUERY_HEADS * HEAD_SIZE :], KEY_VALUE_HEADS)
    value = split_heads(qkv[:, ROPED:].astype(BF16), KEY_VALUE_HEADS)
    scores = jnp.einsum("stgja,suga->sgjtu", query, key, preferred_element_type=F32)
    scores = jnp.where(allowed, scores * HEAD_SIZE ** (-0.5), MASKED_SCORE)
    probs = jax.nn.softmax(scores, axis=-1)
    attended = jnp.einsum(
        "sgjtu,suga->stgja", probs.astype(BF16), value, preferred_element_type=F32
    )
    attended = attended.reshape(-1, QUERY_HEADS * HEAD_SIZE).astype(BF16)
    middle = hidden + jnp.dot(attended, w_out, preferred_element_type=F32)
    scale_two = rms_scale(middle)
    normed_two = (middle * scale_two * gains[1]).astype(BF16)
    gate_up = jnp.dot(normed_two, w_gateup, preferred_element_type=F32)
    acted = (jax.nn.silu(gate_up[:, :FEED_UNITS]) * gate_up[:, FEED_UNITS:]).astype(BF16)
    output = middle + jnp.dot(acted, w_down, preferred_element_type=F32)
    kept = (
        hidden, scale_one, normed, query, key, value, probs, attended,
        middle, scale_two, normed_two, gate_up, acted,
    )
    return output, kept


def against(left, right):
    return lax.dot_general(left, right, (((0,), (0,)), ((), ())), preferred_element_type=F32)


def times_t(left, right):
    return lax.dot_general(left, right, (((1,), (1,)), ((), ())), preferred_element_type=F32)


def layer_backward(kept, pieces, rope, grad_output):
    w_qkv, w_out, w_gateup, w_down, gains = pieces
    cos_full, sin_full = rope
    gains = gains.astype(F32)
    (
        hidden, scale_one, normed, query, key, value, probs, attended,
        middle, scale_two, normed_two, gate_up, acted,
    ) = kept
    scaling = HEAD_SIZE ** (-0.5)
    rows = hidden.shape[0]
    grad_low = grad_output.astype(BF16)
    grad_act = times_t(grad_low, w_down).astype(BF16).astype(F32)
    gate, up = gate_up[:, :FEED_UNITS], gate_up[:, FEED_UNITS:]
    sigma = jax.nn.sigmoid(gate)
    grad_up = grad_act * (gate * sigma)
    grad_gate = grad_act * up * (sigma * (1.0 + gate * (1.0 - sigma)))
    grad_gu = jnp.concatenate([grad_gate, grad_up], 1).astype(BF16)
    grad_normed_two = times_t(grad_gu, w_gateup)
    grad_mid, grad_gain_two = rms_back(middle, scale_two, gains[1], grad_normed_two)
    grad_mid = grad_mid + grad_output
    grad_mid_low = grad_mid.astype(BF16)
    grad_att = times_t(grad_mid_low, w_out).astype(BF16).reshape(query.shape)
    grad_probs = jnp.einsum("stgja,suga->sgjtu", grad_att, value, preferred_element_type=F32)
    grad_value = jnp.einsum(
        "sgjtu,stgja->suga", probs.astype(BF16), grad_att, preferred_element_type=F32
    )
    grad_scores = (
        probs * (grad_probs - jnp.sum(grad_probs * probs, axis=-1, keepdims=True))
    ).astype(BF16)
    grad_query = (
        jnp.einsum("sgjtu,suga->stgja", grad_scores, key, preferred_element_type=F32) * scaling
    )
    grad_key = (
        jnp.einsum("sgjtu,stgja->suga", grad_scores, query, preferred_element_type=F32) * scaling
    )
    turned = jnp.concatenate(
        [grad_query.reshape(rows, -1).astype(BF16), grad_key.reshape(rows, -1).astype(BF16)], 1
    ).astype(F32)
    straight = (turned * cos_full - swap_halves(turned) * sin_full).astype(BF16)
    grad_qkv = jnp.concatenate([straight, grad_value.reshape(rows, -1).astype(BF16)], 1)
    grad_normed = times_t(grad_qkv, w_qkv)
    grad_input, grad_gain_one = rms_back(hidden, scale_one, gains[0], grad_normed)
    grad_input = grad_input + grad_mid
    pairs = [
        (normed, grad_qkv), (attended, grad_mid_low), (normed_two, grad_gu), (acted, grad_low),
    ]
    return grad_input, pairs, flat_rows(grad_gain_one, grad_gain_two)


def flat_rows(first, second):
    return jnp.concatenate([first, second]).reshape(-1, 128)


def token_bits(tokens):
    return tokens.bit_length() - 1


def for_chunks(keys_ref, lines_ref, span_ref, columns, run):
    bits = token_bits(keys_ref.shape[0])
    base = span_ref[2]
    places = lax.broadcasted_iota(jnp.int32, (LANES, LANES), 1)

    def chunk_step(chunk, _):
        line = lines_ref[pl.ds(chunk, 1), :]
        ids = jnp.transpose(jnp.broadcast_to(lax.shift_right_logical(line, bits), (LANES, LANES)))
        low = lax.shift_right_logical(keys_ref[chunk * LANES], bits) - base
        high = lax.shift_right_logical(keys_ref[chunk * LANES + LANES - 1], bits) - base
        first = jnp.maximum(low, 0) // COLUMNS
        last = jnp.minimum(high, columns - 1) // COLUMNS

        def hot(block):
            parts = []
            for k in range(COLUMNS // LANES):
                match = ids - (base + block * COLUMNS + k * LANES) == places
                parts.append(jnp.where(match, 1.0, 0.0).astype(BF16))
            return jnp.concatenate(parts, 1)

        run(chunk, first, last + 1, hot)
        return 0

    lax.fori_loop(span_ref[0] // LANES, (span_ref[1] + LANES - 1) // LANES, chunk_step, 0)


def row_of(keys_ref, at):
    return keys_ref[at] & (keys_ref.shape[0] - 1)


def embed_kernel(keys_ref, span_ref, lines_ref, table_ref, out_ref, low_ref, rows_ref, found_ref):
    features, columns = table_ref.shape
    blocks, _, width = out_ref.shape
    low_ref[:features, :] = table_ref[...].astype(BF16)
    low_ref[features:, :] = jnp.zeros((LANES - features, columns), BF16)
    for k in range(blocks):
        rows_ref[k * width : (k + 1) * width, :] = jnp.zeros((width, LANES), F32)

    def run(chunk, first, last, hot):
        def block_step(block, total):
            at = pl.multiple_of(block * COLUMNS, COLUMNS)
            return total + times_t(hot(block), low_ref[:, pl.ds(at, COLUMNS)])

        found_ref[...] = lax.fori_loop(first, last, block_step, jnp.zeros((LANES, LANES), F32))

        def move(k, _):
            for j in range(8):
                row = row_of(keys_ref, chunk * LANES + k * 8 + j)
                rows_ref[pl.ds(row, 1), :] = found_ref[pl.ds(k * 8 + j, 1), :]
            return 0

        lax.fori_loop(0, LANES // 8, move, 0)

    for_chunks(keys_ref, lines_ref, span_ref, columns, run)

    def finish(k, _):
        at = pl.multiple_of(k * width, width)
        out_ref[k] = jnp.transpose(rows_ref[pl.ds(at, width), :])[:features].astype(BF16)
        return 0

    lax.fori_loop(0, blocks, finish, 0)


def embed_rows(keys, span, table, blocks):
    tokens = keys.shape[0]
    features, columns = table.shape
    scalars = pl.BlockSpec(memory_space=pltpu.SMEM)
    in_place = pl.BlockSpec(memory_space=pltpu.VMEM)
    return pl.pallas_call(
        embed_kernel,
        in_specs=[scalars, scalars, in_place, in_place],
        out_specs=in_place,
        out_shape=jax.ShapeDtypeStruct((blocks, features, tokens // blocks), BF16),
        scratch_shapes=[
            pltpu.VMEM((LANES, columns), BF16),
            pltpu.VMEM((tokens, LANES), F32),
            pltpu.VMEM((LANES, LANES), F32),
        ],
        compiler_params=pltpu.CompilerParams(vmem_limit_bytes=VMEM_LIMIT),
        cost_estimate=pl.CostEstimate(
            flops=2 * tokens * LANES * COLUMNS, bytes_accessed=4 * table.size, transcendentals=0
        ),
        name="embed_rows",
    )(keys, span, keys.reshape(-1, LANES), table)


def spread_kernel(keys_ref, span_ref, place_ref, lines_ref, *refs):
    parts, (base_ref, out_ref, rows_ref, packed_ref) = refs[:-4], refs[-4:]
    features, columns = base_ref.shape
    count, _, width = parts[0].shape
    for k, part in enumerate(parts):
        def unfold(j, _):
            at = pl.multiple_of(place_ref[k * count + j] * width, width)
            flat = part[j].astype(F32)
            flat = jnp.concatenate([flat, jnp.zeros((LANES - features, width), F32)], 0)
            rows_ref[pl.ds(at, width), :] = jnp.transpose(flat)
            return 0

        lax.fori_loop(0, count, unfold, 0)
    out_ref[...] = base_ref[...]

    def run(chunk, first, last, hot):
        def move(k, _):
            for j in range(8):
                row = row_of(keys_ref, chunk * LANES + k * 8 + j)
                packed_ref[pl.ds(k * 8 + j, 1), :] = rows_ref[pl.ds(row, 1), :]
            return 0

        lax.fori_loop(0, LANES // 8, move, 0)
        packed = packed_ref[...].astype(BF16)

        def block_step(block, _):
            at = pl.multiple_of(block * COLUMNS, COLUMNS)
            out_ref[:, pl.ds(at, COLUMNS)] += against(packed, hot(block))[:features]
            return 0

        lax.fori_loop(first, last, block_step, 0)

    for_chunks(keys_ref, lines_ref, span_ref, columns, run)


def spread_rows(keys, span, places, parts, base):
    tokens = keys.shape[0]
    scalars = pl.BlockSpec(memory_space=pltpu.SMEM)
    in_place = pl.BlockSpec(memory_space=pltpu.VMEM)
    return pl.pallas_call(
        spread_kernel,
        in_specs=[scalars] * 3 + [in_place] * (2 + len(parts)),
        out_specs=in_place,
        out_shape=jax.ShapeDtypeStruct(base.shape, F32),
        scratch_shapes=[
            pltpu.VMEM((tokens, LANES), F32),
            pltpu.VMEM((LANES, LANES), F32),
        ],
        compiler_params=pltpu.CompilerParams(vmem_limit_bytes=VMEM_LIMIT),
        cost_estimate=pl.CostEstimate(
            flops=2 * tokens * LANES * COLUMNS, bytes_accessed=8 * base.size, transcendentals=0
        ),
        name="spread_rows",
    )(keys, span, places, keys.reshape(-1, LANES), *parts, base)


def block_count(count_ref):
    per = BLOCK // GRANULE
    return (count_ref[0] + per - 1) // per


def block_at(i, count_ref, list_ref):
    return (jnp.minimum(i, jnp.maximum(block_count(count_ref) - 1, 0)), 0)


def head_kernel(
    count_ref, list_ref, rows_ref, table_ref,
    exp_ref, back_ref, sum_ref, peak_ref,
    packed, even, odd,
):
    columns = table_ref.shape[1]
    chunk = even.shape[1]
    chunks = columns // chunk
    logits = (even, odd)
    per = BLOCK // GRANULE
    block = pl.program_id(0)

    @pl.when(block == 0)
    def _():
        back_ref[...] = jnp.zeros(back_ref.shape, F32)
        sum_ref[...] = jnp.ones(sum_ref.shape, F32)
        peak_ref[...] = jnp.zeros(peak_ref.shape, F32)

    def spot(g):
        return pl.multiple_of(list_ref[block * per + g] * GRANULE, GRANULE)

    def dot_chunk(k):
        return jnp.dot(
            packed[...], table_ref[:, k * chunk : (k + 1) * chunk], preferred_element_type=F32
        )

    def put(stat_ref, line):
        for g in range(per):
            lane = g * GRANULE // 128 * 128
            part = line[:, lane : lane + 128]
            if g * GRANULE % 128:
                part = pltpu.roll(part, 128 - g * GRANULE % 128, 1)
            stat_ref[pl.ds(list_ref[block * per + g], 1), :] = part

    def run(peak):
        total = jnp.zeros((BLOCK, 128), F32)
        logits[0][...] = dot_chunk(0)
        for k in range(chunks):
            if k + 1 < chunks:
                logits[(k + 1) % 2][...] = dot_chunk(k + 1)
            here = logits[k % 2][...]
            powers = jnp.exp(here if peak is None else here - peak)
            for j in range(chunk // 128):
                total = total + powers[:, j * 128 : (j + 1) * 128]
            exp_ref[:, k * chunk : (k + 1) * chunk] = powers.astype(BF16)
        line = jnp.sum(jnp.transpose(total), axis=0, keepdims=True)
        put(sum_ref, line)
        back = times_t(exp_ref[...], table_ref[...])
        for g in range(per):
            back_ref[pl.ds(spot(g), GRANULE), :] = back[g * GRANULE : (g + 1) * GRANULE]
        return line

    @pl.when(block < block_count(count_ref))
    def _():
        for g in range(per):
            packed[g * GRANULE : (g + 1) * GRANULE, :] = rows_ref[pl.ds(spot(g), GRANULE), :]
        sums = run(None)
        fits = jnp.min(jnp.where((sums > 1e-20) & (sums < 1e30), 1.0, 0.0))

        @pl.when(fits < 0.5)
        def _():
            wide = jnp.full((BLOCK, 128), -jnp.inf, F32)
            for k in range(chunks):
                here = dot_chunk(k)
                for j in range(chunk // 128):
                    wide = jnp.maximum(wide, here[:, j * 128 : (j + 1) * 128])
            put(peak_ref, jnp.max(jnp.transpose(wide), axis=0, keepdims=True))
            run(jnp.max(wide, axis=1, keepdims=True))


def head_forward(count, order, rows, table):
    height, columns = rows.shape[0], table.shape[1]
    granules = height // GRANULE
    chunk = min(CHUNK // 2, columns // 2)
    whole = pl.Buffered(1)

    def once(i, count_ref, list_ref):
        return (0, 0)

    return pl.pallas_call(
        head_kernel,
        grid_spec=pltpu.PrefetchScalarGridSpec(
            num_scalar_prefetch=2,
            grid=(height // BLOCK,),
            in_specs=[
                pl.BlockSpec(rows.shape, once, pipeline_mode=whole),
                pl.BlockSpec(table.shape, once, pipeline_mode=whole),
            ],
            out_specs=[
                pl.BlockSpec((BLOCK, columns), block_at),
                pl.BlockSpec((height, MODEL_WIDTH), once, pipeline_mode=whole),
                pl.BlockSpec((granules, 128), once),
                pl.BlockSpec((granules, 128), once),
            ],
            scratch_shapes=[
                pltpu.VMEM((BLOCK, MODEL_WIDTH), BF16),
                pltpu.VMEM((BLOCK, chunk), F32),
                pltpu.VMEM((BLOCK, chunk), F32),
            ],
        ),
        out_shape=[
            jax.ShapeDtypeStruct((height, columns), BF16),
            jax.ShapeDtypeStruct((height, MODEL_WIDTH), F32),
            jax.ShapeDtypeStruct((granules, 128), F32),
            jax.ShapeDtypeStruct((granules, 128), F32),
        ],
        compiler_params=pltpu.CompilerParams(vmem_limit_bytes=VMEM_LIMIT),
        cost_estimate=pl.CostEstimate(
            flops=4 * height * table.size,
            bytes_accessed=2 * height * columns,
            transcendentals=height * columns,
        ),
        name="head_forward",
    )(count, order, rows, table)


def table_kernel(count_ref, list_ref, rows_ref, exp_ref, out_ref, packed, total):
    per = BLOCK // GRANULE
    block = pl.program_id(0)
    columns = exp_ref.shape[1]
    chunk = min(CHUNK, columns)

    @pl.when(block == 0)
    def _():
        total[...] = jnp.zeros(total.shape, F32)

    @pl.when(block < block_count(count_ref))
    def _():
        for g in range(per):
            at = block * per + g
            spot = pl.multiple_of(list_ref[at] * GRANULE, GRANULE)
            part = rows_ref[pl.ds(spot, GRANULE), :]
            packed[g * GRANULE : (g + 1) * GRANULE, :] = jnp.where(
                at < count_ref[0], part, jnp.zeros_like(part)
            )
        for k in range(columns // chunk):
            at = slice(k * chunk, (k + 1) * chunk)
            total[:, at] += against(packed[...], exp_ref[:, at])

    @pl.when(block == pl.num_programs(0) - 1)
    def _():
        out_ref[...] = total[...].astype(BF16)


def table_backward(count, order, rows, powers):
    height, columns = powers.shape
    whole = pl.Buffered(1)

    def once(i, count_ref, list_ref):
        return (0, 0)

    return pl.pallas_call(
        table_kernel,
        grid_spec=pltpu.PrefetchScalarGridSpec(
            num_scalar_prefetch=2,
            grid=(height // BLOCK,),
            in_specs=[
                pl.BlockSpec(rows.shape, once, pipeline_mode=whole),
                pl.BlockSpec((BLOCK, columns), block_at),
            ],
            out_specs=pl.BlockSpec((MODEL_WIDTH, columns), once, pipeline_mode=whole),
            scratch_shapes=[
                pltpu.VMEM((BLOCK, MODEL_WIDTH), BF16),
                pltpu.VMEM((MODEL_WIDTH, columns), F32),
            ],
        ),
        out_shape=jax.ShapeDtypeStruct((MODEL_WIDTH, columns), BF16),
        compiler_params=pltpu.CompilerParams(vmem_limit_bytes=VMEM_LIMIT),
        cost_estimate=pl.CostEstimate(
            flops=2 * MODEL_WIDTH * powers.size, bytes_accessed=2 * powers.size, transcendentals=0
        ),
        name="table_backward",
    )(count, order, rows, powers)


def shards(
    token_ids,
    lengths,
    deal_order,
    embed_table,
    table_mom,
    table_avg,
    model_flat,
    model_mom,
    model_avg,
):
    dp_size, shard_size = lax.axis_size("dp"), lax.axis_size("shard")
    shard_idx, dp_idx = lax.axis_index("shard"), lax.axis_index("dp")
    device_idx = lax.axis_index(("dp", "shard"))
    core = dp_bit(1)
    seqs = token_ids.shape[0]
    own_rows = seqs * LEN
    group = 2 * shard_size
    groups = dp_size // 2
    slots = group * seqs
    seq_total = groups * slots
    target_count = jnp.float32((MEAN_LENGTH - 1) * seq_total)
    features, columns = embed_table.shape
    half = columns // 2
    vocab_start = shard_idx * columns + core * half
    length = model_flat.shape[0]

    tiny = jnp.concatenate([token_ids, jnp.broadcast_to(lengths[:, None], (seqs, LEN))], 0)
    tiny = tiny.reshape((1,) * (len(bits_below(dp_size)) + len(bits_below(shard_size))) + tiny.shape)
    for k, bit in enumerate(bits_below(dp_size)[::-1]):
        tiny = join(tiny, flip_dp(tiny, bit), bit, k)
    for k, bit in enumerate(bits_below(shard_size)[::-1]):
        other = flip_shard(tiny, bit)
        axis = len(bits_below(dp_size)) + k
        tiny = jnp.where(
            (shard_idx // bit) % 2 == 0,
            jnp.concatenate([tiny, other], axis),
            jnp.concatenate([other, tiny], axis),
        )
    tiny = tiny.reshape(dp_size * shard_size, 2 * seqs, LEN)
    all_ids = tiny[:, :seqs].reshape(seq_total, LEN)
    all_lens = tiny[:, seqs:, 0].reshape(seq_total)
    here = jnp.arange(seq_total)
    longer = all_lens[None, :] > all_lens[:, None]
    tie = (all_lens[None, :] == all_lens[:, None]) & (here[None, :] < here[:, None])
    rank = jnp.sum((longer | tie).astype(jnp.int32), axis=1)
    turn, seat = rank // groups, rank % groups
    group_of = jnp.where(turn % 2 == 0, seat, groups - 1 - seat)
    place_of = group_of * slots + turn
    hits = (place_of[None, :] == here[:, None]).astype(jnp.int32)
    seq_at = jnp.sum(hits * here[None, :], axis=1)
    dealt_ids = all_ids[seq_at]
    dealt_lens = jnp.sum(hits * all_lens[None, :], axis=1)
    my_group = dp_idx // 2
    group_ids = lax.dynamic_slice_in_dim(dealt_ids, my_group * slots, slots, 0)
    group_lens = lax.dynamic_slice_in_dim(dealt_lens, my_group * slots, slots, 0)
    own_at = core * shard_size + shard_idx
    own_lens = lax.dynamic_slice_in_dim(group_lens, own_at * seqs, seqs, 0)
    own_seqs = lax.dynamic_slice_in_dim(seq_at, (my_group * group + own_at) * seqs, seqs, 0)

    places = jnp.arange(LEN)
    weight_one = (places[None, :] + 1 < group_lens[:, None]).astype(F32)
    weight_two = SECOND_WEIGHT * (places[None, :] + 2 < group_lens[:, None]).astype(F32)
    weights = jnp.stack([weight_one, weight_two]) / target_count

    per_seq = LEN // GRANULE
    starts = jnp.arange(per_seq) * GRANULE
    useful = jnp.stack([starts[None, :] + k + 1 < group_lens[:, None] for k in range(2)])
    useful = useful.reshape(-1)
    index = jnp.arange(useful.shape[0])
    before = jnp.sum((useful[None, :] & (index[None, :] < index[:, None])).astype(jnp.int32), axis=1)
    count = jnp.sum(useful.astype(jnp.int32))
    last = jnp.max(jnp.where(useful, index, 0))
    found = useful[None, :] & (before[None, :] == index[:, None])
    order = jnp.sum(jnp.where(found, index[None, :], 0), axis=1)
    order = jnp.where(index < count, order, last).astype(jnp.int32)
    count = count.reshape(1)

    everything = lax.all_gather(own_blocks(model_flat), ("dp", "shard"))

    tokens = seq_total * LEN
    bits = token_bits(tokens)
    keys = jnp.sort(dealt_ids.reshape(-1) * tokens + jnp.arange(tokens, dtype=jnp.int32))
    first_id = shard_idx * columns
    span = jnp.stack(
        [
            jnp.sum((keys < first_id * tokens).astype(jnp.int32)),
            jnp.sum(((keys >> bits) < first_id + columns).astype(jnp.int32)),
            first_id,
        ]
    ).astype(jnp.int32)
    devices = dp_size * shard_size
    picked = embed_rows(keys, span, embed_table, devices)
    picked = picked.reshape(dp_size, shard_size, features, own_rows)
    mine = ring_reduce(picked.transpose(1, 0, 2, 3)).astype(BF16)
    parts = [pick(mine, dp_idx, 0)]
    parts += [flip_dp(pick(mine, dp_idx ^ k, 0), k) for k in range(1, dp_size)]
    embedded = jnp.stack(parts)[jnp.arange(dp_size) ^ dp_idx]
    embedded = embedded.reshape(MODEL_WIDTH, own_rows).T.astype(F32)

    held_table, everything = lax.optimization_barrier((embed_table, everything))
    table_low = gather_table(held_table)
    middle_rows = PL // 128
    low_rows = middle_rows // 16 * 16
    total_devices = dp_size * shard_size
    per = GRAIN // 128
    end_row = block_starts(length, total_devices)[-1] * per
    tail = 2 * MODEL_WIDTH // 128
    square = MODEL_WIDTH * MODEL_WIDTH // 128
    *layer_zero, gains_zero = unpack_rows(
        everything, length, 0, low_rows + 16, LAYER_SHAPES, {}, 0, ((middle_rows - tail, 16),)
    )
    gain_row = middle_rows - low_rows + middle_rows - tail
    second_row = gain_row + tail + square
    base_one = gain_row // 16 * 16
    base_two = second_row // 16 * 16 - 16
    *layer_one, w_second, gains_one, gains_head = unpack_rows(
        everything, length, low_rows, end_row, LAYER_SHAPES + SQUARE, {3: tail},
        middle_rows - low_rows, ((base_one, 32), (base_two, 32)),
    )

    def gain_pair(rows, at):
        return rows[at : at + tail].reshape(2, MODEL_WIDTH)

    layer_zero.append(gain_pair(gains_zero, 0))
    layer_one.append(gain_pair(gains_one, gain_row - base_one))
    head_gains = gain_pair(gains_head, second_row - base_two).astype(F32)

    allowed = (places[None, :] <= places[:, None])[None] & (
        places[None, None, :] < own_lens[:, None, None]
    )
    allowed = allowed[:, None, None]
    rope = rope_rows(own_rows)
    hidden, kept_zero = layer_forward(embedded, layer_zero, allowed, rope)
    hidden, kept_one = layer_forward(hidden, layer_one, allowed, rope)
    scale_final = rms_scale(hidden)
    head_one = (hidden * scale_final * head_gains[0]).astype(BF16)
    all_one = group_gather(head_one).reshape(-1, MODEL_WIDTH)
    projected = jnp.dot(all_one, w_second, preferred_element_type=F32)
    scale_second = rms_scale(projected)
    all_two = (projected * scale_second * head_gains[1]).astype(BF16)
    both = jnp.concatenate([all_one, all_two], 0)
    group_rows = all_one.shape[0]

    powers, back, sums, peaks = head_forward(count, order, both, table_low)
    sums = sums[:, :GRANULE].reshape(-1, 128)
    peaks = peaks[:, :GRANULE].reshape(-1, 128)
    sum_all_rows, peak_all = sums, peaks
    for flip, bits in ((flip_shard, bits_below(shard_size)), (flip_dp, [1])):
        for bit in bits:
            stats = flip(jnp.stack([sum_all_rows, peak_all]), bit)
            top = jnp.maximum(peak_all, stats[1])
            sum_all_rows = sum_all_rows * jnp.exp(peak_all - top) + stats[0] * jnp.exp(
                stats[1] - top
            )
            peak_all = top
    log_total = (peak_all + jnp.log(sum_all_rows)).reshape(2, group, seqs, LEN)
    row_scale = (
        weights.reshape(-1, 128) * jnp.exp(peaks - peak_all) / sum_all_rows
    ).reshape(-1, 1)

    own_log = pick(log_total, own_at, 1)
    own_weights = pick(weights.reshape(2, group, seqs, LEN), own_at, 1)
    words = embedded.reshape(seqs, LEN, MODEL_WIDTH)
    next_one = jnp.roll(words, -1, 1).reshape(own_rows, MODEL_WIDTH)
    next_two = jnp.roll(words, -2, 1).reshape(own_rows, MODEL_WIDTH)
    head_two = lax.dynamic_slice_in_dim(all_two, own_at * own_rows, own_rows, 0)
    chosen_one = jnp.sum(head_one.astype(F32) * next_one, axis=-1)
    chosen_two = jnp.sum(head_two.astype(F32) * next_two, axis=-1)
    chosen = jnp.stack([chosen_one, chosen_two]).reshape(2, seqs, LEN)
    own_loss = jnp.sum(own_weights * (own_log - chosen), axis=(0, 2))

    weight_col = own_weights.reshape(2, own_rows, 1)
    grad_rows = back * row_scale
    part_two = grad_rows[group_rows:]
    own_two = lax.dynamic_slice_in_dim(part_two, own_at * own_rows, own_rows, 0)
    part_two = lax.dynamic_update_slice_in_dim(
        part_two, own_two - weight_col[1] * next_two, own_at * own_rows, 0
    )
    grad_proj, grad_gain_second = rms_back(projected, scale_second, head_gains[1], part_two)
    grad_proj_low = grad_proj.astype(BF16)
    part_one = grad_rows[:group_rows] + times_t(grad_proj_low, w_second)
    grad_final = group_reduce(part_one.reshape(2, shard_size, own_rows, MODEL_WIDTH))
    scaled_rows = (both.astype(F32) * row_scale).astype(BF16)
    head_grad = table_backward(count, order, scaled_rows, powers)
    table_part = to_owner(reduce_table(head_grad, features), features)
    grad_final = grad_final - weight_col[0] * next_one
    grad_hidden, grad_gain_final = rms_back(hidden, scale_final, head_gains[0], grad_final)

    sub_rows = owner_sub_rows(length)
    height_zero = length * (total_devices // 2 - 1) // GRAIN * per + 2 * sub_rows
    height_one = length * (total_devices - 1) // GRAIN * per + 2 * sub_rows - low_rows
    keep = height_zero - low_rows
    grad_hidden, pairs, gain_grads = layer_backward(kept_one, layer_one, rope, grad_hidden)
    own_one, send_one, kept_rows = pack_half(
        owner_rows(length, 1, low_rows),
        pairs + [(all_one, grad_proj_low)],
        [gain_grads, flat_rows(grad_gain_final, grad_gain_second)],
        None, middle_rows - low_rows, {3: tail, 4: tail}, height_one, sub_rows, keep, 0,
    )
    grad_hidden, own_one, send_one = lax.optimization_barrier((grad_hidden, own_one, send_one))
    reduced_one = reduce_half(own_one, send_one, 1)
    grad_hidden, pairs, gain_grads = layer_backward(kept_zero, layer_zero, rope, grad_hidden)
    own_zero, send_zero = pack_half(
        owner_rows(length, 0, 0), pairs, [gain_grads],
        (kept_rows, height_zero - middle_rows), 0, {3: tail}, height_zero, sub_rows, 0,
        middle_rows - low_rows,
    )
    reduced_zero = reduce_half(own_zero, send_zero, 0)
    model_sum = own_part((reduced_zero, reduced_one), length)

    one_terms = (weight_col[0] * head_one.astype(F32)).reshape(seqs, LEN, MODEL_WIDTH)
    two_terms = (weight_col[1] * head_two.astype(F32)).reshape(seqs, LEN, MODEL_WIDTH)
    token_grad = (
        grad_hidden.astype(BF16).astype(F32)
        - jnp.roll(one_terms, 1, 1).reshape(own_rows, MODEL_WIDTH)
        - jnp.roll(two_terms, 2, 1).reshape(own_rows, MODEL_WIDTH)
    ).astype(BF16)
    token_parts = token_grad.T.reshape(dp_size, features, own_rows)
    parts = [pick(token_parts, dp_idx, 0)]
    parts += [flip_dp(pick(token_parts, dp_idx ^ k, 0), k) for k in range(1, dp_size)]
    chain = [jnp.stack(parts)]
    for _ in range(shard_size - 1):
        chain.append(next_shard(chain[-1]))
    from_dp = (jnp.arange(dp_size) ^ dp_idx)[None, :]
    from_shard = (shard_idx - jnp.arange(shard_size))[:, None] % shard_size
    spots = (from_dp * shard_size + from_shard).reshape(-1).astype(jnp.int32)
    table_sum = spread_rows(keys, span, spots, chain, table_part)

    square_sum = sum_all(
        (jnp.sum(table_sum * table_sum) + jnp.sum(model_sum * model_sum)).reshape(1, 1)
    )[0, 0]
    grad_norm = jnp.sqrt(square_sum)
    factor = jnp.minimum(1.0, CLIP_NORM / (grad_norm + 1e-06))

    spots = jnp.sum(
        jnp.where(own_seqs[:, None] == here[None, :], own_loss[:, None], 0.0), axis=0
    )[None]
    all_loss = sum_all(spots)[0]
    loss_total = jnp.sum(all_loss)
    seq_loss = lax.dynamic_slice_in_dim(all_loss, device_idx * seqs, seqs, 0)
    own_slots = lax.dynamic_slice_in_dim(deal_order, device_idx * seqs, seqs, 0)
    slot_loss = all_loss[own_slots]

    results = []
    for weights_in, gradient, moment, average in (
        (embed_table, table_sum, table_mom, table_avg),
        (model_flat, model_sum, model_mom, model_avg),
    ):
        clipped = gradient * factor
        new_moment = MOMENTUM * moment + clipped
        new_weight = weights_in - LEARN_RATE * (clipped + MOMENTUM * new_moment)
        new_average = AVERAGE_KEEP * average + (1.0 - AVERAGE_KEEP) * new_weight
        results.append(
            (clipped, new_weight, new_moment, new_average, new_weight.astype(BF16))
        )
    return (loss_total, seq_loss, slot_loss, grad_norm) + results[0] + results[1]


def solution(mesh):
    both = P(("dp", "shard"))
    block = P("dp", "shard")
    return jax.shard_map(
        shards,
        mesh=mesh,
        in_specs=(P(("dp", "shard"), None), both, P(), block, block, block, both, both, both),
        out_specs=(P(), both, both, P()) + (block,) * 5 + (both,) * 5,
        check_vma=False,
    )
```

time: 2260 us -> 879 us (0.39); the launches traced: 2230 us -> 872 us
  local copies, waits for them, and re-layouts: 686 us -> 98.2 us
  matrix products: 421 us -> 39.7 us
  blocking collectives: 330 us -> 0 us
  Pallas kernels: 0 us -> 227 us
  waiting for transfers between devices: 454 us -> 260 us
  other arithmetic: 310 us -> 147 us
  starting transfers between devices: 1.5 us -> 76.6 us
    unnamed x21 -> x1, waiting for transfers between devices: 454 us -> 0.02 us
    dot_general x90 -> x28, matrix products: 412 us -> 35.7 us  [the longest x9 13.1 us: times_t(): lax.dot_general(left, right, (((1,), (1,)), ((), ())), preferred_element_...]
    scatter-add x12 -> x0, local copies, waits for them, and re-layouts: 262 us -> none  [add_packed(): flat = flat.at[offset:offset + count_here].add(piece.reshape(-1))]
    ppermute x0 -> x75, waiting for transfers between devices: none -> 260 us  [the longest x46 121 us: flip_dp(): lax.ppermute(values, 'dp', [(i, i ^ bit) for i in range(lax.axis_size('dp...]
    all_gather x13 -> x0, blocking collectives: 251 us -> none  [the longest x6 79.3 us: combined_all(): everything = jax.tree.map(lambda part: lax.all_gather(part, axis), shard)]
    pallas_call x0 -> x8, Pallas kernels: none -> 227 us  [the longest x1 88.2 us: head_forward(): pl.pallas_call(head_kernel, grid_spec=pltpu.PrefetchScalarGridSpec(num_sc...]
    unnamed x639 -> x408, local copies, waits for them, and re-layouts: 181 us -> 36.9 us
    scatter-add x20 -> x0, other arithmetic: 98.8 us -> none  [the longest x2 53.9 us: shards(): table_grad = table_grad.at[:, safe_ids].add(embed_terms)]
  transfers between devices with their start and end apart: 11 -> 76, of which waited for: 4 -> 46; matrix products, arithmetic and copies ran while one was open for 34% -> 19% of each run, Pallas kernels for 0% -> 13%
where the time goes in v1:
time: 879 us; the launch traced here: 872 us
  waiting for transfers between devices  260 us (30%)
  Pallas kernels  227 us (26%)
  other arithmetic  147 us (17%)
  local copies, waits for them, and re-layouts  98.2 us (11%)
  starting transfers between devices  76.6 us (9%)
  matrix products  39.7 us (5%)
  between operations  23.9 us (3%)
    ppermute x46, waiting for transfers between devices, flip_dp(): lax.ppermute(values, 'dp', [(i, i ^ bit) for i in range(lax.axis_size('dp...  121 us
    ppermute x18, waiting for transfers between devices, next_shard(): lax.ppermute(values, 'shard', [(i, (i + 1) % size) for i in range(size)])  115 us
    pallas_call x1, Pallas kernels, head_forward(): pl.pallas_call(head_kernel, grid_spec=pltpu.PrefetchScalarGridSpec(num_sc...  88.2 us
    ppermute x46, starting transfers between devices, flip_dp(): lax.ppermute(values, 'dp', [(i, i ^ bit) for i in range(lax.axis_size('dp...  40.8 us
    pallas_call x1, Pallas kernels, table_backward(): pl.pallas_call(table_kernel, grid_spec=pltpu.PrefetchScalarGridSpec(num_s...  38.2 us
    unnamed x408, local copies, waits for them, and re-layouts  36.9 us
    pallas_call x1, Pallas kernels, spread_rows(): pl.pallas_call(spread_kernel, in_specs=[scalars] * 3 + [in_place] * (2 +...  27.5 us
    pallas_call x1, Pallas kernels, embed_rows(): pl.pallas_call(embed_kernel, in_specs=[scalars, scalars, in_place, in_pla...  24.6 us
  transfers between devices with their start and end apart: 76, of which 46 were waited for; matrix products, arithmetic and copies ran while one was open for 19% of the time, Pallas kernels for 13%

profile of v1, /device:TPU:0, one launch (start us, length us, event | category | flops | bytes accessed | tf_op | source)
XLA Modules:
  0.0 871.9 jit_solution(9867648408956073084)
XLA Ops:
  8.6 4.9 collective-permute-start.15
  18.6 5.2 collective-permute-start
  26.8 3.0 collective-permute-done.1
  31.0 5.4 collective-permute-done.3
  43.2 6.8 sort.14
  52.5 24.6 %embed_rows.1 = bf16[32,72,256]{2,1,0:T(8,128)(2,1)} custom-call(s32[8192]{0:T(1024)} %copy-done.83, s32[3]{0:T(128)} %pad_add_fusion.4.span_ref, s32[64,128]{1,0:T(8,128)} %bitcast.742, f32[72,12288]{1,0:T(8,128)} %table_ref.1), custom_call_target="tpu_custom_call" | custom-call | flops 536870912 | bytes 3538944 | tf_op jit(solution)/shard_map/embed_rows/pallas_call | solution.py:673
  79.2 15.4 %collective-permute-done.5 = bf16[8,72,256]{2,1,0:T(8,128)(2,1)S(1)} collective-permute-done((bf16[8,72,256]{2,1,0:T(8,128)(2,1)S(1)}, bf16[8,72,256]{2,1,0:T(8,128)(2,1)S(1)}, u32[]{:S(2)}, u32[]{:S(2)}) %collective-permute-start.5) | collective-permute-done | bytes 294944 | tf_op jit(solution)/shard_map/ppermute | solution.py:51
  95.8 15.9 %collective-permute-done.6 = bf16[8,72,256]{2,1,0:T(8,128)(2,1)S(1)} collective-permute-done((bf16[8,72,256]{2,1,0:T(8,128)(2,1)S(1)}, bf16[8,72,256]{2,1,0:T(8,128)(2,1)S(1)}, u32[]{:S(2)}, u32[]{:S(2)}) %collective-permute-start.6) | collective-permute-done | bytes 294944 | tf_op jit(solution)/shard_map/ppermute | solution.py:51
  112.7 11.6 %collective-permute-start.7 = (bf16[8,72,256]{2,1,0:T(8,128)(2,1)S(1)}, bf16[8,72,256]{2,1,0:T(8,128)(2,1)S(1)}, u32[]{:S(2)}, u32[]{:S(2)}) collective-permute-start(bf16[8,72,256]{2,1,0:T(8,128)(2,1)S(1)} %fusion.68), channel_id=1, source_target_pairs={{0,1},{1,2},{2,3},{3,0},{4,5},{5,6},{6,7},{7,4},{8,9},{9,10},{10,1... | collective-permute-start | bytes 884744 | tf_op jit(solution)/shard_map/ppermute | solution.py:51
  125.1 16.2 %collective-permute-done.7 = bf16[8,72,256]{2,1,0:T(8,128)(2,1)S(1)} collective-permute-done((bf16[8,72,256]{2,1,0:T(8,128)(2,1)S(1)}, bf16[8,72,256]{2,1,0:T(8,128)(2,1)S(1)}, u32[]{:S(2)}, u32[]{:S(2)}) %collective-permute-start.7) | collective-permute-done | bytes 294944 | tf_op jit(solution)/shard_map/ppermute | solution.py:51
  152.9 11.1 %unpack_rows.2 = (bf16[576,960]{1,0:T(8,128)(2,1)}, bf16[576,576]{1,0:T(8,128)(2,1)}, bf16[576,3072]{1,0:T(8,128)(2,1)}, bf16[1536,576]{1,0:T(8,128)(2,1)}, bf16[16,128]{1,0:T(8,128)(2,1)}) custom-call(bf16[32,1824,128]{2,1,0:T(8,128)(2,1)} %all-gather.2.cloned.1.call-done.all_ref), custom_call_target="tpu_custom_call" | custom-call | bytes 14163968 | tf_op jit(solution)/shard_map/unpack_rows/pallas_call | solution.py:261
  178.2 12.5 %unpack_rows.3 = (bf16[576,960]{1,0:T(8,128)(2,1)}, bf16[576,576]{1,0:T(8,128)(2,1)}, bf16[576,3072]{1,0:T(8,128)(2,1)}, bf16[1536,576]{1,0:T(8,128)(2,1)}, bf16...) custom-call(bf16[32,1824,128]{2,1,0:T(8,128)(2,1)} %all-gather.2.cloned.1.call-done.all_ref), custom_call_target="tpu_custom_call" | custom-call | bytes 15499264 | tf_op jit(solution)/shard_map/unpack_rows/pallas_call | solution.py:261
  232.0 10.3 %collective-permute-done.16 = bf16[256,576]{1,0:T(8,128)(2,1)S(1)} collective-permute-done((bf16[256,576]{1,0:T(8,128)(2,1)S(1)}, bf16[256,576]{1,0:T(8,128)(2,1)S(1)}, u32[]{:S(2)}, u32[]{:S(2)}) %collective-permute-start.16) | collective-permute-done | bytes 294944 | tf_op jit(solution)/shard_map/ppermute | solution.py:51
  242.5 10.7 %collective-permute-done.17 = bf16[256,576]{1,0:T(8,128)(2,1)S(1)} collective-permute-done((bf16[256,576]{1,0:T(8,128)(2,1)S(1)}, bf16[256,576]{1,0:T(8,128)(2,1)S(1)}, u32[]{:S(2)}, u32[]{:S(2)}) %collective-permute-start.17) | collective-permute-done | bytes 294944 | tf_op jit(solution)/shard_map/ppermute | solution.py:51
  259.2 4.3 collective-permute-done.18
  268.3 8.9 %collective-permute-done.21 = bf16[1,1,144,3072]{3,2,1,0:T(8,128)(2,1)} collective-permute-done((bf16[1,1,144,3072]{3,2,1,0:T(8,128)(2,1)}, bf16[1,1,144,3072]{3,2,1,0:T(8,128)(2,1)}, u32[]{:S(2)}, u32[]{:S(2)}) %collective-permute-start.21) | collective-permute-done | bytes 884768 | tf_op jit(solution)/shard_map/ppermute | solution.py:42
  277.2 3.6 maximum_select_fusion.5
  281.9 3.5 maximum_select_fusion.6
  288.6 4.4 copy.437
  293.0 6.0 multiply_reduce_fusion.2
  299.0 5.8 copy.438
  304.8 3.2 multiply_convert_fusion.1
  308.1 3.2 pad_maximum_fusion.1.rows_ref
  311.3 8.0 collective-permute-done.22
  319.3 3.8 maximum_select_fusion
  323.6 5.2 maximum_select_fusion.1
  328.7 5.5 pad_maximum_fusion.table_ref
  334.2 88.2 %head_forward.1 = (bf16[4096,6144]{1,0:T(8,128)(2,1)}, f32[4096,576]{1,0:T(8,128)}, f32[256,128]{1,0:T(8,128)}, f32[256,128]{1,0:T(8,128)}) custom-call(s32[1]{0:T(128)} %bitcast.16.count_ref, s32[256]{0:T(256)} %compare_select_fusion.9.list_ref, bf16[4096,576]{1,0:T(8,128)(2,1)} %pad_maximum_fusion.1.rows_ref, bf16[576,6144]{1,0:T(8,128)(2,1)} %pad_maximum_fusion.table_ref), custom_call_target="tpu_custom_call" | custom-call | flops 57982058496 | bytes 50331648 | tf_op jit(solution)/shard_map/head_forward/pallas_call | solution.py:835
  424.7 3.8 collective-permute-done.25
  430.9 3.4 collective-permute-done.26
  438.9 10.0 %multiply_convert_fusion = (bf16[4096,576]{1,0:T(8,128)(2,1)}, f32[4096,576]{1,0:T(8,128)S(1)}) fusion(f32[4096]{0:T(1024)S(1)} %fusion.140, bf16[2048,576]{1,0:T(8,128)(2,1)} %copy-done.3, bf16[2048,576]{1,0:T(8,128)(2,1)} %bitcast.686, f32[4096,576]{1,0:T(8,128)} %get-tuple-element.59), kind=kLoop, calls=%fused_computation.5 | loop fusion | flops 16515072 | bytes 28327936 | tf_op jit(solution)/shard_map/convert_element_type | solution.py:1114
  455.1 2.8 slice_add_fusion
  462.4 38.2 %table_backward.1 = bf16[576,6144]{1,0:T(8,128)(2,1)} custom-call(s32[1]{0:T(128)} %bitcast.16.count_ref, s32[256]{0:T(256)} %compare_select_fusion.9.list_ref, bf16[4096,576]{1,0:T(8,128)(2,1)} %get-tuple-element.178.rows_ref, bf16[4096,6144]{1,0:T(8,128)(2,1)} %get-tuple-element.63.exp_ref), custom_call_target="tpu_custom_call" | custom-call | flops 28991029248 | bytes 50331648 | tf_op jit(solution)/shard_map/table_backward/pallas_call | solution.py:907
  500.7 3.6 fusion.227
  517.1 9.0 %collective-permute-done.34 = bf16[256,576]{1,0:T(8,128)(2,1)S(1)} collective-permute-done((bf16[256,576]{1,0:T(8,128)(2,1)S(1)}, bf16[256,576]{1,0:T(8,128)(2,1)S(1)}, u32[]{:S(2)}, u32[]{:S(2)}) %collective-permute-start.34) | collective-permute-done | bytes 294944 | tf_op jit(solution)/shard_map/ppermute | solution.py:51
  526.3 20.4 %collective-permute-done.49 = bf16[2,144,3072]{2,1,0:T(8,128)(2,1)} collective-permute-done((bf16[2,144,3072]{2,1,0:T(8,128)(2,1)}, bf16[2,144,3072]{2,1,0:T(8,128)(2,1)}, u32[]{:S(2)}, u32[]{:S(2)}) %collective-permute-start.49) | collective-permute-done | bytes 1769504 | tf_op jit(solution)/shard_map/ppermute | solution.py:42
  556.4 7.9 collective-permute-done.36
  586.8 14.4 %pack_half.2 = (bf16[16,928,128]{2,1,0:T(8,128)(2,1)}, bf16[16,928,128]{2,1,0:T(8,128)(2,1)}, bf16[1344,128]{1,0:T(8,128)(2,1)}) custom-call(s32[32]{0:T(128)} %pad_add_fusion.5.info_ref, bf16[256,576]{1,0:T(8,128)(2,1)} %copy-done.67, bf16[256,576]{1,0:T(8,128)(2,1)} %copy.465.refs_1_, bf16[256,576]{1,0:T(8,128)(2,1)} %copy-done.62, ...), custom_call_target="tpu_custom_call" | custom-call | flops 3170893824 | bytes 15515648 | tf_op jit(solution)/shard_map/pack_half/pallas_call | solution.py:373
  602.4 3.7 multiply_convert_fusion.3
  631.0 10.2 %pack_half.3 = (bf16[16,928,128]{2,1,0:T(8,128)(2,1)}, bf16[16,928,128]{2,1,0:T(8,128)(2,1)}) custom-call(s32[32]{0:T(128)} %pad_add_fusion.6.info_ref, bf16[256,576]{1,0:T(8,128)(2,1)} %copy-done.66, bf16[256,576]{1,0:T(8,128)(2,1)} %copy.488.refs_1_, bf16[256,576]{1,0:T(8,128)(2,1)} %copy-done.61, bf16[256,1536]{1,0:T(8,128)(2,1)} %copy-done.45, ...), custom_call_target="tpu_custom_call" | custom-call | flops 1811939328 | bytes 14843904 | tf_op jit(solution)/shard_map/pack_half/pallas_call | solution.py:373
  643.0 2.7 collective-permute-done.38
  646.3 2.8 collective-permute-done.39
  653.7 2.8 collective-permute-done.41
  658.4 2.9 collective-permute-done.42
  661.9 3.7 collective-permute-done.43
  681.3 19.4 %collective-permute-done.63 = bf16[2,2,928,128]{3,2,1,0:T(8,128)(2,1)S(1)} collective-permute-done((bf16[2,2,928,128]{3,2,1,0:T(8,128)(2,1)S(1)}, bf16[2,2,928,128]{3,2,1,0:T(8,128)(2,1)S(1)}, u32[]{:S(2)}, u32[]{:S(2)}) %collective-permute-start.63) | collective-permute-done | bytes 950304 | tf_op jit(solution)/shard_map/ppermute | solution.py:42
  702.3 16.3 %collective-permute-done.55 = bf16[2,2,928,128]{3,2,1,0:T(8,128)(2,1)S(1)} collective-permute-done((bf16[2,2,928,128]{3,2,1,0:T(8,128)(2,1)S(1)}, bf16[2,2,928,128]{3,2,1,0:T(8,128)(2,1)S(1)}, u32[]{:S(2)}, u32[]{:S(2)}) %collective-permute-start.55) | collective-permute-done | bytes 950304 | tf_op jit(solution)/shard_map/ppermute | solution.py:42
  721.3 8.4 collective-permute-done.64
  732.1 7.7 collective-permute-done.56
  743.1 5.9 collective-permute-done.65
  754.9 4.8 collective-permute-done.66
  761.8 4.3 collective-permute-done.45.refs_2_
  766.0 5.2 collective-permute-done.58
  773.0 3.2 collective-permute-done.67
  777.0 3.5 collective-permute-start.68
  780.6 4.3 maximum_select_fusion.2.refs_4_
  784.9 27.5 %spread_rows.1 = f32[72,12288]{1,0:T(8,128)} custom-call(s32[8192]{0:T(1024)} %copy-done.83, s32[3]{0:T(128)} %pad_add_fusion.4.span_ref, s32[32]{0:T(128)} %add.1010.place_ref, s32[64,128]{1,0:T(8,128)} %bitcast.743, bf16[8,72,256]{2,1,0:T(8,128)(2,1)} %constant_dynamic-update-slice_fusion.8.refs_0_, bf16[8,72,256]{2,1,0:T(8,128)(2,1)} %copy-done.101, ...), custom_call_target="tpu_custom_call" | custom-call | flops 536870912 | bytes 7077888 | tf_op jit(solution)/shard_map/spread_rows/pallas_call | solution.py:730
  815.3 3.5 multiply_reduce_fusion.3
  818.8 3.0 collective-permute-done.69
  841.1 3.1 collective-permute-done.74
  845.0 4.0 fusion.220
  849.0 6.5 fusion.221
  855.5 3.8 multiply_add_fusion.2
  859.3 4.4 multiply_add_fusion
  (837 shorter events, 259.8 us)
Async XLA Ops:
  7.2 145.7 %all-gather.2.cloned.1.call-start = ((), (), s32[]{:S(2)}) async-start(), calls=%async_computation | async-start | bytes 15409152 | tf_op jit(solution)/shard_map/all_gather | solution.py:1009
  8.6 6.2 collective-permute-start.15
  18.6 7.5 collective-permute-start
  31.0 5.5 collective-permute-start.3
  36.4 5.0 collective-permute-start.4
  78.1 16.4 %collective-permute-start.5 = (bf16[8,72,256]{2,1,0:T(8,128)(2,1)S(1)}, bf16[8,72,256]{2,1,0:T(8,128)(2,1)S(1)}, u32[]{:S(2)}, u32[]{:S(2)}) collective-permute-start(bf16[8,72,256]{2,1,0:T(8,128)(2,1)S(1)} %dynamic-slice_bitcast_fusion.7), channel_id=1, source_target_pairs={{0,1},{1,2},{2,3},{3,0},{4,5},{5,6},{6,7},{7,4},{8,9},{9,10},{10,1... | collective-permute-start | bytes 884744 | tf_op jit(solution)/shard_map/ppermute | solution.py:51
  95.6 16.1 %collective-permute-start.6 = (bf16[8,72,256]{2,1,0:T(8,128)(2,1)S(1)}, bf16[8,72,256]{2,1,0:T(8,128)(2,1)S(1)}, u32[]{:S(2)}, u32[]{:S(2)}) collective-permute-start(bf16[8,72,256]{2,1,0:T(8,128)(2,1)S(1)} %fusion.67), channel_id=1, source_target_pairs={{0,1},{1,2},{2,3},{3,0},{4,5},{5,6},{6,7},{7,4},{8,9},{9,10},{10,1... | collective-permute-start | bytes 884744 | tf_op jit(solution)/shard_map/ppermute | solution.py:51
  112.7 28.6 %collective-permute-start.7 = (bf16[8,72,256]{2,1,0:T(8,128)(2,1)S(1)}, bf16[8,72,256]{2,1,0:T(8,128)(2,1)S(1)}, u32[]{:S(2)}, u32[]{:S(2)}) collective-permute-start(bf16[8,72,256]{2,1,0:T(8,128)(2,1)S(1)} %fusion.68), channel_id=1, source_target_pairs={{0,1},{1,2},{2,3},{3,0},{4,5},{5,6},{6,7},{7,4},{8,9},{9,10},{10,1... | collective-permute-start | bytes 884744 | tf_op jit(solution)/shard_map/ppermute | solution.py:51
  142.4 4.2 collective-permute-start.8
  143.0 4.6 collective-permute-start.9
  143.6 5.7 collective-permute-start.10
  144.9 4.4 collective-permute-start.11
  145.2 4.1 collective-permute-start.12
  146.5 4.9 collective-permute-start.13
  147.6 4.3 collective-permute-start.14
  217.8 35.8 %collective-permute-start.20 = (bf16[72,6144]{1,0:T(8,128)(2,1)}, bf16[72,6144]{1,0:T(8,128)(2,1)}, u32[]{:S(2)}, u32[]{:S(2)}) collective-permute-start(bf16[72,6144]{1,0:T(8,128)(2,1)} %get-tuple-element.133), channel_id=1, source_target_pairs={{0,4},{4,0},{8,12},{12,8},{16,20},{20,16},{24,28},{28,24},{1,5},{5... | collective-permute-start | bytes 2654216 | tf_op jit(solution)/shard_map/ppermute | solution.py:42
  230.6 11.7 %collective-permute-start.16 = (bf16[256,576]{1,0:T(8,128)(2,1)S(1)}, bf16[256,576]{1,0:T(8,128)(2,1)S(1)}, u32[]{:S(2)}, u32[]{:S(2)}) collective-permute-start(bf16[256,576]{1,0:T(8,128)(2,1)S(1)} %get-tuple-element.107), channel_id=1, source_target_pairs={{0,1},{1,2},{2,3},{3,0},{4,5},{5,6},{6,7},{7,4},{8,9},{9,10},{10,1... | collective-permute-start | bytes 884744 | tf_op jit(solution)/shard_map/ppermute | solution.py:51
  242.3 10.9 %collective-permute-start.17 = (bf16[256,576]{1,0:T(8,128)(2,1)S(1)}, bf16[256,576]{1,0:T(8,128)(2,1)S(1)}, u32[]{:S(2)}, u32[]{:S(2)}) collective-permute-start(bf16[256,576]{1,0:T(8,128)(2,1)S(1)} %collective-permute-done.16), channel_id=1, source_target_pairs={{0,1},{1,2},{2,3},{3,0},{4,5},{5,6},{6,7},{7,4},{8,9},{9,10},{10,1... | collective-permute-start | bytes 884744 | tf_op jit(solution)/shard_map/ppermute | solution.py:51
  253.2 10.4 %collective-permute-start.18 = (bf16[256,576]{1,0:T(8,128)(2,1)S(1)}, bf16[256,576]{1,0:T(8,128)(2,1)S(1)}, u32[]{:S(2)}, u32[]{:S(2)}) collective-permute-start(bf16[256,576]{1,0:T(8,128)(2,1)S(1)} %collective-permute-done.17), channel_id=1, source_target_pairs={{0,1},{1,2},{2,3},{3,0},{4,5},{5,6},{6,7},{7,4},{8,9},{9,10},{10,1... | collective-permute-start | bytes 884744 | tf_op jit(solution)/shard_map/ppermute | solution.py:51
  256.8 20.4 %collective-permute-start.21 = (bf16[1,1,144,3072]{3,2,1,0:T(8,128)(2,1)}, bf16[1,1,144,3072]{3,2,1,0:T(8,128)(2,1)}, u32[]{:S(2)}, u32[]{:S(2)}) collective-permute-start(bf16[1,1,144,3072]{3,2,1,0:T(8,128)(2,1)} %get-tuple-element.130), channel_id=1, source_target_pairs={{0,8},{4,12},{8,0},{12,4},{16,24},{20,28},{24,16},{28,20},{1,9},{5... | collective-permute-start | bytes 2654216 | tf_op jit(solution)/shard_map/ppermute | solution.py:42
  257.7 24.2 %collective-permute-start.23 = (bf16[1,1,144,3072]{3,2,1,0:T(8,128)(2,1)}, bf16[1,1,144,3072]{3,2,1,0:T(8,128)(2,1)}, u32[]{:S(2)}, u32[]{:S(2)}) collective-permute-start(bf16[1,1,144,3072]{3,2,1,0:T(8,128)(2,1)} %get-tuple-element.131), channel_id=1, source_target_pairs={{0,16},{4,20},{8,24},{12,28},{16,0},{20,4},{24,8},{28,12},{1,17},{... | collective-permute-start | bytes 2654216 | tf_op jit(solution)/shard_map/ppermute | solution.py:42
  264.7 22.1 %collective-permute-start.19 = (bf16[4,256,576]{1,2,0:T(8,128)(2,1)S(1)}, bf16[4,256,576]{1,2,0:T(8,128)(2,1)S(1)}, u32[]{:S(2)}, u32[]{:S(2)}) collective-permute-start(bf16[4,256,576]{1,2,0:T(8,128)(2,1)S(1)} %copy.435), channel_id=1, source_target_pairs={{0,4},{4,0},{8,12},{12,8},{16,20},{20,16},{24,28},{28,24},{1,5},{5... | collective-permute-start | bytes 3538952 | tf_op jit(solution)/shard_map/ppermute | solution.py:42
  280.9 38.5 %collective-permute-start.22 = (bf16[1,2,144,3072]{3,2,1,0:T(8,128)(2,1)}, bf16[1,2,144,3072]{3,2,1,0:T(8,128)(2,1)}, u32[]{:S(2)}, u32[]{:S(2)}) collective-permute-start(bf16[1,2,144,3072]{3,2,1,0:T(8,128)(2,1)} %maximum_select_fusion.5), channel_id=1, source_target_pairs={{0,16},{4,20},{8,24},{12,28},{16,0},{20,4},{24,8},{28,12},{1,17},{... | collective-permute-start | bytes 5308424 | tf_op jit(solution)/shard_map/ppermute | solution.py:42
  285.4 38.2 %collective-permute-start.24 = (bf16[2,1,144,3072]{3,2,1,0:T(8,128)(2,1)}, bf16[2,1,144,3072]{3,2,1,0:T(8,128)(2,1)}, u32[]{:S(2)}, u32[]{:S(2)}) collective-permute-start(bf16[2,1,144,3072]{3,2,1,0:T(8,128)(2,1)} %maximum_select_fusion.6), channel_id=1, source_target_pairs={{0,8},{4,12},{8,0},{12,4},{16,24},{20,28},{24,16},{28,20},{1,9},{5... | collective-permute-start | bytes 5308424 | tf_op jit(solution)/shard_map/ppermute | solution.py:42
  424.5 4.1 collective-permute-start.25
  429.2 5.2 collective-permute-start.26
  461.9 49.1 %collective-permute-start.33 = (bf16[4,256,576]{1,2,0:T(8,128)(2,1)}, bf16[4,256,576]{1,2,0:T(8,128)(2,1)}, u32[]{:S(2)}, u32[]{:S(2)}) collective-permute-start(bf16[4,256,576]{1,2,0:T(8,128)(2,1)} %bitcast.734), channel_id=1, source_target_pairs={{0,4},{4,0},{8,12},{12,8},{16,20},{20,16},{24,28},{28,24},{1,5},{5... | collective-permute-start | bytes 3538952 | tf_op jit(solution)/shard_map/ppermute | solution.py:42
  505.8 40.8 %collective-permute-start.49 = (bf16[2,144,3072]{2,1,0:T(8,128)(2,1)}, bf16[2,144,3072]{2,1,0:T(8,128)(2,1)}, u32[]{:S(2)}, u32[]{:S(2)}) collective-permute-start(bf16[2,144,3072]{2,1,0:T(8,128)(2,1)} %dynamic-slice_bitcast_fusion), channel_id=1, source_target_pairs={{0,16},{4,20},{8,24},{12,28},{16,0},{20,4},{24,8},{28,12},{1,17},{... | collective-permute-start | bytes 5308424 | tf_op jit(solution)/shard_map/ppermute | solution.py:42
  508.4 43.1 %collective-permute-start.47 = (bf16[2,144,3072]{2,1,0:T(8,128)(2,1)}, bf16[2,144,3072]{2,1,0:T(8,128)(2,1)}, u32[]{:S(2)}, u32[]{:S(2)}) collective-permute-start(bf16[2,144,3072]{2,1,0:T(8,128)(2,1)} %dynamic-slice_bitcast_fusion.1), channel_id=1, source_target_pairs={{0,8},{4,12},{8,0},{12,4},{16,24},{20,28},{24,16},{28,20},{1,9},{5... | collective-permute-start | bytes 5308424 | tf_op jit(solution)/shard_map/ppermute | solution.py:42
  515.0 11.2 %collective-permute-start.34 = (bf16[256,576]{1,0:T(8,128)(2,1)S(1)}, bf16[256,576]{1,0:T(8,128)(2,1)S(1)}, u32[]{:S(2)}, u32[]{:S(2)}) collective-permute-start(bf16[256,576]{1,0:T(8,128)(2,1)S(1)} %fusion.79), channel_id=1, source_target_pairs={{0,1},{1,2},{2,3},{3,0},{4,5},{5,6},{6,7},{7,4},{8,9},{9,10},{10,1... | collective-permute-start | bytes 884744 | tf_op jit(solution)/shard_map/ppermute | solution.py:51
  526.2 27.5 %collective-permute-start.35 = (bf16[256,576]{1,0:T(8,128)(2,1)S(1)}, bf16[256,576]{1,0:T(8,128)(2,1)S(1)}, u32[]{:S(2)}, u32[]{:S(2)}) collective-permute-start(bf16[256,576]{1,0:T(8,128)(2,1)S(1)} %fusion.54), channel_id=1, source_target_pairs={{0,1},{1,2},{2,3},{3,0},{4,5},{5,6},{6,7},{7,4},{8,9},{9,10},{10,1... | collective-permute-start | bytes 884744 | tf_op jit(solution)/shard_map/ppermute | solution.py:51
  550.1 117.7 %collective-permute-start.50 = (bf16[144,3072]{1,0:T(8,128)(2,1)}, bf16[144,3072]{1,0:T(8,128)(2,1)}, u32[]{:S(2)}, u32[]{:S(2)}) collective-permute-start(bf16[144,3072]{1,0:T(8,128)(2,1)} %fusion.37), channel_id=1, source_target_pairs={{0,8},{4,12},{8,0},{12,4},{16,24},{20,28},{24,16},{28,20},{1,9},{5... | collective-permute-start | bytes 2654216 | tf_op jit(solution)/shard_map/ppermute | solution.py:42
  553.8 10.6 %collective-permute-start.36 = (bf16[256,576]{1,0:T(8,128)(2,1)S(1)}, bf16[256,576]{1,0:T(8,128)(2,1)S(1)}, u32[]{:S(2)}, u32[]{:S(2)}) collective-permute-start(bf16[256,576]{1,0:T(8,128)(2,1)S(1)} %fusion.55), channel_id=1, source_target_pairs={{0,1},{1,2},{2,3},{3,0},{4,5},{5,6},{6,7},{7,4},{8,9},{9,10},{10,1... | collective-permute-start | bytes 884744 | tf_op jit(solution)/shard_map/ppermute | solution.py:51
  555.6 114.8 %collective-permute-start.48 = (bf16[144,3072]{1,0:T(8,128)(2,1)}, bf16[144,3072]{1,0:T(8,128)(2,1)}, u32[]{:S(2)}, u32[]{:S(2)}) collective-permute-start(bf16[144,3072]{1,0:T(8,128)(2,1)} %fusion.36), channel_id=1, source_target_pairs={{0,16},{4,20},{8,24},{12,28},{16,0},{20,4},{24,8},{28,12},{1,17},{... | collective-permute-start | bytes 2654216 | tf_op jit(solution)/shard_map/ppermute | solution.py:42
  625.1 16.6 %collective-permute-start.37 = (bf16[72,256]{1,0:T(8,128)(2,1)S(1)}, bf16[72,256]{1,0:T(8,128)(2,1)S(1)}, u32[]{:S(2)}, u32[]{:S(2)}) collective-permute-start(bf16[72,256]{1,0:T(8,128)(2,1)S(1)} %get-tuple-element.160), channel_id=1, source_target_pairs={{0,4},{4,0},{8,12},{12,8},{16,20},{20,16},{24,28},{28,24},{1,5},{5... | collective-permute-start | bytes 110600 | tf_op jit(solution)/shard_map/ppermute | solution.py:42
  631.0 10.3 %collective-permute-start.31 = (f32[1,64]{1,0:T(1,128)S(1)}, f32[1,64]{1,0:T(1,128)S(1)}, u32[]{:S(2)}, u32[]{:S(2)}) collective-permute-start(f32[1,64]{1,0:T(1,128)S(1)} %add.1001), channel_id=1, source_target_pairs={{0,1},{1,0},{2,3},{3,2},{4,5},{5,4},{6,7},{7,6},{8,9},{9,8},{10,11... | collective-permute-start | bytes 776 | tf_op jit(solution)/shard_map/ppermute | solution.py:46
  641.2 37.6 %collective-permute-start.52 = (bf16[16,928,128]{2,1,0:T(8,128)(2,1)}, bf16[16,928,128]{2,1,0:T(8,128)(2,1)S(1)}, u32[]{:S(2)}, u32[]{:S(2)}) collective-permute-start(bf16[16,928,128]{2,1,0:T(8,128)(2,1)} %get-tuple-element.66), channel_id=1, source_target_pairs={{0,4},{4,0},{8,12},{12,8},{16,20},{20,16},{24,28},{28,24},{1,5},{5... | collective-permute-start | bytes 11403272 | tf_op jit(solution)/shard_map/ppermute | solution.py:42
  641.3 32.9 %collective-permute-start.60 = (bf16[16,928,128]{2,1,0:T(8,128)(2,1)}, bf16[16,928,128]{2,1,0:T(8,128)(2,1)S(1)}, u32[]{:S(2)}, u32[]{:S(2)}) collective-permute-start(bf16[16,928,128]{2,1,0:T(8,128)(2,1)} %get-tuple-element.68), channel_id=1, source_target_pairs={{0,4},{4,0},{8,12},{12,8},{16,20},{20,16},{24,28},{28,24},{1,5},{5... | collective-permute-start | bytes 11403272 | tf_op jit(solution)/shard_map/ppermute | solution.py:42
  641.8 4.0 collective-permute-start.38
  649.1 4.0 collective-permute-start.40
  656.4 4.9 collective-permute-start.42
  661.3 4.3 collective-permute-start.43
  665.6 83.6 %collective-permute-start.32 = (f32[1,64]{1,0:T(1,128)S(1)}, f32[1,64]{1,0:T(1,128)S(1)}, u32[]{:S(2)}, u32[]{:S(2)}) collective-permute-start(f32[1,64]{1,0:T(1,128)S(1)} %add.1002), channel_id=1, source_target_pairs={{0,2},{1,3},{2,0},{3,1},{4,6},{5,7},{6,4},{7,5},{8,10},{9,11},{10,... | collective-permute-start | bytes 776 | tf_op jit(solution)/shard_map/ppermute | solution.py:46
  667.8 82.0 %collective-permute-start.44 = (bf16[8,72,256]{2,1,0:T(8,128)(2,1)}, bf16[8,72,256]{2,1,0:T(8,128)(2,1)S(1)}, u32[]{:S(2)}, u32[]{:S(2)}) collective-permute-start(bf16[8,72,256]{2,1,0:T(8,128)(2,1)} %constant_dynamic-update-slice_fusion.8.refs_0_), channel_id=1, source_target_pairs={{0,1},{1,2},{2,3},{3,0},{4,5},{5,6},{6,7},{7,4},{8,9},{9,10},{10,1... | collective-permute-start | bytes 884744 | tf_op jit(solution)/shard_map/ppermute | solution.py:51
  676.7 24.1 %collective-permute-start.63 = (bf16[2,2,928,128]{3,2,1,0:T(8,128)(2,1)S(1)}, bf16[2,2,928,128]{3,2,1,0:T(8,128)(2,1)S(1)}, u32[]{:S(2)}, u32[]{:S(2)}) collective-permute-start(bf16[2,2,928,128]{3,2,1,0:T(8,128)(2,1)S(1)} %dynamic-slice_bitcast_fusion.2), channel_id=1, source_target_pairs={{0,16},{4,20},{8,24},{12,28},{16,0},{20,4},{24,8},{28,12},{1,17},{... | collective-permute-start | bytes 2850824 | tf_op jit(solution)/shard_map/ppermute | solution.py:42
  677.8 24.2 %collective-permute-start.61 = (bf16[2,2,928,128]{3,2,1,0:T(8,128)(2,1)S(1)}, bf16[2,2,928,128]{3,2,1,0:T(8,128)(2,1)S(1)}, u32[]{:S(2)}, u32[]{:S(2)}) collective-permute-start(bf16[2,2,928,128]{3,2,1,0:T(8,128)(2,1)S(1)} %dynamic-slice_bitcast_fusion.3), channel_id=1, source_target_pairs={{0,8},{4,12},{8,0},{12,4},{16,24},{20,28},{24,16},{28,20},{1,9},{5... | collective-permute-start | bytes 2850824 | tf_op jit(solution)/shard_map/ppermute | solution.py:42
  680.1 38.5 %collective-permute-start.55 = (bf16[2,2,928,128]{3,2,1,0:T(8,128)(2,1)S(1)}, bf16[2,2,928,128]{3,2,1,0:T(8,128)(2,1)S(1)}, u32[]{:S(2)}, u32[]{:S(2)}) collective-permute-start(bf16[2,2,928,128]{3,2,1,0:T(8,128)(2,1)S(1)} %dynamic-slice_bitcast_fusion.4), channel_id=1, source_target_pairs={{0,16},{4,20},{8,24},{12,28},{16,0},{20,4},{24,8},{28,12},{1,17},{... | collective-permute-start | bytes 2850824 | tf_op jit(solution)/shard_map/ppermute | solution.py:42
  700.7 19.4 %collective-permute-start.53 = (bf16[2,2,928,128]{3,2,1,0:T(8,128)(2,1)S(1)}, bf16[2,2,928,128]{3,2,1,0:T(8,128)(2,1)S(1)}, u32[]{:S(2)}, u32[]{:S(2)}) collective-permute-start(bf16[2,2,928,128]{3,2,1,0:T(8,128)(2,1)S(1)} %dynamic-slice_bitcast_fusion.5), channel_id=1, source_target_pairs={{0,8},{4,12},{8,0},{12,4},{16,24},{20,28},{24,16},{28,20},{1,9},{5... | collective-permute-start | bytes 2850824 | tf_op jit(solution)/shard_map/ppermute | solution.py:42
  702.0 78.6 %collective-permute-start.51 = (f32[72,6144]{1,0:T(8,128)}, f32[72,6144]{1,0:T(8,128)}, u32[]{:S(2)}, u32[]{:S(2)}) collective-permute-start(f32[72,6144]{1,0:T(8,128)} %get-tuple-element.127), channel_id=1, source_target_pairs={{0,4},{4,0},{8,12},{12,8},{16,20},{20,16},{24,28},{28,24},{1,5},{5... | collective-permute-start | bytes 5308424 | tf_op jit(solution)/shard_map/ppermute | solution.py:42
  718.6 11.1 %collective-permute-start.64 = (bf16[2,928,128]{2,1,0:T(8,128)(2,1)S(1)}, bf16[2,928,128]{2,1,0:T(8,128)(2,1)S(1)}, u32[]{:S(2)}, u32[]{:S(2)}) collective-permute-start(bf16[2,928,128]{2,1,0:T(8,128)(2,1)S(1)} %fusion.72), channel_id=1, source_target_pairs={{0,8},{4,12},{8,0},{12,4},{16,24},{20,28},{24,16},{28,20},{1,9},{5... | collective-permute-start | bytes 1425416 | tf_op jit(solution)/shard_map/ppermute | solution.py:42
  720.1 10.8 %collective-permute-start.62 = (bf16[2,928,128]{2,1,0:T(8,128)(2,1)S(1)}, bf16[2,928,128]{2,1,0:T(8,128)(2,1)S(1)}, u32[]{:S(2)}, u32[]{:S(2)}) collective-permute-start(bf16[2,928,128]{2,1,0:T(8,128)(2,1)S(1)} %fusion.71), channel_id=1, source_target_pairs={{0,16},{4,20},{8,24},{12,28},{16,0},{20,4},{24,8},{28,12},{1,17},{... | collective-permute-start | bytes 1425416 | tf_op jit(solution)/shard_map/ppermute | solution.py:42
  729.7 10.2 %collective-permute-start.56 = (bf16[2,928,128]{2,1,0:T(8,128)(2,1)S(1)}, bf16[2,928,128]{2,1,0:T(8,128)(2,1)S(1)}, u32[]{:S(2)}, u32[]{:S(2)}) collective-permute-start(bf16[2,928,128]{2,1,0:T(8,128)(2,1)S(1)} %fusion.70), channel_id=1, source_target_pairs={{0,8},{4,12},{8,0},{12,4},{16,24},{20,28},{24,16},{28,20},{1,9},{5... | collective-permute-start | bytes 1425416 | tf_op jit(solution)/shard_map/ppermute | solution.py:42
  730.9 10.1 %collective-permute-start.54 = (bf16[2,928,128]{2,1,0:T(8,128)(2,1)S(1)}, bf16[2,928,128]{2,1,0:T(8,128)(2,1)S(1)}, u32[]{:S(2)}, u32[]{:S(2)}) collective-permute-start(bf16[2,928,128]{2,1,0:T(8,128)(2,1)S(1)} %fusion.69), channel_id=1, source_target_pairs={{0,16},{4,20},{8,24},{12,28},{16,0},{20,4},{24,8},{28,12},{1,17},{... | collective-permute-start | bytes 1425416 | tf_op jit(solution)/shard_map/ppermute | solution.py:42
  739.9 9.1 %collective-permute-start.65 = (bf16[928,128]{1,0:T(8,128)(2,1)S(1)}, bf16[928,128]{1,0:T(8,128)(2,1)S(1)}, u32[]{:S(2)}, u32[]{:S(2)}) collective-permute-start(bf16[928,128]{1,0:T(8,128)(2,1)S(1)} %fusion.101), channel_id=1, source_target_pairs={{0,1},{1,2},{2,3},{3,0},{4,5},{5,6},{6,7},{7,4},{8,9},{9,10},{10,1... | collective-permute-start | bytes 712712 | tf_op jit(solution)/shard_map/ppermute | solution.py:51
  741.2 12.9 %collective-permute-start.57 = (bf16[928,128]{1,0:T(8,128)(2,1)S(1)}, bf16[928,128]{1,0:T(8,128)(2,1)S(1)}, u32[]{:S(2)}, u32[]{:S(2)}) collective-permute-start(bf16[928,128]{1,0:T(8,128)(2,1)S(1)} %fusion.109), channel_id=1, source_target_pairs={{0,1},{1,2},{2,3},{3,0},{4,5},{5,6},{6,7},{7,4},{8,9},{9,10},{10,1... | collective-permute-start | bytes 712712 | tf_op jit(solution)/shard_map/ppermute | solution.py:51
  749.2 10.6 %collective-permute-start.66 = (bf16[928,128]{1,0:T(8,128)(2,1)S(1)}, bf16[928,128]{1,0:T(8,128)(2,1)S(1)}, u32[]{:S(2)}, u32[]{:S(2)}) collective-permute-start(bf16[928,128]{1,0:T(8,128)(2,1)S(1)} %fusion.73), channel_id=1, source_target_pairs={{0,1},{1,2},{2,3},{3,0},{4,5},{5,6},{6,7},{7,4},{8,9},{9,10},{10,1... | collective-permute-start | bytes 712712 | tf_op jit(solution)/shard_map/ppermute | solution.py:51
  749.8 16.2 %collective-permute-start.45 = (bf16[8,72,256]{2,1,0:T(8,128)(2,1)S(1)}, bf16[8,72,256]{2,1,0:T(8,128)(2,1)S(1)}, u32[]{:S(2)}, u32[]{:S(2)}) collective-permute-start(bf16[8,72,256]{2,1,0:T(8,128)(2,1)S(1)} %collective-permute-done.44.refs_1_), channel_id=1, source_target_pairs={{0,1},{1,2},{2,3},{3,0},{4,5},{5,6},{6,7},{7,4},{8,9},{9,10},{10,1... | collective-permute-start | bytes 884744 | tf_op jit(solution)/shard_map/ppermute | solution.py:51
  754.9 16.3 %collective-permute-start.58 = (bf16[928,128]{1,0:T(8,128)(2,1)}, bf16[928,128]{1,0:T(8,128)(2,1)}, u32[]{:S(2)}, u32[]{:S(2)}) collective-permute-start(bf16[928,128]{1,0:T(8,128)(2,1)} %fusion.75), channel_id=1, source_target_pairs={{0,1},{1,2},{2,3},{3,0},{4,5},{5,6},{6,7},{7,4},{8,9},{9,10},{10,1... | collective-permute-start | bytes 712712 | tf_op jit(solution)/shard_map/ppermute | solution.py:51
  759.9 16.4 %collective-permute-start.67 = (bf16[928,128]{1,0:T(8,128)(2,1)S(1)}, bf16[928,128]{1,0:T(8,128)(2,1)S(1)}, u32[]{:S(2)}, u32[]{:S(2)}) collective-permute-start(bf16[928,128]{1,0:T(8,128)(2,1)S(1)} %fusion.74), channel_id=1, source_target_pairs={{0,1},{1,2},{2,3},{3,0},{4,5},{5,6},{6,7},{7,4},{8,9},{9,10},{10,1... | collective-permute-start | bytes 712712 | tf_op jit(solution)/shard_map/ppermute | solution.py:51
  766.0 18.9 %collective-permute-start.46 = (bf16[8,72,256]{2,1,0:T(8,128)(2,1)S(1)}, bf16[8,72,256]{2,1,0:T(8,128)(2,1)}, u32[]{:S(2)}, u32[]{:S(2)}) collective-permute-start(bf16[8,72,256]{2,1,0:T(8,128)(2,1)S(1)} %collective-permute-done.45.refs_2_), channel_id=1, source_target_pairs={{0,1},{1,2},{2,3},{3,0},{4,5},{5,6},{6,7},{7,4},{8,9},{9,10},{10,1... | collective-permute-start | bytes 884744 | tf_op jit(solution)/shard_map/ppermute | solution.py:51
  773.0 39.4 %collective-permute-start.59 = (bf16[928,128]{1,0:T(8,128)(2,1)}, bf16[928,128]{1,0:T(8,128)(2,1)}, u32[]{:S(2)}, u32[]{:S(2)}) collective-permute-start(bf16[928,128]{1,0:T(8,128)(2,1)} %fusion.76), channel_id=1, source_target_pairs={{0,1},{1,2},{2,3},{3,0},{4,5},{5,6},{6,7},{7,4},{8,9},{9,10},{10,1... | collective-permute-start | bytes 712712 | tf_op jit(solution)/shard_map/ppermute | solution.py:51
  777.0 35.3 %collective-permute-start.68 = (bf16[928,128]{1,0:T(8,128)(2,1)}, bf16[928,128]{1,0:T(8,128)(2,1)}, u32[]{:S(2)}, u32[]{:S(2)}) collective-permute-start(bf16[928,128]{1,0:T(8,128)(2,1)} %fusion.78), channel_id=1, source_target_pairs={{0,16},{4,20},{8,24},{12,28},{1,17},{5,21},{9,25},{13,29},{2,18},{... | collective-permute-start | bytes 712712 | tf_op jit(solution)/shard_map/ppermute | solution.py:422
  813.6 8.1 collective-permute-start.69
  839.8 4.5 collective-permute-start.74
  (196 other events, 2031.8 us)
Sparse Core Ops, SparseCore 0:
  18.5 124.2 all-gather.1

commit v2 on v1

--- a/solution.py
+++ b/solution.py
@@ -83,30 +83,53 @@
     return out.reshape((-1,) + values.shape)
 
 
-def reduce_cube(values, order):
-    bits = sorted(order, reverse=True)
-    left = list(bits)
-    out = values.reshape((2,) * len(bits) + values.shape[1:])
-    for bit in order:
-        axis = left.index(bit)
+class Cube:
+    def __init__(self, values, order):
+        self.left = sorted(order, reverse=True)
+        self.order = list(order)
+        self.out = values.reshape((2,) * len(order) + values.shape[1:])
+        self.start()
+
+    def start(self):
+        bit = self.order[0]
+        axis = self.left.index(bit)
         mine = dp_bit(bit)
-        got = flip_dp(pick(out, 1 - mine, axis).astype(BF16), bit)
-        out = pick(out, mine, axis).astype(F32) + got.astype(F32)
-        left.remove(bit)
-    return out
-
-
-def ring_gather(values):
+        self.got = flip_dp(pick(self.out, 1 - mine, axis).astype(BF16), bit)
+        self.keep = pick(self.out, mine, axis)
+
+    def step(self):
+        self.out = self.keep.astype(F32) + self.got.astype(F32)
+        self.left.remove(self.order.pop(0))
+        if self.order:
+            self.start()
+        return bool(self.order)
+
+    def finish(self):
+        while self.order:
+            self.step()
+        return self.out
+
+
+def tie(main, cubes):
+    main, gots = lax.optimization_barrier((main, [cube.got for cube in cubes]))
+    for cube, got in zip(cubes, gots):
+        cube.got = got
+    return main
+
+
+def ring_gather(values, hook=None):
     size = lax.axis_size("shard")
     me = lax.axis_index("shard")
     parts = [values]
-    for _ in range(size - 1):
+    for k in range(size - 1):
         parts.append(next_shard(parts[-1]))
+        if hook is not None and k == 1:
+            parts[-1] = hook(parts[-1])
     stacked = jnp.stack(parts[::-1])
     return jnp.roll(stacked, me + 1, axis=0)
 
 
-def ring_reduce(values):
+def ring_reduce(values, hooks=()):
     size = lax.axis_size("shard")
     me = lax.axis_index("shard")
     total = None
@@ -114,20 +137,23 @@
         term = pick(values, (me - 1 - step) % size, 0).astype(F32)
         if total is not None:
             term = term + total
-        total = next_shard(term.astype(BF16)).astype(F32)
+        got = next_shard(term.astype(BF16))
+        if step < len(hooks):
+            got = hooks[step](got)
+        total = got.astype(F32)
     return total + pick(values, me, 0).astype(F32)
 
 
-def group_gather(rows):
-    parts = ring_gather(rows)
+def group_gather(rows, hook=None):
+    parts = ring_gather(rows, hook)
     other = flip_dp(parts, 1)
     return join(parts[None], other[None], 1, 0)
 
 
-def group_reduce(parts):
+def group_reduce(parts, hooks):
     mine = dp_bit(1)
-    got = flip_dp(pick(parts, 1 - mine, 0).astype(BF16), 1)
-    return ring_reduce(pick(parts, mine, 0).astype(F32) + got.astype(F32))
+    got = hooks[0](flip_dp(pick(parts, 1 - mine, 0).astype(BF16), 1))
+    return ring_reduce(pick(parts, mine, 0).astype(F32) + got.astype(F32), hooks[1:])
 
 
 def sum_all(value):
@@ -408,19 +434,23 @@
     return (blocks + blocks % 2) * (GRAIN // 128) // 2
 
 
-def reduce_half(own, send, which):
-    dp_size, shard_size = lax.axis_size("dp"), lax.axis_size("shard")
-    paired = (own.astype(F32) + flip_dp(send, 1).astype(F32)).astype(BF16)
+def half_cubes(own, got):
+    shard_size = lax.axis_size("shard")
+    paired = (own.astype(F32) + got.astype(F32)).astype(BF16)
     paired = paired.reshape((-1, shard_size) + own.shape[1:])
     half = shard_size // 2
     order = high_bits()
-    first = reduce_cube(paired[:, :half], order)
-    second = reduce_cube(paired[:, half:], order[::-1])
-    done = ring_reduce(jnp.concatenate([first, second], 0).astype(BF16))
+    return [Cube(paired[:, :half], order), Cube(paired[:, half:], order[::-1])]
+
+
+def finish_cubes(cubes):
+    return ring_reduce(jnp.concatenate([cube.finish() for cube in cubes], 0).astype(BF16))
+
+
+def to_top(done, which):
     top = top_bit()
-    away = [(i, i ^ top) for i in range(dp_size) if (i // top) % 2 != which]
-    got = lax.ppermute(done.astype(BF16), "dp", away).astype(F32)
-    return done, got
+    away = [(i, i ^ top) for i in range(lax.axis_size("dp")) if (i // top) % 2 != which]
+    return done, lax.ppermute(done.astype(BF16), "dp", away).astype(F32)
 
 
 def own_part(halves, length):
@@ -433,40 +463,51 @@
     return lax.dynamic_slice_in_dim(flat, shift, length, 0)
 
 
-def gather_table(embed_table):
-    low = embed_table.astype(BF16)
-    half = low.shape[1] // 2
+class TableGather:
+    def __init__(self, embed_table):
+        low = embed_table.astype(BF16)
+        half = low.shape[1] // 2
+        core = dp_bit(1)
+        own = lax.dynamic_slice_in_dim(low, core * half, half, 1)
+        send = lax.dynamic_slice_in_dim(low, (1 - core) * half, half, 1)
+        pair = join(own, flip_dp(send, 1), 1, 0)
+        self.bits = sorted(high_bits(), reverse=True)
+        shape = (1,) * len(self.bits) + (pair.shape[0], half // 2)
+        self.sides = [pair[:, : half // 2].reshape(shape), pair[:, half // 2 :].reshape(shape)]
+        self.orders = [high_bits(), high_bits()[::-1]]
+        self.start()
+
+    def start(self):
+        self.got = [flip_dp(side, order[0]) for side, order in zip(self.sides, self.orders)]
+
+    def step(self):
+        self.sides = [
+            join(side, other, order[0], self.bits.index(order[0]))
+            for side, other, order in zip(self.sides, self.got, self.orders)
+        ]
+        self.orders = [order[1:] for order in self.orders]
+        if self.orders[0]:
+            self.start()
+
+    def tied(self, main):
+        main, self.got = lax.optimization_barrier((main, self.got))
+        return main
+
+    def finish(self):
+        while self.orders[0]:
+            self.step()
+        return jnp.concatenate([side.reshape(MODEL_WIDTH, -1) for side in self.sides], 1)
+
+
+def owner_flip(joined, features):
     core = dp_bit(1)
-    own = lax.dynamic_slice_in_dim(low, core * half, half, 1)
-    send = lax.dynamic_slice_in_dim(low, (1 - core) * half, half, 1)
-    pair = join(own, flip_dp(send, 1), 1, 0)
-    bits = sorted(high_bits(), reverse=True)
-    shape = (1,) * len(bits) + (pair.shape[0], half // 2)
-    sides = [pair[:, : half // 2].reshape(shape), pair[:, half // 2 :].reshape(shape)]
-    orders = [high_bits(), high_bits()[::-1]]
-    for k in range(len(bits)):
-        got = [flip_dp(side, order[k]) for side, order in zip(sides, orders)]
-        sides = [
-            join(side, other, order[k], bits.index(order[k]))
-            for side, other, order in zip(sides, got, orders)
-        ]
-    return jnp.concatenate([side.reshape(MODEL_WIDTH, -1) for side in sides], 1)
-
-
-def reduce_table(table_grad, features):
-    half = table_grad.shape[1]
-    parts = table_grad.reshape(-1, 2 * features, half)
-    order = high_bits()
-    first = reduce_cube(parts[:, :, : half // 2], order)
-    second = reduce_cube(parts[:, :, half // 2 :], order[::-1])
-    return jnp.concatenate([first, second], 1)
-
-
-def to_owner(joined, features):
-    core = dp_bit(1)
-    own = lax.dynamic_slice_in_dim(joined, core * features, features, 0)
     send = lax.dynamic_slice_in_dim(joined, (1 - core) * features, features, 0)
-    return join(own, flip_dp(send, 1), 1, 1)
+    return flip_dp(send, 1)
+
+
+def owner_join(joined, got, features):
+    own = lax.dynamic_slice_in_dim(joined, dp_bit(1) * features, features, 0)
+    return join(own, got, 1, 1)
 
 
 def rms_scale(values):
@@ -492,51 +533,6 @@
     return cos_full, sin_full
 
 
-def swap_halves(values):
-    halves = HEAD_SIZE // 2
-    lanes = lax.broadcasted_iota(jnp.int32, values.shape, 1) % HEAD_SIZE
-    return jnp.where(lanes < halves, jnp.roll(values, -halves, 1), jnp.roll(values, halves, 1))
-
-
-def split_heads(rows, heads):
-    return rows.reshape(-1, LEN, heads, HEAD_SIZE)
-
-
-def layer_forward(hidden, pieces, allowed, rope):
-    w_qkv, w_out, w_gateup, w_down, gains = pieces
-    cos_full, sin_full = rope
-    gains = gains.astype(F32)
-    group = QUERY_HEADS // KEY_VALUE_HEADS
-    scale_one = rms_scale(hidden)
-    normed = (hidden * scale_one * gains[0]).astype(BF16)
-    qkv = jnp.dot(normed, w_qkv, preferred_element_type=F32)
-    straight = qkv[:, :ROPED]
-    turned = (straight * cos_full + swap_halves(straight) * sin_full).astype(BF16)
-    query = turned[:, : QUERY_HEADS * HEAD_SIZE].reshape(
-        -1, LEN, KEY_VALUE_HEADS, group, HEAD_SIZE
-    )
-    key = split_heads(turned[:, QUERY_HEADS * HEAD_SIZE :], KEY_VALUE_HEADS)
-    value = split_heads(qkv[:, ROPED:].astype(BF16), KEY_VALUE_HEADS)
-    scores = jnp.einsum("stgja,suga->sgjtu", query, key, preferred_element_type=F32)
-    scores = jnp.where(allowed, scores * HEAD_SIZE ** (-0.5), MASKED_SCORE)
-    probs = jax.nn.softmax(scores, axis=-1)
-    attended = jnp.einsum(
-        "sgjtu,suga->stgja", probs.astype(BF16), value, preferred_element_type=F32
-    )
-    attended = attended.reshape(-1, QUERY_HEADS * HEAD_SIZE).astype(BF16)
-    middle = hidden + jnp.dot(attended, w_out, preferred_element_type=F32)
-    scale_two = rms_scale(middle)
-    normed_two = (middle * scale_two * gains[1]).astype(BF16)
-    gate_up = jnp.dot(normed_two, w_gateup, preferred_element_type=F32)
-    acted = (jax.nn.silu(gate_up[:, :FEED_UNITS]) * gate_up[:, FEED_UNITS:]).astype(BF16)
-    output = middle + jnp.dot(acted, w_down, preferred_element_type=F32)
-    kept = (
-        hidden, scale_one, normed, query, key, value, probs, attended,
-        middle, scale_two, normed_two, gate_up, acted,
-    )
-    return output, kept
-
-
 def against(left, right):
     return lax.dot_general(left, right, (((0,), (0,)), ((), ())), preferred_element_type=F32)
 
@@ -545,53 +541,176 @@
     return lax.dot_general(left, right, (((1,), (1,)), ((), ())), preferred_element_type=F32)
 
 
-def layer_backward(kept, pieces, rope, grad_output):
-    w_qkv, w_out, w_gateup, w_down, gains = pieces
-    cos_full, sin_full = rope
-    gains = gains.astype(F32)
-    (
-        hidden, scale_one, normed, query, key, value, probs, attended,
-        middle, scale_two, normed_two, gate_up, acted,
-    ) = kept
-    scaling = HEAD_SIZE ** (-0.5)
+QUERY_WIDTH = QUERY_HEADS * HEAD_SIZE
+VALUE_WIDTH = KEY_VALUE_HEADS * HEAD_SIZE
+SCALING = HEAD_SIZE ** (-0.5)
+
+
+def swap_halves(values):
+    halves, width = HEAD_SIZE // 2, values.shape[1]
+    lanes = lax.broadcasted_iota(jnp.int32, values.shape, 1) % HEAD_SIZE
+    return jnp.where(
+        lanes < halves, pltpu.roll(values, width - halves, 1), pltpu.roll(values, halves, 1)
+    )
+
+
+def head_cols(idx):
+    return slice(idx * HEAD_SIZE, (idx + 1) * HEAD_SIZE)
+
+
+def attention_probs(query, key, allowed):
+    scores = jnp.where(allowed, times_t(query, key) * SCALING, MASKED_SCORE)
+    powers = jnp.exp(scores - jnp.max(scores, axis=1, keepdims=True))
+    return powers / jnp.sum(powers, axis=1, keepdims=True)
+
+
+def allowed_pairs(length):
+    later = lax.broadcasted_iota(jnp.int32, (LEN, LEN), 0)
+    sooner = lax.broadcasted_iota(jnp.int32, (LEN, LEN), 1)
+    return (sooner <= later) & (sooner < length)
+
+
+def forward_kernel(
+    len_ref, hidden_ref, qkv_ref, out_ref, gateup_ref, down_ref, gain_ref, cos_ref, sin_ref,
+    output_ref, normed_ref, turned_ref, value_ref, attended_ref, middle_ref, normed_two_ref,
+    gate_up_ref, acted_ref,
+):
+    hidden = hidden_ref[...]
+    normed_ref[...] = (hidden * rms_scale(hidden) * gain_ref[0:1, :]).astype(BF16)
+    qkv = jnp.dot(normed_ref[...], qkv_ref[...], preferred_element_type=F32)
+    straight = qkv[:, :ROPED]
+    turned_ref[...] = (straight * cos_ref[...] + swap_halves(straight) * sin_ref[...]).astype(BF16)
+    value_ref[...] = qkv[:, ROPED:].astype(BF16)
+    group = QUERY_HEADS // KEY_VALUE_HEADS
+    for seq in range(hidden.shape[0] // LEN):
+        rows = slice(seq * LEN, (seq + 1) * LEN)
+        allowed = allowed_pairs(len_ref[seq])
+        for head in range(QUERY_HEADS):
+            key = turned_ref[rows, head_cols(QUERY_HEADS + head // group)]
+            value = value_ref[rows, head_cols(head // group)]
+            probs = attention_probs(turned_ref[rows, head_cols(head)], key, allowed)
+            attended_ref[rows, head_cols(head)] = jnp.dot(
+                probs.astype(BF16), value, preferred_element_type=F32
+            ).astype(BF16)
+    middle = hidden + jnp.dot(attended_ref[...], out_ref[...], preferred_element_type=F32)
+    middle_ref[...] = middle
+    normed_two_ref[...] = (middle * rms_scale(middle) * gain_ref[1:2, :]).astype(BF16)
+    gate_up_ref[...] = jnp.dot(normed_two_ref[...], gateup_ref[...], preferred_element_type=F32)
+    gate = gate_up_ref[:, :FEED_UNITS]
+    acted_ref[...] = (gate / (1.0 + jnp.exp(-gate)) * gate_up_ref[:, FEED_UNITS:]).astype(BF16)
+    output_ref[...] = middle + jnp.dot(acted_ref[...], down_ref[...], preferred_element_type=F32)
+
+
+def backward_kernel(
+    len_ref, grad_ref, hidden_ref, qkv_ref, out_ref, gateup_ref, down_ref, gain_ref, cos_ref,
+    sin_ref, turned_ref, value_ref, middle_ref, gate_up_ref,
+    grad_in_ref, low_ref, grad_gu_ref, grad_mid_ref, grad_qkv_ref, gains_out_ref,
+    grad_att_ref, grad_turned_ref,
+):
+    grad = grad_ref[...]
+    low_ref[...] = grad.astype(BF16)
+    grad_act = times_t(low_ref[...], down_ref[...]).astype(BF16).astype(F32)
+    gate, up = gate_up_ref[:, :FEED_UNITS], gate_up_ref[:, FEED_UNITS:]
+    sigma = 1.0 / (1.0 + jnp.exp(-gate))
+    grad_gu_ref[:, FEED_UNITS:] = (grad_act * (gate * sigma)).astype(BF16)
+    grad_gu_ref[:, :FEED_UNITS] = (
+        grad_act * up * (sigma * (1.0 + gate * (1.0 - sigma)))
+    ).astype(BF16)
+    middle = middle_ref[...]
+    grad_mid, gain_two = rms_back(
+        middle, rms_scale(middle), gain_ref[1:2, :], times_t(grad_gu_ref[...], gateup_ref[...])
+    )
+    grad_mid = grad_mid + grad
+    grad_mid_ref[...] = grad_mid.astype(BF16)
+    grad_att_ref[...] = times_t(grad_mid_ref[...], out_ref[...]).astype(BF16)
+    group = QUERY_HEADS // KEY_VALUE_HEADS
+    for seq in range(grad.shape[0] // LEN):
+        rows = slice(seq * LEN, (seq + 1) * LEN)
+        allowed = allowed_pairs(len_ref[seq])
+        for kv in range(KEY_VALUE_HEADS):
+            key = turned_ref[rows, head_cols(QUERY_HEADS + kv)]
+            value = value_ref[rows, head_cols(kv)]
+            grad_key = jnp.zeros((LEN, HEAD_SIZE), F32)
+            grad_value = jnp.zeros((LEN, HEAD_SIZE), F32)
+            for head in range(kv * group, (kv + 1) * group):
+                query = turned_ref[rows, head_cols(head)]
+                grad_out = grad_att_ref[rows, head_cols(head)]
+                probs = attention_probs(query, key, allowed)
+                grad_probs = times_t(grad_out, value)
+                grad_value = grad_value + against(probs.astype(BF16), grad_out)
+                inner = jnp.sum(grad_probs * probs, axis=1, keepdims=True)
+                grad_scores = (probs * (grad_probs - inner)).astype(BF16)
+                grad_query = jnp.dot(grad_scores, key, preferred_element_type=F32) * SCALING
+                grad_turned_ref[rows, head_cols(head)] = grad_query.astype(BF16).astype(F32)
+                grad_key = grad_key + against(grad_scores, query)
+            grad_turned_ref[rows, head_cols(QUERY_HEADS + kv)] = (
+                (grad_key * SCALING).astype(BF16).astype(F32)
+            )
+            at = slice(ROPED + kv * HEAD_SIZE, ROPED + (kv + 1) * HEAD_SIZE)
+            grad_qkv_ref[rows, at] = grad_value.astype(BF16)
+    turned = grad_turned_ref[...]
+    grad_qkv_ref[:, :ROPED] = (
+        turned * cos_ref[...] - swap_halves(turned) * sin_ref[...]
+    ).astype(BF16)
+    hidden = hidden_ref[...]
+    grad_hidden, gain_one = rms_back(
+        hidden, rms_scale(hidden), gain_ref[0:1, :], times_t(grad_qkv_ref[...], qkv_ref[...])
+    )
+    grad_in_ref[...] = grad_hidden + grad_mid
+    gains_out_ref[...] = jnp.concatenate([gain_one[None], gain_two[None]], 0)
+
+
+def layer_call(kernel, name, lens, operands, outs, scratch, flops):
+    in_place = pl.BlockSpec(memory_space=pltpu.VMEM)
+    return pl.pallas_call(
+        kernel,
+        in_specs=[pl.BlockSpec(memory_space=pltpu.SMEM)] + [in_place] * len(operands),
+        out_specs=[in_place] * len(outs),
+        out_shape=[jax.ShapeDtypeStruct(shape, dtype) for shape, dtype in outs],
+        scratch_shapes=scratch,
+        compiler_params=pltpu.CompilerParams(vmem_limit_bytes=VMEM_LIMIT),
+        cost_estimate=pl.CostEstimate(flops=flops, bytes_accessed=8 * PL, transcendentals=0),
+        name=name,
+    )(lens, *operands)
+
+
+def layer_forward(hidden, pieces, lens, rope):
     rows = hidden.shape[0]
-    grad_low = grad_output.astype(BF16)
-    grad_act = times_t(grad_low, w_down).astype(BF16).astype(F32)
-    gate, up = gate_up[:, :FEED_UNITS], gate_up[:, FEED_UNITS:]
-    sigma = jax.nn.sigmoid(gate)
-    grad_up = grad_act * (gate * sigma)
-    grad_gate = grad_act * up * (sigma * (1.0 + gate * (1.0 - sigma)))
-    grad_gu = jnp.concatenate([grad_gate, grad_up], 1).astype(BF16)
-    grad_normed_two = times_t(grad_gu, w_gateup)
-    grad_mid, grad_gain_two = rms_back(middle, scale_two, gains[1], grad_normed_two)
-    grad_mid = grad_mid + grad_output
-    grad_mid_low = grad_mid.astype(BF16)
-    grad_att = times_t(grad_mid_low, w_out).astype(BF16).reshape(query.shape)
-    grad_probs = jnp.einsum("stgja,suga->sgjtu", grad_att, value, preferred_element_type=F32)
-    grad_value = jnp.einsum(
-        "sgjtu,stgja->suga", probs.astype(BF16), grad_att, preferred_element_type=F32
-    )
-    grad_scores = (
-        probs * (grad_probs - jnp.sum(grad_probs * probs, axis=-1, keepdims=True))
-    ).astype(BF16)
-    grad_query = (
-        jnp.einsum("sgjtu,suga->stgja", grad_scores, key, preferred_element_type=F32) * scaling
-    )
-    grad_key = (
-        jnp.einsum("sgjtu,stgja->suga", grad_scores, query, preferred_element_type=F32) * scaling
-    )
-    turned = jnp.concatenate(
-        [grad_query.reshape(rows, -1).astype(BF16), grad_key.reshape(rows, -1).astype(BF16)], 1
-    ).astype(F32)
-    straight = (turned * cos_full - swap_halves(turned) * sin_full).astype(BF16)
-    grad_qkv = jnp.concatenate([straight, grad_value.reshape(rows, -1).astype(BF16)], 1)
-    grad_normed = times_t(grad_qkv, w_qkv)
-    grad_input, grad_gain_one = rms_back(hidden, scale_one, gains[0], grad_normed)
-    grad_input = grad_input + grad_mid
-    pairs = [
-        (normed, grad_qkv), (attended, grad_mid_low), (normed_two, grad_gu), (acted, grad_low),
+    outs = [
+        ((rows, MODEL_WIDTH), F32),
+        ((rows, MODEL_WIDTH), BF16),
+        ((rows, ROPED), BF16),
+        ((rows, VALUE_WIDTH), BF16),
+        ((rows, QUERY_WIDTH), BF16),
+        ((rows, MODEL_WIDTH), F32),
+        ((rows, MODEL_WIDTH), BF16),
+        ((rows, 2 * FEED_UNITS), F32),
+        ((rows, FEED_UNITS), BF16),
     ]
-    return grad_input, pairs, flat_rows(grad_gain_one, grad_gain_two)
+    output, *kept = layer_call(
+        forward_kernel, "layer_forward", lens, [hidden, *pieces, *rope], outs, [], 2 * rows * PL
+    )
+    return output, (hidden, *kept)
+
+
+def layer_backward(kept, pieces, lens, rope, grad_output):
+    hidden, normed, turned, value, attended, middle, normed_two, gate_up, acted = kept
+    rows = hidden.shape[0]
+    outs = [
+        ((rows, MODEL_WIDTH), F32),
+        ((rows, MODEL_WIDTH), BF16),
+        ((rows, 2 * FEED_UNITS), BF16),
+        ((rows, MODEL_WIDTH), BF16),
+        ((rows, QKV), BF16),
+        ((2, MODEL_WIDTH), F32),
+    ]
+    scratch = [pltpu.VMEM((rows, QUERY_WIDTH), BF16), pltpu.VMEM((rows, ROPED), F32)]
+    operands = [grad_output, hidden, *pieces, *rope, turned, value, middle, gate_up]
+    grad_input, low, grad_gu, grad_mid, grad_qkv, gains = layer_call(
+        backward_kernel, "layer_backward", lens, operands, outs, scratch, 2 * rows * PL
+    )
+    pairs = [(normed, grad_qkv), (attended, grad_mid), (normed_two, grad_gu), (acted, low)]
+    return grad_input, pairs, gains.reshape(-1, 128)
 
 
 def flat_rows(first, second):
@@ -869,63 +988,119 @@
     )(count, order, rows, table)
 
 
-def table_kernel(count_ref, list_ref, rows_ref, exp_ref, out_ref, packed, total):
+def scale_kernel(
+    count_ref, list_ref, rows_ref, back_ref, scale_ref, grad_ref, turned_ref, scaled, packed
+):
     per = BLOCK // GRANULE
-    block = pl.program_id(0)
-    columns = exp_ref.shape[1]
-    chunk = min(CHUNK, columns)
-
-    @pl.when(block == 0)
+    step, blocks = pl.program_id(0), pl.num_programs(0) // 2
+
+    @pl.when(step < blocks)
     def _():
-        total[...] = jnp.zeros(total.shape, F32)
-
-    @pl.when(block < block_count(count_ref))
+        for k in range(BLOCK // LANES):
+            at = slice(k * LANES, (k + 1) * LANES)
+            line = scale_ref[pl.ds(step * (BLOCK // LANES) + k, 1), :]
+            column = jnp.transpose(jnp.broadcast_to(line, (LANES, LANES)))[:, :1]
+            grad_ref[at, :] = back_ref[at, :] * column
+            row = pl.multiple_of(step * BLOCK + k * LANES, LANES)
+            scaled[pl.ds(row, LANES), :] = (rows_ref[at, :].astype(F32) * column).astype(BF16)
+
+    block = step - blocks
+
+    @pl.when((block >= 0) & (block < block_count(count_ref)))
     def _():
         for g in range(per):
             at = block * per + g
             spot = pl.multiple_of(list_ref[at] * GRANULE, GRANULE)
-            part = rows_ref[pl.ds(spot, GRANULE), :]
+            part = scaled[pl.ds(spot, GRANULE), :].astype(F32)
             packed[g * GRANULE : (g + 1) * GRANULE, :] = jnp.where(
                 at < count_ref[0], part, jnp.zeros_like(part)
             )
-        for k in range(columns // chunk):
-            at = slice(k * chunk, (k + 1) * chunk)
-            total[:, at] += against(packed[...], exp_ref[:, at])
-
-    @pl.when(block == pl.num_programs(0) - 1)
+        turned_ref[...] = jnp.transpose(packed[...]).astype(BF16)
+
+
+def scale_rows(count, order, rows, back, scale):
+    height = rows.shape[0]
+    blocks = height // BLOCK
+
+    def first(i, count_ref, list_ref):
+        return (jnp.minimum(i, blocks - 1), 0)
+
+    def second(i, count_ref, list_ref):
+        return (0, block_at(jnp.maximum(i - blocks, 0), count_ref, list_ref)[0])
+
+    return pl.pallas_call(
+        scale_kernel,
+        grid_spec=pltpu.PrefetchScalarGridSpec(
+            num_scalar_prefetch=2,
+            grid=(2 * blocks,),
+            in_specs=[
+                pl.BlockSpec((BLOCK, MODEL_WIDTH), first),
+                pl.BlockSpec((BLOCK, MODEL_WIDTH), first),
+                pl.BlockSpec(scale.shape, lambda i, count_ref, list_ref: (0, 0)),
+            ],
+            out_specs=[
+                pl.BlockSpec((BLOCK, MODEL_WIDTH), first),
+                pl.BlockSpec((MODEL_WIDTH, BLOCK), second),
+            ],
+            scratch_shapes=[
+                pltpu.VMEM((height, MODEL_WIDTH), BF16),
+                pltpu.VMEM((BLOCK, MODEL_WIDTH), F32),
+            ],
+        ),
+        out_shape=[
+            jax.ShapeDtypeStruct((height, MODEL_WIDTH), F32),
+            jax.ShapeDtypeStruct((MODEL_WIDTH, height), BF16),
+        ],
+        compiler_params=pltpu.CompilerParams(vmem_limit_bytes=VMEM_LIMIT),
+        cost_estimate=pl.CostEstimate(flops=0, bytes_accessed=12 * rows.size, transcendentals=0),
+        name="scale_rows",
+    )(count, order, rows, back, scale)
+
+
+def table_kernel(count_ref, turned_ref, exp_ref, out_ref):
+    used = block_count(count_ref)
+
+    @pl.when(used == 0)
     def _():
-        out_ref[...] = total[...].astype(BF16)
-
-
-def table_backward(count, order, rows, powers):
-    height, columns = powers.shape
-    whole = pl.Buffered(1)
-
-    def once(i, count_ref, list_ref):
-        return (0, 0)
-
+        out_ref[...] = jnp.zeros(out_ref.shape, BF16)
+
+    for blocks in range(1, exp_ref.shape[0] // BLOCK + 1):
+
+        @pl.when(used == blocks)
+        def _():
+            out_ref[...] = jnp.dot(
+                turned_ref[:, : blocks * BLOCK],
+                exp_ref[: blocks * BLOCK, :],
+                preferred_element_type=F32,
+            ).astype(BF16)
+
+
+def table_backward(count, turned, powers, part, parts):
+    height, columns = powers.shape[0], powers.shape[1] // parts
+    chunk = 512 if columns % 512 == 0 else 256
+    steps = columns // chunk
     return pl.pallas_call(
         table_kernel,
         grid_spec=pltpu.PrefetchScalarGridSpec(
-            num_scalar_prefetch=2,
-            grid=(height // BLOCK,),
+            num_scalar_prefetch=1,
+            grid=(steps,),
             in_specs=[
-                pl.BlockSpec(rows.shape, once, pipeline_mode=whole),
-                pl.BlockSpec((BLOCK, columns), block_at),
+                pl.BlockSpec(
+                    turned.shape, lambda i, count_ref: (0, 0), pipeline_mode=pl.Buffered(1)
+                ),
+                pl.BlockSpec((height, chunk), lambda i, count_ref: (0, part * steps + i)),
             ],
-            out_specs=pl.BlockSpec((MODEL_WIDTH, columns), once, pipeline_mode=whole),
-            scratch_shapes=[
-                pltpu.VMEM((BLOCK, MODEL_WIDTH), BF16),
-                pltpu.VMEM((MODEL_WIDTH, columns), F32),
-            ],
+            out_specs=pl.BlockSpec((MODEL_WIDTH, chunk), lambda i, count_ref: (0, i)),
         ),
         out_shape=jax.ShapeDtypeStruct((MODEL_WIDTH, columns), BF16),
         compiler_params=pltpu.CompilerParams(vmem_limit_bytes=VMEM_LIMIT),
         cost_estimate=pl.CostEstimate(
-            flops=2 * MODEL_WIDTH * powers.size, bytes_accessed=2 * powers.size, transcendentals=0
+            flops=2 * MODEL_WIDTH * powers.size // parts,
+            bytes_accessed=2 * powers.size // parts,
+            transcendentals=0,
         ),
         name="table_backward",
-    )(count, order, rows, powers)
+    )(count, turned, powers)
 
 
 def shards(
@@ -972,8 +1147,8 @@
     all_lens = tiny[:, seqs:, 0].reshape(seq_total)
     here = jnp.arange(seq_total)
     longer = all_lens[None, :] > all_lens[:, None]
-    tie = (all_lens[None, :] == all_lens[:, None]) & (here[None, :] < here[:, None])
-    rank = jnp.sum((longer | tie).astype(jnp.int32), axis=1)
+    equal = (all_lens[None, :] == all_lens[:, None]) & (here[None, :] < here[:, None])
+    rank = jnp.sum((longer | equal).astype(jnp.int32), axis=1)
     turn, seat = rank // groups, rank % groups
     group_of = jnp.where(turn % 2 == 0, seat, groups - 1 - seat)
     place_of = group_of * slots + turn
@@ -1010,7 +1185,8 @@
 
     tokens = seq_total * LEN
     bits = token_bits(tokens)
-    keys = jnp.sort(dealt_ids.reshape(-1) * tokens + jnp.arange(tokens, dtype=jnp.int32))
+    kept_ids = jnp.where(places[None, :] < dealt_lens[:, None], dealt_ids, columns * shard_size)
+    keys = jnp.sort(kept_ids.reshape(-1) * tokens + jnp.arange(tokens, dtype=jnp.int32))
     first_id = shard_idx * columns
     span = jnp.stack(
         [
@@ -1029,7 +1205,7 @@
     embedded = embedded.reshape(MODEL_WIDTH, own_rows).T.astype(F32)
 
     held_table, everything = lax.optimization_barrier((embed_table, everything))
-    table_low = gather_table(held_table)
+    table_gather = TableGather(held_table)
     middle_rows = PL // 128
     low_rows = middle_rows // 16 * 16
     total_devices = dp_size * shard_size
@@ -1052,20 +1228,19 @@
     def gain_pair(rows, at):
         return rows[at : at + tail].reshape(2, MODEL_WIDTH)
 
-    layer_zero.append(gain_pair(gains_zero, 0))
-    layer_one.append(gain_pair(gains_one, gain_row - base_one))
+    layer_zero.append(gain_pair(gains_zero, 0).astype(F32))
+    layer_one.append(gain_pair(gains_one, gain_row - base_one).astype(F32))
     head_gains = gain_pair(gains_head, second_row - base_two).astype(F32)
 
-    allowed = (places[None, :] <= places[:, None])[None] & (
-        places[None, None, :] < own_lens[:, None, None]
-    )
-    allowed = allowed[:, None, None]
     rope = rope_rows(own_rows)
-    hidden, kept_zero = layer_forward(embedded, layer_zero, allowed, rope)
-    hidden, kept_one = layer_forward(hidden, layer_one, allowed, rope)
+    hidden, kept_zero = layer_forward(embedded, layer_zero, own_lens, rope)
+    hidden = table_gather.tied(hidden)
+    table_gather.step()
+    hidden, kept_one = layer_forward(hidden, layer_one, own_lens, rope)
     scale_final = rms_scale(hidden)
     head_one = (hidden * scale_final * head_gains[0]).astype(BF16)
-    all_one = group_gather(head_one).reshape(-1, MODEL_WIDTH)
+    all_one = group_gather(head_one, table_gather.tied).reshape(-1, MODEL_WIDTH)
+    table_low = table_gather.finish()
     projected = jnp.dot(all_one, w_second, preferred_element_type=F32)
     scale_second = rms_scale(projected)
     all_two = (projected * scale_second * head_gains[1]).astype(BF16)
@@ -1085,9 +1260,8 @@
             )
             peak_all = top
     log_total = (peak_all + jnp.log(sum_all_rows)).reshape(2, group, seqs, LEN)
-    row_scale = (
-        weights.reshape(-1, 128) * jnp.exp(peaks - peak_all) / sum_all_rows
-    ).reshape(-1, 1)
+    row_scale = weights.reshape(-1, 128) * jnp.exp(peaks - peak_all) / sum_all_rows
+    grad_rows, turned_rows = scale_rows(count, order, both, back, row_scale)
 
     own_log = pick(log_total, own_at, 1)
     own_weights = pick(weights.reshape(2, group, seqs, LEN), own_at, 1)
@@ -1101,7 +1275,6 @@
     own_loss = jnp.sum(own_weights * (own_log - chosen), axis=(0, 2))
 
     weight_col = own_weights.reshape(2, own_rows, 1)
-    grad_rows = back * row_scale
     part_two = grad_rows[group_rows:]
     own_two = lax.dynamic_slice_in_dim(part_two, own_at * own_rows, own_rows, 0)
     part_two = lax.dynamic_update_slice_in_dim(
@@ -1110,10 +1283,24 @@
     grad_proj, grad_gain_second = rms_back(projected, scale_second, head_gains[1], part_two)
     grad_proj_low = grad_proj.astype(BF16)
     part_one = grad_rows[:group_rows] + times_t(grad_proj_low, w_second)
-    grad_final = group_reduce(part_one.reshape(2, shard_size, own_rows, MODEL_WIDTH))
-    scaled_rows = (both.astype(F32) * row_scale).astype(BF16)
-    head_grad = table_backward(count, order, scaled_rows, powers)
-    table_part = to_owner(reduce_table(head_grad, features), features)
+    quarters = 4
+    cubes = [None] * quarters
+    running = [turned_rows]
+
+    def quarter_hook(k):
+        def hook(got):
+            part = table_backward(count, running[0], powers, k, quarters)
+            got, part, running[0] = lax.optimization_barrier((got, part, running[0]))
+            bits = high_bits() if k < quarters // 2 else high_bits()[::-1]
+            cubes[k] = Cube(part.reshape(-1, 2 * features, part.shape[1]), bits)
+            return got
+
+        return hook
+
+    grad_final = group_reduce(
+        part_one.reshape(2, shard_size, own_rows, MODEL_WIDTH),
+        [quarter_hook(k) for k in (0, 2, 1, 3)],
+    )
     grad_final = grad_final - weight_col[0] * next_one
     grad_hidden, grad_gain_final = rms_back(hidden, scale_final, head_gains[0], grad_final)
 
@@ -1121,24 +1308,34 @@
     height_zero = length * (total_devices // 2 - 1) // GRAIN * per + 2 * sub_rows
     height_one = length * (total_devices - 1) // GRAIN * per + 2 * sub_rows - low_rows
     keep = height_zero - low_rows
-    grad_hidden, pairs, gain_grads = layer_backward(kept_one, layer_one, rope, grad_hidden)
+    grad_hidden = tie(grad_hidden, [cubes[0], cubes[2]])
+    cubes[0].step(), cubes[2].step()
+    grad_hidden, pairs, gain_grads = layer_backward(
+        kept_one, layer_one, own_lens, rope, grad_hidden
+    )
+    gain_grads = tie(gain_grads, [cubes[1], cubes[3]])
+    cubes[1].step(), cubes[3].step()
     own_one, send_one, kept_rows = pack_half(
         owner_rows(length, 1, low_rows),
         pairs + [(all_one, grad_proj_low)],
         [gain_grads, flat_rows(grad_gain_final, grad_gain_second)],
         None, middle_rows - low_rows, {3: tail, 4: tail}, height_one, sub_rows, keep, 0,
     )
-    grad_hidden, own_one, send_one = lax.optimization_barrier((grad_hidden, own_one, send_one))
-    reduced_one = reduce_half(own_one, send_one, 1)
-    grad_hidden, pairs, gain_grads = layer_backward(kept_zero, layer_zero, rope, grad_hidden)
+    got_one = flip_dp(send_one, 1)
+    grad_hidden, own_one = lax.optimization_barrier((grad_hidden, own_one))
+    grad_hidden, pairs, gain_grads = layer_backward(
+        kept_zero, layer_zero, own_lens, rope, grad_hidden
+    )
+    gain_grads, got_one = lax.optimization_barrier((gain_grads, got_one))
+    gain_grads = tie(gain_grads, cubes)
+    joined = jnp.concatenate([cube.finish() for cube in cubes], 1)
+    flipped = owner_flip(joined, features)
+    cubes_one = half_cubes(own_one, got_one)
     own_zero, send_zero = pack_half(
         owner_rows(length, 0, 0), pairs, [gain_grads],
         (kept_rows, height_zero - middle_rows), 0, {3: tail}, height_zero, sub_rows, 0,
         middle_rows - low_rows,
     )
-    reduced_zero = reduce_half(own_zero, send_zero, 0)
-    model_sum = own_part((reduced_zero, reduced_one), length)
-
     one_terms = (weight_col[0] * head_one.astype(F32)).reshape(seqs, LEN, MODEL_WIDTH)
     two_terms = (weight_col[1] * head_two.astype(F32)).reshape(seqs, LEN, MODEL_WIDTH)
     token_grad = (
@@ -1149,9 +1346,27 @@
     token_parts = token_grad.T.reshape(dp_size, features, own_rows)
     parts = [pick(token_parts, dp_idx, 0)]
     parts += [flip_dp(pick(token_parts, dp_idx ^ k, 0), k) for k in range(1, dp_size)]
+    got_zero, parts, flipped = lax.optimization_barrier((flip_dp(send_zero, 1), parts, flipped))
+    table_part = owner_join(joined, flipped, features)
+    cubes_zero = half_cubes(own_zero, got_zero)
     chain = [jnp.stack(parts)]
-    for _ in range(shard_size - 1):
+    chain[0] = tie(chain[0], cubes_one)
+    for cube in cubes_one:
+        cube.step()
+    chain.append(next_shard(chain[0]))
+    chain[1] = tie(chain[1], cubes_one)
+    sums_one = jnp.concatenate([cube.finish() for cube in cubes_one], 0).astype(BF16)
+    sums_one = tie(sums_one, cubes_zero)
+    for cube in cubes_zero:
+        cube.step()
+    done_one = ring_reduce(sums_one)
+    done_one = tie(done_one, cubes_zero)
+    for _ in range(shard_size - 2):
         chain.append(next_shard(chain[-1]))
+    done_zero, top_zero = to_top(finish_cubes(cubes_zero), 0)
+    done_one, top_one = to_top(done_one, 1)
+    model_sum = own_part(((done_zero, top_zero), (done_one, top_one)), length)
+    chain[-1], done_zero = lax.optimization_barrier((chain[-1], done_zero))
     from_dp = (jnp.arange(dp_size) ^ dp_idx)[None, :]
     from_shard = (shard_idx - jnp.arange(shard_size))[:, None] % shard_size
     spots = (from_dp * shard_size + from_shard).reshape(-1).astype(jnp.int32)

time: 879 us -> 822 us (0.935)
  waiting for transfers between devices: 260 us -> 161 us
  Pallas kernels: 227 us -> 308 us
  matrix products: 39.7 us -> 7.09 us
  starting transfers between devices: 76.6 us -> 103 us
  local copies, waits for them, and re-layouts: 98.2 us -> 76.7 us
  other arithmetic: 147 us -> 131 us
    pallas_call x0 -> x5, Pallas kernels: none -> 82.2 us  [the longest x4 64.1 us: layer_call(): pl.pallas_call(kernel, in_specs=[pl.BlockSpec(memory_space=pltpu.SMEM)] +...]
    ppermute x46 -> x50, waiting for transfers between devices: 121 us -> 50.4 us  [flip_dp(): lax.ppermute(values, 'dp', [(i, i ^ bit) for i in range(lax.axis_size('dp...]
    ppermute x18, waiting for transfers between devices: 115 us -> 91.8 us  [next_shard(): lax.ppermute(values, 'shard', [(i, (i + 1) % size) for i in range(size)])]
    unnamed x408 -> x203, local copies, waits for them, and re-layouts: 36.9 us -> 17.4 us
    dot_general x18 -> x0, matrix products: 16.7 us -> none  [the longest x2 4.12 us: layer_forward(): qkv = jnp.dot(normed, w_qkv, preferred_element_type=F32)]
    convert_element_type x32 -> x14, other arithmetic: 32.2 us -> 16.6 us  [the longest x8 9.09 us: ring_reduce(): got = next_shard(term.astype(BF16))]
    slice x25 -> x2, local copies, waits for them, and re-layouts: 14.5 us -> 0.49 us  [half_cubes(): return [Cube(paired[:, :half], order), Cube(paired[:, half:], order[::-1])]]
    pallas_call x1 -> x4, Pallas kernels: 38.2 us -> 49.7 us  [table_backward(): pl.pallas_call(table_kernel, grid_spec=pltpu.PrefetchScalarGridSpec(num_s...]
  transfers between devices with their start and end apart: 76 -> 80, of which waited for: 46 -> 38; matrix products, arithmetic and copies ran while one was open for 19% -> 16% of each run, Pallas kernels for 13% -> 22%
where the time goes in v2:
time: 822 us; the launch traced here: 809 us
  Pallas kernels  308 us (37%)
  waiting for transfers between devices  161 us (20%)
  other arithmetic  131 us (16%)
  starting transfers between devices  103 us (13%)
  local copies, waits for them, and re-layouts  76.7 us (9%)
  between operations  21.8 us (3%)
    ppermute x18, waiting for transfers between devices, next_shard(): lax.ppermute(values, 'shard', [(i, (i + 1) % size) for i in range(size)])  91.8 us
    pallas_call x1, Pallas kernels, head_forward(): pl.pallas_call(head_kernel, grid_spec=pltpu.PrefetchScalarGridSpec(num_sc...  88.1 us
    pallas_call x4, Pallas kernels, layer_call(): pl.pallas_call(kernel, in_specs=[pl.BlockSpec(memory_space=pltpu.SMEM)] +...  64.1 us
    ppermute x50, waiting for transfers between devices, flip_dp(): lax.ppermute(values, 'dp', [(i, i ^ bit) for i in range(lax.axis_size('dp...  50.4 us
    ppermute x50, starting transfers between devices, flip_dp(): lax.ppermute(values, 'dp', [(i, i ^ bit) for i in range(lax.axis_size('dp...  49.8 us
    pallas_call x4, Pallas kernels, table_backward(): pl.pallas_call(table_kernel, grid_spec=pltpu.PrefetchScalarGridSpec(num_s...  49.7 us
    ppermute x18, starting transfers between devices, next_shard(): lax.ppermute(values, 'shard', [(i, (i + 1) % size) for i in range(size)])  29.9 us
    pallas_call x2, Pallas kernels, pack_half(): pl.pallas_call(kernel, in_specs=[pl.BlockSpec(memory_space=pltpu.SMEM)] +...  24.2 us
  transfers between devices with their start and end apart: 80, of which 38 were waited for; matrix products, arithmetic and copies ran while one was open for 16% of the time, Pallas kernels for 22%

profile of v2, /device:TPU:0, one launch (start us, length us, event | category | flops | bytes accessed | tf_op | source)
XLA Modules:
  0.0 808.9 jit_solution(12367204833372784238)
XLA Ops:
  8.6 4.9 collective-permute-start.15
  18.6 5.2 collective-permute-start
  26.5 3.0 collective-permute-done.1
  30.7 5.4 collective-permute-done.3
  43.6 6.8 sort.14
  52.9 18.7 %embed_rows.1 = bf16[32,72,256]{2,1,0:T(8,128)(2,1)} custom-call(s32[8192]{0:T(1024)} %copy-done.39, s32[3]{0:T(128)} %pad_add_fusion.4.span_ref, s32[64,128]{1,0:T(8,128)} %bitcast.533, f32[72,12288]{1,0:T(8,128)} %table_ref.1), custom_call_target="tpu_custom_call" | custom-call | flops 536870912 | bytes 3538944 | tf_op jit(solution)/shard_map/embed_rows/pallas_call | solution.py:792
  73.4 3.4 collective-permute-start.5
  77.7 10.0 %collective-permute-done.5 = bf16[8,72,256]{2,1,0:T(8,128)(2,1)} collective-permute-done((bf16[8,72,256]{2,1,0:T(8,128)(2,1)}, bf16[8,72,256]{2,1,0:T(8,128)(2,1)}, u32[]{:S(2)}, u32[]{:S(2)}) %collective-permute-start.5) | collective-permute-done | bytes 294944 | tf_op jit(solution)/shard_map/ppermute | solution.py:51
  91.5 12.9 %collective-permute-done.6 = bf16[8,72,256]{2,1,0:T(8,128)(2,1)S(1)} collective-permute-done((bf16[8,72,256]{2,1,0:T(8,128)(2,1)S(1)}, bf16[8,72,256]{2,1,0:T(8,128)(2,1)S(1)}, u32[]{:S(2)}, u32[]{:S(2)}) %collective-permute-start.6) | collective-permute-done | bytes 294944 | tf_op jit(solution)/shard_map/ppermute | solution.py:51
  105.5 4.4 collective-permute-start.7
  110.6 15.3 %collective-permute-done.7 = bf16[8,72,256]{2,1,0:T(8,128)(2,1)S(1)} collective-permute-done((bf16[8,72,256]{2,1,0:T(8,128)(2,1)S(1)}, bf16[8,72,256]{2,1,0:T(8,128)(2,1)S(1)}, u32[]{:S(2)}, u32[]{:S(2)}) %collective-permute-start.7) | collective-permute-done | bytes 294944 | tf_op jit(solution)/shard_map/ppermute | solution.py:51
  152.6 11.2 %unpack_rows.2 = (bf16[576,960]{1,0:T(8,128)(2,1)}, bf16[576,576]{1,0:T(8,128)(2,1)}, bf16[576,3072]{1,0:T(8,128)(2,1)}, bf16[1536,576]{1,0:T(8,128)(2,1)}, bf16[16,128]{1,0:T(8,128)(2,1)}) custom-call(bf16[32,1824,128]{2,1,0:T(8,128)(2,1)} %all-gather.2.cloned.1.call-done.all_ref), custom_call_target="tpu_custom_call" | custom-call | bytes 14163968 | tf_op jit(solution)/shard_map/unpack_rows/pallas_call | solution.py:287
  163.8 12.4 %unpack_rows.3 = (bf16[576,960]{1,0:T(8,128)(2,1)}, bf16[576,576]{1,0:T(8,128)(2,1)}, bf16[576,3072]{1,0:T(8,128)(2,1)}, bf16[1536,576]{1,0:T(8,128)(2,1)}, bf16...) custom-call(bf16[32,1824,128]{2,1,0:T(8,128)(2,1)} %all-gather.2.cloned.1.call-done.all_ref), custom_call_target="tpu_custom_call" | custom-call | bytes 15499264 | tf_op jit(solution)/shard_map/unpack_rows/pallas_call | solution.py:287
  176.9 14.7 %layer_forward.2 = (f32[256,576]{1,0:T(8,128)}, bf16[256,576]{1,0:T(8,128)(2,1)}, bf16[256,768]{1,0:T(8,128)(2,1)}, bf16[256,192]{1,0:T(8,128)(2,1)}, bf16[256,5...) custom-call(s32[2]{0:T(128)} %dynamic_slice.259.len_ref, ...), custom_call_target="tpu_custom_call" | custom-call | flops 1812529152 | bytes 28320768 | tf_op jit(solution)/shard_map/layer_forward/pallas_call | solution.py:665
  195.1 3.1 maximum_select_fusion.5
  199.2 14.7 %layer_forward.3 = (f32[256,576]{1,0:T(8,128)}, bf16[256,576]{1,0:T(8,128)(2,1)}, bf16[256,768]{1,0:T(8,128)(2,1)}, bf16[256,192]{1,0:T(8,128)(2,1)}, bf16[256,5...) custom-call(s32[2]{0:T(128)} %dynamic_slice.259.len_ref, ...), custom_call_target="tpu_custom_call" | custom-call | flops 1812529152 | bytes 28320768 | tf_op jit(solution)/shard_map/layer_forward/pallas_call | solution.py:665
  217.3 6.7 collective-permute-start.19
  225.1 7.1 collective-permute-done.19
  235.4 6.6 collective-permute-done.20
  242.0 2.8 collective-permute-start.23
  244.8 3.7 maximum_select_fusion
  248.4 3.7 collective-permute-done.23
  256.1 5.2 maximum_select_fusion.1
  261.4 5.7 pad_maximum_fusion.table_ref
  268.8 3.2 copy.160
  272.0 4.3 multiply_reduce_fusion.2
  276.3 5.8 copy.161
  282.1 3.0 multiply_convert_fusion
  285.1 3.1 pad_maximum_fusion.1.rows_ref
  288.3 88.1 %head_forward.1 = (bf16[4096,6144]{1,0:T(8,128)(2,1)}, f32[4096,576]{1,0:T(8,128)}, f32[256,128]{1,0:T(8,128)}, f32[256,128]{1,0:T(8,128)}) custom-call(s32[1]{0:T(128)} %bitcast.16.count_ref, s32[256]{0:T(256)} %compare_select_fusion.9.list_ref, bf16[4096,576]{1,0:T(8,128)(2,1)} %pad_maximum_fusion.1.rows_ref, bf16[576,6144]{1,0:T(8,128)(2,1)} %pad_maximum_fusion.table_ref), custom_call_target="tpu_custom_call" | custom-call | flops 57982058496 | bytes 50331648 | tf_op jit(solution)/shard_map/head_forward/pallas_call | solution.py:954
  383.2 3.2 collective-permute-start.26
  390.7 18.0 %scale_rows.1 = (f32[4096,576]{1,0:T(8,128)}, bf16[576,4096]{1,0:T(8,128)(2,1)}) custom-call(s32[1]{0:T(128)} %bitcast.16.count_ref, s32[256]{0:T(256)} %compare_select_fusion.9.list_ref, bf16[4096,576]{1,0:T(8,128)(2,1)} %pad_maximum_fusion.1.rows_ref, f32[4096,576]{1,0:T(8,128)} %get-tuple-element.155.back_ref, f32[32,128]{1,0:T(8,128)} %fusion.41.scale_ref), custom_call_target="tpu_custom_call" | custom-call | bytes 28311552 | tf_op jit(solution)/shard_map/scale_rows/pallas_call | solution.py:1031
  408.8 3.0 slice.142
  418.3 2.8 slice_add_fusion
  426.5 12.1 %table_backward.4 = bf16[576,1536]{1,0:T(8,128)(2,1)} custom-call(s32[1]{0:T(128)} %bitcast.16.count_ref, bf16[576,4096]{1,0:T(8,128)(2,1)} %get-tuple-element.164.turned_ref, bf16[4096,6144]{1,0:T(8,128)(2,1)} %get-tuple-element.158.exp_ref), custom_call_target="tpu_custom_call" | custom-call | flops 7247757312 | bytes 12582912 | tf_op jit(solution)/shard_map/table_backward/pallas_call | solution.py:1082
  445.6 12.3 %table_backward.5 = bf16[576,1536]{1,0:T(8,128)(2,1)} custom-call(s32[1]{0:T(128)} %bitcast.16.count_ref, bf16[576,4096]{1,0:T(8,128)(2,1)} %get-tuple-element.164.turned_ref, bf16[4096,6144]{1,0:T(8,128)(2,1)} %get-tuple-element.158.exp_ref), custom_call_target="tpu_custom_call" | custom-call | flops 7247757312 | bytes 12582912 | tf_op jit(solution)/shard_map/table_backward/pallas_call | solution.py:1082
  464.4 12.4 %table_backward.6 = bf16[576,1536]{1,0:T(8,128)(2,1)} custom-call(s32[1]{0:T(128)} %bitcast.16.count_ref, bf16[576,4096]{1,0:T(8,128)(2,1)} %get-tuple-element.164.turned_ref, bf16[4096,6144]{1,0:T(8,128)(2,1)} %get-tuple-element.158.exp_ref), custom_call_target="tpu_custom_call" | custom-call | flops 7247757312 | bytes 12582912 | tf_op jit(solution)/shard_map/table_backward/pallas_call | solution.py:1082
  481.8 12.8 %table_backward.7 = bf16[576,1536]{1,0:T(8,128)(2,1)} custom-call(s32[1]{0:T(128)} %bitcast.16.count_ref, bf16[576,4096]{1,0:T(8,128)(2,1)} %get-tuple-element.164.turned_ref, bf16[4096,6144]{1,0:T(8,128)(2,1)} %get-tuple-element.158.exp_ref), custom_call_target="tpu_custom_call" | custom-call | flops 7247757312 | bytes 12582912 | tf_op jit(solution)/shard_map/table_backward/pallas_call | solution.py:1082
  505.1 17.4 %layer_backward.2 = (f32[256,576]{1,0:T(8,128)}, bf16[256,576]{1,0:T(8,128)(2,1)}, bf16[256,3072]{1,0:T(8,128)(2,1)}, bf16[256,576]{1,0:T(8,128)(2,1)}, bf16[256,960]{1,0:T(8,128)(2,1)}, /*index=5*/f32[2,576]{1,0:T(2,128)}) custom-call(s32[2]{0:T(128)} %dynamic_slice.259.len_ref, f32[256,576]{1,0:T(8,128)} %multiply_subtract_fusion.2.grad_ref, ...), custom_call_target="tpu_custom_call" | custom-call | flops 1812529152 | bytes 28320768 | tf_op jit(solution)/shard_map/layer_backward/pallas_call | solution.py:665
  523.8 14.0 %pack_half.2 = (bf16[16,928,128]{2,1,0:T(8,128)(2,1)}, bf16[16,928,128]{2,1,0:T(8,128)(2,1)}, bf16[1344,128]{1,0:T(8,128)(2,1)}) custom-call(s32[32]{0:T(128)} %pad_add_fusion.6.info_ref, bf16[256,576]{1,0:T(8,128)(2,1)} %get-tuple-element.174.refs_0_, bf16[256,576]{1,0:T(8,128)(2,1)} %get-tuple-element.175.refs_1_, ...), custom_call_target="tpu_custom_call" | custom-call | flops 3170893824 | bytes 15515648 | tf_op jit(solution)/shard_map/pack_half/pallas_call | solution.py:399
  554.6 17.4 %layer_backward.3 = (f32[256,576]{1,0:T(8,128)}, bf16[256,576]{1,0:T(8,128)(2,1)}, bf16[256,3072]{1,0:T(8,128)(2,1)}, bf16[256,576]{1,0:T(8,128)(2,1)}, bf16[256,960]{1,0:T(8,128)(2,1)}, /*index=5*/f32[2,576]{1,0:T(2,128)}) custom-call(s32[2]{0:T(128)} %dynamic_slice.259.len_ref, f32[256,576]{1,0:T(8,128)} %get-tuple-element.187.grad_ref, ...), custom_call_target="tpu_custom_call" | custom-call | flops 1812529152 | bytes 28320768 | tf_op jit(solution)/shard_map/layer_backward/pallas_call | solution.py:665
  580.1 10.1 %pack_half.3 = (bf16[16,928,128]{2,1,0:T(8,128)(2,1)}, bf16[16,928,128]{2,1,0:T(8,128)(2,1)}) custom-call(s32[32]{0:T(128)} %pad_add_fusion.5.info_ref, bf16[256,576]{1,0:T(8,128)(2,1)} %get-tuple-element.151.refs_0_, bf16[256,576]{1,0:T(8,128)(2,1)} %get-tuple-element.152.refs_1_, bf16[256,576]{1,0:T(8,128)(2,1)} %get-tuple-element.153.refs_2_, ...), custom_call_target="tpu_custom_call" | custom-call | flops 1811939328 | bytes 14843904 | tf_op jit(solution)/shard_map/pack_half/pallas_call | solution.py:399
  599.2 4.2 add_convert_fusion.1
  612.5 3.1 add_convert_fusion
  616.6 16.2 %collective-permute-done.56 = bf16[2,2,928,128]{3,2,1,0:T(8,128)(2,1)S(1)} collective-permute-done((bf16[2,2,928,128]{3,2,1,0:T(8,128)(2,1)S(1)}, bf16[2,2,928,128]{3,2,1,0:T(8,128)(2,1)S(1)}, u32[]{:S(2)}, u32[]{:S(2)}) %collective-permute-start.56) | collective-permute-done | bytes 950304 | tf_op jit(solution)/shard_map/ppermute | solution.py:42
  638.3 8.4 %collective-permute-done.57.refs_1_ = bf16[8,72,256]{2,1,0:T(8,128)(2,1)S(1)} collective-permute-done((bf16[8,72,256]{2,1,0:T(8,128)(2,1)S(1)}, bf16[8,72,256]{2,1,0:T(8,128)(2,1)S(1)}, u32[]{:S(2)}, u32[]{:S(2)}) %collective-permute-start.57) | collective-permute-done | bytes 294944 | tf_op jit(solution)/shard_map/ppermute | solution.py:51
  647.7 15.6 %collective-permute-done.58 = bf16[2,928,128]{2,1,0:T(8,128)(2,1)S(1)} collective-permute-done((bf16[2,928,128]{2,1,0:T(8,128)(2,1)S(1)}, bf16[2,928,128]{2,1,0:T(8,128)(2,1)S(1)}, u32[]{:S(2)}, u32[]{:S(2)}) %collective-permute-start.58) | collective-permute-done | bytes 475168 | tf_op jit(solution)/shard_map/ppermute | solution.py:42
  663.7 2.7 collective-permute-done.62
  668.9 5.5 collective-permute-done.64
  676.7 5.7 collective-permute-done.65
  683.6 6.9 collective-permute-done.66
  699.3 3.0 collective-permute-done.31
  711.0 5.4 collective-permute-done.60.refs_2_
  716.4 3.9 collective-permute-start.72
  722.1 4.3 maximum_select_fusion.2.refs_4_
  726.4 3.6 collective-permute-done.71
  732.9 21.4 %spread_rows.1 = f32[72,12288]{1,0:T(8,128)} custom-call(s32[8192]{0:T(1024)} %copy-done.39, s32[3]{0:T(128)} %pad_add_fusion.4.span_ref, s32[32]{0:T(128)} %add.906.place_ref, s32[64,128]{1,0:T(8,128)} %bitcast.534, bf16[8,72,256]{2,1,0:T(8,128)(2,1)} %copy-done.42, bf16[8,72,256]{2,1,0:T(8,128)(2,1)} %copy-done.43, ...), custom_call_target="tpu_custom_call" | custom-call | flops 536870912 | bytes 7077888 | tf_op jit(solution)/shard_map/spread_rows/pallas_call | solution.py:849
  754.4 3.6 multiply_reduce_fusion.3
  767.4 4.0 collective-permute-start.76
  776.5 4.3 collective-permute-start.78
  781.8 4.0 fusion.99
  785.8 6.5 fusion.100
  792.3 3.8 multiply_add_fusion.2
  796.1 4.4 multiply_add_fusion
  (550 shorter events, 216.0 us)
Async XLA Ops:
  7.2 131.4 %all-gather.2.cloned.1.call-start = ((), (), s32[]{:S(2)}) async-start(), calls=%async_computation | async-start | bytes 15409152 | tf_op jit(solution)/shard_map/all_gather | solution.py:1184
  8.6 6.2 collective-permute-start.15
  18.6 7.3 collective-permute-start
  30.7 5.4 collective-permute-start.3
  36.1 5.1 collective-permute-start.4
  73.4 14.3 %collective-permute-start.5 = (bf16[8,72,256]{2,1,0:T(8,128)(2,1)}, bf16[8,72,256]{2,1,0:T(8,128)(2,1)}, u32[]{:S(2)}, u32[]{:S(2)}) collective-permute-start(bf16[8,72,256]{2,1,0:T(8,128)(2,1)} %dynamic-slice_bitcast_fusion.9), channel_id=1, source_target_pairs={{0,1},{1,2},{2,3},{3,0},{4,5},{5,6},{6,7},{7,4},{8,9},{9,10},{10,1... | collective-permute-start | bytes 884744 | tf_op jit(solution)/shard_map/ppermute | solution.py:51
  88.9 15.6 %collective-permute-start.6 = (bf16[8,72,256]{2,1,0:T(8,128)(2,1)S(1)}, bf16[8,72,256]{2,1,0:T(8,128)(2,1)S(1)}, u32[]{:S(2)}, u32[]{:S(2)}) collective-permute-start(bf16[8,72,256]{2,1,0:T(8,128)(2,1)S(1)} %fusion.12), channel_id=1, source_target_pairs={{0,1},{1,2},{2,3},{3,0},{4,5},{5,6},{6,7},{7,4},{8,9},{9,10},{10,1... | collective-permute-start | bytes 884744 | tf_op jit(solution)/shard_map/ppermute | solution.py:51
  105.5 20.5 %collective-permute-start.7 = (bf16[8,72,256]{2,1,0:T(8,128)(2,1)S(1)}, bf16[8,72,256]{2,1,0:T(8,128)(2,1)S(1)}, u32[]{:S(2)}, u32[]{:S(2)}) collective-permute-start(bf16[8,72,256]{2,1,0:T(8,128)(2,1)S(1)} %fusion.13), channel_id=1, source_target_pairs={{0,1},{1,2},{2,3},{3,0},{4,5},{5,6},{6,7},{7,4},{8,9},{9,10},{10,1... | collective-permute-start | bytes 884744 | tf_op jit(solution)/shard_map/ppermute | solution.py:51
  127.7 5.2 collective-permute-start.8
  128.9 6.0 collective-permute-start.9
  129.7 9.2 %collective-permute-start.10 = (bf16[72,256]{1,0:T(8,128)(2,1)}, bf16[72,256]{1,0:T(8,128)(2,1)}, u32[]{:S(2)}, u32[]{:S(2)}) collective-permute-start(bf16[72,256]{1,0:T(8,128)(2,1)} %get-tuple-element.296), channel_id=1, source_target_pairs={{0,12},{4,8},{8,4},{12,0},{16,28},{20,24},{24,20},{28,16},{1,13},{... | collective-permute-start | bytes 110600 | tf_op jit(solution)/shard_map/ppermute | solution.py:42
  130.7 10.0 %collective-permute-start.11 = (bf16[72,256]{1,0:T(8,128)(2,1)}, bf16[72,256]{1,0:T(8,128)(2,1)}, u32[]{:S(2)}, u32[]{:S(2)}) collective-permute-start(bf16[72,256]{1,0:T(8,128)(2,1)} %get-tuple-element.295), channel_id=1, source_target_pairs={{0,16},{4,20},{8,24},{12,28},{16,0},{20,4},{24,8},{28,12},{1,17},{... | collective-permute-start | bytes 110600 | tf_op jit(solution)/shard_map/ppermute | solution.py:42
  132.9 9.2 %collective-permute-start.12 = (bf16[72,256]{1,0:T(8,128)(2,1)}, bf16[72,256]{1,0:T(8,128)(2,1)}, u32[]{:S(2)}, u32[]{:S(2)}) collective-permute-start(bf16[72,256]{1,0:T(8,128)(2,1)} %get-tuple-element.294), channel_id=1, source_target_pairs={{0,20},{4,16},{8,28},{12,24},{16,4},{20,0},{24,12},{28,8},{1,21},{... | collective-permute-start | bytes 110600 | tf_op jit(solution)/shard_map/ppermute | solution.py:42
  132.9 10.6 %collective-permute-start.13 = (bf16[72,256]{1,0:T(8,128)(2,1)}, bf16[72,256]{1,0:T(8,128)(2,1)}, u32[]{:S(2)}, u32[]{:S(2)}) collective-permute-start(bf16[72,256]{1,0:T(8,128)(2,1)} %get-tuple-element.293), channel_id=1, source_target_pairs={{0,24},{4,28},{8,16},{12,20},{16,8},{20,12},{24,0},{28,4},{1,25},{... | collective-permute-start | bytes 110600 | tf_op jit(solution)/shard_map/ppermute | solution.py:42
  134.9 13.5 %collective-permute-start.14 = (bf16[72,256]{1,0:T(8,128)(2,1)}, bf16[72,256]{1,0:T(8,128)(2,1)}, u32[]{:S(2)}, u32[]{:S(2)}) collective-permute-start(bf16[72,256]{1,0:T(8,128)(2,1)} %get-tuple-element.292), channel_id=1, source_target_pairs={{0,28},{4,24},{8,20},{12,16},{16,12},{20,8},{24,4},{28,0},{1,29},{... | collective-permute-start | bytes 110600 | tf_op jit(solution)/shard_map/ppermute | solution.py:42
  139.0 5.9 collective-permute-start.16
  145.4 46.3 %collective-permute-start.17 = (bf16[1,1,144,3072]{3,2,1,0:T(8,128)(2,1)S(1)}, bf16[1,1,144,3072]{3,2,1,0:T(8,128)(2,1)}, u32[]{:S(2)}, u32[]{:S(2)}) collective-permute-start(bf16[1,1,144,3072]{3,2,1,0:T(8,128)(2,1)S(1)} %get-tuple-element.279), channel_id=1, source_target_pairs={{0,8},{4,12},{8,0},{12,4},{16,24},{20,28},{24,16},{28,20},{1,9},{5... | collective-permute-start | bytes 2654216 | tf_op jit(solution)/shard_map/ppermute | solution.py:42
  146.8 44.9 %collective-permute-start.18 = (bf16[1,1,144,3072]{3,2,1,0:T(8,128)(2,1)S(1)}, bf16[1,1,144,3072]{3,2,1,0:T(8,128)(2,1)}, u32[]{:S(2)}, u32[]{:S(2)}) collective-permute-start(bf16[1,1,144,3072]{3,2,1,0:T(8,128)(2,1)S(1)} %get-tuple-element.278), channel_id=1, source_target_pairs={{0,16},{4,20},{8,24},{12,28},{16,0},{20,4},{24,8},{28,12},{1,17},{... | collective-permute-start | bytes 2654216 | tf_op jit(solution)/shard_map/ppermute | solution.py:42
  194.1 47.8 %collective-permute-start.22 = (bf16[2,1,144,3072]{3,2,1,0:T(8,128)(2,1)S(1)}, bf16[2,1,144,3072]{3,2,1,0:T(8,128)(2,1)}, u32[]{:S(2)}, u32[]{:S(2)}) collective-permute-start(bf16[2,1,144,3072]{3,2,1,0:T(8,128)(2,1)S(1)} %maximum_select_fusion.6), channel_id=1, source_target_pairs={{0,8},{4,12},{8,0},{12,4},{16,24},{20,28},{24,16},{28,20},{1,9},{5... | collective-permute-start | bytes 5308424 | tf_op jit(solution)/shard_map/ppermute | solution.py:42
  198.2 43.8 %collective-permute-start.21 = (bf16[1,2,144,3072]{3,2,1,0:T(8,128)(2,1)}, bf16[1,2,144,3072]{3,2,1,0:T(8,128)(2,1)}, u32[]{:S(2)}, u32[]{:S(2)}) collective-permute-start(bf16[1,2,144,3072]{3,2,1,0:T(8,128)(2,1)} %maximum_select_fusion.5), channel_id=1, source_target_pairs={{0,16},{4,20},{8,24},{12,28},{16,0},{20,4},{24,8},{28,12},{1,17},{... | collective-permute-start | bytes 5308424 | tf_op jit(solution)/shard_map/ppermute | solution.py:42
  217.3 14.8 %collective-permute-start.19 = (bf16[256,576]{1,0:T(8,128)(2,1)S(1)}, bf16[256,576]{1,0:T(8,128)(2,1)S(1)}, u32[]{:S(2)}, u32[]{:S(2)}) collective-permute-start(bf16[256,576]{1,0:T(8,128)(2,1)S(1)} %get-tuple-element.260), channel_id=1, source_target_pairs={{0,1},{1,2},{2,3},{3,0},{4,5},{5,6},{6,7},{7,4},{8,9},{9,10},{10,1... | collective-permute-start | bytes 884744 | tf_op jit(solution)/shard_map/ppermute | solution.py:51
  232.2 9.8 %collective-permute-start.20 = (bf16[256,576]{1,0:T(8,128)(2,1)S(1)}, bf16[256,576]{1,0:T(8,128)(2,1)S(1)}, u32[]{:S(2)}, u32[]{:S(2)}) collective-permute-start(bf16[256,576]{1,0:T(8,128)(2,1)S(1)} %collective-permute-done.19), channel_id=1, source_target_pairs={{0,1},{1,2},{2,3},{3,0},{4,5},{5,6},{6,7},{7,4},{8,9},{9,10},{10,1... | collective-permute-start | bytes 884744 | tf_op jit(solution)/shard_map/ppermute | solution.py:51
  242.0 10.2 %collective-permute-start.23 = (bf16[256,576]{1,0:T(8,128)(2,1)S(1)}, bf16[256,576]{1,0:T(8,128)(2,1)S(1)}, u32[]{:S(2)}, u32[]{:S(2)}) collective-permute-start(bf16[256,576]{1,0:T(8,128)(2,1)S(1)} %collective-permute-done.20), channel_id=1, source_target_pairs={{0,1},{1,2},{2,3},{3,0},{4,5},{5,6},{6,7},{7,4},{8,9},{9,10},{10,1... | collective-permute-start | bytes 884744 | tf_op jit(solution)/shard_map/ppermute | solution.py:51
  256.1 10.9 %collective-permute-start.24 = (bf16[4,256,576]{1,2,0:T(8,128)(2,1)}, bf16[4,256,576]{1,2,0:T(8,128)(2,1)S(1)}, u32[]{:S(2)}, u32[]{:S(2)}) collective-permute-start(bf16[4,256,576]{1,2,0:T(8,128)(2,1)} %copy.158), channel_id=1, source_target_pairs={{0,4},{4,0},{8,12},{12,8},{16,20},{20,16},{24,28},{28,24},{1,5},{5... | collective-permute-start | bytes 3538952 | tf_op jit(solution)/shard_map/ppermute | solution.py:42
  383.2 5.1 collective-permute-start.26
  424.2 14.4 %collective-permute-start.33 = (bf16[4,256,576]{1,2,0:T(8,128)(2,1)S(1)}, bf16[4,256,576]{1,2,0:T(8,128)(2,1)}, u32[]{:S(2)}, u32[]{:S(2)}) collective-permute-start(bf16[4,256,576]{1,2,0:T(8,128)(2,1)S(1)} %bitcast.531), channel_id=1, source_target_pairs={{0,4},{4,0},{8,12},{12,8},{16,20},{20,16},{24,28},{28,24},{1,5},{5... | collective-permute-start | bytes 3538952 | tf_op jit(solution)/shard_map/ppermute | solution.py:42
  444.6 15.4 %collective-permute-start.34 = (bf16[256,576]{1,0:T(8,128)(2,1)}, bf16[256,576]{1,0:T(8,128)(2,1)}, u32[]{:S(2)}, u32[]{:S(2)}) collective-permute-start(bf16[256,576]{1,0:T(8,128)(2,1)} %fusion.26), channel_id=1, source_target_pairs={{0,1},{1,2},{2,3},{3,0},{4,5},{5,6},{6,7},{7,4},{8,9},{9,10},{10,1... | collective-permute-start | bytes 884744 | tf_op jit(solution)/shard_map/ppermute | solution.py:51
  458.9 46.2 %collective-permute-start.37 = (bf16[2,144,1536]{2,1,0:T(8,128)(2,1)}, bf16[2,144,1536]{2,1,0:T(8,128)(2,1)}, u32[]{:S(2)}, u32[]{:S(2)}) collective-permute-start(bf16[2,144,1536]{2,1,0:T(8,128)(2,1)} %dynamic-slice_bitcast_fusion.7), channel_id=1, source_target_pairs={{0,8},{4,12},{8,0},{12,4},{16,24},{20,28},{24,16},{28,20},{1,9},{5... | collective-permute-start | bytes 2654216 | tf_op jit(solution)/shard_map/ppermute | solution.py:42
  461.9 17.5 %collective-permute-start.35 = (bf16[256,576]{1,0:T(8,128)(2,1)}, bf16[256,576]{1,0:T(8,128)(2,1)}, u32[]{:S(2)}, u32[]{:S(2)}) collective-permute-start(bf16[256,576]{1,0:T(8,128)(2,1)} %fusion.8), channel_id=1, source_target_pairs={{0,1},{1,2},{2,3},{3,0},{4,5},{5,6},{6,7},{7,4},{8,9},{9,10},{10,1... | collective-permute-start | bytes 884744 | tf_op jit(solution)/shard_map/ppermute | solution.py:51
  478.9 26.2 %collective-permute-start.38 = (bf16[2,144,1536]{2,1,0:T(8,128)(2,1)}, bf16[2,144,1536]{2,1,0:T(8,128)(2,1)}, u32[]{:S(2)}, u32[]{:S(2)}) collective-permute-start(bf16[2,144,1536]{2,1,0:T(8,128)(2,1)} %dynamic-slice_bitcast_fusion.6), channel_id=1, source_target_pairs={{0,16},{4,20},{8,24},{12,28},{16,0},{20,4},{24,8},{28,12},{1,17},{... | collective-permute-start | bytes 2654216 | tf_op jit(solution)/shard_map/ppermute | solution.py:42
  481.4 16.2 %collective-permute-start.36 = (bf16[256,576]{1,0:T(8,128)(2,1)}, bf16[256,576]{1,0:T(8,128)(2,1)}, u32[]{:S(2)}, u32[]{:S(2)}) collective-permute-start(bf16[256,576]{1,0:T(8,128)(2,1)} %fusion.9), channel_id=1, source_target_pairs={{0,1},{1,2},{2,3},{3,0},{4,5},{5,6},{6,7},{7,4},{8,9},{9,10},{10,1... | collective-permute-start | bytes 884744 | tf_op jit(solution)/shard_map/ppermute | solution.py:51
  497.0 26.8 %collective-permute-start.39 = (bf16[2,144,1536]{2,1,0:T(8,128)(2,1)}, bf16[2,144,1536]{2,1,0:T(8,128)(2,1)}, u32[]{:S(2)}, u32[]{:S(2)}) collective-permute-start(bf16[2,144,1536]{2,1,0:T(8,128)(2,1)} %dynamic-slice_bitcast_fusion.5), channel_id=1, source_target_pairs={{0,8},{4,12},{8,0},{12,4},{16,24},{20,28},{24,16},{28,20},{1,9},{5... | collective-permute-start | bytes 2654216 | tf_op jit(solution)/shard_map/ppermute | solution.py:42
  499.8 24.0 %collective-permute-start.40 = (bf16[2,144,1536]{2,1,0:T(8,128)(2,1)}, bf16[2,144,1536]{2,1,0:T(8,128)(2,1)}, u32[]{:S(2)}, u32[]{:S(2)}) collective-permute-start(bf16[2,144,1536]{2,1,0:T(8,128)(2,1)} %dynamic-slice_bitcast_fusion.4), channel_id=1, source_target_pairs={{0,16},{4,20},{8,24},{12,28},{16,0},{20,4},{24,8},{28,12},{1,17},{... | collective-permute-start | bytes 2654216 | tf_op jit(solution)/shard_map/ppermute | solution.py:42
  537.9 35.4 %collective-permute-start.41 = (bf16[16,928,128]{2,1,0:T(8,128)(2,1)}, bf16[16,928,128]{2,1,0:T(8,128)(2,1)}, u32[]{:S(2)}, u32[]{:S(2)}) collective-permute-start(bf16[16,928,128]{2,1,0:T(8,128)(2,1)} %get-tuple-element.197), channel_id=1, source_target_pairs={{0,4},{4,0},{8,12},{12,8},{16,20},{20,16},{24,28},{28,24},{1,5},{5... | collective-permute-start | bytes 11403272 | tf_op jit(solution)/shard_map/ppermute | solution.py:42
  540.5 32.8 %collective-permute-start.44 = (bf16[144,1536]{1,0:T(8,128)(2,1)}, bf16[144,1536]{1,0:T(8,128)(2,1)}, u32[]{:S(2)}, u32[]{:S(2)}) collective-permute-start(bf16[144,1536]{1,0:T(8,128)(2,1)} %fusion.24), channel_id=1, source_target_pairs={{0,8},{4,12},{8,0},{12,4},{16,24},{20,28},{24,16},{28,20},{1,9},{5... | collective-permute-start | bytes 1327112 | tf_op jit(solution)/shard_map/ppermute | solution.py:42
  543.8 29.4 %collective-permute-start.42 = (bf16[144,1536]{1,0:T(8,128)(2,1)}, bf16[144,1536]{1,0:T(8,128)(2,1)}, u32[]{:S(2)}, u32[]{:S(2)}) collective-permute-start(bf16[144,1536]{1,0:T(8,128)(2,1)} %fusion.22), channel_id=1, source_target_pairs={{0,16},{4,20},{8,24},{12,28},{16,0},{20,4},{24,8},{28,12},{1,17},{... | collective-permute-start | bytes 1327112 | tf_op jit(solution)/shard_map/ppermute | solution.py:42
  546.6 26.7 %collective-permute-start.45 = (bf16[144,1536]{1,0:T(8,128)(2,1)}, bf16[144,1536]{1,0:T(8,128)(2,1)}, u32[]{:S(2)}, u32[]{:S(2)}) collective-permute-start(bf16[144,1536]{1,0:T(8,128)(2,1)} %fusion.25), channel_id=1, source_target_pairs={{0,8},{4,12},{8,0},{12,4},{16,24},{20,28},{24,16},{28,20},{1,9},{5... | collective-permute-start | bytes 1327112 | tf_op jit(solution)/shard_map/ppermute | solution.py:42
  551.0 22.3 %collective-permute-start.43 = (bf16[144,1536]{1,0:T(8,128)(2,1)}, bf16[144,1536]{1,0:T(8,128)(2,1)}, u32[]{:S(2)}, u32[]{:S(2)}) collective-permute-start(bf16[144,1536]{1,0:T(8,128)(2,1)} %fusion.23), channel_id=1, source_target_pairs={{0,16},{4,20},{8,24},{12,28},{16,0},{20,4},{24,8},{28,12},{1,17},{... | collective-permute-start | bytes 1327112 | tf_op jit(solution)/shard_map/ppermute | solution.py:42
  590.2 22.3 %collective-permute-start.46 = (bf16[16,928,128]{2,1,0:T(8,128)(2,1)}, bf16[16,928,128]{2,1,0:T(8,128)(2,1)}, u32[]{:S(2)}, u32[]{:S(2)}) collective-permute-start(bf16[16,928,128]{2,1,0:T(8,128)(2,1)} %get-tuple-element.205), channel_id=1, source_target_pairs={{0,4},{4,0},{8,12},{12,8},{16,20},{20,16},{24,28},{28,24},{1,5},{5... | collective-permute-start | bytes 11403272 | tf_op jit(solution)/shard_map/ppermute | solution.py:42
  594.7 17.8 %collective-permute-start.54 = (f32[72,6144]{1,0:T(8,128)}, f32[72,6144]{1,0:T(8,128)}, u32[]{:S(2)}, u32[]{:S(2)}) collective-permute-start(f32[72,6144]{1,0:T(8,128)} %get-tuple-element.275), channel_id=1, source_target_pairs={{0,4},{4,0},{8,12},{12,8},{16,20},{20,16},{24,28},{28,24},{1,5},{5... | collective-permute-start | bytes 5308424 | tf_op jit(solution)/shard_map/ppermute | solution.py:42
  597.3 6.4 collective-permute-start.47
  597.7 6.6 collective-permute-start.48
  598.8 7.1 collective-permute-start.49
  608.4 24.4 %collective-permute-start.56 = (bf16[2,2,928,128]{3,2,1,0:T(8,128)(2,1)S(1)}, bf16[2,2,928,128]{3,2,1,0:T(8,128)(2,1)S(1)}, u32[]{:S(2)}, u32[]{:S(2)}) collective-permute-start(bf16[2,2,928,128]{3,2,1,0:T(8,128)(2,1)S(1)} %dynamic-slice_bitcast_fusion.2), channel_id=1, source_target_pairs={{0,16},{4,20},{8,24},{12,28},{16,0},{20,4},{24,8},{28,12},{1,17},{... | collective-permute-start | bytes 2850824 | tf_op jit(solution)/shard_map/ppermute | solution.py:42
  610.8 22.8 %collective-permute-start.55 = (bf16[2,2,928,128]{3,2,1,0:T(8,128)(2,1)S(1)}, bf16[2,2,928,128]{3,2,1,0:T(8,128)(2,1)S(1)}, u32[]{:S(2)}, u32[]{:S(2)}) collective-permute-start(bf16[2,2,928,128]{3,2,1,0:T(8,128)(2,1)S(1)} %dynamic-slice_bitcast_fusion.3), channel_id=1, source_target_pairs={{0,8},{4,12},{8,0},{12,4},{16,24},{20,28},{24,16},{28,20},{1,9},{5... | collective-permute-start | bytes 2850824 | tf_op jit(solution)/shard_map/ppermute | solution.py:42
  615.9 47.8 %collective-permute-start.63 = (bf16[2,2,928,128]{3,2,1,0:T(8,128)(2,1)S(1)}, bf16[2,2,928,128]{3,2,1,0:T(8,128)(2,1)S(1)}, u32[]{:S(2)}, u32[]{:S(2)}) collective-permute-start(bf16[2,2,928,128]{3,2,1,0:T(8,128)(2,1)S(1)} %dynamic-slice_bitcast_fusion), channel_id=1, source_target_pairs={{0,16},{4,20},{8,24},{12,28},{16,0},{20,4},{24,8},{28,12},{1,17},{... | collective-permute-start | bytes 2850824 | tf_op jit(solution)/shard_map/ppermute | solution.py:42
  633.9 13.9 %collective-permute-start.59 = (bf16[2,928,128]{2,1,0:T(8,128)(2,1)S(1)}, bf16[2,928,128]{2,1,0:T(8,128)(2,1)S(1)}, u32[]{:S(2)}, u32[]{:S(2)}) collective-permute-start(bf16[2,928,128]{2,1,0:T(8,128)(2,1)S(1)} %fusion.15), channel_id=1, source_target_pairs={{0,8},{4,12},{8,0},{12,4},{16,24},{20,28},{24,16},{28,20},{1,9},{5... | collective-permute-start | bytes 1425416 | tf_op jit(solution)/shard_map/ppermute | solution.py:42
  635.2 28.2 %collective-permute-start.58 = (bf16[2,928,128]{2,1,0:T(8,128)(2,1)S(1)}, bf16[2,928,128]{2,1,0:T(8,128)(2,1)S(1)}, u32[]{:S(2)}, u32[]{:S(2)}) collective-permute-start(bf16[2,928,128]{2,1,0:T(8,128)(2,1)S(1)} %fusion.14), channel_id=1, source_target_pairs={{0,16},{4,20},{8,24},{12,28},{16,0},{20,4},{24,8},{28,12},{1,17},{... | collective-permute-start | bytes 1425416 | tf_op jit(solution)/shard_map/ppermute | solution.py:42
  635.7 30.7 %collective-permute-start.62 = (bf16[2,2,928,128]{3,2,1,0:T(8,128)(2,1)S(1)}, bf16[2,2,928,128]{3,2,1,0:T(8,128)(2,1)S(1)}, u32[]{:S(2)}, u32[]{:S(2)}) collective-permute-start(bf16[2,2,928,128]{3,2,1,0:T(8,128)(2,1)S(1)} %dynamic-slice_bitcast_fusion.1), channel_id=1, source_target_pairs={{0,8},{4,12},{8,0},{12,4},{16,24},{20,28},{24,16},{28,20},{1,9},{5... | collective-permute-start | bytes 2850824 | tf_op jit(solution)/shard_map/ppermute | solution.py:42
  636.8 9.9 %collective-permute-start.57 = (bf16[8,72,256]{2,1,0:T(8,128)(2,1)S(1)}, bf16[8,72,256]{2,1,0:T(8,128)(2,1)S(1)}, u32[]{:S(2)}, u32[]{:S(2)}) collective-permute-start(bf16[8,72,256]{2,1,0:T(8,128)(2,1)S(1)} %constant_dynamic-update-slice_fusion.8.refs_0_), channel_id=1, source_target_pairs={{0,1},{1,2},{2,3},{3,0},{4,5},{5,6},{6,7},{7,4},{8,9},{9,10},{10,1... | collective-permute-start | bytes 884744 | tf_op jit(solution)/shard_map/ppermute | solution.py:51
  666.4 8.0 collective-permute-start.64
  667.7 22.8 %collective-permute-start.68 = (bf16[2,928,128]{2,1,0:T(8,128)(2,1)S(1)}, bf16[2,928,128]{2,1,0:T(8,128)(2,1)S(1)}, u32[]{:S(2)}, u32[]{:S(2)}) collective-permute-start(bf16[2,928,128]{2,1,0:T(8,128)(2,1)S(1)} %fusion.17), channel_id=1, source_target_pairs={{0,8},{4,12},{8,0},{12,4},{16,24},{20,28},{24,16},{28,20},{1,9},{5... | collective-permute-start | bytes 1425416 | tf_op jit(solution)/shard_map/ppermute | solution.py:42
  674.5 8.0 collective-permute-start.65
  674.8 15.7 %collective-permute-start.67 = (bf16[2,928,128]{2,1,0:T(8,128)(2,1)S(1)}, bf16[2,928,128]{2,1,0:T(8,128)(2,1)S(1)}, u32[]{:S(2)}, u32[]{:S(2)}) collective-permute-start(bf16[2,928,128]{2,1,0:T(8,128)(2,1)S(1)} %fusion.16), channel_id=1, source_target_pairs={{0,16},{4,20},{8,24},{12,28},{16,0},{20,4},{24,8},{28,12},{1,17},{... | collective-permute-start | bytes 1425416 | tf_op jit(solution)/shard_map/ppermute | solution.py:42
  682.5 8.0 collective-permute-start.66
  683.6 8.0 collective-permute-start.28
  691.6 15.1 %collective-permute-start.69 = (bf16[928,128]{1,0:T(8,128)(2,1)}, bf16[928,128]{1,0:T(8,128)(2,1)}, u32[]{:S(2)}, u32[]{:S(2)}) collective-permute-start(bf16[928,128]{1,0:T(8,128)(2,1)} %fusion.36), channel_id=1, source_target_pairs={{0,1},{1,2},{2,3},{3,0},{4,5},{5,6},{6,7},{7,4},{8,9},{9,10},{10,1... | collective-permute-start | bytes 712712 | tf_op jit(solution)/shard_map/ppermute | solution.py:51
  702.4 6.3 collective-permute-start.32
  704.7 11.7 %collective-permute-start.60 = (bf16[8,72,256]{2,1,0:T(8,128)(2,1)S(1)}, bf16[8,72,256]{2,1,0:T(8,128)(2,1)}, u32[]{:S(2)}, u32[]{:S(2)}) collective-permute-start(bf16[8,72,256]{2,1,0:T(8,128)(2,1)S(1)} %copy-done.44), channel_id=1, source_target_pairs={{0,1},{1,2},{2,3},{3,0},{4,5},{5,6},{6,7},{7,4},{8,9},{9,10},{10,1... | collective-permute-start | bytes 884744 | tf_op jit(solution)/shard_map/ppermute | solution.py:51
  708.4 12.5 %collective-permute-start.70 = (bf16[928,128]{1,0:T(8,128)(2,1)}, bf16[928,128]{1,0:T(8,128)(2,1)}, u32[]{:S(2)}, u32[]{:S(2)}) collective-permute-start(bf16[928,128]{1,0:T(8,128)(2,1)} %fusion.18), channel_id=1, source_target_pairs={{0,1},{1,2},{2,3},{3,0},{4,5},{5,6},{6,7},{7,4},{8,9},{9,10},{10,1... | collective-permute-start | bytes 712712 | tf_op jit(solution)/shard_map/ppermute | solution.py:51
  716.4 15.8 %collective-permute-start.61 = (bf16[8,72,256]{2,1,0:T(8,128)(2,1)}, bf16[8,72,256]{2,1,0:T(8,128)(2,1)S(1)}, u32[]{:S(2)}, u32[]{:S(2)}) collective-permute-start(bf16[8,72,256]{2,1,0:T(8,128)(2,1)} %collective-permute-done.60.refs_2_), channel_id=1, source_target_pairs={{0,1},{1,2},{2,3},{3,0},{4,5},{5,6},{6,7},{7,4},{8,9},{9,10},{10,1... | collective-permute-start | bytes 884744 | tf_op jit(solution)/shard_map/ppermute | solution.py:51
  716.4 10.0 %collective-permute-start.72 = (bf16[928,128]{1,0:T(8,128)(2,1)S(1)}, bf16[928,128]{1,0:T(8,128)(2,1)S(1)}, u32[]{:S(2)}, u32[]{:S(2)}) collective-permute-start(bf16[928,128]{1,0:T(8,128)(2,1)S(1)} %convert_element_type.534), channel_id=1, source_target_pairs={{0,16},{4,20},{8,24},{12,28},{1,17},{5,21},{9,25},{13,29},{2,18},{... | collective-permute-start | bytes 712712 | tf_op jit(solution)/shard_map/ppermute | solution.py:453
  722.0 8.0 collective-permute-start.71
  730.9 27.0 %collective-permute-start.73 = (bf16[928,128]{1,0:T(8,128)(2,1)S(1)}, bf16[928,128]{1,0:T(8,128)(2,1)S(1)}, u32[]{:S(2)}, u32[]{:S(2)}) collective-permute-start(bf16[928,128]{1,0:T(8,128)(2,1)S(1)} %get-tuple-element.258), channel_id=1, source_target_pairs={{16,0},{20,4},{24,8},{28,12},{17,1},{21,5},{25,9},{29,13},{18,2},{... | collective-permute-start | bytes 712712 | tf_op jit(solution)/shard_map/ppermute | solution.py:453
  (106 other events, 1493.6 us)
Sparse Core Ops, SparseCore 0:
  18.5 120.0 all-gather.1

commit v3 on v2

--- a/solution.py
+++ b/solution.py
@@ -395,7 +395,6 @@
             count=count, sub_rows=sub_rows, keep=keep, first_loose=skip,
         )
 
-    flops = sum(2 * left.size * right.shape[1] for left, right in pairs)
     return pl.pallas_call(
         kernel,
         in_specs=[pl.BlockSpec(memory_space=pltpu.SMEM)] + [in_place] * len(operands),
@@ -409,7 +408,7 @@
         ],
         compiler_params=pltpu.CompilerParams(vmem_limit_bytes=VMEM_LIMIT),
         cost_estimate=pl.CostEstimate(
-            flops=flops, bytes_accessed=512 * height, transcendentals=0
+            flops=0, bytes_accessed=32 * height, transcendentals=0
         ),
         name="pack_half",
     )(info, *operands)
@@ -443,24 +442,14 @@
     return [Cube(paired[:, :half], order), Cube(paired[:, half:], order[::-1])]
 
 
-def finish_cubes(cubes):
-    return ring_reduce(jnp.concatenate([cube.finish() for cube in cubes], 0).astype(BF16))
-
-
-def to_top(done, which):
-    top = top_bit()
-    away = [(i, i ^ top) for i in range(lax.axis_size("dp")) if (i // top) % 2 != which]
-    return done, lax.ppermute(done.astype(BF16), "dp", away).astype(F32)
-
-
-def own_part(halves, length):
-    (done_zero, got_zero), (done_one, got_one) = halves
+def own_part(sums_zero, sums_one, length):
+    done = ring_reduce(jnp.stack([sums_zero, sums_one], 1).astype(BF16))
     top = dp_bit(top_bit())
-    lower = jnp.where(top == 0, done_zero, got_one)
-    upper = jnp.where(top == 0, got_zero, done_one)
+    got = flip_dp(pick(done, 1 - top, 0).astype(BF16), top_bit()).astype(F32)
+    own = pick(done, top, 0)
+    both = jnp.where(top == 0, jnp.concatenate([own, got], 0), jnp.concatenate([got, own], 0))
     shift = (length * lax.axis_index(("dp", "shard"))) % GRAIN
-    flat = jnp.concatenate([lower, upper], 0).reshape(-1)
-    return lax.dynamic_slice_in_dim(flat, shift, length, 0)
+    return lax.dynamic_slice_in_dim(both.reshape(-1), shift, length, 0)
 
 
 class TableGather:
@@ -863,6 +852,39 @@
     )(keys, span, places, keys.reshape(-1, LANES), *parts, base)
 
 
+def second_kernel(rows_ref, weight_ref, gain_ref, both_ref, projected_ref):
+    projected = jnp.dot(rows_ref[...], weight_ref[...], preferred_element_type=F32)
+    projected_ref[...] = projected
+    both_ref[0] = rows_ref[...]
+    both_ref[1] = (projected * rms_scale(projected) * gain_ref[...]).astype(BF16)
+
+
+def second_head(rows, weight, gain):
+    count = rows.shape[0]
+    return pl.pallas_call(
+        second_kernel,
+        grid=(count // BLOCK,),
+        in_specs=[
+            pl.BlockSpec((BLOCK, MODEL_WIDTH), lambda i: (i, 0)),
+            pl.BlockSpec(weight.shape, lambda i: (0, 0)),
+            pl.BlockSpec(gain.shape, lambda i: (0, 0)),
+        ],
+        out_specs=[
+            pl.BlockSpec((2, BLOCK, MODEL_WIDTH), lambda i: (0, i, 0)),
+            pl.BlockSpec((BLOCK, MODEL_WIDTH), lambda i: (i, 0)),
+        ],
+        out_shape=[
+            jax.ShapeDtypeStruct((2, count, MODEL_WIDTH), BF16),
+            jax.ShapeDtypeStruct((count, MODEL_WIDTH), F32),
+        ],
+        compiler_params=pltpu.CompilerParams(vmem_limit_bytes=VMEM_LIMIT),
+        cost_estimate=pl.CostEstimate(
+            flops=2 * count * weight.size, bytes_accessed=10 * rows.size, transcendentals=0
+        ),
+        name="second_head",
+    )(rows, weight, gain)
+
+
 def block_count(count_ref):
     per = BLOCK // GRANULE
     return (count_ref[0] + per - 1) // per
@@ -1241,10 +1263,10 @@
     head_one = (hidden * scale_final * head_gains[0]).astype(BF16)
     all_one = group_gather(head_one, table_gather.tied).reshape(-1, MODEL_WIDTH)
     table_low = table_gather.finish()
-    projected = jnp.dot(all_one, w_second, preferred_element_type=F32)
+    both, projected = second_head(all_one, w_second, head_gains[1:2])
+    all_two = both[1]
+    both = both.reshape(-1, MODEL_WIDTH)
     scale_second = rms_scale(projected)
-    all_two = (projected * scale_second * head_gains[1]).astype(BF16)
-    both = jnp.concatenate([all_one, all_two], 0)
     group_rows = all_one.shape[0]
 
     powers, back, sums, peaks = head_forward(count, order, both, table_low)
@@ -1322,15 +1344,14 @@
         None, middle_rows - low_rows, {3: tail, 4: tail}, height_one, sub_rows, keep, 0,
     )
     got_one = flip_dp(send_one, 1)
-    grad_hidden, own_one = lax.optimization_barrier((grad_hidden, own_one))
+    grad_hidden, own_one, got_one = lax.optimization_barrier((grad_hidden, own_one, got_one))
+    cubes_one = half_cubes(own_one, got_one)
     grad_hidden, pairs, gain_grads = layer_backward(
         kept_zero, layer_zero, own_lens, rope, grad_hidden
     )
-    gain_grads, got_one = lax.optimization_barrier((gain_grads, got_one))
     gain_grads = tie(gain_grads, cubes)
     joined = jnp.concatenate([cube.finish() for cube in cubes], 1)
     flipped = owner_flip(joined, features)
-    cubes_one = half_cubes(own_one, got_one)
     own_zero, send_zero = pack_half(
         owner_rows(length, 0, 0), pairs, [gain_grads],
         (kept_rows, height_zero - middle_rows), 0, {3: tail}, height_zero, sub_rows, 0,
@@ -1346,42 +1367,37 @@
     token_parts = token_grad.T.reshape(dp_size, features, own_rows)
     parts = [pick(token_parts, dp_idx, 0)]
     parts += [flip_dp(pick(token_parts, dp_idx ^ k, 0), k) for k in range(1, dp_size)]
+    own_zero = tie(own_zero, cubes_one)
+    for cube in cubes_one:
+        cube.step()
     got_zero, parts, flipped = lax.optimization_barrier((flip_dp(send_zero, 1), parts, flipped))
     table_part = owner_join(joined, flipped, features)
     cubes_zero = half_cubes(own_zero, got_zero)
     chain = [jnp.stack(parts)]
-    chain[0] = tie(chain[0], cubes_one)
-    for cube in cubes_one:
-        cube.step()
-    chain.append(next_shard(chain[0]))
-    chain[1] = tie(chain[1], cubes_one)
-    sums_one = jnp.concatenate([cube.finish() for cube in cubes_one], 0).astype(BF16)
-    sums_one = tie(sums_one, cubes_zero)
+    for k in range(shard_size - 1):
+        chain.append(next_shard(chain[-1]))
+        if k == 0:
+            chain[-1] = tie(chain[-1], cubes_one)
+            sums_one = jnp.concatenate([cube.finish() for cube in cubes_one], 0)
+    chain[-1] = tie(chain[-1], cubes_zero)
     for cube in cubes_zero:
         cube.step()
-    done_one = ring_reduce(sums_one)
-    done_one = tie(done_one, cubes_zero)
-    for _ in range(shard_size - 2):
-        chain.append(next_shard(chain[-1]))
-    done_zero, top_zero = to_top(finish_cubes(cubes_zero), 0)
-    done_one, top_one = to_top(done_one, 1)
-    model_sum = own_part(((done_zero, top_zero), (done_one, top_one)), length)
-    chain[-1], done_zero = lax.optimization_barrier((chain[-1], done_zero))
     from_dp = (jnp.arange(dp_size) ^ dp_idx)[None, :]
     from_shard = (shard_idx - jnp.arange(shard_size))[:, None] % shard_size
     spots = (from_dp * shard_size + from_shard).reshape(-1).astype(jnp.int32)
     table_sum = spread_rows(keys, span, spots, chain, table_part)
-
-    square_sum = sum_all(
-        (jnp.sum(table_sum * table_sum) + jnp.sum(model_sum * model_sum)).reshape(1, 1)
-    )[0, 0]
-    grad_norm = jnp.sqrt(square_sum)
+    table_sum = tie(table_sum, cubes_zero)
+    sums_zero = jnp.concatenate([cube.finish() for cube in cubes_zero], 0)
+    model_sum = own_part(sums_zero, sums_one, length)
+
+    square_sum = jnp.sum(table_sum * table_sum) + jnp.sum(model_sum * model_sum)
+    losses = jnp.sum(
+        jnp.where(own_seqs[:, None] == here[None, :], own_loss[:, None], 0.0), axis=0
+    )
+    totals = sum_all(jnp.concatenate([losses, square_sum.reshape(1)])[None])[0]
+    grad_norm = jnp.sqrt(totals[seq_total])
     factor = jnp.minimum(1.0, CLIP_NORM / (grad_norm + 1e-06))
-
-    spots = jnp.sum(
-        jnp.where(own_seqs[:, None] == here[None, :], own_loss[:, None], 0.0), axis=0
-    )[None]
-    all_loss = sum_all(spots)[0]
+    all_loss = totals[:seq_total]
     loss_total = jnp.sum(all_loss)
     seq_loss = lax.dynamic_slice_in_dim(all_loss, device_idx * seqs, seqs, 0)
     own_slots = lax.dynamic_slice_in_dim(deal_order, device_idx * seqs, seqs, 0)

time: 822 us -> 776 us (0.944)
  starting transfers between devices: 103 us -> 79.6 us
  waiting for transfers between devices: 161 us -> 145 us
    ppermute x50 -> x48, waiting for transfers between devices: 50.4 us -> 27 us  [flip_dp(): lax.ppermute(values, 'dp', [(i, i ^ bit) for i in range(lax.axis_size('dp...]
    ppermute x8 -> x6, starting transfers between devices: 13.7 us -> 3.33 us  [flip_shard(): lax.ppermute(values, 'shard', [(i, i ^ bit) for i in range(lax.axis_size(...]
    ppermute x18 -> x15, waiting for transfers between devices: 91.8 us -> 99.2 us  [next_shard(): lax.ppermute(values, 'shard', [(i, (i + 1) % size) for i in range(size)])]
    ppermute x18 -> x15, starting transfers between devices: 29.9 us -> 25.6 us  [next_shard(): lax.ppermute(values, 'shard', [(i, (i + 1) % size) for i in range(size)])]
    ppermute x50 -> x48, starting transfers between devices: 49.8 us -> 45.7 us  [flip_dp(): lax.ppermute(values, 'dp', [(i, i ^ bit) for i in range(lax.axis_size('dp...]
    ppermute x8 -> x6, waiting for transfers between devices: 15.8 us -> 17 us  [flip_shard(): lax.ppermute(values, 'shard', [(i, i ^ bit) for i in range(lax.axis_size(...]
    unnamed x203 -> x185, local copies, waits for them, and re-layouts: 17.4 us -> 16.3 us
  transfers between devices with their start and end apart: 80 -> 71, of which waited for: 38 -> 32; matrix products, arithmetic and copies ran while one was open for 16% -> 18% of each run, Pallas kernels for 22% -> 25%
where the time goes in v3:
time: 776 us; the launch traced here: 767 us
  Pallas kernels  316 us (41%)
  waiting for transfers between devices  145 us (19%)
  other arithmetic  132 us (17%)
  starting transfers between devices  79.6 us (10%)
  local copies, waits for them, and re-layouts  71.3 us (9%)
  between operations  19.5 us (3%)
    ppermute x15, waiting for transfers between devices, next_shard(): lax.ppermute(values, 'shard', [(i, (i + 1) % size) for i in range(size)])  99.2 us
    pallas_call x1, Pallas kernels, head_forward(): pl.pallas_call(head_kernel, grid_spec=pltpu.PrefetchScalarGridSpec(num_sc...  88.1 us
    pallas_call x4, Pallas kernels, layer_call(): pl.pallas_call(kernel, in_specs=[pl.BlockSpec(memory_space=pltpu.SMEM)] +...  64.4 us
    pallas_call x4, Pallas kernels, table_backward(): pl.pallas_call(table_kernel, grid_spec=pltpu.PrefetchScalarGridSpec(num_s...  49.7 us
    ppermute x48, starting transfers between devices, flip_dp(): lax.ppermute(values, 'dp', [(i, i ^ bit) for i in range(lax.axis_size('dp...  45.7 us
    ppermute x48, waiting for transfers between devices, flip_dp(): lax.ppermute(values, 'dp', [(i, i ^ bit) for i in range(lax.axis_size('dp...  27 us
    ppermute x15, starting transfers between devices, next_shard(): lax.ppermute(values, 'shard', [(i, (i + 1) % size) for i in range(size)])  25.6 us
    pallas_call x2, Pallas kernels, pack_half(): pl.pallas_call(kernel, in_specs=[pl.BlockSpec(memory_space=pltpu.SMEM)] +...  24.1 us
  transfers between devices with their start and end apart: 71, of which 32 were waited for; matrix products, arithmetic and copies ran while one was open for 18% of the time, Pallas kernels for 25%

profile of v3, /device:TPU:0, one launch (start us, length us, event | category | flops | bytes accessed | tf_op | source)
XLA Modules:
  0.0 766.8 jit_solution(16342201477362432954)
XLA Ops:
  8.6 4.9 collective-permute-start.15
  14.8 2.5 concatenate.431
  18.6 5.2 collective-permute-start
  27.0 3.0 collective-permute-done.1
  31.2 5.4 collective-permute-done.3
  43.8 6.8 sort.14
  53.1 18.7 %embed_rows.1 = bf16[32,72,256]{2,1,0:T(8,128)(2,1)} custom-call(s32[8192]{0:T(1024)} %copy-done.44, s32[3]{0:T(128)} %pad_add_fusion.4.span_ref, s32[64,128]{1,0:T(8,128)} %bitcast.542, f32[72,12288]{1,0:T(8,128)} %table_ref.1), custom_call_target="tpu_custom_call" | custom-call | flops 536870912 | bytes 3538944 | tf_op jit(solution)/shard_map/embed_rows/pallas_call | solution.py:781
  73.0 2.7 collective-permute-start.5
  76.9 6.5 collective-permute-done.5
  89.0 13.6 %collective-permute-done.6 = bf16[8,72,256]{2,1,0:T(8,128)(2,1)} collective-permute-done((bf16[8,72,256]{2,1,0:T(8,128)(2,1)}, bf16[8,72,256]{2,1,0:T(8,128)(2,1)}, u32[]{:S(2)}, u32[]{:S(2)}) %collective-permute-start.6) | collective-permute-done | bytes 294944 | tf_op jit(solution)/shard_map/ppermute | solution.py:51
  104.5 2.7 collective-permute-start.7
  109.3 14.9 %collective-permute-done.7 = bf16[8,72,256]{2,1,0:T(8,128)(2,1)} collective-permute-done((bf16[8,72,256]{2,1,0:T(8,128)(2,1)}, bf16[8,72,256]{2,1,0:T(8,128)(2,1)}, u32[]{:S(2)}, u32[]{:S(2)}) %collective-permute-start.7) | collective-permute-done | bytes 294944 | tf_op jit(solution)/shard_map/ppermute | solution.py:51
  129.4 3.7 collective-permute-start.11
  151.8 11.1 %unpack_rows.2 = (bf16[576,960]{1,0:T(8,128)(2,1)}, bf16[576,576]{1,0:T(8,128)(2,1)}, bf16[576,3072]{1,0:T(8,128)(2,1)}, bf16[1536,576]{1,0:T(8,128)(2,1)}, bf16[16,128]{1,0:T(8,128)(2,1)}) custom-call(bf16[32,1824,128]{2,1,0:T(8,128)(2,1)} %all-gather.2.cloned.1.call-done.all_ref), custom_call_target="tpu_custom_call" | custom-call | bytes 14163968 | tf_op jit(solution)/shard_map/unpack_rows/pallas_call | solution.py:287
  163.0 12.4 %unpack_rows.3 = (bf16[576,960]{1,0:T(8,128)(2,1)}, bf16[576,576]{1,0:T(8,128)(2,1)}, bf16[576,3072]{1,0:T(8,128)(2,1)}, bf16[1536,576]{1,0:T(8,128)(2,1)}, bf16...) custom-call(bf16[32,1824,128]{2,1,0:T(8,128)(2,1)} %all-gather.2.cloned.1.call-done.all_ref), custom_call_target="tpu_custom_call" | custom-call | bytes 15499264 | tf_op jit(solution)/shard_map/unpack_rows/pallas_call | solution.py:287
  178.2 14.7 %layer_forward.2 = (f32[256,576]{1,0:T(8,128)}, bf16[256,576]{1,0:T(8,128)(2,1)}, bf16[256,768]{1,0:T(8,128)(2,1)}, bf16[256,192]{1,0:T(8,128)(2,1)}, bf16[256,5...) custom-call(s32[2]{0:T(128)} %dynamic_slice.254.len_ref, ...), custom_call_target="tpu_custom_call" | custom-call | flops 1812529152 | bytes 28320768 | tf_op jit(solution)/shard_map/layer_forward/pallas_call | solution.py:654
  192.9 2.4 maximum_select_fusion.6
  196.2 3.0 maximum_select_fusion.5
  200.6 14.8 %layer_forward.3 = (f32[256,576]{1,0:T(8,128)}, bf16[256,576]{1,0:T(8,128)(2,1)}, bf16[256,768]{1,0:T(8,128)(2,1)}, bf16[256,192]{1,0:T(8,128)(2,1)}, bf16[256,5...) custom-call(s32[2]{0:T(128)} %dynamic_slice.254.len_ref, ...), custom_call_target="tpu_custom_call" | custom-call | flops 1812529152 | bytes 28320768 | tf_op jit(solution)/shard_map/layer_forward/pallas_call | solution.py:654
  218.8 7.4 collective-permute-start.19
  227.0 7.3 collective-permute-done.19
  238.0 6.4 collective-permute-done.20
  246.3 3.7 maximum_select_fusion
  250.1 4.1 collective-permute-done.23
  255.7 2.4 copy.150
  258.2 5.2 maximum_select_fusion.1
  263.4 5.7 pad_maximum_fusion.table_ref
  269.5 2.6 copy.152
  272.1 7.9 %second_head.1 = (bf16[2,2048,576]{2,1,0:T(8,128)(2,1)}, f32[2048,576]{1,0:T(8,128)}) custom-call(bf16[2048,576]{1,0:T(8,128)(2,1)} %bitcast.499, bf16[576,576]{1,0:T(8,128)(2,1)} %get-tuple-element.146.weight_ref, f32[1,576]{1,0:T(1,128)} %get-tuple-element.307.gain_ref), custom_call_target="tpu_custom_call" | custom-call | flops 1358954496 | bytes 11796480 | tf_op jit(solution)/shard_map/second_head/pallas_call | solution.py:864
  279.9 88.1 %head_forward.1 = (bf16[4096,6144]{1,0:T(8,128)(2,1)}, f32[4096,576]{1,0:T(8,128)}, f32[256,128]{1,0:T(8,128)}, f32[256,128]{1,0:T(8,128)}) custom-call(s32[1]{0:T(128)} %bitcast.16.count_ref, s32[256]{0:T(256)} %compare_select_fusion.9.list_ref, bf16[4096,576]{1,0:T(8,128)(2,1)} %bitcast.495, bf16[576,6144]{1,0:T(8,128)(2,1)} %pad_maximum_fusion.table_ref), custom_call_target="tpu_custom_call" | custom-call | flops 57982058496 | bytes 50331648 | tf_op jit(solution)/shard_map/head_forward/pallas_call | solution.py:976
  370.7 3.1 multiply_reduce_fusion.2
  374.1 2.6 collective-permute-start.26
  381.1 18.1 %scale_rows.1 = (f32[4096,576]{1,0:T(8,128)}, bf16[576,4096]{1,0:T(8,128)(2,1)}) custom-call(s32[1]{0:T(128)} %bitcast.16.count_ref, s32[256]{0:T(256)} %compare_select_fusion.9.list_ref, bf16[4096,576]{1,0:T(8,128)(2,1)} %bitcast.496, f32[4096,576]{1,0:T(8,128)} %get-tuple-element.156.back_ref, f32[32,128]{1,0:T(8,128)} %fusion.41.scale_ref), custom_call_target="tpu_custom_call" | custom-call | bytes 28311552 | tf_op jit(solution)/shard_map/scale_rows/pallas_call | solution.py:1053
  399.3 3.0 slice.156
  407.7 2.8 slice_add_fusion
  414.9 12.1 %table_backward.4 = bf16[576,1536]{1,0:T(8,128)(2,1)} custom-call(s32[1]{0:T(128)} %bitcast.16.count_ref, bf16[576,4096]{1,0:T(8,128)(2,1)} %get-tuple-element.166.turned_ref, bf16[4096,6144]{1,0:T(8,128)(2,1)} %get-tuple-element.160.exp_ref), custom_call_target="tpu_custom_call" | custom-call | flops 7247757312 | bytes 12582912 | tf_op jit(solution)/shard_map/table_backward/pallas_call | solution.py:1104
  433.9 12.4 %table_backward.5 = bf16[576,1536]{1,0:T(8,128)(2,1)} custom-call(s32[1]{0:T(128)} %bitcast.16.count_ref, bf16[576,4096]{1,0:T(8,128)(2,1)} %get-tuple-element.166.turned_ref, bf16[4096,6144]{1,0:T(8,128)(2,1)} %get-tuple-element.160.exp_ref), custom_call_target="tpu_custom_call" | custom-call | flops 7247757312 | bytes 12582912 | tf_op jit(solution)/shard_map/table_backward/pallas_call | solution.py:1104
  452.4 12.4 %table_backward.6 = bf16[576,1536]{1,0:T(8,128)(2,1)} custom-call(s32[1]{0:T(128)} %bitcast.16.count_ref, bf16[576,4096]{1,0:T(8,128)(2,1)} %get-tuple-element.166.turned_ref, bf16[4096,6144]{1,0:T(8,128)(2,1)} %get-tuple-element.160.exp_ref), custom_call_target="tpu_custom_call" | custom-call | flops 7247757312 | bytes 12582912 | tf_op jit(solution)/shard_map/table_backward/pallas_call | solution.py:1104
  470.5 12.8 %table_backward.7 = bf16[576,1536]{1,0:T(8,128)(2,1)} custom-call(s32[1]{0:T(128)} %bitcast.16.count_ref, bf16[576,4096]{1,0:T(8,128)(2,1)} %get-tuple-element.166.turned_ref, bf16[4096,6144]{1,0:T(8,128)(2,1)} %get-tuple-element.160.exp_ref), custom_call_target="tpu_custom_call" | custom-call | flops 7247757312 | bytes 12582912 | tf_op jit(solution)/shard_map/table_backward/pallas_call | solution.py:1104
  490.6 2.3 multiply_reduce_fusion.5
  494.6 17.4 %layer_backward.2 = (f32[256,576]{1,0:T(8,128)}, bf16[256,576]{1,0:T(8,128)(2,1)}, bf16[256,3072]{1,0:T(8,128)(2,1)}, bf16[256,576]{1,0:T(8,128)(2,1)}, bf16[256,960]{1,0:T(8,128)(2,1)}, /*index=5*/f32[2,576]{1,0:T(2,128)}) custom-call(s32[2]{0:T(128)} %dynamic_slice.254.len_ref, f32[256,576]{1,0:T(8,128)} %multiply_subtract_fusion.2.grad_ref, ...), custom_call_target="tpu_custom_call" | custom-call | flops 1812529152 | bytes 28320768 | tf_op jit(solution)/shard_map/layer_backward/pallas_call | solution.py:654
  513.3 14.1 %pack_half.2 = (bf16[16,928,128]{2,1,0:T(8,128)(2,1)}, bf16[16,928,128]{2,1,0:T(8,128)(2,1)}, bf16[1344,128]{1,0:T(8,128)(2,1)}) custom-call(s32[32]{0:T(128)} %pad_add_fusion.6.info_ref, bf16[256,576]{1,0:T(8,128)(2,1)} %get-tuple-element.176.refs_0_, bf16[256,576]{1,0:T(8,128)(2,1)} %get-tuple-element.177.refs_1_, ...), custom_call_target="tpu_custom_call" | custom-call | bytes 969728 | tf_op jit(solution)/shard_map/pack_half/pallas_call | solution.py:398
  543.2 3.1 add_convert_fusion.1
  549.2 17.6 %layer_backward.3 = (f32[256,576]{1,0:T(8,128)}, bf16[256,576]{1,0:T(8,128)(2,1)}, bf16[256,3072]{1,0:T(8,128)(2,1)}, bf16[256,576]{1,0:T(8,128)(2,1)}, bf16[256,960]{1,0:T(8,128)(2,1)}, /*index=5*/f32[2,576]{1,0:T(2,128)}) custom-call(s32[2]{0:T(128)} %dynamic_slice.254.len_ref, f32[256,576]{1,0:T(8,128)} %get-tuple-element.190.grad_ref, ...), custom_call_target="tpu_custom_call" | custom-call | flops 1812529152 | bytes 28320768 | tf_op jit(solution)/shard_map/layer_backward/pallas_call | solution.py:654
  576.4 10.0 %pack_half.3 = (bf16[16,928,128]{2,1,0:T(8,128)(2,1)}, bf16[16,928,128]{2,1,0:T(8,128)(2,1)}) custom-call(s32[32]{0:T(128)} %pad_add_fusion.5.info_ref, bf16[256,576]{1,0:T(8,128)(2,1)} %get-tuple-element.152.refs_0_, bf16[256,576]{1,0:T(8,128)(2,1)} %get-tuple-element.153.refs_1_, bf16[256,576]{1,0:T(8,128)(2,1)} %get-tuple-element.154.refs_2_, ...), custom_call_target="tpu_custom_call" | custom-call | bytes 927744 | tf_op jit(solution)/shard_map/pack_half/pallas_call | solution.py:398
  608.8 3.1 add_convert_fusion
  611.9 5.6 collective-permute-done.54
  622.1 7.2 collective-permute-done.55.refs_2_
  629.3 4.4 maximum_select_fusion.2.refs_4_
  633.7 4.9 collective-permute-done.56.refs_3_
  638.6 3.7 collective-permute-done.58
  647.2 21.8 %spread_rows.1 = f32[72,12288]{1,0:T(8,128)} custom-call(s32[8192]{0:T(1024)} %copy-done.44, s32[3]{0:T(128)} %pad_add_fusion.4.span_ref, s32[32]{0:T(128)} %add.869.place_ref, s32[64,128]{1,0:T(8,128)} %bitcast.543, bf16[8,72,256]{2,1,0:T(8,128)(2,1)} %copy-done.47, bf16[8,72,256]{2,1,0:T(8,128)(2,1)} %copy-done.48, bf16[8,72,256]{2,1,0:T(8,128)(2,1)} %copy-done.49, ...), custom_call_target="tpu_custom_call" | custom-call | flops 536870912 | bytes 7077888 | tf_op jit(solution)/shard_map/spread_rows/pallas_call | solution.py:838
  673.8 12.1 %collective-permute-done.61 = bf16[2,928,128]{2,1,0:T(8,128)(2,1)S(1)} collective-permute-done((bf16[2,928,128]{2,1,0:T(8,128)(2,1)S(1)}, bf16[2,928,128]{2,1,0:T(8,128)(2,1)S(1)}, u32[]{:S(2)}, u32[]{:S(2)}) %collective-permute-start.61) | collective-permute-done | bytes 475168 | tf_op jit(solution)/shard_map/ppermute | solution.py:51
  686.3 11.4 %collective-permute-done.62 = bf16[2,928,128]{2,1,0:T(8,128)(2,1)S(1)} collective-permute-done((bf16[2,928,128]{2,1,0:T(8,128)(2,1)S(1)}, bf16[2,928,128]{2,1,0:T(8,128)(2,1)S(1)}, u32[]{:S(2)}, u32[]{:S(2)}) %collective-permute-start.62) | collective-permute-done | bytes 475168 | tf_op jit(solution)/shard_map/ppermute | solution.py:51
  698.9 10.7 %collective-permute-done.63 = bf16[2,928,128]{2,1,0:T(8,128)(2,1)} collective-permute-done((bf16[2,928,128]{2,1,0:T(8,128)(2,1)}, bf16[2,928,128]{2,1,0:T(8,128)(2,1)}, u32[]{:S(2)}, u32[]{:S(2)}) %collective-permute-start.63) | collective-permute-done | bytes 475168 | tf_op jit(solution)/shard_map/ppermute | solution.py:51
  713.5 3.6 collective-permute-done.64
  722.5 2.6 collective-permute-done.66
  726.1 2.6 collective-permute-done.67
  728.8 3.5 collective-permute-done.68
  732.2 4.4 collective-permute-done.69
  738.6 4.0 fusion.97
  742.6 6.5 fusion.98
  749.8 3.1 multiply_add_fusion.2
  752.9 4.4 multiply_add_fusion
  (515 shorter events, 194.1 us)
Async XLA Ops:
  7.2 131.6 %all-gather.2.cloned.1.call-start = ((), (), s32[]{:S(2)}) async-start(), calls=%async_computation | async-start | bytes 15409152 | tf_op jit(solution)/shard_map/all_gather | solution.py:1206
  8.6 6.2 collective-permute-start.15
  18.6 7.8 %collective-permute-start = (s32[1,1,1,1,1,4,128]{6,5,4,3,2,1,0:T(4,128)S(1)}, s32[1,1,1,1,1,4,128]{6,5,4,3,2,1,0:T(4,128)S(1)}, u32[]{:S(2)}, u32[]{:S(2)}) collective-permute-start(s32[1,1,1,1,1,4,128]{6,5,4,3,2,1,0:T(4,128)S(1)} %get-tuple-element.313), channel_id=1, source_target_pairs={{0,16},{4,20},{8,24},{12,28},{16,0},{20,4},{24,8},{28,12},{1,17},{... | collective-permute-start | bytes 6152 | tf_op jit(solution)/shard_map/ppermute | solution.py:42
  26.4 3.7 collective-permute-start.1
  31.2 5.5 collective-permute-start.3
  36.7 4.8 collective-permute-start.4
  73.0 10.5 %collective-permute-start.5 = (bf16[8,72,256]{2,1,0:T(8,128)(2,1)S(1)}, bf16[8,72,256]{2,1,0:T(8,128)(2,1)S(1)}, u32[]{:S(2)}, u32[]{:S(2)}) collective-permute-start(bf16[8,72,256]{2,1,0:T(8,128)(2,1)S(1)} %dynamic-slice_bitcast_fusion.10), channel_id=1, source_target_pairs={{0,1},{1,2},{2,3},{3,0},{4,5},{5,6},{6,7},{7,4},{8,9},{9,10},{10,1... | collective-permute-start | bytes 884744 | tf_op jit(solution)/shard_map/ppermute | solution.py:51
  85.2 17.5 %collective-permute-start.6 = (bf16[8,72,256]{2,1,0:T(8,128)(2,1)}, bf16[8,72,256]{2,1,0:T(8,128)(2,1)}, u32[]{:S(2)}, u32[]{:S(2)}) collective-permute-start(bf16[8,72,256]{2,1,0:T(8,128)(2,1)} %fusion.15), channel_id=1, source_target_pairs={{0,1},{1,2},{2,3},{3,0},{4,5},{5,6},{6,7},{7,4},{8,9},{9,10},{10,1... | collective-permute-start | bytes 884744 | tf_op jit(solution)/shard_map/ppermute | solution.py:51
  104.5 19.7 %collective-permute-start.7 = (bf16[8,72,256]{2,1,0:T(8,128)(2,1)}, bf16[8,72,256]{2,1,0:T(8,128)(2,1)}, u32[]{:S(2)}, u32[]{:S(2)}) collective-permute-start(bf16[8,72,256]{2,1,0:T(8,128)(2,1)} %fusion.16), channel_id=1, source_target_pairs={{0,1},{1,2},{2,3},{3,0},{4,5},{5,6},{6,7},{7,4},{8,9},{9,10},{10,1... | collective-permute-start | bytes 884744 | tf_op jit(solution)/shard_map/ppermute | solution.py:51
  126.1 7.1 collective-permute-start.8
  127.4 8.5 %collective-permute-start.9 = (bf16[72,256]{1,0:T(8,128)(2,1)S(1)}, bf16[72,256]{1,0:T(8,128)(2,1)S(1)}, u32[]{:S(2)}, u32[]{:S(2)}) collective-permute-start(bf16[72,256]{1,0:T(8,128)(2,1)S(1)} %get-tuple-element.291), channel_id=1, source_target_pairs={{0,8},{4,12},{8,0},{12,4},{16,24},{20,28},{24,16},{28,20},{1,9},{5... | collective-permute-start | bytes 110600 | tf_op jit(solution)/shard_map/ppermute | solution.py:42
  129.3 7.5 collective-permute-start.10
  129.4 8.0 %collective-permute-start.11 = (bf16[72,256]{1,0:T(8,128)(2,1)S(1)}, bf16[72,256]{1,0:T(8,128)(2,1)S(1)}, u32[]{:S(2)}, u32[]{:S(2)}) collective-permute-start(bf16[72,256]{1,0:T(8,128)(2,1)S(1)} %get-tuple-element.289), channel_id=1, source_target_pairs={{0,16},{4,20},{8,24},{12,28},{16,0},{20,4},{24,8},{28,12},{1,17},{... | collective-permute-start | bytes 110600 | tf_op jit(solution)/shard_map/ppermute | solution.py:42
  133.1 6.4 collective-permute-start.12
  133.1 7.7 %collective-permute-start.13 = (bf16[72,256]{1,0:T(8,128)(2,1)}, bf16[72,256]{1,0:T(8,128)(2,1)}, u32[]{:S(2)}, u32[]{:S(2)}) collective-permute-start(bf16[72,256]{1,0:T(8,128)(2,1)} %get-tuple-element.287), channel_id=1, source_target_pairs={{0,24},{4,28},{8,16},{12,20},{16,8},{20,12},{24,0},{28,4},{1,25},{... | collective-permute-start | bytes 110600 | tf_op jit(solution)/shard_map/ppermute | solution.py:42
  136.0 6.3 collective-permute-start.14
  139.1 6.5 collective-permute-start.16
  147.8 45.1 %collective-permute-start.17 = (bf16[1,1,144,3072]{3,2,1,0:T(8,128)(2,1)S(1)}, bf16[1,1,144,3072]{3,2,1,0:T(8,128)(2,1)}, u32[]{:S(2)}, u32[]{:S(2)}) collective-permute-start(bf16[1,1,144,3072]{3,2,1,0:T(8,128)(2,1)S(1)} %get-tuple-element.275), channel_id=1, source_target_pairs={{0,8},{4,12},{8,0},{12,4},{16,24},{20,28},{24,16},{28,20},{1,9},{5... | collective-permute-start | bytes 2654216 | tf_op jit(solution)/shard_map/ppermute | solution.py:42
  149.3 43.6 %collective-permute-start.18 = (bf16[1,1,144,3072]{3,2,1,0:T(8,128)(2,1)S(1)}, bf16[1,1,144,3072]{3,2,1,0:T(8,128)(2,1)}, u32[]{:S(2)}, u32[]{:S(2)}) collective-permute-start(bf16[1,1,144,3072]{3,2,1,0:T(8,128)(2,1)S(1)} %get-tuple-element.274), channel_id=1, source_target_pairs={{0,16},{4,20},{8,24},{12,28},{16,0},{20,4},{24,8},{28,12},{1,17},{... | collective-permute-start | bytes 2654216 | tf_op jit(solution)/shard_map/ppermute | solution.py:42
  195.3 49.1 %collective-permute-start.22 = (bf16[2,1,144,3072]{3,2,1,0:T(8,128)(2,1)S(1)}, bf16[2,1,144,3072]{3,2,1,0:T(8,128)(2,1)}, u32[]{:S(2)}, u32[]{:S(2)}) collective-permute-start(bf16[2,1,144,3072]{3,2,1,0:T(8,128)(2,1)S(1)} %maximum_select_fusion.6), channel_id=1, source_target_pairs={{0,8},{4,12},{8,0},{12,4},{16,24},{20,28},{24,16},{28,20},{1,9},{5... | collective-permute-start | bytes 5308424 | tf_op jit(solution)/shard_map/ppermute | solution.py:42
  199.2 45.3 %collective-permute-start.21 = (bf16[1,2,144,3072]{3,2,1,0:T(8,128)(2,1)}, bf16[1,2,144,3072]{3,2,1,0:T(8,128)(2,1)}, u32[]{:S(2)}, u32[]{:S(2)}) collective-permute-start(bf16[1,2,144,3072]{3,2,1,0:T(8,128)(2,1)} %maximum_select_fusion.5), channel_id=1, source_target_pairs={{0,16},{4,20},{8,24},{12,28},{16,0},{20,4},{24,8},{28,12},{1,17},{... | collective-permute-start | bytes 5308424 | tf_op jit(solution)/shard_map/ppermute | solution.py:42
  218.8 15.5 %collective-permute-start.19 = (bf16[256,576]{1,0:T(8,128)(2,1)S(1)}, bf16[256,576]{1,0:T(8,128)(2,1)S(1)}, u32[]{:S(2)}, u32[]{:S(2)}) collective-permute-start(bf16[256,576]{1,0:T(8,128)(2,1)S(1)} %get-tuple-element.263), channel_id=1, source_target_pairs={{0,1},{1,2},{2,3},{3,0},{4,5},{5,6},{6,7},{7,4},{8,9},{9,10},{10,1... | collective-permute-start | bytes 884744 | tf_op jit(solution)/shard_map/ppermute | solution.py:51
  234.3 10.1 %collective-permute-start.20 = (bf16[256,576]{1,0:T(8,128)(2,1)S(1)}, bf16[256,576]{1,0:T(8,128)(2,1)S(1)}, u32[]{:S(2)}, u32[]{:S(2)}) collective-permute-start(bf16[256,576]{1,0:T(8,128)(2,1)S(1)} %collective-permute-done.19), channel_id=1, source_target_pairs={{0,1},{1,2},{2,3},{3,0},{4,5},{5,6},{6,7},{7,4},{8,9},{9,10},{10,1... | collective-permute-start | bytes 884744 | tf_op jit(solution)/shard_map/ppermute | solution.py:51
  244.4 9.7 %collective-permute-start.23 = (bf16[256,576]{1,0:T(8,128)(2,1)S(1)}, bf16[256,576]{1,0:T(8,128)(2,1)S(1)}, u32[]{:S(2)}, u32[]{:S(2)}) collective-permute-start(bf16[256,576]{1,0:T(8,128)(2,1)S(1)} %collective-permute-done.20), channel_id=1, source_target_pairs={{0,1},{1,2},{2,3},{3,0},{4,5},{5,6},{6,7},{7,4},{8,9},{9,10},{10,1... | collective-permute-start | bytes 884744 | tf_op jit(solution)/shard_map/ppermute | solution.py:51
  258.2 10.9 %collective-permute-start.24 = (bf16[4,256,576]{1,2,0:T(8,128)(2,1)}, bf16[4,256,576]{1,2,0:T(8,128)(2,1)S(1)}, u32[]{:S(2)}, u32[]{:S(2)}) collective-permute-start(bf16[4,256,576]{1,2,0:T(8,128)(2,1)} %copy.150), channel_id=1, source_target_pairs={{0,4},{4,0},{8,12},{12,8},{16,20},{20,16},{24,28},{28,24},{1,5},{5... | collective-permute-start | bytes 3538952 | tf_op jit(solution)/shard_map/ppermute | solution.py:42
  370.1 4.0 collective-permute-start.25
  374.1 5.1 collective-permute-start.26
  413.7 13.3 %collective-permute-start.28 = (bf16[4,256,576]{1,2,0:T(8,128)(2,1)S(1)}, bf16[4,256,576]{1,2,0:T(8,128)(2,1)}, u32[]{:S(2)}, u32[]{:S(2)}) collective-permute-start(bf16[4,256,576]{1,2,0:T(8,128)(2,1)S(1)} %bitcast.540), channel_id=1, source_target_pairs={{0,4},{4,0},{8,12},{12,8},{16,20},{20,16},{24,28},{28,24},{1,5},{5... | collective-permute-start | bytes 3538952 | tf_op jit(solution)/shard_map/ppermute | solution.py:42
  433.0 15.3 %collective-permute-start.29 = (bf16[256,576]{1,0:T(8,128)(2,1)}, bf16[256,576]{1,0:T(8,128)(2,1)}, u32[]{:S(2)}, u32[]{:S(2)}) collective-permute-start(bf16[256,576]{1,0:T(8,128)(2,1)} %fusion.33), channel_id=1, source_target_pairs={{0,1},{1,2},{2,3},{3,0},{4,5},{5,6},{6,7},{7,4},{8,9},{9,10},{10,1... | collective-permute-start | bytes 884744 | tf_op jit(solution)/shard_map/ppermute | solution.py:51
  447.3 47.3 %collective-permute-start.32 = (bf16[2,144,1536]{2,1,0:T(8,128)(2,1)}, bf16[2,144,1536]{2,1,0:T(8,128)(2,1)}, u32[]{:S(2)}, u32[]{:S(2)}) collective-permute-start(bf16[2,144,1536]{2,1,0:T(8,128)(2,1)} %dynamic-slice_bitcast_fusion.7), channel_id=1, source_target_pairs={{0,8},{4,12},{8,0},{12,4},{16,24},{20,28},{24,16},{28,20},{1,9},{5... | collective-permute-start | bytes 2654216 | tf_op jit(solution)/shard_map/ppermute | solution.py:42
  450.2 16.9 %collective-permute-start.30 = (bf16[256,576]{1,0:T(8,128)(2,1)}, bf16[256,576]{1,0:T(8,128)(2,1)}, u32[]{:S(2)}, u32[]{:S(2)}) collective-permute-start(bf16[256,576]{1,0:T(8,128)(2,1)} %fusion.10), channel_id=1, source_target_pairs={{0,1},{1,2},{2,3},{3,0},{4,5},{5,6},{6,7},{7,4},{8,9},{9,10},{10,1... | collective-permute-start | bytes 884744 | tf_op jit(solution)/shard_map/ppermute | solution.py:51
  466.9 27.7 %collective-permute-start.33 = (bf16[2,144,1536]{2,1,0:T(8,128)(2,1)}, bf16[2,144,1536]{2,1,0:T(8,128)(2,1)}, u32[]{:S(2)}, u32[]{:S(2)}) collective-permute-start(bf16[2,144,1536]{2,1,0:T(8,128)(2,1)} %dynamic-slice_bitcast_fusion.6), channel_id=1, source_target_pairs={{0,16},{4,20},{8,24},{12,28},{16,0},{20,4},{24,8},{28,12},{1,17},{... | collective-permute-start | bytes 2654216 | tf_op jit(solution)/shard_map/ppermute | solution.py:42
  469.1 17.5 %collective-permute-start.31 = (bf16[256,576]{1,0:T(8,128)(2,1)}, bf16[256,576]{1,0:T(8,128)(2,1)}, u32[]{:S(2)}, u32[]{:S(2)}) collective-permute-start(bf16[256,576]{1,0:T(8,128)(2,1)} %fusion.11), channel_id=1, source_target_pairs={{0,1},{1,2},{2,3},{3,0},{4,5},{5,6},{6,7},{7,4},{8,9},{9,10},{10,1... | collective-permute-start | bytes 884744 | tf_op jit(solution)/shard_map/ppermute | solution.py:51
  485.7 27.6 %collective-permute-start.34 = (bf16[2,144,1536]{2,1,0:T(8,128)(2,1)}, bf16[2,144,1536]{2,1,0:T(8,128)(2,1)}, u32[]{:S(2)}, u32[]{:S(2)}) collective-permute-start(bf16[2,144,1536]{2,1,0:T(8,128)(2,1)} %dynamic-slice_bitcast_fusion.5), channel_id=1, source_target_pairs={{0,8},{4,12},{8,0},{12,4},{16,24},{20,28},{24,16},{28,20},{1,9},{5... | collective-permute-start | bytes 2654216 | tf_op jit(solution)/shard_map/ppermute | solution.py:42
  488.7 24.6 %collective-permute-start.35 = (bf16[2,144,1536]{2,1,0:T(8,128)(2,1)}, bf16[2,144,1536]{2,1,0:T(8,128)(2,1)}, u32[]{:S(2)}, u32[]{:S(2)}) collective-permute-start(bf16[2,144,1536]{2,1,0:T(8,128)(2,1)} %dynamic-slice_bitcast_fusion.4), channel_id=1, source_target_pairs={{0,16},{4,20},{8,24},{12,28},{16,0},{20,4},{24,8},{28,12},{1,17},{... | collective-permute-start | bytes 2654216 | tf_op jit(solution)/shard_map/ppermute | solution.py:42
  527.4 15.7 %collective-permute-start.36 = (bf16[16,928,128]{2,1,0:T(8,128)(2,1)}, bf16[16,928,128]{2,1,0:T(8,128)(2,1)}, u32[]{:S(2)}, u32[]{:S(2)}) collective-permute-start(bf16[16,928,128]{2,1,0:T(8,128)(2,1)} %get-tuple-element.189), channel_id=1, source_target_pairs={{0,4},{4,0},{8,12},{12,8},{16,20},{20,16},{24,28},{28,24},{1,5},{5... | collective-permute-start | bytes 11403272 | tf_op jit(solution)/shard_map/ppermute | solution.py:42
  531.5 37.7 %collective-permute-start.39 = (bf16[144,1536]{1,0:T(8,128)(2,1)}, bf16[144,1536]{1,0:T(8,128)(2,1)}, u32[]{:S(2)}, u32[]{:S(2)}) collective-permute-start(bf16[144,1536]{1,0:T(8,128)(2,1)} %fusion.31), channel_id=1, source_target_pairs={{0,8},{4,12},{8,0},{12,4},{16,24},{20,28},{24,16},{28,20},{1,9},{5... | collective-permute-start | bytes 1327112 | tf_op jit(solution)/shard_map/ppermute | solution.py:42
  535.4 34.7 %collective-permute-start.37 = (bf16[144,1536]{1,0:T(8,128)(2,1)}, bf16[144,1536]{1,0:T(8,128)(2,1)}, u32[]{:S(2)}, u32[]{:S(2)}) collective-permute-start(bf16[144,1536]{1,0:T(8,128)(2,1)} %fusion.29), channel_id=1, source_target_pairs={{0,16},{4,20},{8,24},{12,28},{16,0},{20,4},{24,8},{28,12},{1,17},{... | collective-permute-start | bytes 1327112 | tf_op jit(solution)/shard_map/ppermute | solution.py:42
  537.9 32.2 %collective-permute-start.40 = (bf16[144,1536]{1,0:T(8,128)(2,1)}, bf16[144,1536]{1,0:T(8,128)(2,1)}, u32[]{:S(2)}, u32[]{:S(2)}) collective-permute-start(bf16[144,1536]{1,0:T(8,128)(2,1)} %fusion.32), channel_id=1, source_target_pairs={{0,8},{4,12},{8,0},{12,4},{16,24},{20,28},{24,16},{28,20},{1,9},{5... | collective-permute-start | bytes 1327112 | tf_op jit(solution)/shard_map/ppermute | solution.py:42
  541.3 28.8 %collective-permute-start.38 = (bf16[144,1536]{1,0:T(8,128)(2,1)}, bf16[144,1536]{1,0:T(8,128)(2,1)}, u32[]{:S(2)}, u32[]{:S(2)}) collective-permute-start(bf16[144,1536]{1,0:T(8,128)(2,1)} %fusion.30), channel_id=1, source_target_pairs={{0,16},{4,20},{8,24},{12,28},{16,0},{20,4},{24,8},{28,12},{1,17},{... | collective-permute-start | bytes 1327112 | tf_op jit(solution)/shard_map/ppermute | solution.py:42
  548.8 45.3 %collective-permute-start.52 = (bf16[2,2,928,128]{3,2,1,0:T(8,128)(2,1)}, bf16[2,2,928,128]{3,2,1,0:T(8,128)(2,1)}, u32[]{:S(2)}, u32[]{:S(2)}) collective-permute-start(bf16[2,2,928,128]{3,2,1,0:T(8,128)(2,1)} %dynamic-slice_bitcast_fusion.2), channel_id=1, source_target_pairs={{0,16},{4,20},{8,24},{12,28},{16,0},{20,4},{24,8},{28,12},{1,17},{... | collective-permute-start | bytes 2850824 | tf_op jit(solution)/shard_map/ppermute | solution.py:42
  569.2 26.0 %collective-permute-start.51 = (bf16[2,2,928,128]{3,2,1,0:T(8,128)(2,1)}, bf16[2,2,928,128]{3,2,1,0:T(8,128)(2,1)}, u32[]{:S(2)}, u32[]{:S(2)}) collective-permute-start(bf16[2,2,928,128]{3,2,1,0:T(8,128)(2,1)} %dynamic-slice_bitcast_fusion.3), channel_id=1, source_target_pairs={{0,8},{4,12},{8,0},{12,4},{16,24},{20,28},{24,16},{28,20},{1,9},{5... | collective-permute-start | bytes 2850824 | tf_op jit(solution)/shard_map/ppermute | solution.py:42
  586.5 21.2 %collective-permute-start.41 = (bf16[16,928,128]{2,1,0:T(8,128)(2,1)}, bf16[16,928,128]{2,1,0:T(8,128)(2,1)}, u32[]{:S(2)}, u32[]{:S(2)}) collective-permute-start(bf16[16,928,128]{2,1,0:T(8,128)(2,1)} %get-tuple-element.206), channel_id=1, source_target_pairs={{0,4},{4,0},{8,12},{12,8},{16,20},{20,16},{24,28},{28,24},{1,5},{5... | collective-permute-start | bytes 11403272 | tf_op jit(solution)/shard_map/ppermute | solution.py:42
  591.8 15.9 %collective-permute-start.49 = (f32[72,6144]{1,0:T(8,128)}, f32[72,6144]{1,0:T(8,128)}, u32[]{:S(2)}, u32[]{:S(2)}) collective-permute-start(f32[72,6144]{1,0:T(8,128)} %get-tuple-element.273), channel_id=1, source_target_pairs={{0,4},{4,0},{8,12},{12,8},{16,20},{20,16},{24,28},{28,24},{1,5},{5... | collective-permute-start | bytes 5308424 | tf_op jit(solution)/shard_map/ppermute | solution.py:42
  593.7 5.1 collective-permute-start.42
  594.0 6.5 collective-permute-start.43
  595.2 5.8 collective-permute-start.44
  598.8 4.3 collective-permute-start.45
  601.0 4.9 collective-permute-start.47
  603.1 4.6 collective-permute-start.48
  604.1 13.4 %collective-permute-start.54 = (bf16[2,928,128]{2,1,0:T(8,128)(2,1)S(1)}, bf16[2,928,128]{2,1,0:T(8,128)(2,1)S(1)}, u32[]{:S(2)}, u32[]{:S(2)}) collective-permute-start(bf16[2,928,128]{2,1,0:T(8,128)(2,1)S(1)} %fusion.18), channel_id=1, source_target_pairs={{0,8},{4,12},{8,0},{12,4},{16,24},{20,28},{24,16},{28,20},{1,9},{5... | collective-permute-start | bytes 1425416 | tf_op jit(solution)/shard_map/ppermute | solution.py:42
  605.8 13.2 %collective-permute-start.53 = (bf16[2,928,128]{2,1,0:T(8,128)(2,1)S(1)}, bf16[2,928,128]{2,1,0:T(8,128)(2,1)S(1)}, u32[]{:S(2)}, u32[]{:S(2)}) collective-permute-start(bf16[2,928,128]{2,1,0:T(8,128)(2,1)S(1)} %fusion.17), channel_id=1, source_target_pairs={{0,16},{4,20},{8,24},{12,28},{16,0},{20,4},{24,8},{28,12},{1,17},{... | collective-permute-start | bytes 1425416 | tf_op jit(solution)/shard_map/ppermute | solution.py:42
  607.8 11.2 %collective-permute-start.50 = (bf16[8,72,256]{2,1,0:T(8,128)(2,1)S(1)}, bf16[8,72,256]{2,1,0:T(8,128)(2,1)S(1)}, u32[]{:S(2)}, u32[]{:S(2)}) collective-permute-start(bf16[8,72,256]{2,1,0:T(8,128)(2,1)S(1)} %constant_dynamic-update-slice_fusion.8.refs_0_), channel_id=1, source_target_pairs={{0,1},{1,2},{2,3},{3,0},{4,5},{5,6},{6,7},{7,4},{8,9},{9,10},{10,1... | collective-permute-start | bytes 884744 | tf_op jit(solution)/shard_map/ppermute | solution.py:51
  619.0 10.3 %collective-permute-start.55 = (bf16[8,72,256]{2,1,0:T(8,128)(2,1)S(1)}, bf16[8,72,256]{2,1,0:T(8,128)(2,1)S(1)}, u32[]{:S(2)}, u32[]{:S(2)}) collective-permute-start(bf16[8,72,256]{2,1,0:T(8,128)(2,1)S(1)} %collective-permute-done.50.refs_1_), channel_id=1, source_target_pairs={{0,1},{1,2},{2,3},{3,0},{4,5},{5,6},{6,7},{7,4},{8,9},{9,10},{10,1... | collective-permute-start | bytes 884744 | tf_op jit(solution)/shard_map/ppermute | solution.py:51
  619.8 22.6 %collective-permute-start.58 = (bf16[2,2,928,128]{3,2,1,0:T(8,128)(2,1)S(1)}, bf16[2,2,928,128]{3,2,1,0:T(8,128)(2,1)S(1)}, u32[]{:S(2)}, u32[]{:S(2)}) collective-permute-start(bf16[2,2,928,128]{3,2,1,0:T(8,128)(2,1)S(1)} %dynamic-slice_bitcast_fusion), channel_id=1, source_target_pairs={{0,16},{4,20},{8,24},{12,28},{16,0},{20,4},{24,8},{28,12},{1,17},{... | collective-permute-start | bytes 2850824 | tf_op jit(solution)/shard_map/ppermute | solution.py:42
  621.1 21.7 %collective-permute-start.57 = (bf16[2,2,928,128]{3,2,1,0:T(8,128)(2,1)S(1)}, bf16[2,2,928,128]{3,2,1,0:T(8,128)(2,1)S(1)}, u32[]{:S(2)}, u32[]{:S(2)}) collective-permute-start(bf16[2,2,928,128]{3,2,1,0:T(8,128)(2,1)S(1)} %dynamic-slice_bitcast_fusion.1), channel_id=1, source_target_pairs={{0,8},{4,12},{8,0},{12,4},{16,24},{20,28},{24,16},{28,20},{1,9},{5... | collective-permute-start | bytes 2850824 | tf_op jit(solution)/shard_map/ppermute | solution.py:42
  629.3 9.4 %collective-permute-start.56 = (bf16[8,72,256]{2,1,0:T(8,128)(2,1)S(1)}, bf16[8,72,256]{2,1,0:T(8,128)(2,1)S(1)}, u32[]{:S(2)}, u32[]{:S(2)}) collective-permute-start(bf16[8,72,256]{2,1,0:T(8,128)(2,1)S(1)} %collective-permute-done.55.refs_2_), channel_id=1, source_target_pairs={{0,1},{1,2},{2,3},{3,0},{4,5},{5,6},{6,7},{7,4},{8,9},{9,10},{10,1... | collective-permute-start | bytes 884744 | tf_op jit(solution)/shard_map/ppermute | solution.py:51
  643.1 25.8 %collective-permute-start.60 = (bf16[2,928,128]{2,1,0:T(8,128)(2,1)S(1)}, bf16[2,928,128]{2,1,0:T(8,128)(2,1)S(1)}, u32[]{:S(2)}, u32[]{:S(2)}) collective-permute-start(bf16[2,928,128]{2,1,0:T(8,128)(2,1)S(1)} %fusion.20), channel_id=1, source_target_pairs={{0,8},{4,12},{8,0},{12,4},{16,24},{20,28},{24,16},{28,20},{1,9},{5... | collective-permute-start | bytes 1425416 | tf_op jit(solution)/shard_map/ppermute | solution.py:42
  645.4 23.5 %collective-permute-start.59 = (bf16[2,928,128]{2,1,0:T(8,128)(2,1)}, bf16[2,928,128]{2,1,0:T(8,128)(2,1)}, u32[]{:S(2)}, u32[]{:S(2)}) collective-permute-start(bf16[2,928,128]{2,1,0:T(8,128)(2,1)} %fusion.19), channel_id=1, source_target_pairs={{0,16},{4,20},{8,24},{12,28},{16,0},{20,4},{24,8},{28,12},{1,17},{... | collective-permute-start | bytes 1425416 | tf_op jit(solution)/shard_map/ppermute | solution.py:42
  671.9 14.0 %collective-permute-start.61 = (bf16[2,928,128]{2,1,0:T(8,128)(2,1)S(1)}, bf16[2,928,128]{2,1,0:T(8,128)(2,1)S(1)}, u32[]{:S(2)}, u32[]{:S(2)}) collective-permute-start(bf16[2,928,128]{2,1,0:T(8,128)(2,1)S(1)} %fusion.28), channel_id=1, source_target_pairs={{0,1},{1,2},{2,3},{3,0},{4,5},{5,6},{6,7},{7,4},{8,9},{9,10},{10,1... | collective-permute-start | bytes 1425416 | tf_op jit(solution)/shard_map/ppermute | solution.py:51
  686.0 11.8 %collective-permute-start.62 = (bf16[2,928,128]{2,1,0:T(8,128)(2,1)S(1)}, bf16[2,928,128]{2,1,0:T(8,128)(2,1)S(1)}, u32[]{:S(2)}, u32[]{:S(2)}) collective-permute-start(bf16[2,928,128]{2,1,0:T(8,128)(2,1)S(1)} %fusion.1), channel_id=1, source_target_pairs={{0,1},{1,2},{2,3},{3,0},{4,5},{5,6},{6,7},{7,4},{8,9},{9,10},{10,1... | collective-permute-start | bytes 1425416 | tf_op jit(solution)/shard_map/ppermute | solution.py:51
  698.7 10.8 %collective-permute-start.63 = (bf16[2,928,128]{2,1,0:T(8,128)(2,1)}, bf16[2,928,128]{2,1,0:T(8,128)(2,1)}, u32[]{:S(2)}, u32[]{:S(2)}) collective-permute-start(bf16[2,928,128]{2,1,0:T(8,128)(2,1)} %fusion.2), channel_id=1, source_target_pairs={{0,1},{1,2},{2,3},{3,0},{4,5},{5,6},{6,7},{7,4},{8,9},{9,10},{10,1... | collective-permute-start | bytes 1425416 | tf_op jit(solution)/shard_map/ppermute | solution.py:51
  710.9 6.2 collective-permute-start.64
  732.2 4.4 collective-permute-start.69
  (88 other events, 853.9 us)
Sparse Core Ops, SparseCore 0:
  18.5 120.2 all-gather.1

commit v4 on v3

--- a/solution.py
+++ b/solution.py
@@ -29,7 +29,8 @@
 
 GRAIN = 2048
 GRANULE = 16
-BLOCK = 512
+BLOCK = 256
+STEP = 1024
 CHUNK = 1024
 LANES = 128
 COLUMNS = 256
@@ -115,18 +116,6 @@
     for cube, got in zip(cubes, gots):
         cube.got = got
     return main
-
-
-def ring_gather(values, hook=None):
-    size = lax.axis_size("shard")
-    me = lax.axis_index("shard")
-    parts = [values]
-    for k in range(size - 1):
-        parts.append(next_shard(parts[-1]))
-        if hook is not None and k == 1:
-            parts[-1] = hook(parts[-1])
-    stacked = jnp.stack(parts[::-1])
-    return jnp.roll(stacked, me + 1, axis=0)
 
 
 def ring_reduce(values, hooks=()):
@@ -144,6 +133,18 @@
     return total + pick(values, me, 0).astype(F32)
 
 
+def ring_gather(values, hook=None):
+    size = lax.axis_size("shard")
+    me = lax.axis_index("shard")
+    parts = [values]
+    for k in range(size - 1):
+        parts.append(next_shard(parts[-1]))
+        if hook is not None and k == 1:
+            parts[-1] = hook(parts[-1])
+    stacked = jnp.stack(parts[::-1])
+    return jnp.roll(stacked, me + 1, axis=0)
+
+
 def group_gather(rows, hook=None):
     parts = ring_gather(rows, hook)
     other = flip_dp(parts, 1)
@@ -178,12 +179,9 @@
     total = lax.axis_size("dp") * lax.axis_size("shard")
     device = lax.axis_index(("dp", "shard"))
     low = model_flat.astype(BF16)
-    before = lax.ppermute(
-        low[length - GRAIN :], ("dp", "shard"), [(i, i + 1) for i in range(total - 1)]
-    )
     starts = block_starts(length, total)
-    blocks = max(starts[i + 1] - starts[i] for i in range(total))
-    extended = jnp.concatenate([before, low, jnp.zeros((3 * GRAIN,), BF16)])
+    blocks = max(starts[i + 1] - starts[i] for i in range(total)) + 1
+    extended = jnp.pad(low, (GRAIN, 3 * GRAIN))
     shift = (length * device) % GRAIN
     whole = lax.dynamic_slice_in_dim(extended, GRAIN - shift, blocks * GRAIN, 0)
     return whole.reshape(-1, 128)
@@ -249,38 +247,59 @@
     total = lax.axis_size("dp") * lax.axis_size("shard")
     starts = block_starts(length, total)
     per = GRAIN // 128
-    moves = []
+    moves, seams = [], []
     for owner in range(total):
         low = max(starts[owner] * per, first_row)
         high = min(starts[owner + 1] * per, last_row)
         if low < high:
             moves.append((owner, low - starts[owner] * per, low - first_row, high - low))
+            if owner and low == starts[owner] * per:
+                source = (starts[owner] - starts[owner - 1]) * per
+                seams.append((owner - 1, source, low - first_row))
     outs = [jax.ShapeDtypeStruct(shape, BF16) for shape in shapes]
     outs += [jax.ShapeDtypeStruct((rows, 128), BF16) for _, rows in tails]
     wide_rows = TALL * max(shape[1] for shape in shapes) // 128 + 16
     height = last_row - first_row
 
     def kernel(all_ref, *refs):
-        outs, (flat_ref, wide_ref, tall_ref, sems) = refs[:-4], refs[-4:]
+        outs, (flat_ref, seam_ref, wide_ref, tall_ref, sems) = refs[:-5], refs[-5:]
         copies = [
             pltpu.make_async_copy(
                 all_ref.at[owner, pl.ds(source, rows)], flat_ref.at[pl.ds(at, rows)], sems.at[k]
             )
             for k, (owner, source, at, rows) in enumerate(moves)
         ]
-        for copy in copies:
+        edges = [
+            pltpu.make_async_copy(
+                all_ref.at[owner, pl.ds(source, per)],
+                seam_ref.at[pl.ds(k * per, per)],
+                sems.at[len(moves) + k],
+            )
+            for k, (owner, source, _) in enumerate(seams)
+        ]
+        for copy in edges + copies:
             copy.start()
+        for copy in edges:
+            copy.wait()
         arrived = 0
         at = lead
+
+        def arrive(k):
+            copies[k].wait()
+            for j, (owner, _, row) in enumerate(seams):
+                if owner == moves[k][0] - 1:
+                    rows = slice(row, row + per)
+                    flat_ref[rows, :] = flat_ref[rows, :] + seam_ref[j * per : (j + 1) * per, :]
+
         for k, (tall, wide) in enumerate(shapes):
             end = at + tall * wide // 128
             while arrived < len(moves) and moves[arrived][2] < end:
-                copies[arrived].wait()
+                arrive(arrived)
                 arrived += 1
             unpack_matrix(flat_ref, at, outs[k], wide_ref, tall_ref)
             at = end + gaps.get(k, 0)
-        for copy in copies[arrived:]:
-            copy.wait()
+        for k in range(arrived, len(moves)):
+            arrive(k)
         for k, (start, rows) in enumerate(tails):
             outs[len(shapes) + k][...] = flat_ref[pl.ds(start, rows), :]
 
@@ -291,9 +310,10 @@
         out_shape=outs,
         scratch_shapes=[
             pltpu.VMEM((height, 128), BF16),
+            pltpu.VMEM((len(seams) * per, 128), BF16),
             pltpu.VMEM((wide_rows, 128), F32),
             pltpu.VMEM((8, TALL, 128), F32),
-            pltpu.SemaphoreType.DMA((len(moves),)),
+            pltpu.SemaphoreType.DMA((len(moves) + len(seams),)),
         ],
         compiler_params=pltpu.CompilerParams(vmem_limit_bytes=VMEM_LIMIT),
         cost_estimate=pl.CostEstimate(flops=0, bytes_accessed=512 * height, transcendentals=0),
@@ -1013,22 +1033,22 @@
 def scale_kernel(
     count_ref, list_ref, rows_ref, back_ref, scale_ref, grad_ref, turned_ref, scaled, packed
 ):
-    per = BLOCK // GRANULE
+    per = STEP // GRANULE
     step, blocks = pl.program_id(0), pl.num_programs(0) // 2
 
     @pl.when(step < blocks)
     def _():
-        for k in range(BLOCK // LANES):
+        for k in range(STEP // LANES):
             at = slice(k * LANES, (k + 1) * LANES)
-            line = scale_ref[pl.ds(step * (BLOCK // LANES) + k, 1), :]
+            line = scale_ref[pl.ds(step * (STEP // LANES) + k, 1), :]
             column = jnp.transpose(jnp.broadcast_to(line, (LANES, LANES)))[:, :1]
             grad_ref[at, :] = back_ref[at, :] * column
-            row = pl.multiple_of(step * BLOCK + k * LANES, LANES)
+            row = pl.multiple_of(step * STEP + k * LANES, LANES)
             scaled[pl.ds(row, LANES), :] = (rows_ref[at, :].astype(F32) * column).astype(BF16)
 
     block = step - blocks
 
-    @pl.when((block >= 0) & (block < block_count(count_ref)))
+    @pl.when((block >= 0) & (block * per < count_ref[0]))
     def _():
         for g in range(per):
             at = block * per + g
@@ -1042,13 +1062,14 @@
 
 def scale_rows(count, order, rows, back, scale):
     height = rows.shape[0]
-    blocks = height // BLOCK
+    blocks = height // STEP
 
     def first(i, count_ref, list_ref):
         return (jnp.minimum(i, blocks - 1), 0)
 
     def second(i, count_ref, list_ref):
-        return (0, block_at(jnp.maximum(i - blocks, 0), count_ref, list_ref)[0])
+        used = (count_ref[0] + STEP // GRANULE - 1) // (STEP // GRANULE)
+        return (0, jnp.minimum(jnp.maximum(i - blocks, 0), jnp.maximum(used - 1, 0)))
 
     return pl.pallas_call(
         scale_kernel,
@@ -1056,17 +1077,17 @@
             num_scalar_prefetch=2,
             grid=(2 * blocks,),
             in_specs=[
-                pl.BlockSpec((BLOCK, MODEL_WIDTH), first),
-                pl.BlockSpec((BLOCK, MODEL_WIDTH), first),
+                pl.BlockSpec((STEP, MODEL_WIDTH), first),
+                pl.BlockSpec((STEP, MODEL_WIDTH), first),
                 pl.BlockSpec(scale.shape, lambda i, count_ref, list_ref: (0, 0)),
             ],
             out_specs=[
-                pl.BlockSpec((BLOCK, MODEL_WIDTH), first),
-                pl.BlockSpec((MODEL_WIDTH, BLOCK), second),
+                pl.BlockSpec((STEP, MODEL_WIDTH), first),
+                pl.BlockSpec((MODEL_WIDTH, STEP), second),
             ],
             scratch_shapes=[
                 pltpu.VMEM((height, MODEL_WIDTH), BF16),
-                pltpu.VMEM((BLOCK, MODEL_WIDTH), F32),
+                pltpu.VMEM((STEP, MODEL_WIDTH), F32),
             ],
         ),
         out_shape=[
@@ -1079,14 +1100,28 @@
     )(count, order, rows, back, scale)
 
 
-def table_kernel(count_ref, turned_ref, exp_ref, out_ref):
+def table_kernel(count_ref, turned_ref, exp_ref, out_ref, total):
     used = block_count(count_ref)
-
-    @pl.when(used == 0)
+    most = exp_ref.shape[0] // BLOCK
+    straight = most * 5 // 8
+
+    @pl.when(used < straight)
     def _():
-        out_ref[...] = jnp.zeros(out_ref.shape, BF16)
-
-    for blocks in range(1, exp_ref.shape[0] // BLOCK + 1):
+        total[...] = jnp.zeros(total.shape, F32)
+
+        def step(k, _):
+            at = pl.multiple_of(k * BLOCK, BLOCK)
+            total[...] += jnp.dot(
+                turned_ref[:, pl.ds(at, BLOCK)],
+                exp_ref[pl.ds(at, BLOCK), :],
+                preferred_element_type=F32,
+            )
+            return 0
+
+        lax.fori_loop(0, used, step, 0)
+        out_ref[...] = total[...].astype(BF16)
+
+    for blocks in range(straight, most + 1):
 
         @pl.when(used == blocks)
         def _():
@@ -1113,6 +1148,7 @@
                 pl.BlockSpec((height, chunk), lambda i, count_ref: (0, part * steps + i)),
             ],
             out_specs=pl.BlockSpec((MODEL_WIDTH, chunk), lambda i, count_ref: (0, i)),
+            scratch_shapes=[pltpu.VMEM((MODEL_WIDTH, chunk), F32)],
         ),
         out_shape=jax.ShapeDtypeStruct((MODEL_WIDTH, columns), BF16),
         compiler_params=pltpu.CompilerParams(vmem_limit_bytes=VMEM_LIMIT),
@@ -1226,7 +1262,9 @@
     embedded = jnp.stack(parts)[jnp.arange(dp_size) ^ dp_idx]
     embedded = embedded.reshape(MODEL_WIDTH, own_rows).T.astype(F32)
 
-    held_table, everything = lax.optimization_barrier((embed_table, everything))
+    held_table, everything, embedded = lax.optimization_barrier(
+        (embed_table, everything, embedded)
+    )
     table_gather = TableGather(held_table)
     middle_rows = PL // 128
     low_rows = middle_rows // 16 * 16
@@ -1255,9 +1293,9 @@
     head_gains = gain_pair(gains_head, second_row - base_two).astype(F32)
 
     rope = rope_rows(own_rows)
-    hidden, kept_zero = layer_forward(embedded, layer_zero, own_lens, rope)
-    hidden = table_gather.tied(hidden)
+    first_hidden = table_gather.tied(embedded)
     table_gather.step()
+    hidden, kept_zero = layer_forward(first_hidden, layer_zero, own_lens, rope)
     hidden, kept_one = layer_forward(hidden, layer_one, own_lens, rope)
     scale_final = rms_scale(hidden)
     head_one = (hidden * scale_final * head_gains[0]).astype(BF16)

time: 776 us -> 774 us (level)
  starting transfers between devices: 79.6 us -> 62.6 us
  waiting for transfers between devices: 145 us -> 159 us
    ppermute x15, waiting for transfers between devices: 99.2 us -> 111 us  [next_shard(): lax.ppermute(values, 'shard', [(i, (i + 1) % size) for i in range(size)])]
    ppermute x15, starting transfers between devices: 25.6 us -> 16.9 us  [next_shard(): lax.ppermute(values, 'shard', [(i, (i + 1) % size) for i in range(size)])]
    unnamed x185 -> x179, local copies, waits for them, and re-layouts: 16.3 us -> 17 us
  transfers between devices with their start and end apart: 71 -> 70, of which waited for: 32 -> 33; matrix products, arithmetic and copies ran while one was open for 18% -> 18% of each run, Pallas kernels for 25% -> 25%
where the time goes in v4:
time: 774 us; the launch traced here: 765 us
  Pallas kernels  321 us (41%)
  waiting for transfers between devices  159 us (21%)
  other arithmetic  127 us (16%)
  local copies, waits for them, and re-layouts  73.5 us (9%)
  starting transfers between devices  62.6 us (8%)
  between operations  19.4 us (3%)
    ppermute x15, waiting for transfers between devices, next_shard(): lax.ppermute(values, 'shard', [(i, (i + 1) % size) for i in range(size)])  111 us
    pallas_call x1, Pallas kernels, head_forward(): pl.pallas_call(head_kernel, grid_spec=pltpu.PrefetchScalarGridSpec(num_sc...  93.3 us
    pallas_call x4, Pallas kernels, layer_call(): pl.pallas_call(kernel, in_specs=[pl.BlockSpec(memory_space=pltpu.SMEM)] +...  64.5 us
    pallas_call x4, Pallas kernels, table_backward(): pl.pallas_call(table_kernel, grid_spec=pltpu.PrefetchScalarGridSpec(num_s...  48.9 us
    ppermute x48, starting transfers between devices, flip_dp(): lax.ppermute(values, 'dp', [(i, i ^ bit) for i in range(lax.axis_size('dp...  40.4 us
    ppermute x48, waiting for transfers between devices, flip_dp(): lax.ppermute(values, 'dp', [(i, i ^ bit) for i in range(lax.axis_size('dp...  29.5 us
    pallas_call x2, Pallas kernels, pack_half(): pl.pallas_call(kernel, in_specs=[pl.BlockSpec(memory_space=pltpu.SMEM)] +...  24.2 us
    pallas_call x2, Pallas kernels, unpack_rows(): pl.pallas_call(kernel, in_specs=[pl.BlockSpec(memory_space=pl.ANY)], out_...  24.1 us
  transfers between devices with their start and end apart: 70, of which 33 were waited for; matrix products, arithmetic and copies ran while one was open for 18% of the time, Pallas kernels for 25%

profile of v4, /device:TPU:0, one launch (start us, length us, event | category | flops | bytes accessed | tf_op | source)
XLA Modules:
  0.0 765.5 jit_solution(12113493273931382186)
XLA Ops:
  9.9 3.0 collective-permute-start
  19.2 3.1 collective-permute-start.3
  26.0 3.5 collective-permute-done.4
  31.8 6.8 sort.14
  41.1 19.2 %embed_rows.1 = bf16[32,72,256]{2,1,0:T(8,128)(2,1)} custom-call(s32[8192]{0:T(1024)} %copy-done.43, s32[3]{0:T(128)} %pad_add_fusion.4.span_ref, s32[64,128]{1,0:T(8,128)} %bitcast.541, f32[72,12288]{1,0:T(8,128)} %table_ref.1), custom_call_target="tpu_custom_call" | custom-call | flops 536870912 | bytes 3538944 | tf_op jit(solution)/shard_map/embed_rows/pallas_call | solution.py:801
  63.1 13.5 %collective-permute-done.5 = bf16[8,72,256]{2,1,0:T(8,128)(2,1)S(1)} collective-permute-done((bf16[8,72,256]{2,1,0:T(8,128)(2,1)S(1)}, bf16[8,72,256]{2,1,0:T(8,128)(2,1)S(1)}, u32[]{:S(2)}, u32[]{:S(2)}) %collective-permute-start.5) | collective-permute-done | bytes 294944 | tf_op jit(solution)/shard_map/ppermute | solution.py:52
  78.0 17.1 %collective-permute-done.6 = bf16[8,72,256]{2,1,0:T(8,128)(2,1)S(1)} collective-permute-done((bf16[8,72,256]{2,1,0:T(8,128)(2,1)S(1)}, bf16[8,72,256]{2,1,0:T(8,128)(2,1)S(1)}, u32[]{:S(2)}, u32[]{:S(2)}) %collective-permute-start.6) | collective-permute-done | bytes 294944 | tf_op jit(solution)/shard_map/ppermute | solution.py:52
  97.4 16.8 %collective-permute-done.7 = bf16[8,72,256]{2,1,0:T(8,128)(2,1)S(1)} collective-permute-done((bf16[8,72,256]{2,1,0:T(8,128)(2,1)S(1)}, bf16[8,72,256]{2,1,0:T(8,128)(2,1)S(1)}, u32[]{:S(2)}, u32[]{:S(2)}) %collective-permute-start.7) | collective-permute-done | bytes 294944 | tf_op jit(solution)/shard_map/ppermute | solution.py:52
  119.3 2.5 copy.147.sin_ref
  146.5 11.4 %unpack_rows.2 = (bf16[576,960]{1,0:T(8,128)(2,1)}, bf16[576,576]{1,0:T(8,128)(2,1)}, bf16[576,3072]{1,0:T(8,128)(2,1)}, bf16[1536,576]{1,0:T(8,128)(2,1)}, bf16[16,128]{1,0:T(8,128)(2,1)}) custom-call(bf16[32,1840,128]{2,1,0:T(8,128)(2,1)} %all-gather.2.cloned.1.call-done.all_ref), custom_call_target="tpu_custom_call" | custom-call | bytes 14163968 | tf_op jit(solution)/shard_map/unpack_rows/pallas_call | solution.py:306
  157.9 12.7 %unpack_rows.3 = (bf16[576,960]{1,0:T(8,128)(2,1)}, bf16[576,576]{1,0:T(8,128)(2,1)}, bf16[576,3072]{1,0:T(8,128)(2,1)}, bf16[1536,576]{1,0:T(8,128)(2,1)}, bf16...) custom-call(bf16[32,1840,128]{2,1,0:T(8,128)(2,1)} %all-gather.2.cloned.1.call-done.all_ref), custom_call_target="tpu_custom_call" | custom-call | bytes 15499264 | tf_op jit(solution)/shard_map/unpack_rows/pallas_call | solution.py:306
  176.8 3.6 maximum_select_fusion.5
  184.2 14.9 %layer_forward.2 = (f32[256,576]{1,0:T(8,128)}, bf16[256,576]{1,0:T(8,128)(2,1)}, bf16[256,768]{1,0:T(8,128)(2,1)}, bf16[256,192]{1,0:T(8,128)(2,1)}, bf16[256,5...) custom-call(s32[2]{0:T(128)} %dynamic_slice.254.len_ref, ...), custom_call_target="tpu_custom_call" | custom-call | flops 1812529152 | bytes 28320768 | tf_op jit(solution)/shard_map/layer_forward/pallas_call | solution.py:674
  199.1 14.7 %layer_forward.3 = (f32[256,576]{1,0:T(8,128)}, bf16[256,576]{1,0:T(8,128)(2,1)}, bf16[256,768]{1,0:T(8,128)(2,1)}, bf16[256,192]{1,0:T(8,128)(2,1)}, bf16[256,5...) custom-call(s32[2]{0:T(128)} %dynamic_slice.254.len_ref, ...), custom_call_target="tpu_custom_call" | custom-call | flops 1812529152 | bytes 28320768 | tf_op jit(solution)/shard_map/layer_forward/pallas_call | solution.py:674
  217.8 4.2 collective-permute-start.18
  222.8 10.5 %collective-permute-done.18 = bf16[256,576]{1,0:T(8,128)(2,1)S(1)} collective-permute-done((bf16[256,576]{1,0:T(8,128)(2,1)S(1)}, bf16[256,576]{1,0:T(8,128)(2,1)S(1)}, u32[]{:S(2)}, u32[]{:S(2)}) %collective-permute-start.18) | collective-permute-done | bytes 294944 | tf_op jit(solution)/shard_map/ppermute | solution.py:52
  236.2 7.4 collective-permute-done.19
  243.7 3.8 maximum_select_fusion
  247.4 5.5 collective-permute-done.22
  254.5 2.4 copy.150
  257.0 5.2 maximum_select_fusion.1
  262.1 5.7 pad_maximum_fusion.table_ref
  268.2 2.6 copy.152
  270.8 9.6 %second_head.1 = (bf16[2,2048,576]{2,1,0:T(8,128)(2,1)}, f32[2048,576]{1,0:T(8,128)}) custom-call(bf16[2048,576]{1,0:T(8,128)(2,1)} %bitcast.498, bf16[576,576]{1,0:T(8,128)(2,1)} %get-tuple-element.148.weight_ref, f32[1,576]{1,0:T(1,128)} %get-tuple-element.309.gain_ref), custom_call_target="tpu_custom_call" | custom-call | flops 1358954496 | bytes 11796480 | tf_op jit(solution)/shard_map/second_head/pallas_call | solution.py:884
  280.4 93.3 %head_forward.1 = (bf16[4096,6144]{1,0:T(8,128)(2,1)}, f32[4096,576]{1,0:T(8,128)}, f32[256,128]{1,0:T(8,128)}, f32[256,128]{1,0:T(8,128)}) custom-call(s32[1]{0:T(128)} %bitcast.16.count_ref, s32[256]{0:T(256)} %compare_select_fusion.9.list_ref, bf16[4096,576]{1,0:T(8,128)(2,1)} %bitcast.494, bf16[576,6144]{1,0:T(8,128)(2,1)} %pad_maximum_fusion.table_ref), custom_call_target="tpu_custom_call" | custom-call | flops 57982058496 | bytes 50331648 | tf_op jit(solution)/shard_map/head_forward/pallas_call | solution.py:996
  375.8 3.1 multiply_reduce_fusion.2
  380.1 4.7 collective-permute-done.25
  386.8 14.9 %scale_rows.1 = (f32[4096,576]{1,0:T(8,128)}, bf16[576,4096]{1,0:T(8,128)(2,1)}) custom-call(s32[1]{0:T(128)} %bitcast.16.count_ref, s32[256]{0:T(256)} %compare_select_fusion.9.list_ref, bf16[4096,576]{1,0:T(8,128)(2,1)} %bitcast.495, f32[4096,576]{1,0:T(8,128)} %get-tuple-element.158.back_ref, f32[32,128]{1,0:T(8,128)} %fusion.42.scale_ref), custom_call_target="tpu_custom_call" | custom-call | bytes 28311552 | tf_op jit(solution)/shard_map/scale_rows/pallas_call | solution.py:1074
  401.7 3.0 slice.152
  410.1 2.8 slice_add_fusion
  413.0 2.3 copy-done.8
  417.2 12.2 %table_backward.4 = bf16[576,1536]{1,0:T(8,128)(2,1)} custom-call(s32[1]{0:T(128)} %bitcast.16.count_ref, bf16[576,4096]{1,0:T(8,128)(2,1)} %get-tuple-element.168.turned_ref, bf16[4096,6144]{1,0:T(8,128)(2,1)} %get-tuple-element.162.exp_ref), custom_call_target="tpu_custom_call" | custom-call | flops 7247757312 | bytes 12582912 | tf_op jit(solution)/shard_map/table_backward/pallas_call | solution.py:1139
  436.4 12.1 %table_backward.5 = bf16[576,1536]{1,0:T(8,128)(2,1)} custom-call(s32[1]{0:T(128)} %bitcast.16.count_ref, bf16[576,4096]{1,0:T(8,128)(2,1)} %get-tuple-element.168.turned_ref, bf16[4096,6144]{1,0:T(8,128)(2,1)} %get-tuple-element.162.exp_ref), custom_call_target="tpu_custom_call" | custom-call | flops 7247757312 | bytes 12582912 | tf_op jit(solution)/shard_map/table_backward/pallas_call | solution.py:1139
  452.1 12.1 %table_backward.6 = bf16[576,1536]{1,0:T(8,128)(2,1)} custom-call(s32[1]{0:T(128)} %bitcast.16.count_ref, bf16[576,4096]{1,0:T(8,128)(2,1)} %get-tuple-element.168.turned_ref, bf16[4096,6144]{1,0:T(8,128)(2,1)} %get-tuple-element.162.exp_ref), custom_call_target="tpu_custom_call" | custom-call | flops 7247757312 | bytes 12582912 | tf_op jit(solution)/shard_map/table_backward/pallas_call | solution.py:1139
  470.4 12.5 %table_backward.7 = bf16[576,1536]{1,0:T(8,128)(2,1)} custom-call(s32[1]{0:T(128)} %bitcast.16.count_ref, bf16[576,4096]{1,0:T(8,128)(2,1)} %get-tuple-element.168.turned_ref, bf16[4096,6144]{1,0:T(8,128)(2,1)} %get-tuple-element.162.exp_ref), custom_call_target="tpu_custom_call" | custom-call | flops 7247757312 | bytes 12582912 | tf_op jit(solution)/shard_map/table_backward/pallas_call | solution.py:1139
  483.0 2.3 dynamic-slice_bitcast_fusion.5
  489.6 2.3 multiply_reduce_fusion.5
  493.7 17.4 %layer_backward.2 = (f32[256,576]{1,0:T(8,128)}, bf16[256,576]{1,0:T(8,128)(2,1)}, bf16[256,3072]{1,0:T(8,128)(2,1)}, bf16[256,576]{1,0:T(8,128)(2,1)}, bf16[256,960]{1,0:T(8,128)(2,1)}, /*index=5*/f32[2,576]{1,0:T(2,128)}) custom-call(s32[2]{0:T(128)} %dynamic_slice.254.len_ref, f32[256,576]{1,0:T(8,128)} %multiply_subtract_fusion.2.grad_ref, ...), custom_call_target="tpu_custom_call" | custom-call | flops 1812529152 | bytes 28320768 | tf_op jit(solution)/shard_map/layer_backward/pallas_call | solution.py:674
  512.4 14.1 %pack_half.2 = (bf16[16,928,128]{2,1,0:T(8,128)(2,1)}, bf16[16,928,128]{2,1,0:T(8,128)(2,1)}, bf16[1344,128]{1,0:T(8,128)(2,1)}) custom-call(s32[32]{0:T(128)} %pad_add_fusion.6.info_ref, bf16[256,576]{1,0:T(8,128)(2,1)} %get-tuple-element.178.refs_0_, bf16[256,576]{1,0:T(8,128)(2,1)} %get-tuple-element.179.refs_1_, ...), custom_call_target="tpu_custom_call" | custom-call | bytes 969728 | tf_op jit(solution)/shard_map/pack_half/pallas_call | solution.py:418
  542.0 3.1 add_convert_fusion.1
  548.5 17.6 %layer_backward.3 = (f32[256,576]{1,0:T(8,128)}, bf16[256,576]{1,0:T(8,128)(2,1)}, bf16[256,3072]{1,0:T(8,128)(2,1)}, bf16[256,576]{1,0:T(8,128)(2,1)}, bf16[256,960]{1,0:T(8,128)(2,1)}, /*index=5*/f32[2,576]{1,0:T(2,128)}) custom-call(s32[2]{0:T(128)} %dynamic_slice.254.len_ref, f32[256,576]{1,0:T(8,128)} %get-tuple-element.192.grad_ref, ...), custom_call_target="tpu_custom_call" | custom-call | flops 1812529152 | bytes 28320768 | tf_op jit(solution)/shard_map/layer_backward/pallas_call | solution.py:674
  569.4 2.3 bitcast_add_fusion.8
  575.7 10.0 %pack_half.3 = (bf16[16,928,128]{2,1,0:T(8,128)(2,1)}, bf16[16,928,128]{2,1,0:T(8,128)(2,1)}) custom-call(s32[32]{0:T(128)} %pad_add_fusion.5.info_ref, bf16[256,576]{1,0:T(8,128)(2,1)} %get-tuple-element.154.refs_0_, bf16[256,576]{1,0:T(8,128)(2,1)} %get-tuple-element.155.refs_1_, bf16[256,576]{1,0:T(8,128)(2,1)} %get-tuple-element.156.refs_2_, ...), custom_call_target="tpu_custom_call" | custom-call | bytes 927744 | tf_op jit(solution)/shard_map/pack_half/pallas_call | solution.py:418
  606.8 3.1 collective-permute-start.49
  609.9 3.1 add_convert_fusion
  613.0 3.7 collective-permute-done.53
  617.8 3.0 collective-permute-start.54
  623.1 4.5 collective-permute-done.54.refs_2_
  628.9 4.4 maximum_select_fusion.2.refs_4_
  633.3 3.3 collective-permute-done.55.refs_3_
  636.6 6.5 collective-permute-done.57
  647.9 22.3 %spread_rows.1 = f32[72,12288]{1,0:T(8,128)} custom-call(s32[8192]{0:T(1024)} %copy-done.43, s32[3]{0:T(128)} %pad_add_fusion.4.span_ref, s32[32]{0:T(128)} %add.871.place_ref, s32[64,128]{1,0:T(8,128)} %bitcast.542, bf16[8,72,256]{2,1,0:T(8,128)(2,1)} %copy-done.46, bf16[8,72,256]{2,1,0:T(8,128)(2,1)} %copy-done.47, bf16[8,72,256]{2,1,0:T(8,128)(2,1)} %copy-done.48, ...), custom_call_target="tpu_custom_call" | custom-call | flops 536870912 | bytes 7077888 | tf_op jit(solution)/shard_map/spread_rows/pallas_call | solution.py:858
  674.4 10.7 %collective-permute-done.60 = bf16[2,928,128]{2,1,0:T(8,128)(2,1)S(1)} collective-permute-done((bf16[2,928,128]{2,1,0:T(8,128)(2,1)S(1)}, bf16[2,928,128]{2,1,0:T(8,128)(2,1)S(1)}, u32[]{:S(2)}, u32[]{:S(2)}) %collective-permute-start.60) | collective-permute-done | bytes 475168 | tf_op jit(solution)/shard_map/ppermute | solution.py:52
  685.8 10.7 %collective-permute-done.61 = bf16[2,928,128]{2,1,0:T(8,128)(2,1)S(1)} collective-permute-done((bf16[2,928,128]{2,1,0:T(8,128)(2,1)S(1)}, bf16[2,928,128]{2,1,0:T(8,128)(2,1)S(1)}, u32[]{:S(2)}, u32[]{:S(2)}) %collective-permute-start.61) | collective-permute-done | bytes 475168 | tf_op jit(solution)/shard_map/ppermute | solution.py:52
  697.6 10.6 %collective-permute-done.62 = bf16[2,928,128]{2,1,0:T(8,128)(2,1)} collective-permute-done((bf16[2,928,128]{2,1,0:T(8,128)(2,1)}, bf16[2,928,128]{2,1,0:T(8,128)(2,1)}, u32[]{:S(2)}, u32[]{:S(2)}) %collective-permute-start.62) | collective-permute-done | bytes 475168 | tf_op jit(solution)/shard_map/ppermute | solution.py:52
  711.5 4.2 collective-permute-done.63
  720.7 3.1 collective-permute-done.65
  724.2 3.2 collective-permute-done.66
  727.4 3.5 collective-permute-done.67
  730.9 4.4 collective-permute-done.68
  737.3 4.0 fusion.98
  741.3 6.5 fusion.99
  748.4 3.1 multiply_add_fusion.2
  751.5 4.4 multiply_add_fusion
  (503 shorter events, 182.4 us)
Async XLA Ops:
  7.2 132.3 %all-gather.2.cloned.1.call-start = ((), (), s32[]{:S(2)}) async-start(), calls=%async_computation | async-start | bytes 15544320 | tf_op jit(solution)/shard_map/all_gather | solution.py:1242
  9.9 4.5 collective-permute-start
  14.4 3.6 collective-permute-start.1
  19.2 4.8 collective-permute-start.3
  24.0 5.5 collective-permute-start.4
  61.3 15.3 %collective-permute-start.5 = (bf16[8,72,256]{2,1,0:T(8,128)(2,1)S(1)}, bf16[8,72,256]{2,1,0:T(8,128)(2,1)S(1)}, u32[]{:S(2)}, u32[]{:S(2)}) collective-permute-start(bf16[8,72,256]{2,1,0:T(8,128)(2,1)S(1)} %dynamic-slice_bitcast_fusion.9), channel_id=1, source_target_pairs={{0,1},{1,2},{2,3},{3,0},{4,5},{5,6},{6,7},{7,4},{8,9},{9,10},{10,1... | collective-permute-start | bytes 884744 | tf_op jit(solution)/shard_map/ppermute | solution.py:52
  77.8 17.4 %collective-permute-start.6 = (bf16[8,72,256]{2,1,0:T(8,128)(2,1)S(1)}, bf16[8,72,256]{2,1,0:T(8,128)(2,1)S(1)}, u32[]{:S(2)}, u32[]{:S(2)}) collective-permute-start(bf16[8,72,256]{2,1,0:T(8,128)(2,1)S(1)} %fusion.15), channel_id=1, source_target_pairs={{0,1},{1,2},{2,3},{3,0},{4,5},{5,6},{6,7},{7,4},{8,9},{9,10},{10,1... | collective-permute-start | bytes 884744 | tf_op jit(solution)/shard_map/ppermute | solution.py:52
  96.2 18.0 %collective-permute-start.7 = (bf16[8,72,256]{2,1,0:T(8,128)(2,1)S(1)}, bf16[8,72,256]{2,1,0:T(8,128)(2,1)S(1)}, u32[]{:S(2)}, u32[]{:S(2)}) collective-permute-start(bf16[8,72,256]{2,1,0:T(8,128)(2,1)S(1)} %fusion.16), channel_id=1, source_target_pairs={{0,1},{1,2},{2,3},{3,0},{4,5},{5,6},{6,7},{7,4},{8,9},{9,10},{10,1... | collective-permute-start | bytes 884744 | tf_op jit(solution)/shard_map/ppermute | solution.py:52
  116.0 9.4 %collective-permute-start.8 = (bf16[72,256]{1,0:T(8,128)(2,1)}, bf16[72,256]{1,0:T(8,128)(2,1)}, u32[]{:S(2)}, u32[]{:S(2)}) collective-permute-start(bf16[72,256]{1,0:T(8,128)(2,1)} %get-tuple-element.294), channel_id=1, source_target_pairs={{0,4},{4,0},{8,12},{12,8},{16,20},{20,16},{24,28},{28,24},{1,5},{5... | collective-permute-start | bytes 110600 | tf_op jit(solution)/shard_map/ppermute | solution.py:43
  121.9 6.1 collective-permute-start.9
  122.9 7.2 collective-permute-start.10
  123.8 7.0 collective-permute-start.11
  125.4 6.0 collective-permute-start.12
  125.4 6.6 collective-permute-start.13
  128.0 4.7 collective-permute-start.14
  144.3 32.4 %collective-permute-start.16 = (bf16[1,1,144,3072]{3,2,1,0:T(8,128)(2,1)}, bf16[1,1,144,3072]{3,2,1,0:T(8,128)(2,1)}, u32[]{:S(2)}, u32[]{:S(2)}) collective-permute-start(bf16[1,1,144,3072]{3,2,1,0:T(8,128)(2,1)} %get-tuple-element.277), channel_id=1, source_target_pairs={{0,8},{4,12},{8,0},{12,4},{16,24},{20,28},{24,16},{28,20},{1,9},{5... | collective-permute-start | bytes 2654216 | tf_op jit(solution)/shard_map/ppermute | solution.py:43
  146.0 30.8 %collective-permute-start.17 = (bf16[1,1,144,3072]{3,2,1,0:T(8,128)(2,1)S(1)}, bf16[1,1,144,3072]{3,2,1,0:T(8,128)(2,1)}, u32[]{:S(2)}, u32[]{:S(2)}) collective-permute-start(bf16[1,1,144,3072]{3,2,1,0:T(8,128)(2,1)S(1)} %get-tuple-element.276), channel_id=1, source_target_pairs={{0,16},{4,20},{8,24},{12,28},{16,0},{20,4},{24,8},{28,12},{1,17},{... | collective-permute-start | bytes 2654216 | tf_op jit(solution)/shard_map/ppermute | solution.py:43
  180.4 63.2 %collective-permute-start.20 = (bf16[1,2,144,3072]{3,2,1,0:T(8,128)(2,1)}, bf16[1,2,144,3072]{3,2,1,0:T(8,128)(2,1)}, u32[]{:S(2)}, u32[]{:S(2)}) collective-permute-start(bf16[1,2,144,3072]{3,2,1,0:T(8,128)(2,1)} %maximum_select_fusion.5), channel_id=1, source_target_pairs={{0,16},{4,20},{8,24},{12,28},{16,0},{20,4},{24,8},{28,12},{1,17},{... | collective-permute-start | bytes 5308424 | tf_op jit(solution)/shard_map/ppermute | solution.py:43
  183.8 59.8 %collective-permute-start.21 = (bf16[2,1,144,3072]{3,2,1,0:T(8,128)(2,1)S(1)}, bf16[2,1,144,3072]{3,2,1,0:T(8,128)(2,1)}, u32[]{:S(2)}, u32[]{:S(2)}) collective-permute-start(bf16[2,1,144,3072]{3,2,1,0:T(8,128)(2,1)S(1)} %maximum_select_fusion.6), channel_id=1, source_target_pairs={{0,8},{4,12},{8,0},{12,4},{16,24},{20,28},{24,16},{28,20},{1,9},{5... | collective-permute-start | bytes 5308424 | tf_op jit(solution)/shard_map/ppermute | solution.py:43
  217.8 15.5 %collective-permute-start.18 = (bf16[256,576]{1,0:T(8,128)(2,1)S(1)}, bf16[256,576]{1,0:T(8,128)(2,1)S(1)}, u32[]{:S(2)}, u32[]{:S(2)}) collective-permute-start(bf16[256,576]{1,0:T(8,128)(2,1)S(1)} %get-tuple-element.265), channel_id=1, source_target_pairs={{0,1},{1,2},{2,3},{3,0},{4,5},{5,6},{6,7},{7,4},{8,9},{9,10},{10,1... | collective-permute-start | bytes 884744 | tf_op jit(solution)/shard_map/ppermute | solution.py:52
  233.4 10.2 %collective-permute-start.19 = (bf16[256,576]{1,0:T(8,128)(2,1)S(1)}, bf16[256,576]{1,0:T(8,128)(2,1)S(1)}, u32[]{:S(2)}, u32[]{:S(2)}) collective-permute-start(bf16[256,576]{1,0:T(8,128)(2,1)S(1)} %collective-permute-done.18), channel_id=1, source_target_pairs={{0,1},{1,2},{2,3},{3,0},{4,5},{5,6},{6,7},{7,4},{8,9},{9,10},{10,1... | collective-permute-start | bytes 884744 | tf_op jit(solution)/shard_map/ppermute | solution.py:52
  243.6 9.4 %collective-permute-start.22 = (bf16[256,576]{1,0:T(8,128)(2,1)S(1)}, bf16[256,576]{1,0:T(8,128)(2,1)S(1)}, u32[]{:S(2)}, u32[]{:S(2)}) collective-permute-start(bf16[256,576]{1,0:T(8,128)(2,1)S(1)} %collective-permute-done.19), channel_id=1, source_target_pairs={{0,1},{1,2},{2,3},{3,0},{4,5},{5,6},{6,7},{7,4},{8,9},{9,10},{10,1... | collective-permute-start | bytes 884744 | tf_op jit(solution)/shard_map/ppermute | solution.py:52
  257.0 10.9 %collective-permute-start.23 = (bf16[4,256,576]{1,2,0:T(8,128)(2,1)}, bf16[4,256,576]{1,2,0:T(8,128)(2,1)S(1)}, u32[]{:S(2)}, u32[]{:S(2)}) collective-permute-start(bf16[4,256,576]{1,2,0:T(8,128)(2,1)} %copy.150), channel_id=1, source_target_pairs={{0,4},{4,0},{8,12},{12,8},{16,20},{20,16},{24,28},{28,24},{1,5},{5... | collective-permute-start | bytes 3538952 | tf_op jit(solution)/shard_map/ppermute | solution.py:43
  375.7 4.0 collective-permute-start.24
  379.7 5.1 collective-permute-start.25
  416.0 13.4 %collective-permute-start.27 = (bf16[4,256,576]{1,2,0:T(8,128)(2,1)S(1)}, bf16[4,256,576]{1,2,0:T(8,128)(2,1)}, u32[]{:S(2)}, u32[]{:S(2)}) collective-permute-start(bf16[4,256,576]{1,2,0:T(8,128)(2,1)S(1)} %bitcast.539), channel_id=1, source_target_pairs={{0,4},{4,0},{8,12},{12,8},{16,20},{20,16},{24,28},{28,24},{1,5},{5... | collective-permute-start | bytes 3538952 | tf_op jit(solution)/shard_map/ppermute | solution.py:43
  435.4 14.5 %collective-permute-start.28 = (bf16[256,576]{1,0:T(8,128)(2,1)}, bf16[256,576]{1,0:T(8,128)(2,1)}, u32[]{:S(2)}, u32[]{:S(2)}) collective-permute-start(bf16[256,576]{1,0:T(8,128)(2,1)} %fusion.34), channel_id=1, source_target_pairs={{0,1},{1,2},{2,3},{3,0},{4,5},{5,6},{6,7},{7,4},{8,9},{9,10},{10,1... | collective-permute-start | bytes 884744 | tf_op jit(solution)/shard_map/ppermute | solution.py:52
  449.5 44.2 %collective-permute-start.31 = (bf16[2,144,1536]{2,1,0:T(8,128)(2,1)}, bf16[2,144,1536]{2,1,0:T(8,128)(2,1)}, u32[]{:S(2)}, u32[]{:S(2)}) collective-permute-start(bf16[2,144,1536]{2,1,0:T(8,128)(2,1)} %dynamic-slice_bitcast_fusion.7), channel_id=1, source_target_pairs={{0,8},{4,12},{8,0},{12,4},{16,24},{20,28},{24,16},{28,20},{1,9},{5... | collective-permute-start | bytes 2654216 | tf_op jit(solution)/shard_map/ppermute | solution.py:43
  452.0 15.7 %collective-permute-start.29 = (bf16[256,576]{1,0:T(8,128)(2,1)}, bf16[256,576]{1,0:T(8,128)(2,1)}, u32[]{:S(2)}, u32[]{:S(2)}) collective-permute-start(bf16[256,576]{1,0:T(8,128)(2,1)} %fusion.10), channel_id=1, source_target_pairs={{0,1},{1,2},{2,3},{3,0},{4,5},{5,6},{6,7},{7,4},{8,9},{9,10},{10,1... | collective-permute-start | bytes 884744 | tf_op jit(solution)/shard_map/ppermute | solution.py:52
  466.3 27.4 %collective-permute-start.32 = (bf16[2,144,1536]{2,1,0:T(8,128)(2,1)}, bf16[2,144,1536]{2,1,0:T(8,128)(2,1)}, u32[]{:S(2)}, u32[]{:S(2)}) collective-permute-start(bf16[2,144,1536]{2,1,0:T(8,128)(2,1)} %dynamic-slice_bitcast_fusion.6), channel_id=1, source_target_pairs={{0,16},{4,20},{8,24},{12,28},{16,0},{20,4},{24,8},{28,12},{1,17},{... | collective-permute-start | bytes 2654216 | tf_op jit(solution)/shard_map/ppermute | solution.py:43
  469.6 16.3 %collective-permute-start.30 = (bf16[256,576]{1,0:T(8,128)(2,1)}, bf16[256,576]{1,0:T(8,128)(2,1)}, u32[]{:S(2)}, u32[]{:S(2)}) collective-permute-start(bf16[256,576]{1,0:T(8,128)(2,1)} %fusion.11), channel_id=1, source_target_pairs={{0,1},{1,2},{2,3},{3,0},{4,5},{5,6},{6,7},{7,4},{8,9},{9,10},{10,1... | collective-permute-start | bytes 884744 | tf_op jit(solution)/shard_map/ppermute | solution.py:52
  485.2 27.2 %collective-permute-start.33 = (bf16[2,144,1536]{2,1,0:T(8,128)(2,1)}, bf16[2,144,1536]{2,1,0:T(8,128)(2,1)}, u32[]{:S(2)}, u32[]{:S(2)}) collective-permute-start(bf16[2,144,1536]{2,1,0:T(8,128)(2,1)} %dynamic-slice_bitcast_fusion.5), channel_id=1, source_target_pairs={{0,8},{4,12},{8,0},{12,4},{16,24},{20,28},{24,16},{28,20},{1,9},{5... | collective-permute-start | bytes 2654216 | tf_op jit(solution)/shard_map/ppermute | solution.py:43
  488.0 24.4 %collective-permute-start.34 = (bf16[2,144,1536]{2,1,0:T(8,128)(2,1)}, bf16[2,144,1536]{2,1,0:T(8,128)(2,1)}, u32[]{:S(2)}, u32[]{:S(2)}) collective-permute-start(bf16[2,144,1536]{2,1,0:T(8,128)(2,1)} %dynamic-slice_bitcast_fusion.4), channel_id=1, source_target_pairs={{0,16},{4,20},{8,24},{12,28},{16,0},{20,4},{24,8},{28,12},{1,17},{... | collective-permute-start | bytes 2654216 | tf_op jit(solution)/shard_map/ppermute | solution.py:43
  526.5 15.5 %collective-permute-start.35 = (bf16[16,928,128]{2,1,0:T(8,128)(2,1)}, bf16[16,928,128]{2,1,0:T(8,128)(2,1)}, u32[]{:S(2)}, u32[]{:S(2)}) collective-permute-start(bf16[16,928,128]{2,1,0:T(8,128)(2,1)} %get-tuple-element.191), channel_id=1, source_target_pairs={{0,4},{4,0},{8,12},{12,8},{16,20},{20,16},{24,28},{28,24},{1,5},{5... | collective-permute-start | bytes 11403272 | tf_op jit(solution)/shard_map/ppermute | solution.py:43
  530.6 37.8 %collective-permute-start.38 = (bf16[144,1536]{1,0:T(8,128)(2,1)}, bf16[144,1536]{1,0:T(8,128)(2,1)}, u32[]{:S(2)}, u32[]{:S(2)}) collective-permute-start(bf16[144,1536]{1,0:T(8,128)(2,1)} %fusion.32), channel_id=1, source_target_pairs={{0,8},{4,12},{8,0},{12,4},{16,24},{20,28},{24,16},{28,20},{1,9},{5... | collective-permute-start | bytes 1327112 | tf_op jit(solution)/shard_map/ppermute | solution.py:43
  533.9 35.5 %collective-permute-start.36 = (bf16[144,1536]{1,0:T(8,128)(2,1)}, bf16[144,1536]{1,0:T(8,128)(2,1)}, u32[]{:S(2)}, u32[]{:S(2)}) collective-permute-start(bf16[144,1536]{1,0:T(8,128)(2,1)} %fusion.30), channel_id=1, source_target_pairs={{0,16},{4,20},{8,24},{12,28},{16,0},{20,4},{24,8},{28,12},{1,17},{... | collective-permute-start | bytes 1327112 | tf_op jit(solution)/shard_map/ppermute | solution.py:43
  537.4 31.9 %collective-permute-start.39 = (bf16[144,1536]{1,0:T(8,128)(2,1)}, bf16[144,1536]{1,0:T(8,128)(2,1)}, u32[]{:S(2)}, u32[]{:S(2)}) collective-permute-start(bf16[144,1536]{1,0:T(8,128)(2,1)} %fusion.33), channel_id=1, source_target_pairs={{0,8},{4,12},{8,0},{12,4},{16,24},{20,28},{24,16},{28,20},{1,9},{5... | collective-permute-start | bytes 1327112 | tf_op jit(solution)/shard_map/ppermute | solution.py:43
  540.9 28.5 %collective-permute-start.37 = (bf16[144,1536]{1,0:T(8,128)(2,1)}, bf16[144,1536]{1,0:T(8,128)(2,1)}, u32[]{:S(2)}, u32[]{:S(2)}) collective-permute-start(bf16[144,1536]{1,0:T(8,128)(2,1)} %fusion.31), channel_id=1, source_target_pairs={{0,16},{4,20},{8,24},{12,28},{16,0},{20,4},{24,8},{28,12},{1,17},{... | collective-permute-start | bytes 1327112 | tf_op jit(solution)/shard_map/ppermute | solution.py:43
  547.6 45.7 %collective-permute-start.51 = (bf16[2,2,928,128]{3,2,1,0:T(8,128)(2,1)}, bf16[2,2,928,128]{3,2,1,0:T(8,128)(2,1)}, u32[]{:S(2)}, u32[]{:S(2)}) collective-permute-start(bf16[2,2,928,128]{3,2,1,0:T(8,128)(2,1)} %dynamic-slice_bitcast_fusion.2), channel_id=1, source_target_pairs={{0,16},{4,20},{8,24},{12,28},{16,0},{20,4},{24,8},{28,12},{1,17},{... | collective-permute-start | bytes 2850824 | tf_op jit(solution)/shard_map/ppermute | solution.py:43
  568.4 26.0 %collective-permute-start.50 = (bf16[2,2,928,128]{3,2,1,0:T(8,128)(2,1)}, bf16[2,2,928,128]{3,2,1,0:T(8,128)(2,1)}, u32[]{:S(2)}, u32[]{:S(2)}) collective-permute-start(bf16[2,2,928,128]{3,2,1,0:T(8,128)(2,1)} %dynamic-slice_bitcast_fusion.3), channel_id=1, source_target_pairs={{0,8},{4,12},{8,0},{12,4},{16,24},{20,28},{24,16},{28,20},{1,9},{5... | collective-permute-start | bytes 2850824 | tf_op jit(solution)/shard_map/ppermute | solution.py:43
  585.8 20.9 %collective-permute-start.40 = (bf16[16,928,128]{2,1,0:T(8,128)(2,1)}, bf16[16,928,128]{2,1,0:T(8,128)(2,1)}, u32[]{:S(2)}, u32[]{:S(2)}) collective-permute-start(bf16[16,928,128]{2,1,0:T(8,128)(2,1)} %get-tuple-element.208), channel_id=1, source_target_pairs={{0,4},{4,0},{8,12},{12,8},{16,20},{20,16},{24,28},{28,24},{1,5},{5... | collective-permute-start | bytes 11403272 | tf_op jit(solution)/shard_map/ppermute | solution.py:43
  591.0 15.7 %collective-permute-start.48 = (f32[72,6144]{1,0:T(8,128)}, f32[72,6144]{1,0:T(8,128)}, u32[]{:S(2)}, u32[]{:S(2)}) collective-permute-start(f32[72,6144]{1,0:T(8,128)} %get-tuple-element.275), channel_id=1, source_target_pairs={{0,4},{4,0},{8,12},{12,8},{16,20},{20,16},{24,28},{28,24},{1,5},{5... | collective-permute-start | bytes 5308424 | tf_op jit(solution)/shard_map/ppermute | solution.py:43
  592.9 5.1 collective-permute-start.41
  593.3 6.2 collective-permute-start.42
  594.4 5.8 collective-permute-start.43
  598.1 4.0 collective-permute-start.44
  600.2 4.9 collective-permute-start.46
  602.1 4.6 collective-permute-start.47
  603.0 13.7 %collective-permute-start.53 = (bf16[2,928,128]{2,1,0:T(8,128)(2,1)S(1)}, bf16[2,928,128]{2,1,0:T(8,128)(2,1)S(1)}, u32[]{:S(2)}, u32[]{:S(2)}) collective-permute-start(bf16[2,928,128]{2,1,0:T(8,128)(2,1)S(1)} %fusion.18), channel_id=1, source_target_pairs={{0,8},{4,12},{8,0},{12,4},{16,24},{20,28},{24,16},{28,20},{1,9},{5... | collective-permute-start | bytes 1425416 | tf_op jit(solution)/shard_map/ppermute | solution.py:43
  605.1 12.7 %collective-permute-start.52 = (bf16[2,928,128]{2,1,0:T(8,128)(2,1)S(1)}, bf16[2,928,128]{2,1,0:T(8,128)(2,1)S(1)}, u32[]{:S(2)}, u32[]{:S(2)}) collective-permute-start(bf16[2,928,128]{2,1,0:T(8,128)(2,1)S(1)} %fusion.17), channel_id=1, source_target_pairs={{0,16},{4,20},{8,24},{12,28},{16,0},{20,4},{24,8},{28,12},{1,17},{... | collective-permute-start | bytes 1425416 | tf_op jit(solution)/shard_map/ppermute | solution.py:43
  606.8 11.0 %collective-permute-start.49 = (bf16[8,72,256]{2,1,0:T(8,128)(2,1)S(1)}, bf16[8,72,256]{2,1,0:T(8,128)(2,1)S(1)}, u32[]{:S(2)}, u32[]{:S(2)}) collective-permute-start(bf16[8,72,256]{2,1,0:T(8,128)(2,1)S(1)} %constant_dynamic-update-slice_fusion.8.refs_0_), channel_id=1, source_target_pairs={{0,1},{1,2},{2,3},{3,0},{4,5},{5,6},{6,7},{7,4},{8,9},{9,10},{10,1... | collective-permute-start | bytes 884744 | tf_op jit(solution)/shard_map/ppermute | solution.py:52
  617.8 9.8 %collective-permute-start.54 = (bf16[8,72,256]{2,1,0:T(8,128)(2,1)S(1)}, bf16[8,72,256]{2,1,0:T(8,128)(2,1)S(1)}, u32[]{:S(2)}, u32[]{:S(2)}) collective-permute-start(bf16[8,72,256]{2,1,0:T(8,128)(2,1)S(1)} %collective-permute-done.49.refs_1_), channel_id=1, source_target_pairs={{0,1},{1,2},{2,3},{3,0},{4,5},{5,6},{6,7},{7,4},{8,9},{9,10},{10,1... | collective-permute-start | bytes 884744 | tf_op jit(solution)/shard_map/ppermute | solution.py:52
  621.2 21.9 %collective-permute-start.57 = (bf16[2,2,928,128]{3,2,1,0:T(8,128)(2,1)S(1)}, bf16[2,2,928,128]{3,2,1,0:T(8,128)(2,1)S(1)}, u32[]{:S(2)}, u32[]{:S(2)}) collective-permute-start(bf16[2,2,928,128]{3,2,1,0:T(8,128)(2,1)S(1)} %dynamic-slice_bitcast_fusion), channel_id=1, source_target_pairs={{0,16},{4,20},{8,24},{12,28},{16,0},{20,4},{24,8},{28,12},{1,17},{... | collective-permute-start | bytes 2850824 | tf_op jit(solution)/shard_map/ppermute | solution.py:43
  621.9 21.8 %collective-permute-start.56 = (bf16[2,2,928,128]{3,2,1,0:T(8,128)(2,1)S(1)}, bf16[2,2,928,128]{3,2,1,0:T(8,128)(2,1)S(1)}, u32[]{:S(2)}, u32[]{:S(2)}) collective-permute-start(bf16[2,2,928,128]{3,2,1,0:T(8,128)(2,1)S(1)} %dynamic-slice_bitcast_fusion.1), channel_id=1, source_target_pairs={{0,8},{4,12},{8,0},{12,4},{16,24},{20,28},{24,16},{28,20},{1,9},{5... | collective-permute-start | bytes 2850824 | tf_op jit(solution)/shard_map/ppermute | solution.py:43
  627.7 8.9 %collective-permute-start.55 = (bf16[8,72,256]{2,1,0:T(8,128)(2,1)S(1)}, bf16[8,72,256]{2,1,0:T(8,128)(2,1)S(1)}, u32[]{:S(2)}, u32[]{:S(2)}) collective-permute-start(bf16[8,72,256]{2,1,0:T(8,128)(2,1)S(1)} %collective-permute-done.54.refs_2_), channel_id=1, source_target_pairs={{0,1},{1,2},{2,3},{3,0},{4,5},{5,6},{6,7},{7,4},{8,9},{9,10},{10,1... | collective-permute-start | bytes 884744 | tf_op jit(solution)/shard_map/ppermute | solution.py:52
  644.0 26.1 %collective-permute-start.59 = (bf16[2,928,128]{2,1,0:T(8,128)(2,1)S(1)}, bf16[2,928,128]{2,1,0:T(8,128)(2,1)S(1)}, u32[]{:S(2)}, u32[]{:S(2)}) collective-permute-start(bf16[2,928,128]{2,1,0:T(8,128)(2,1)S(1)} %fusion.20), channel_id=1, source_target_pairs={{0,8},{4,12},{8,0},{12,4},{16,24},{20,28},{24,16},{28,20},{1,9},{5... | collective-permute-start | bytes 1425416 | tf_op jit(solution)/shard_map/ppermute | solution.py:43
  646.2 24.0 %collective-permute-start.58 = (bf16[2,928,128]{2,1,0:T(8,128)(2,1)}, bf16[2,928,128]{2,1,0:T(8,128)(2,1)}, u32[]{:S(2)}, u32[]{:S(2)}) collective-permute-start(bf16[2,928,128]{2,1,0:T(8,128)(2,1)} %fusion.19), channel_id=1, source_target_pairs={{0,16},{4,20},{8,24},{12,28},{16,0},{20,4},{24,8},{28,12},{1,17},{... | collective-permute-start | bytes 1425416 | tf_op jit(solution)/shard_map/ppermute | solution.py:43
  673.1 12.0 %collective-permute-start.60 = (bf16[2,928,128]{2,1,0:T(8,128)(2,1)S(1)}, bf16[2,928,128]{2,1,0:T(8,128)(2,1)S(1)}, u32[]{:S(2)}, u32[]{:S(2)}) collective-permute-start(bf16[2,928,128]{2,1,0:T(8,128)(2,1)S(1)} %fusion.28), channel_id=1, source_target_pairs={{0,1},{1,2},{2,3},{3,0},{4,5},{5,6},{6,7},{7,4},{8,9},{9,10},{10,1... | collective-permute-start | bytes 1425416 | tf_op jit(solution)/shard_map/ppermute | solution.py:52
  685.2 11.3 %collective-permute-start.61 = (bf16[2,928,128]{2,1,0:T(8,128)(2,1)S(1)}, bf16[2,928,128]{2,1,0:T(8,128)(2,1)S(1)}, u32[]{:S(2)}, u32[]{:S(2)}) collective-permute-start(bf16[2,928,128]{2,1,0:T(8,128)(2,1)S(1)} %fusion.1), channel_id=1, source_target_pairs={{0,1},{1,2},{2,3},{3,0},{4,5},{5,6},{6,7},{7,4},{8,9},{9,10},{10,1... | collective-permute-start | bytes 1425416 | tf_op jit(solution)/shard_map/ppermute | solution.py:52
  697.4 10.8 %collective-permute-start.62 = (bf16[2,928,128]{2,1,0:T(8,128)(2,1)}, bf16[2,928,128]{2,1,0:T(8,128)(2,1)}, u32[]{:S(2)}, u32[]{:S(2)}) collective-permute-start(bf16[2,928,128]{2,1,0:T(8,128)(2,1)} %fusion.2), channel_id=1, source_target_pairs={{0,1},{1,2},{2,3},{3,0},{4,5},{5,6},{6,7},{7,4},{8,9},{9,10},{10,1... | collective-permute-start | bytes 1425416 | tf_op jit(solution)/shard_map/ppermute | solution.py:52
  709.5 6.2 collective-permute-start.63
  723.8 3.5 collective-permute-start.66
  727.3 3.5 collective-permute-start.67
  730.9 4.4 collective-permute-start.68
  (84 other events, 604.4 us)
Sparse Core Ops, SparseCore 0:
  11.4 124.4 all-gather.1

commit v5 on v4

--- a/solution.py
+++ b/solution.py
@@ -776,12 +776,12 @@
         found_ref[...] = lax.fori_loop(first, last, block_step, jnp.zeros((LANES, LANES), F32))
 
         def move(k, _):
-            for j in range(8):
-                row = row_of(keys_ref, chunk * LANES + k * 8 + j)
-                rows_ref[pl.ds(row, 1), :] = found_ref[pl.ds(k * 8 + j, 1), :]
+            for j in range(32):
+                row = row_of(keys_ref, chunk * LANES + k * 32 + j)
+                rows_ref[pl.ds(row, 1), :] = found_ref[pl.ds(k * 32 + j, 1), :]
             return 0
 
-        lax.fori_loop(0, LANES // 8, move, 0)
+        lax.fori_loop(0, LANES // 32, move, 0)
 
     for_chunks(keys_ref, lines_ref, span_ref, columns, run)
 
@@ -833,12 +833,12 @@
 
     def run(chunk, first, last, hot):
         def move(k, _):
-            for j in range(8):
-                row = row_of(keys_ref, chunk * LANES + k * 8 + j)
-                packed_ref[pl.ds(k * 8 + j, 1), :] = rows_ref[pl.ds(row, 1), :]
+            for j in range(32):
+                row = row_of(keys_ref, chunk * LANES + k * 32 + j)
+                packed_ref[pl.ds(k * 32 + j, 1), :] = rows_ref[pl.ds(row, 1), :]
             return 0
 
-        lax.fori_loop(0, LANES // 8, move, 0)
+        lax.fori_loop(0, LANES // 32, move, 0)
         packed = packed_ref[...].astype(BF16)
 
         def block_step(block, _):

time: 774 us -> 775 us (level)
  no operation moved by 1% of the time
where the time goes in v5:
time: 775 us; the launch traced here: 761 us
  Pallas kernels  318 us (41%)
  waiting for transfers between devices  153 us (20%)
  other arithmetic  128 us (17%)
  local copies, waits for them, and re-layouts  73.7 us (10%)
  starting transfers between devices  65.5 us (8%)
  between operations  19.4 us (3%)
    ppermute x15, waiting for transfers between devices, next_shard(): lax.ppermute(values, 'shard', [(i, (i + 1) % size) for i in range(size)])  104 us
    pallas_call x1, Pallas kernels, head_forward(): pl.pallas_call(head_kernel, grid_spec=pltpu.PrefetchScalarGridSpec(num_sc...  93.3 us
    pallas_call x4, Pallas kernels, layer_call(): pl.pallas_call(kernel, in_specs=[pl.BlockSpec(memory_space=pltpu.SMEM)] +...  64.4 us
    pallas_call x4, Pallas kernels, table_backward(): pl.pallas_call(table_kernel, grid_spec=pltpu.PrefetchScalarGridSpec(num_s...  48.9 us
    ppermute x48, starting transfers between devices, flip_dp(): lax.ppermute(values, 'dp', [(i, i ^ bit) for i in range(lax.axis_size('dp...  39.9 us
    ppermute x48, waiting for transfers between devices, flip_dp(): lax.ppermute(values, 'dp', [(i, i ^ bit) for i in range(lax.axis_size('dp...  29.8 us
    pallas_call x2, Pallas kernels, pack_half(): pl.pallas_call(kernel, in_specs=[pl.BlockSpec(memory_space=pltpu.SMEM)] +...  24.2 us
    pallas_call x2, Pallas kernels, unpack_rows(): pl.pallas_call(kernel, in_specs=[pl.BlockSpec(memory_space=pl.ANY)], out_...  24.1 us
  transfers between devices with their start and end apart: 70, of which 33 were waited for; matrix products, arithmetic and copies ran while one was open for 18% of the time, Pallas kernels for 25%

profile of v5, /device:TPU:0, one launch (start us, length us, event | category | flops | bytes accessed | tf_op | source)
XLA Modules:
  0.0 760.9 jit_solution(10022362979016152080)
XLA Ops:
  9.9 3.0 collective-permute-start
  19.2 3.1 collective-permute-start.3
  26.0 3.5 collective-permute-done.4
  31.8 6.8 sort.14
  41.1 18.1 %embed_rows.1 = bf16[32,72,256]{2,1,0:T(8,128)(2,1)} custom-call(s32[8192]{0:T(1024)} %copy-done.43, s32[3]{0:T(128)} %pad_add_fusion.4.span_ref, s32[64,128]{1,0:T(8,128)} %bitcast.541, f32[72,12288]{1,0:T(8,128)} %table_ref.1), custom_call_target="tpu_custom_call" | custom-call | flops 536870912 | bytes 3538944 | tf_op jit(solution)/shard_map/embed_rows/pallas_call | solution.py:801
  60.2 2.6 collective-permute-start.5
  63.4 13.3 %collective-permute-done.5 = bf16[8,72,256]{2,1,0:T(8,128)(2,1)S(1)} collective-permute-done((bf16[8,72,256]{2,1,0:T(8,128)(2,1)S(1)}, bf16[8,72,256]{2,1,0:T(8,128)(2,1)S(1)}, u32[]{:S(2)}, u32[]{:S(2)}) %collective-permute-start.5) | collective-permute-done | bytes 294944 | tf_op jit(solution)/shard_map/ppermute | solution.py:52
  77.9 16.0 %collective-permute-done.6 = bf16[8,72,256]{2,1,0:T(8,128)(2,1)S(1)} collective-permute-done((bf16[8,72,256]{2,1,0:T(8,128)(2,1)S(1)}, bf16[8,72,256]{2,1,0:T(8,128)(2,1)S(1)}, u32[]{:S(2)}, u32[]{:S(2)}) %collective-permute-start.6) | collective-permute-done | bytes 294944 | tf_op jit(solution)/shard_map/ppermute | solution.py:52
  96.2 14.5 %collective-permute-done.7 = bf16[8,72,256]{2,1,0:T(8,128)(2,1)S(1)} collective-permute-done((bf16[8,72,256]{2,1,0:T(8,128)(2,1)S(1)}, bf16[8,72,256]{2,1,0:T(8,128)(2,1)S(1)}, u32[]{:S(2)}, u32[]{:S(2)}) %collective-permute-start.7) | collective-permute-done | bytes 294944 | tf_op jit(solution)/shard_map/ppermute | solution.py:52
  115.8 2.5 copy.147.sin_ref
  144.3 11.4 %unpack_rows.2 = (bf16[576,960]{1,0:T(8,128)(2,1)}, bf16[576,576]{1,0:T(8,128)(2,1)}, bf16[576,3072]{1,0:T(8,128)(2,1)}, bf16[1536,576]{1,0:T(8,128)(2,1)}, bf16[16,128]{1,0:T(8,128)(2,1)}) custom-call(bf16[32,1840,128]{2,1,0:T(8,128)(2,1)} %all-gather.2.cloned.1.call-done.all_ref), custom_call_target="tpu_custom_call" | custom-call | bytes 14163968 | tf_op jit(solution)/shard_map/unpack_rows/pallas_call | solution.py:306
  155.7 12.7 %unpack_rows.3 = (bf16[576,960]{1,0:T(8,128)(2,1)}, bf16[576,576]{1,0:T(8,128)(2,1)}, bf16[576,3072]{1,0:T(8,128)(2,1)}, bf16[1536,576]{1,0:T(8,128)(2,1)}, bf16...) custom-call(bf16[32,1840,128]{2,1,0:T(8,128)(2,1)} %all-gather.2.cloned.1.call-done.all_ref), custom_call_target="tpu_custom_call" | custom-call | bytes 15499264 | tf_op jit(solution)/shard_map/unpack_rows/pallas_call | solution.py:306
  174.6 3.6 maximum_select_fusion.5
  181.6 14.7 %layer_forward.2 = (f32[256,576]{1,0:T(8,128)}, bf16[256,576]{1,0:T(8,128)(2,1)}, bf16[256,768]{1,0:T(8,128)(2,1)}, bf16[256,192]{1,0:T(8,128)(2,1)}, bf16[256,5...) custom-call(s32[2]{0:T(128)} %dynamic_slice.254.len_ref, ...), custom_call_target="tpu_custom_call" | custom-call | flops 1812529152 | bytes 28320768 | tf_op jit(solution)/shard_map/layer_forward/pallas_call | solution.py:674
  196.3 14.7 %layer_forward.3 = (f32[256,576]{1,0:T(8,128)}, bf16[256,576]{1,0:T(8,128)(2,1)}, bf16[256,768]{1,0:T(8,128)(2,1)}, bf16[256,192]{1,0:T(8,128)(2,1)}, bf16[256,5...) custom-call(s32[2]{0:T(128)} %dynamic_slice.254.len_ref, ...), custom_call_target="tpu_custom_call" | custom-call | flops 1812529152 | bytes 28320768 | tf_op jit(solution)/shard_map/layer_forward/pallas_call | solution.py:674
  215.1 2.4 collective-permute-start.18
  218.2 11.5 %collective-permute-done.18 = bf16[256,576]{1,0:T(8,128)(2,1)S(1)} collective-permute-done((bf16[256,576]{1,0:T(8,128)(2,1)S(1)}, bf16[256,576]{1,0:T(8,128)(2,1)S(1)}, u32[]{:S(2)}, u32[]{:S(2)}) %collective-permute-start.18) | collective-permute-done | bytes 294944 | tf_op jit(solution)/shard_map/ppermute | solution.py:52
  232.5 7.3 collective-permute-done.19
  240.0 3.8 maximum_select_fusion
  243.7 5.5 collective-permute-done.22
  250.8 2.4 copy.150
  253.2 5.2 maximum_select_fusion.1
  258.4 5.7 pad_maximum_fusion.table_ref
  264.5 2.6 copy.152
  267.1 9.6 %second_head.1 = (bf16[2,2048,576]{2,1,0:T(8,128)(2,1)}, f32[2048,576]{1,0:T(8,128)}) custom-call(bf16[2048,576]{1,0:T(8,128)(2,1)} %bitcast.498, bf16[576,576]{1,0:T(8,128)(2,1)} %get-tuple-element.148.weight_ref, f32[1,576]{1,0:T(1,128)} %get-tuple-element.309.gain_ref), custom_call_target="tpu_custom_call" | custom-call | flops 1358954496 | bytes 11796480 | tf_op jit(solution)/shard_map/second_head/pallas_call | solution.py:884
  276.6 93.3 %head_forward.1 = (bf16[4096,6144]{1,0:T(8,128)(2,1)}, f32[4096,576]{1,0:T(8,128)}, f32[256,128]{1,0:T(8,128)}, f32[256,128]{1,0:T(8,128)}) custom-call(s32[1]{0:T(128)} %bitcast.16.count_ref, s32[256]{0:T(256)} %compare_select_fusion.9.list_ref, bf16[4096,576]{1,0:T(8,128)(2,1)} %bitcast.494, bf16[576,6144]{1,0:T(8,128)(2,1)} %pad_maximum_fusion.table_ref), custom_call_target="tpu_custom_call" | custom-call | flops 57982058496 | bytes 50331648 | tf_op jit(solution)/shard_map/head_forward/pallas_call | solution.py:996
  372.0 3.1 multiply_reduce_fusion.2
  376.3 4.8 collective-permute-done.25
  383.0 14.9 %scale_rows.1 = (f32[4096,576]{1,0:T(8,128)}, bf16[576,4096]{1,0:T(8,128)(2,1)}) custom-call(s32[1]{0:T(128)} %bitcast.16.count_ref, s32[256]{0:T(256)} %compare_select_fusion.9.list_ref, bf16[4096,576]{1,0:T(8,128)(2,1)} %bitcast.495, f32[4096,576]{1,0:T(8,128)} %get-tuple-element.158.back_ref, f32[32,128]{1,0:T(8,128)} %fusion.42.scale_ref), custom_call_target="tpu_custom_call" | custom-call | bytes 28311552 | tf_op jit(solution)/shard_map/scale_rows/pallas_call | solution.py:1074
  397.9 3.0 slice.152
  406.3 2.8 slice_add_fusion
  413.5 12.2 %table_backward.4 = bf16[576,1536]{1,0:T(8,128)(2,1)} custom-call(s32[1]{0:T(128)} %bitcast.16.count_ref, bf16[576,4096]{1,0:T(8,128)(2,1)} %get-tuple-element.168.turned_ref, bf16[4096,6144]{1,0:T(8,128)(2,1)} %get-tuple-element.162.exp_ref), custom_call_target="tpu_custom_call" | custom-call | flops 7247757312 | bytes 12582912 | tf_op jit(solution)/shard_map/table_backward/pallas_call | solution.py:1139
  432.7 12.1 %table_backward.5 = bf16[576,1536]{1,0:T(8,128)(2,1)} custom-call(s32[1]{0:T(128)} %bitcast.16.count_ref, bf16[576,4096]{1,0:T(8,128)(2,1)} %get-tuple-element.168.turned_ref, bf16[4096,6144]{1,0:T(8,128)(2,1)} %get-tuple-element.162.exp_ref), custom_call_target="tpu_custom_call" | custom-call | flops 7247757312 | bytes 12582912 | tf_op jit(solution)/shard_map/table_backward/pallas_call | solution.py:1139
  448.4 12.1 %table_backward.6 = bf16[576,1536]{1,0:T(8,128)(2,1)} custom-call(s32[1]{0:T(128)} %bitcast.16.count_ref, bf16[576,4096]{1,0:T(8,128)(2,1)} %get-tuple-element.168.turned_ref, bf16[4096,6144]{1,0:T(8,128)(2,1)} %get-tuple-element.162.exp_ref), custom_call_target="tpu_custom_call" | custom-call | flops 7247757312 | bytes 12582912 | tf_op jit(solution)/shard_map/table_backward/pallas_call | solution.py:1139
  466.9 12.5 %table_backward.7 = bf16[576,1536]{1,0:T(8,128)(2,1)} custom-call(s32[1]{0:T(128)} %bitcast.16.count_ref, bf16[576,4096]{1,0:T(8,128)(2,1)} %get-tuple-element.168.turned_ref, bf16[4096,6144]{1,0:T(8,128)(2,1)} %get-tuple-element.162.exp_ref), custom_call_target="tpu_custom_call" | custom-call | flops 7247757312 | bytes 12582912 | tf_op jit(solution)/shard_map/table_backward/pallas_call | solution.py:1139
  485.9 2.3 multiply_reduce_fusion.5
  489.9 17.3 %layer_backward.2 = (f32[256,576]{1,0:T(8,128)}, bf16[256,576]{1,0:T(8,128)(2,1)}, bf16[256,3072]{1,0:T(8,128)(2,1)}, bf16[256,576]{1,0:T(8,128)(2,1)}, bf16[256,960]{1,0:T(8,128)(2,1)}, /*index=5*/f32[2,576]{1,0:T(2,128)}) custom-call(s32[2]{0:T(128)} %dynamic_slice.254.len_ref, f32[256,576]{1,0:T(8,128)} %multiply_subtract_fusion.2.grad_ref, ...), custom_call_target="tpu_custom_call" | custom-call | flops 1812529152 | bytes 28320768 | tf_op jit(solution)/shard_map/layer_backward/pallas_call | solution.py:674
  508.6 14.1 %pack_half.2 = (bf16[16,928,128]{2,1,0:T(8,128)(2,1)}, bf16[16,928,128]{2,1,0:T(8,128)(2,1)}, bf16[1344,128]{1,0:T(8,128)(2,1)}) custom-call(s32[32]{0:T(128)} %pad_add_fusion.6.info_ref, bf16[256,576]{1,0:T(8,128)(2,1)} %get-tuple-element.178.refs_0_, bf16[256,576]{1,0:T(8,128)(2,1)} %get-tuple-element.179.refs_1_, ...), custom_call_target="tpu_custom_call" | custom-call | bytes 969728 | tf_op jit(solution)/shard_map/pack_half/pallas_call | solution.py:418
  538.2 3.1 add_convert_fusion.1
  545.1 17.6 %layer_backward.3 = (f32[256,576]{1,0:T(8,128)}, bf16[256,576]{1,0:T(8,128)(2,1)}, bf16[256,3072]{1,0:T(8,128)(2,1)}, bf16[256,576]{1,0:T(8,128)(2,1)}, bf16[256,960]{1,0:T(8,128)(2,1)}, /*index=5*/f32[2,576]{1,0:T(2,128)}) custom-call(s32[2]{0:T(128)} %dynamic_slice.254.len_ref, f32[256,576]{1,0:T(8,128)} %get-tuple-element.192.grad_ref, ...), custom_call_target="tpu_custom_call" | custom-call | flops 1812529152 | bytes 28320768 | tf_op jit(solution)/shard_map/layer_backward/pallas_call | solution.py:674
  565.9 2.3 bitcast_add_fusion.8
  572.3 10.0 %pack_half.3 = (bf16[16,928,128]{2,1,0:T(8,128)(2,1)}, bf16[16,928,128]{2,1,0:T(8,128)(2,1)}) custom-call(s32[32]{0:T(128)} %pad_add_fusion.5.info_ref, bf16[256,576]{1,0:T(8,128)(2,1)} %get-tuple-element.154.refs_0_, bf16[256,576]{1,0:T(8,128)(2,1)} %get-tuple-element.155.refs_1_, bf16[256,576]{1,0:T(8,128)(2,1)} %get-tuple-element.156.refs_2_, ...), custom_call_target="tpu_custom_call" | custom-call | bytes 927744 | tf_op jit(solution)/shard_map/pack_half/pallas_call | solution.py:418
  603.1 3.1 collective-permute-start.49
  606.2 3.1 add_convert_fusion
  609.3 3.8 collective-permute-done.53
  613.9 3.1 collective-permute-start.54
  619.8 4.1 collective-permute-done.54.refs_2_
  625.2 4.4 maximum_select_fusion.2.refs_4_
  629.5 3.4 collective-permute-done.55.refs_3_
  632.9 6.4 collective-permute-done.57
  644.1 21.2 %spread_rows.1 = f32[72,12288]{1,0:T(8,128)} custom-call(s32[8192]{0:T(1024)} %copy-done.43, s32[3]{0:T(128)} %pad_add_fusion.4.span_ref, s32[32]{0:T(128)} %add.871.place_ref, s32[64,128]{1,0:T(8,128)} %bitcast.542, bf16[8,72,256]{2,1,0:T(8,128)(2,1)} %copy-done.46, bf16[8,72,256]{2,1,0:T(8,128)(2,1)} %copy-done.47, bf16[8,72,256]{2,1,0:T(8,128)(2,1)} %copy-done.48, ...), custom_call_target="tpu_custom_call" | custom-call | flops 536870912 | bytes 7077888 | tf_op jit(solution)/shard_map/spread_rows/pallas_call | solution.py:858
  668.2 2.8 collective-permute-start.60
  671.0 9.2 %collective-permute-done.60 = bf16[2,928,128]{2,1,0:T(8,128)(2,1)S(1)} collective-permute-done((bf16[2,928,128]{2,1,0:T(8,128)(2,1)S(1)}, bf16[2,928,128]{2,1,0:T(8,128)(2,1)S(1)}, u32[]{:S(2)}, u32[]{:S(2)}) %collective-permute-start.60) | collective-permute-done | bytes 475168 | tf_op jit(solution)/shard_map/ppermute | solution.py:52
  682.4 9.5 %collective-permute-done.61 = bf16[2,928,128]{2,1,0:T(8,128)(2,1)S(1)} collective-permute-done((bf16[2,928,128]{2,1,0:T(8,128)(2,1)S(1)}, bf16[2,928,128]{2,1,0:T(8,128)(2,1)S(1)}, u32[]{:S(2)}, u32[]{:S(2)}) %collective-permute-start.61) | collective-permute-done | bytes 475168 | tf_op jit(solution)/shard_map/ppermute | solution.py:52
  693.4 10.2 %collective-permute-done.62 = bf16[2,928,128]{2,1,0:T(8,128)(2,1)} collective-permute-done((bf16[2,928,128]{2,1,0:T(8,128)(2,1)}, bf16[2,928,128]{2,1,0:T(8,128)(2,1)}, u32[]{:S(2)}, u32[]{:S(2)}) %collective-permute-start.62) | collective-permute-done | bytes 475168 | tf_op jit(solution)/shard_map/ppermute | solution.py:52
  707.0 4.1 collective-permute-done.63
  716.2 3.0 collective-permute-done.65
  719.6 3.1 collective-permute-done.66
  722.8 3.5 collective-permute-done.67
  726.9 3.8 collective-permute-done.68
  732.6 4.0 fusion.98
  736.6 6.5 fusion.99
  743.8 3.1 multiply_add_fusion.2
  746.9 4.4 multiply_add_fusion
  (503 shorter events, 188.0 us)
Async XLA Ops:
  7.2 129.9 %all-gather.2.cloned.1.call-start = ((), (), s32[]{:S(2)}) async-start(), calls=%async_computation | async-start | bytes 15544320 | tf_op jit(solution)/shard_map/all_gather | solution.py:1242
  9.9 4.5 collective-permute-start
  14.4 3.6 collective-permute-start.1
  19.2 4.8 collective-permute-start.3
  24.0 5.5 collective-permute-start.4
  60.2 16.4 %collective-permute-start.5 = (bf16[8,72,256]{2,1,0:T(8,128)(2,1)S(1)}, bf16[8,72,256]{2,1,0:T(8,128)(2,1)S(1)}, u32[]{:S(2)}, u32[]{:S(2)}) collective-permute-start(bf16[8,72,256]{2,1,0:T(8,128)(2,1)S(1)} %dynamic-slice_bitcast_fusion.9), channel_id=1, source_target_pairs={{0,1},{1,2},{2,3},{3,0},{4,5},{5,6},{6,7},{7,4},{8,9},{9,10},{10,1... | collective-permute-start | bytes 884744 | tf_op jit(solution)/shard_map/ppermute | solution.py:52
  77.7 16.2 %collective-permute-start.6 = (bf16[8,72,256]{2,1,0:T(8,128)(2,1)S(1)}, bf16[8,72,256]{2,1,0:T(8,128)(2,1)S(1)}, u32[]{:S(2)}, u32[]{:S(2)}) collective-permute-start(bf16[8,72,256]{2,1,0:T(8,128)(2,1)S(1)} %fusion.15), channel_id=1, source_target_pairs={{0,1},{1,2},{2,3},{3,0},{4,5},{5,6},{6,7},{7,4},{8,9},{9,10},{10,1... | collective-permute-start | bytes 884744 | tf_op jit(solution)/shard_map/ppermute | solution.py:52
  95.0 15.8 %collective-permute-start.7 = (bf16[8,72,256]{2,1,0:T(8,128)(2,1)S(1)}, bf16[8,72,256]{2,1,0:T(8,128)(2,1)S(1)}, u32[]{:S(2)}, u32[]{:S(2)}) collective-permute-start(bf16[8,72,256]{2,1,0:T(8,128)(2,1)S(1)} %fusion.16), channel_id=1, source_target_pairs={{0,1},{1,2},{2,3},{3,0},{4,5},{5,6},{6,7},{7,4},{8,9},{9,10},{10,1... | collective-permute-start | bytes 884744 | tf_op jit(solution)/shard_map/ppermute | solution.py:52
  112.5 9.6 %collective-permute-start.8 = (bf16[72,256]{1,0:T(8,128)(2,1)}, bf16[72,256]{1,0:T(8,128)(2,1)}, u32[]{:S(2)}, u32[]{:S(2)}) collective-permute-start(bf16[72,256]{1,0:T(8,128)(2,1)} %get-tuple-element.294), channel_id=1, source_target_pairs={{0,4},{4,0},{8,12},{12,8},{16,20},{20,16},{24,28},{28,24},{1,5},{5... | collective-permute-start | bytes 110600 | tf_op jit(solution)/shard_map/ppermute | solution.py:43
  118.4 6.3 collective-permute-start.9
  119.1 7.5 collective-permute-start.10
  120.2 7.0 collective-permute-start.11
  122.0 5.9 collective-permute-start.12
  122.1 6.5 collective-permute-start.13
  124.6 4.5 collective-permute-start.14
  141.7 32.9 %collective-permute-start.16 = (bf16[1,1,144,3072]{3,2,1,0:T(8,128)(2,1)}, bf16[1,1,144,3072]{3,2,1,0:T(8,128)(2,1)}, u32[]{:S(2)}, u32[]{:S(2)}) collective-permute-start(bf16[1,1,144,3072]{3,2,1,0:T(8,128)(2,1)} %get-tuple-element.277), channel_id=1, source_target_pairs={{0,8},{4,12},{8,0},{12,4},{16,24},{20,28},{24,16},{28,20},{1,9},{5... | collective-permute-start | bytes 2654216 | tf_op jit(solution)/shard_map/ppermute | solution.py:43
  142.9 31.7 %collective-permute-start.17 = (bf16[1,1,144,3072]{3,2,1,0:T(8,128)(2,1)S(1)}, bf16[1,1,144,3072]{3,2,1,0:T(8,128)(2,1)}, u32[]{:S(2)}, u32[]{:S(2)}) collective-permute-start(bf16[1,1,144,3072]{3,2,1,0:T(8,128)(2,1)S(1)} %get-tuple-element.276), channel_id=1, source_target_pairs={{0,16},{4,20},{8,24},{12,28},{16,0},{20,4},{24,8},{28,12},{1,17},{... | collective-permute-start | bytes 2654216 | tf_op jit(solution)/shard_map/ppermute | solution.py:43
  178.2 61.7 %collective-permute-start.20 = (bf16[1,2,144,3072]{3,2,1,0:T(8,128)(2,1)}, bf16[1,2,144,3072]{3,2,1,0:T(8,128)(2,1)}, u32[]{:S(2)}, u32[]{:S(2)}) collective-permute-start(bf16[1,2,144,3072]{3,2,1,0:T(8,128)(2,1)} %maximum_select_fusion.5), channel_id=1, source_target_pairs={{0,16},{4,20},{8,24},{12,28},{16,0},{20,4},{24,8},{28,12},{1,17},{... | collective-permute-start | bytes 5308424 | tf_op jit(solution)/shard_map/ppermute | solution.py:43
  180.7 59.2 %collective-permute-start.21 = (bf16[2,1,144,3072]{3,2,1,0:T(8,128)(2,1)S(1)}, bf16[2,1,144,3072]{3,2,1,0:T(8,128)(2,1)}, u32[]{:S(2)}, u32[]{:S(2)}) collective-permute-start(bf16[2,1,144,3072]{3,2,1,0:T(8,128)(2,1)S(1)} %maximum_select_fusion.6), channel_id=1, source_target_pairs={{0,8},{4,12},{8,0},{12,4},{16,24},{20,28},{24,16},{28,20},{1,9},{5... | collective-permute-start | bytes 5308424 | tf_op jit(solution)/shard_map/ppermute | solution.py:43
  215.1 14.6 %collective-permute-start.18 = (bf16[256,576]{1,0:T(8,128)(2,1)S(1)}, bf16[256,576]{1,0:T(8,128)(2,1)S(1)}, u32[]{:S(2)}, u32[]{:S(2)}) collective-permute-start(bf16[256,576]{1,0:T(8,128)(2,1)S(1)} %get-tuple-element.265), channel_id=1, source_target_pairs={{0,1},{1,2},{2,3},{3,0},{4,5},{5,6},{6,7},{7,4},{8,9},{9,10},{10,1... | collective-permute-start | bytes 884744 | tf_op jit(solution)/shard_map/ppermute | solution.py:52
  229.7 10.2 %collective-permute-start.19 = (bf16[256,576]{1,0:T(8,128)(2,1)S(1)}, bf16[256,576]{1,0:T(8,128)(2,1)S(1)}, u32[]{:S(2)}, u32[]{:S(2)}) collective-permute-start(bf16[256,576]{1,0:T(8,128)(2,1)S(1)} %collective-permute-done.18), channel_id=1, source_target_pairs={{0,1},{1,2},{2,3},{3,0},{4,5},{5,6},{6,7},{7,4},{8,9},{9,10},{10,1... | collective-permute-start | bytes 884744 | tf_op jit(solution)/shard_map/ppermute | solution.py:52
  239.9 9.3 %collective-permute-start.22 = (bf16[256,576]{1,0:T(8,128)(2,1)S(1)}, bf16[256,576]{1,0:T(8,128)(2,1)S(1)}, u32[]{:S(2)}, u32[]{:S(2)}) collective-permute-start(bf16[256,576]{1,0:T(8,128)(2,1)S(1)} %collective-permute-done.19), channel_id=1, source_target_pairs={{0,1},{1,2},{2,3},{3,0},{4,5},{5,6},{6,7},{7,4},{8,9},{9,10},{10,1... | collective-permute-start | bytes 884744 | tf_op jit(solution)/shard_map/ppermute | solution.py:52
  253.2 10.9 %collective-permute-start.23 = (bf16[4,256,576]{1,2,0:T(8,128)(2,1)}, bf16[4,256,576]{1,2,0:T(8,128)(2,1)S(1)}, u32[]{:S(2)}, u32[]{:S(2)}) collective-permute-start(bf16[4,256,576]{1,2,0:T(8,128)(2,1)} %copy.150), channel_id=1, source_target_pairs={{0,4},{4,0},{8,12},{12,8},{16,20},{20,16},{24,28},{28,24},{1,5},{5... | collective-permute-start | bytes 3538952 | tf_op jit(solution)/shard_map/ppermute | solution.py:43
  371.9 4.0 collective-permute-start.24
  375.9 5.1 collective-permute-start.25
  412.3 13.4 %collective-permute-start.27 = (bf16[4,256,576]{1,2,0:T(8,128)(2,1)S(1)}, bf16[4,256,576]{1,2,0:T(8,128)(2,1)}, u32[]{:S(2)}, u32[]{:S(2)}) collective-permute-start(bf16[4,256,576]{1,2,0:T(8,128)(2,1)S(1)} %bitcast.539), channel_id=1, source_target_pairs={{0,4},{4,0},{8,12},{12,8},{16,20},{20,16},{24,28},{28,24},{1,5},{5... | collective-permute-start | bytes 3538952 | tf_op jit(solution)/shard_map/ppermute | solution.py:43
  431.7 14.6 %collective-permute-start.28 = (bf16[256,576]{1,0:T(8,128)(2,1)}, bf16[256,576]{1,0:T(8,128)(2,1)}, u32[]{:S(2)}, u32[]{:S(2)}) collective-permute-start(bf16[256,576]{1,0:T(8,128)(2,1)} %fusion.34), channel_id=1, source_target_pairs={{0,1},{1,2},{2,3},{3,0},{4,5},{5,6},{6,7},{7,4},{8,9},{9,10},{10,1... | collective-permute-start | bytes 884744 | tf_op jit(solution)/shard_map/ppermute | solution.py:52
  445.7 44.2 %collective-permute-start.31 = (bf16[2,144,1536]{2,1,0:T(8,128)(2,1)}, bf16[2,144,1536]{2,1,0:T(8,128)(2,1)}, u32[]{:S(2)}, u32[]{:S(2)}) collective-permute-start(bf16[2,144,1536]{2,1,0:T(8,128)(2,1)} %dynamic-slice_bitcast_fusion.7), channel_id=1, source_target_pairs={{0,8},{4,12},{8,0},{12,4},{16,24},{20,28},{24,16},{28,20},{1,9},{5... | collective-permute-start | bytes 2654216 | tf_op jit(solution)/shard_map/ppermute | solution.py:43
  448.2 15.9 %collective-permute-start.29 = (bf16[256,576]{1,0:T(8,128)(2,1)}, bf16[256,576]{1,0:T(8,128)(2,1)}, u32[]{:S(2)}, u32[]{:S(2)}) collective-permute-start(bf16[256,576]{1,0:T(8,128)(2,1)} %fusion.10), channel_id=1, source_target_pairs={{0,1},{1,2},{2,3},{3,0},{4,5},{5,6},{6,7},{7,4},{8,9},{9,10},{10,1... | collective-permute-start | bytes 884744 | tf_op jit(solution)/shard_map/ppermute | solution.py:52
  462.6 27.3 %collective-permute-start.32 = (bf16[2,144,1536]{2,1,0:T(8,128)(2,1)}, bf16[2,144,1536]{2,1,0:T(8,128)(2,1)}, u32[]{:S(2)}, u32[]{:S(2)}) collective-permute-start(bf16[2,144,1536]{2,1,0:T(8,128)(2,1)} %dynamic-slice_bitcast_fusion.6), channel_id=1, source_target_pairs={{0,16},{4,20},{8,24},{12,28},{16,0},{20,4},{24,8},{28,12},{1,17},{... | collective-permute-start | bytes 2654216 | tf_op jit(solution)/shard_map/ppermute | solution.py:43
  466.1 16.2 %collective-permute-start.30 = (bf16[256,576]{1,0:T(8,128)(2,1)}, bf16[256,576]{1,0:T(8,128)(2,1)}, u32[]{:S(2)}, u32[]{:S(2)}) collective-permute-start(bf16[256,576]{1,0:T(8,128)(2,1)} %fusion.11), channel_id=1, source_target_pairs={{0,1},{1,2},{2,3},{3,0},{4,5},{5,6},{6,7},{7,4},{8,9},{9,10},{10,1... | collective-permute-start | bytes 884744 | tf_op jit(solution)/shard_map/ppermute | solution.py:52
  481.8 26.8 %collective-permute-start.33 = (bf16[2,144,1536]{2,1,0:T(8,128)(2,1)}, bf16[2,144,1536]{2,1,0:T(8,128)(2,1)}, u32[]{:S(2)}, u32[]{:S(2)}) collective-permute-start(bf16[2,144,1536]{2,1,0:T(8,128)(2,1)} %dynamic-slice_bitcast_fusion.5), channel_id=1, source_target_pairs={{0,8},{4,12},{8,0},{12,4},{16,24},{20,28},{24,16},{28,20},{1,9},{5... | collective-permute-start | bytes 2654216 | tf_op jit(solution)/shard_map/ppermute | solution.py:43
  484.5 24.2 %collective-permute-start.34 = (bf16[2,144,1536]{2,1,0:T(8,128)(2,1)}, bf16[2,144,1536]{2,1,0:T(8,128)(2,1)}, u32[]{:S(2)}, u32[]{:S(2)}) collective-permute-start(bf16[2,144,1536]{2,1,0:T(8,128)(2,1)} %dynamic-slice_bitcast_fusion.4), channel_id=1, source_target_pairs={{0,16},{4,20},{8,24},{12,28},{16,0},{20,4},{24,8},{28,12},{1,17},{... | collective-permute-start | bytes 2654216 | tf_op jit(solution)/shard_map/ppermute | solution.py:43
  522.8 15.5 %collective-permute-start.35 = (bf16[16,928,128]{2,1,0:T(8,128)(2,1)}, bf16[16,928,128]{2,1,0:T(8,128)(2,1)}, u32[]{:S(2)}, u32[]{:S(2)}) collective-permute-start(bf16[16,928,128]{2,1,0:T(8,128)(2,1)} %get-tuple-element.191), channel_id=1, source_target_pairs={{0,4},{4,0},{8,12},{12,8},{16,20},{20,16},{24,28},{28,24},{1,5},{5... | collective-permute-start | bytes 11403272 | tf_op jit(solution)/shard_map/ppermute | solution.py:43
  526.8 38.2 %collective-permute-start.38 = (bf16[144,1536]{1,0:T(8,128)(2,1)}, bf16[144,1536]{1,0:T(8,128)(2,1)}, u32[]{:S(2)}, u32[]{:S(2)}) collective-permute-start(bf16[144,1536]{1,0:T(8,128)(2,1)} %fusion.32), channel_id=1, source_target_pairs={{0,8},{4,12},{8,0},{12,4},{16,24},{20,28},{24,16},{28,20},{1,9},{5... | collective-permute-start | bytes 1327112 | tf_op jit(solution)/shard_map/ppermute | solution.py:43
  530.2 35.8 %collective-permute-start.36 = (bf16[144,1536]{1,0:T(8,128)(2,1)}, bf16[144,1536]{1,0:T(8,128)(2,1)}, u32[]{:S(2)}, u32[]{:S(2)}) collective-permute-start(bf16[144,1536]{1,0:T(8,128)(2,1)} %fusion.30), channel_id=1, source_target_pairs={{0,16},{4,20},{8,24},{12,28},{16,0},{20,4},{24,8},{28,12},{1,17},{... | collective-permute-start | bytes 1327112 | tf_op jit(solution)/shard_map/ppermute | solution.py:43
  534.0 31.9 %collective-permute-start.39 = (bf16[144,1536]{1,0:T(8,128)(2,1)}, bf16[144,1536]{1,0:T(8,128)(2,1)}, u32[]{:S(2)}, u32[]{:S(2)}) collective-permute-start(bf16[144,1536]{1,0:T(8,128)(2,1)} %fusion.33), channel_id=1, source_target_pairs={{0,8},{4,12},{8,0},{12,4},{16,24},{20,28},{24,16},{28,20},{1,9},{5... | collective-permute-start | bytes 1327112 | tf_op jit(solution)/shard_map/ppermute | solution.py:43
  537.4 28.5 %collective-permute-start.37 = (bf16[144,1536]{1,0:T(8,128)(2,1)}, bf16[144,1536]{1,0:T(8,128)(2,1)}, u32[]{:S(2)}, u32[]{:S(2)}) collective-permute-start(bf16[144,1536]{1,0:T(8,128)(2,1)} %fusion.31), channel_id=1, source_target_pairs={{0,16},{4,20},{8,24},{12,28},{16,0},{20,4},{24,8},{28,12},{1,17},{... | collective-permute-start | bytes 1327112 | tf_op jit(solution)/shard_map/ppermute | solution.py:43
  543.9 46.0 %collective-permute-start.51 = (bf16[2,2,928,128]{3,2,1,0:T(8,128)(2,1)}, bf16[2,2,928,128]{3,2,1,0:T(8,128)(2,1)}, u32[]{:S(2)}, u32[]{:S(2)}) collective-permute-start(bf16[2,2,928,128]{3,2,1,0:T(8,128)(2,1)} %dynamic-slice_bitcast_fusion.2), channel_id=1, source_target_pairs={{0,16},{4,20},{8,24},{12,28},{16,0},{20,4},{24,8},{28,12},{1,17},{... | collective-permute-start | bytes 2850824 | tf_op jit(solution)/shard_map/ppermute | solution.py:43
  565.0 26.0 %collective-permute-start.50 = (bf16[2,2,928,128]{3,2,1,0:T(8,128)(2,1)}, bf16[2,2,928,128]{3,2,1,0:T(8,128)(2,1)}, u32[]{:S(2)}, u32[]{:S(2)}) collective-permute-start(bf16[2,2,928,128]{3,2,1,0:T(8,128)(2,1)} %dynamic-slice_bitcast_fusion.3), channel_id=1, source_target_pairs={{0,8},{4,12},{8,0},{12,4},{16,24},{20,28},{24,16},{28,20},{1,9},{5... | collective-permute-start | bytes 2850824 | tf_op jit(solution)/shard_map/ppermute | solution.py:43
  582.3 20.6 %collective-permute-start.40 = (bf16[16,928,128]{2,1,0:T(8,128)(2,1)}, bf16[16,928,128]{2,1,0:T(8,128)(2,1)}, u32[]{:S(2)}, u32[]{:S(2)}) collective-permute-start(bf16[16,928,128]{2,1,0:T(8,128)(2,1)} %get-tuple-element.208), channel_id=1, source_target_pairs={{0,4},{4,0},{8,12},{12,8},{16,20},{20,16},{24,28},{28,24},{1,5},{5... | collective-permute-start | bytes 11403272 | tf_op jit(solution)/shard_map/ppermute | solution.py:43
  587.6 15.4 %collective-permute-start.48 = (f32[72,6144]{1,0:T(8,128)}, f32[72,6144]{1,0:T(8,128)}, u32[]{:S(2)}, u32[]{:S(2)}) collective-permute-start(f32[72,6144]{1,0:T(8,128)} %get-tuple-element.275), channel_id=1, source_target_pairs={{0,4},{4,0},{8,12},{12,8},{16,20},{20,16},{24,28},{28,24},{1,5},{5... | collective-permute-start | bytes 5308424 | tf_op jit(solution)/shard_map/ppermute | solution.py:43
  589.5 5.1 collective-permute-start.41
  589.9 5.9 collective-permute-start.42
  591.0 5.8 collective-permute-start.43
  594.7 4.0 collective-permute-start.44
  596.8 4.9 collective-permute-start.46
  598.7 4.3 collective-permute-start.47
  599.3 13.7 %collective-permute-start.53 = (bf16[2,928,128]{2,1,0:T(8,128)(2,1)S(1)}, bf16[2,928,128]{2,1,0:T(8,128)(2,1)S(1)}, u32[]{:S(2)}, u32[]{:S(2)}) collective-permute-start(bf16[2,928,128]{2,1,0:T(8,128)(2,1)S(1)} %fusion.18), channel_id=1, source_target_pairs={{0,8},{4,12},{8,0},{12,4},{16,24},{20,28},{24,16},{28,20},{1,9},{5... | collective-permute-start | bytes 1425416 | tf_op jit(solution)/shard_map/ppermute | solution.py:43
  601.7 12.2 %collective-permute-start.52 = (bf16[2,928,128]{2,1,0:T(8,128)(2,1)S(1)}, bf16[2,928,128]{2,1,0:T(8,128)(2,1)S(1)}, u32[]{:S(2)}, u32[]{:S(2)}) collective-permute-start(bf16[2,928,128]{2,1,0:T(8,128)(2,1)S(1)} %fusion.17), channel_id=1, source_target_pairs={{0,16},{4,20},{8,24},{12,28},{16,0},{20,4},{24,8},{28,12},{1,17},{... | collective-permute-start | bytes 1425416 | tf_op jit(solution)/shard_map/ppermute | solution.py:43
  603.1 10.8 %collective-permute-start.49 = (bf16[8,72,256]{2,1,0:T(8,128)(2,1)S(1)}, bf16[8,72,256]{2,1,0:T(8,128)(2,1)S(1)}, u32[]{:S(2)}, u32[]{:S(2)}) collective-permute-start(bf16[8,72,256]{2,1,0:T(8,128)(2,1)S(1)} %constant_dynamic-update-slice_fusion.8.refs_0_), channel_id=1, source_target_pairs={{0,1},{1,2},{2,3},{3,0},{4,5},{5,6},{6,7},{7,4},{8,9},{9,10},{10,1... | collective-permute-start | bytes 884744 | tf_op jit(solution)/shard_map/ppermute | solution.py:52
  613.9 10.0 %collective-permute-start.54 = (bf16[8,72,256]{2,1,0:T(8,128)(2,1)S(1)}, bf16[8,72,256]{2,1,0:T(8,128)(2,1)S(1)}, u32[]{:S(2)}, u32[]{:S(2)}) collective-permute-start(bf16[8,72,256]{2,1,0:T(8,128)(2,1)S(1)} %collective-permute-done.49.refs_1_), channel_id=1, source_target_pairs={{0,1},{1,2},{2,3},{3,0},{4,5},{5,6},{6,7},{7,4},{8,9},{9,10},{10,1... | collective-permute-start | bytes 884744 | tf_op jit(solution)/shard_map/ppermute | solution.py:52
  617.3 22.0 %collective-permute-start.57 = (bf16[2,2,928,128]{3,2,1,0:T(8,128)(2,1)S(1)}, bf16[2,2,928,128]{3,2,1,0:T(8,128)(2,1)S(1)}, u32[]{:S(2)}, u32[]{:S(2)}) collective-permute-start(bf16[2,2,928,128]{3,2,1,0:T(8,128)(2,1)S(1)} %dynamic-slice_bitcast_fusion), channel_id=1, source_target_pairs={{0,16},{4,20},{8,24},{12,28},{16,0},{20,4},{24,8},{28,12},{1,17},{... | collective-permute-start | bytes 2850824 | tf_op jit(solution)/shard_map/ppermute | solution.py:43
  618.5 21.9 %collective-permute-start.56 = (bf16[2,2,928,128]{3,2,1,0:T(8,128)(2,1)S(1)}, bf16[2,2,928,128]{3,2,1,0:T(8,128)(2,1)S(1)}, u32[]{:S(2)}, u32[]{:S(2)}) collective-permute-start(bf16[2,2,928,128]{3,2,1,0:T(8,128)(2,1)S(1)} %dynamic-slice_bitcast_fusion.1), channel_id=1, source_target_pairs={{0,8},{4,12},{8,0},{12,4},{16,24},{20,28},{24,16},{28,20},{1,9},{5... | collective-permute-start | bytes 2850824 | tf_op jit(solution)/shard_map/ppermute | solution.py:43
  623.9 9.0 %collective-permute-start.55 = (bf16[8,72,256]{2,1,0:T(8,128)(2,1)S(1)}, bf16[8,72,256]{2,1,0:T(8,128)(2,1)S(1)}, u32[]{:S(2)}, u32[]{:S(2)}) collective-permute-start(bf16[8,72,256]{2,1,0:T(8,128)(2,1)S(1)} %collective-permute-done.54.refs_2_), channel_id=1, source_target_pairs={{0,1},{1,2},{2,3},{3,0},{4,5},{5,6},{6,7},{7,4},{8,9},{9,10},{10,1... | collective-permute-start | bytes 884744 | tf_op jit(solution)/shard_map/ppermute | solution.py:52
  640.7 24.6 %collective-permute-start.59 = (bf16[2,928,128]{2,1,0:T(8,128)(2,1)S(1)}, bf16[2,928,128]{2,1,0:T(8,128)(2,1)S(1)}, u32[]{:S(2)}, u32[]{:S(2)}) collective-permute-start(bf16[2,928,128]{2,1,0:T(8,128)(2,1)S(1)} %fusion.20), channel_id=1, source_target_pairs={{0,8},{4,12},{8,0},{12,4},{16,24},{20,28},{24,16},{28,20},{1,9},{5... | collective-permute-start | bytes 1425416 | tf_op jit(solution)/shard_map/ppermute | solution.py:43
  642.8 22.5 %collective-permute-start.58 = (bf16[2,928,128]{2,1,0:T(8,128)(2,1)}, bf16[2,928,128]{2,1,0:T(8,128)(2,1)}, u32[]{:S(2)}, u32[]{:S(2)}) collective-permute-start(bf16[2,928,128]{2,1,0:T(8,128)(2,1)} %fusion.19), channel_id=1, source_target_pairs={{0,16},{4,20},{8,24},{12,28},{16,0},{20,4},{24,8},{28,12},{1,17},{... | collective-permute-start | bytes 1425416 | tf_op jit(solution)/shard_map/ppermute | solution.py:43
  668.2 12.0 %collective-permute-start.60 = (bf16[2,928,128]{2,1,0:T(8,128)(2,1)S(1)}, bf16[2,928,128]{2,1,0:T(8,128)(2,1)S(1)}, u32[]{:S(2)}, u32[]{:S(2)}) collective-permute-start(bf16[2,928,128]{2,1,0:T(8,128)(2,1)S(1)} %fusion.28), channel_id=1, source_target_pairs={{0,1},{1,2},{2,3},{3,0},{4,5},{5,6},{6,7},{7,4},{8,9},{9,10},{10,1... | collective-permute-start | bytes 1425416 | tf_op jit(solution)/shard_map/ppermute | solution.py:52
  680.4 11.5 %collective-permute-start.61 = (bf16[2,928,128]{2,1,0:T(8,128)(2,1)S(1)}, bf16[2,928,128]{2,1,0:T(8,128)(2,1)S(1)}, u32[]{:S(2)}, u32[]{:S(2)}) collective-permute-start(bf16[2,928,128]{2,1,0:T(8,128)(2,1)S(1)} %fusion.1), channel_id=1, source_target_pairs={{0,1},{1,2},{2,3},{3,0},{4,5},{5,6},{6,7},{7,4},{8,9},{9,10},{10,1... | collective-permute-start | bytes 1425416 | tf_op jit(solution)/shard_map/ppermute | solution.py:52
  692.8 10.8 %collective-permute-start.62 = (bf16[2,928,128]{2,1,0:T(8,128)(2,1)}, bf16[2,928,128]{2,1,0:T(8,128)(2,1)}, u32[]{:S(2)}, u32[]{:S(2)}) collective-permute-start(bf16[2,928,128]{2,1,0:T(8,128)(2,1)} %fusion.2), channel_id=1, source_target_pairs={{0,1},{1,2},{2,3},{3,0},{4,5},{5,6},{6,7},{7,4},{8,9},{9,10},{10,1... | collective-permute-start | bytes 1425416 | tf_op jit(solution)/shard_map/ppermute | solution.py:52
  704.9 6.2 collective-permute-start.63
  719.2 3.5 collective-permute-start.66
  722.7 3.5 collective-permute-start.67
  726.3 4.4 collective-permute-start.68
  (84 other events, 598.8 us)
Sparse Core Ops, SparseCore 0:
  11.4 125.6 all-gather.1
